TPU v7x, 32 devices: a whole 2x2x4 slice. The times are simulated.
32 devices in a mesh: gx: 8 (over y, x, core), gy: 4 (over z).
Axes of the slice: x: 2, y: 2, z: 4, core: 2. Of those that a mesh axis runs over, the one named last changes fastest.
Arguments:
- tokens: bfloat16 [3072, 2048], P('gx', 'gy'), may hold values from -40 to 40
- gain: float32 [2048], replicated, may hold values from 0.1 to 1.9
- w_qkv: bfloat16 [2048, 3, 16, 128], P('gx', None, 'gy'), may hold values from -0.176776695 to 0.176776695
- w_out: bfloat16 [2048, 2048], P('gx', 'gy'), may hold values from -0.125 to 0.125
- lengths: int32 [6], replicated, may hold values from 1 to 2048, 3072 in all
Outputs:
- mixed: bfloat16 [3072, 2048], P('gx', 'gy')
- key_cache: bfloat16 [3072, 16, 128], P('gx', 'gy')
- value_cache: bfloat16 [3072, 16, 128], P('gx', 'gy')
Inputs may be any that keep to these rules, and one draw needn't show every extreme that they name: lengths are positive and sum to 3072; the longest is exactly 2048.
All inputs are finite; a program needn't handle non-finite values.
Results may differ from a plain program's by a relative error of at most 0.012.
The roundings to bfloat16 on the way count: a program that leaves them out, or rounds other values in their place, can miss the bound.
Values may be sent and summed in bfloat16 or wider, within the bound.
No kernel may reach another device: no remote copies, remote signals or barrier semaphores. Data moves between devices by JAX's collectives and lax.ppermute only.
A program may use at most 64 MiB of HBM per device.

v0:
```python
import math

import jax
import jax.numpy as jnp
from jax import lax
from jax.sharding import PartitionSpec as P


def rotate(vectors, position):
    half = vectors.shape[-1] // 2
    freq = 10000.0 ** (-(2.0 * jnp.arange(half, dtype=jnp.float32)) / vectors.shape[-1])
    angle = position.astype(jnp.float32)[:, None, None] * freq[None, None, :]
    cosine = jnp.cos(angle)
    sine = jnp.sin(angle)
    first = vectors[..., :half]
    second = vectors[..., half:]
    return jnp.concatenate(
        [first * cosine - second * sine, second * cosine + first * sine], axis=-1
    )


def block_rows(count):
    size = count
    while size > 1024 and size % 2 == 0:
        size = size // 2
    return size


def local(tokens, gain, w_qkv, w_out, lengths):
    tok_dev = tokens.shape[0]
    hloc = w_qkv.shape[2]
    hsize = w_qkv.shape[3]
    whole = lax.all_gather(tokens, "gy", axis=1, tiled=True)
    wide = whole.astype(jnp.float32)
    meansq = jnp.mean(wide * wide, axis=-1, keepdims=True)
    normed = (wide * lax.rsqrt(meansq + 1e-06) * gain[None, :]).astype(jnp.bfloat16)
    piece = lax.all_gather(w_qkv, "gx", axis=0, tiled=True)
    columns = normed
    projected = jnp.dot(
        columns, piece.reshape(piece.shape[0], -1), preferred_element_type=jnp.float32
    )
    projected = projected.reshape(tok_dev, 3, hloc, hsize)
    mine = lax.axis_index("gx")
    glob = mine * tok_dev + jnp.arange(tok_dev, dtype=jnp.int32)
    doc_start = jnp.cumsum(lengths) - lengths
    begin = jnp.max(jnp.where(doc_start[None, :] <= glob[:, None], doc_start[None, :], 0), axis=1)
    position = glob - begin
    query = rotate(projected[:, 0], position).astype(jnp.bfloat16)
    keys_own = rotate(projected[:, 1], position).astype(jnp.bfloat16)
    vals_own = projected[:, 2].astype(jnp.bfloat16)
    scale = 1.0 / math.sqrt(hsize)

    def tile_step(state, keys_blk, vals_blk, first):
        running, totals, accum = state
        kidx = first + jnp.arange(keys_blk.shape[0], dtype=jnp.int32)
        score = (
            jnp.einsum("qhd,khd->hqk", query, keys_blk, preferred_element_type=jnp.float32) * scale
        )
        keep = (kidx[None, :] >= begin[:, None]) & (kidx[None, :] <= glob[:, None])
        score = jnp.where(keep[None], score, -1e30)
        newmax = jnp.maximum(running, jnp.max(score, axis=-1))
        weight = jnp.where(keep[None], jnp.exp(score - newmax[..., None]), 0.0)
        factor = jnp.exp(running - newmax)
        totals = totals * factor + jnp.sum(weight, axis=-1)
        update = jnp.einsum(
            "hqk,khd->hqd",
            weight.astype(jnp.bfloat16),
            vals_blk,
            preferred_element_type=jnp.float32,
        )
        accum = accum * factor[..., None] + update
        return (newmax, totals, accum)

    initial = (
        jnp.full((hloc, tok_dev), -1e30, jnp.float32),
        jnp.zeros((hloc, tok_dev), jnp.float32),
        jnp.zeros((hloc, tok_dev, hsize), jnp.float32),
    )
    keys_piece = lax.all_gather(keys_own, "gx", axis=0, tiled=True)
    vals_piece = lax.all_gather(vals_own, "gx", axis=0, tiled=True)
    count = keys_piece.shape[0]
    size = block_rows(count)

    def one_tile(number, inner):
        first = (number * size).astype(jnp.int32)
        keys_blk = lax.dynamic_slice_in_dim(keys_piece, first, size, 0)
        vals_blk = lax.dynamic_slice_in_dim(vals_piece, first, size, 0)
        return tile_step(inner, keys_blk, vals_blk, first)

    running, totals, accum = lax.fori_loop(0, count // size, one_tile, initial)
    attended = (accum / totals[..., None]).astype(jnp.bfloat16)
    attended = jnp.transpose(attended, (1, 0, 2)).reshape(tok_dev, hloc * hsize)
    all_heads = lax.all_gather(attended, "gy", axis=1, tiled=True)
    columns = all_heads
    mixed = jnp.dot(
        columns, lax.all_gather(w_out, "gx", axis=0, tiled=True), preferred_element_type=jnp.float32
    ).astype(jnp.bfloat16)
    return (mixed, keys_own, vals_own)


def solution(mesh):
    return jax.shard_map(
        local,
        mesh=mesh,
        in_specs=(P("gx", "gy"), P(), P("gx", None, "gy", None), P("gx", "gy"), P()),
        out_specs=(P("gx", "gy"), P("gx", "gy", None), P("gx", "gy", None)),
        check_vma=False,
    )
```

profile of v0, /device:TPU:0, one launch (start us, length us, event | category | flops | bytes accessed | tf_op | source)
XLA Modules:
  0.0 282.4 jit_solution(10697021689812042305)
XLA Ops:
  7.2 0.0 all-gather.8.cloned.1.call-start
  7.2 0.7 all-gather.8.cloned.1.call-update
  7.9 0.0 all-gather.10.cloned.1.call-start
  7.9 0.7 all-gather.10.cloned.1.call-update
  8.6 0.0 all-gather.12.cloned.1.call-start
  8.7 0.8 reduce-window.9
  9.5 0.7 bitcast_subtract_fusion
  10.2 0.1 select_reduce_fusion
  10.3 0.4 multiply_cosine_fusion
  10.7 38.7 %all-gather.8.cloned.1.call-done = bf16[384,2048]{1,0:T(8,128)(2,1)} async-done(((bf16[384,512]{1,0:T(8,128)(2,1)}), bf16[384,2048]{1,0:T(8,128)(2,1)}) %all-gather.8.cloned.1.call-update) | async-done | bytes 1572880 | tf_op jit(solution)/shard_map/all_gather | solution.py:33
  49.4 1.8 fusion.22
  51.2 0.0 copy-start.2
  51.2 44.5 %all-gather.10.cloned.1.call-done = bf16[2048,3,4,128]{3,2,1,0:T(4,128)(2,1)} async-done(((bf16[256,3,4,128]{3,2,1,0:T(4,128)(2,1)}), bf16[2048,3,4,128]{3,2,1,0:T(4,128)(2,1)}) %all-gather.10.cloned.1.call-update) | async-done | bytes 6291472 | tf_op jit(solution)/shard_map/all_gather | solution.py:37
  95.7 10.6 %copy.41 = bf16[2048,3,4,128]{0,3,2,1:T(8,128)(2,1)} copy(bf16[2048,3,4,128]{3,2,1,0:T(4,128)(2,1)} %all-gather.10.cloned.1.call-done) | data formatting | bytes 12582912 | tf_op jit(solution)/shard_map/reshape | solution.py:40
  106.3 0.0 copy-done.2
  106.3 6.2 %fusion.20 = f32[384,3,4,128]{0,3,2,1:T(8,128)S(1)} fusion(bf16[2048,3,4,128]{0,3,2,1:T(8,128)(2,1)} %copy.41, bf16[384,2048]{1,0:T(8,128)(2,1)} %all-gather.8.cloned.1.call-done, f32[2048]{0:T(1024)S(1)} %copy-done.2, f32[384]{0:T(512)S(1)} %add_rsqrt_fusion), kind=kOutput, calls=%fused_computation.25 | convolution fusion | flops 2419064832 | bytes 10233344 | tf_op jit(solution)/shard_map/dot_general | solution.py:39
  112.5 0.1 slice_bitcast_fusion
  112.6 0.2 subtract_convert_fusion
  112.8 0.8 pad_maximum_fusion
  113.6 0.0 all-gather.12.cloned.1.call-update
  113.6 0.0 all-gather.18.cloned.1.call-start
  113.7 0.8 slice.47
  114.5 0.0 all-gather.18.cloned.1.call-update
  114.5 0.0 all-gather.16.cloned.1.call-start
  114.6 0.5 all-gather.16.cloned.1.call-update
  115.1 0.0 all-gather.14.cloned.1.call-start
  115.2 0.2 copy.34
  115.5 31.2 %all-gather.12.cloned.1.call-done = bf16[3072,4,128]{0,2,1:T(8,128)(2,1)} async-done(((bf16[384,4,128]{0,2,1:T(8,128)(2,1)}), bf16[3072,4,128]{0,2,1:T(8,128)(2,1)}) %all-gather.12.cloned.1.call-update) | async-done | bytes 3145744 | tf_op jit(solution)/shard_map/all_gather | solution.py:79
  146.6 35.1 %all-gather.18.cloned.1.call-done = bf16[3072,1,4,128]{0,3,2,1:T(8,128)(2,1)} async-done(((bf16[384,1,4,128]{0,3,2,1:T(8,128)(2,1)}), bf16[3072,1,4,128]{0,3,2,1:T(8,128)(2,1)}) %all-gather.18.cloned.1.call-update) | async-done | bytes 3145744 | tf_op jit(solution)/shard_map/all_gather | solution.py:80
  181.8 50.4 %while.18 = (s32[]{:T(128)}, f32[4,384]{1,0:T(4,128)S(1)}, f32[4,384]{1,0:T(4,128)S(1)}, f32[4,384,128]{2,1,0:T(8,128)}, s32[384]{0:T(512)S(1)}, /*index=5*/bf16...) while((s32[]{:T(128)}, f32[4,384]{1,0:T(4,128)S(1)}, ...), condition=%wide.region_6.7_spmd.clone, body=%wide.region_3.6_spmd.clone.sunk | while | flops 620798592 | bytes 37858016 | solution.py:90
  181.8 0.3 compare_and_fusion.2
  182.1 4.4 %fusion.42 = (f32[4,384]{1,0:T(4,128)S(1)}, f32[4,768,384]{2,1,0:T(8,128)}) fusion(pred[384,768]{0,1:T(8,128)(4,1)S(1)} %compare_and_fusion.2, bf16[384,4,128]{2,0,1:T(8,128)(2,1)S(1)} %get-tuple-element.368, bf16[3072,4,128]{0,2,1:T(8,128)(2,1)} %get-tuple-element.367, s32[]{:T(128)S(6)} %select_n.63), kind=kOutput, calls=%fused_computation.3.clone.1 | convolution fusion | flops 305527296 | bytes 6199300 | tf_op jit(solution)/shard_map/while/body/eval_jaxpr/qhd,khd->hqk/dot_general | solution.py:57
  186.5 0.0 copy-start
  186.5 3.7 %fusion.43 = f32[4,384]{1,0:T(4,128)S(1)} fusion(f32[4,768,384]{2,1,0:T(8,128)} %get-tuple-element.333, f32[4,384]{1,0:T(4,128)S(1)} %select_maximum_fusion.2, pred[384,768]{0,1:T(8,128)(4,1)S(1)} %compare_and_fusion.2), kind=kLoop, calls=%fused_computation.5.clone.1 | loop fusion | flops 5896704 | bytes 5025792 | tf_op jit(solution)/shard_map/while/body/eval_jaxpr/reduce_sum | solution.py:64
  190.2 0.1 copy-done
  190.3 3.9 %fusion.45 = f32[4,384,128]{2,1,0:T(8,128)} fusion(f32[4,768,384]{2,1,0:T(8,128)S(1)} %copy-done, f32[4,384]{1,0:T(4,128)S(1)} %select_maximum_fusion.2, pred[384,768]{0,1:T(8,128)(4,1)S(1)} %compare_and_fusion.2, f32[4,384,128]{2,1,0:T(8,128)} %get-tuple-element.352, bf16[3072,4,128]{0,2,1:T(8,128)(2,1)} %get-tuple-element.369, s32[]{:T(128)S(6)} %select_n.63, ...), kind=kOutput, calls=%fused_computation.8.clone.1 | convolution fusion | flops 308477952 | bytes 7385093 | tf_op jit(solution)/shard_map/while/body/eval_jaxpr/hqk,khd->hqd/dot_general | solution.py:65
  194.2 0.3 compare_and_fusion.2
  194.5 4.4 %fusion.42 = (f32[4,384]{1,0:T(4,128)S(1)}, f32[4,768,384]{2,1,0:T(8,128)}) fusion(pred[384,768]{0,1:T(8,128)(4,1)S(1)} %compare_and_fusion.2, bf16[384,4,128]{2,0,1:T(8,128)(2,1)S(1)} %get-tuple-element.368, bf16[3072,4,128]{0,2,1:T(8,128)(2,1)} %get-tuple-element.367, s32[]{:T(128)S(6)} %select_n.63), kind=kOutput, calls=%fused_computation.3.clone.1 | convolution fusion | flops 305527296 | bytes 6199300 | tf_op jit(solution)/shard_map/while/body/eval_jaxpr/qhd,khd->hqk/dot_general | solution.py:57
  198.9 0.0 copy-start
  198.9 3.7 %fusion.43 = f32[4,384]{1,0:T(4,128)S(1)} fusion(f32[4,768,384]{2,1,0:T(8,128)} %get-tuple-element.333, f32[4,384]{1,0:T(4,128)S(1)} %select_maximum_fusion.2, pred[384,768]{0,1:T(8,128)(4,1)S(1)} %compare_and_fusion.2), kind=kLoop, calls=%fused_computation.5.clone.1 | loop fusion | flops 5896704 | bytes 5025792 | tf_op jit(solution)/shard_map/while/body/eval_jaxpr/reduce_sum | solution.py:64
  202.6 0.4 copy-done
  203.0 4.1 %fusion.45 = f32[4,384,128]{2,1,0:T(8,128)} fusion(f32[4,768,384]{2,1,0:T(8,128)S(1)} %copy-done, f32[4,384]{1,0:T(4,128)S(1)} %select_maximum_fusion.2, pred[384,768]{0,1:T(8,128)(4,1)S(1)} %compare_and_fusion.2, f32[4,384,128]{2,1,0:T(8,128)} %get-tuple-element.352, bf16[3072,4,128]{0,2,1:T(8,128)(2,1)} %get-tuple-element.369, s32[]{:T(128)S(6)} %select_n.63, ...), kind=kOutput, calls=%fused_computation.8.clone.1 | convolution fusion | flops 308477952 | bytes 7385093 | tf_op jit(solution)/shard_map/while/body/eval_jaxpr/hqk,khd->hqd/dot_general | solution.py:65
  207.1 0.3 compare_and_fusion.2
  207.4 4.4 %fusion.42 = (f32[4,384]{1,0:T(4,128)S(1)}, f32[4,768,384]{2,1,0:T(8,128)}) fusion(pred[384,768]{0,1:T(8,128)(4,1)S(1)} %compare_and_fusion.2, bf16[384,4,128]{2,0,1:T(8,128)(2,1)S(1)} %get-tuple-element.368, bf16[3072,4,128]{0,2,1:T(8,128)(2,1)} %get-tuple-element.367, s32[]{:T(128)S(6)} %select_n.63), kind=kOutput, calls=%fused_computation.3.clone.1 | convolution fusion | flops 305527296 | bytes 6199300 | tf_op jit(solution)/shard_map/while/body/eval_jaxpr/qhd,khd->hqk/dot_general | solution.py:57
  211.8 0.0 copy-start
  211.8 3.7 %fusion.43 = f32[4,384]{1,0:T(4,128)S(1)} fusion(f32[4,768,384]{2,1,0:T(8,128)} %get-tuple-element.333, f32[4,384]{1,0:T(4,128)S(1)} %select_maximum_fusion.2, pred[384,768]{0,1:T(8,128)(4,1)S(1)} %compare_and_fusion.2), kind=kLoop, calls=%fused_computation.5.clone.1 | loop fusion | flops 5896704 | bytes 5025792 | tf_op jit(solution)/shard_map/while/body/eval_jaxpr/reduce_sum | solution.py:64
  215.5 0.1 copy-done
  215.6 4.1 %fusion.45 = f32[4,384,128]{2,1,0:T(8,128)} fusion(f32[4,768,384]{2,1,0:T(8,128)S(1)} %copy-done, f32[4,384]{1,0:T(4,128)S(1)} %select_maximum_fusion.2, pred[384,768]{0,1:T(8,128)(4,1)S(1)} %compare_and_fusion.2, f32[4,384,128]{2,1,0:T(8,128)} %get-tuple-element.352, bf16[3072,4,128]{0,2,1:T(8,128)(2,1)} %get-tuple-element.369, s32[]{:T(128)S(6)} %select_n.63, ...), kind=kOutput, calls=%fused_computation.8.clone.1 | convolution fusion | flops 308477952 | bytes 7385093 | tf_op jit(solution)/shard_map/while/body/eval_jaxpr/hqk,khd->hqd/dot_general | solution.py:65
  219.7 0.3 compare_and_fusion.2
  220.0 4.4 %fusion.42 = (f32[4,384]{1,0:T(4,128)S(1)}, f32[4,768,384]{2,1,0:T(8,128)}) fusion(pred[384,768]{0,1:T(8,128)(4,1)S(1)} %compare_and_fusion.2, bf16[384,4,128]{2,0,1:T(8,128)(2,1)S(1)} %get-tuple-element.368, bf16[3072,4,128]{0,2,1:T(8,128)(2,1)} %get-tuple-element.367, s32[]{:T(128)S(6)} %select_n.63), kind=kOutput, calls=%fused_computation.3.clone.1 | convolution fusion | flops 305527296 | bytes 6199300 | tf_op jit(solution)/shard_map/while/body/eval_jaxpr/qhd,khd->hqk/dot_general | solution.py:57
  224.4 0.0 copy-start
  224.4 3.7 %fusion.43 = f32[4,384]{1,0:T(4,128)S(1)} fusion(f32[4,768,384]{2,1,0:T(8,128)} %get-tuple-element.333, f32[4,384]{1,0:T(4,128)S(1)} %select_maximum_fusion.2, pred[384,768]{0,1:T(8,128)(4,1)S(1)} %compare_and_fusion.2), kind=kLoop, calls=%fused_computation.5.clone.1 | loop fusion | flops 5896704 | bytes 5025792 | tf_op jit(solution)/shard_map/while/body/eval_jaxpr/reduce_sum | solution.py:64
  228.1 0.1 copy-done
  228.1 4.1 %fusion.45 = f32[4,384,128]{2,1,0:T(8,128)} fusion(f32[4,768,384]{2,1,0:T(8,128)S(1)} %copy-done, f32[4,384]{1,0:T(4,128)S(1)} %select_maximum_fusion.2, pred[384,768]{0,1:T(8,128)(4,1)S(1)} %compare_and_fusion.2, f32[4,384,128]{2,1,0:T(8,128)} %get-tuple-element.352, bf16[3072,4,128]{0,2,1:T(8,128)(2,1)} %get-tuple-element.369, s32[]{:T(128)S(6)} %select_n.63, ...), kind=kOutput, calls=%fused_computation.8.clone.1 | convolution fusion | flops 308477952 | bytes 7385093 | tf_op jit(solution)/shard_map/while/body/eval_jaxpr/hqk,khd->hqd/dot_general | solution.py:65
  232.2 0.0 copy-start.1
  232.2 1.4 copy.36
  233.7 0.8 divide_convert_fusion
  234.5 0.0 all-gather.14.cloned.1.call-update
  234.5 0.0 copy-done.1
  234.5 1.0 copy.37
  235.5 1.0 copy.38
  236.5 0.0 all-gather.16.cloned.1.call-done
  236.5 35.2 %all-gather.14.cloned.1.call-done = bf16[384,2048]{0,1:T(8,128)(2,1)} async-done(((bf16[384,512]{0,1:T(8,128)(2,1)}), bf16[384,2048]{0,1:T(8,128)(2,1)}) %all-gather.14.cloned.1.call-update) | async-done | bytes 1572880 | tf_op jit(solution)/shard_map/all_gather | solution.py:93
  271.7 3.8 %convolution_convert_fusion = bf16[384,512]{1,0:T(8,128)(2,1)} fusion(bf16[384,2048]{0,1:T(8,128)(2,1)} %all-gather.14.cloned.1.call-done, bf16[2048,512]{1,0:T(8,128)(2,1)} %all-gather.16.cloned.1.call-done), kind=kOutput, calls=%fused_computation.35 | convolution fusion | flops 805502976 | bytes 4063232 | tf_op jit(solution)/shard_map/dot_general | solution.py:95
  (29 shorter events, 0.3 us)
Async XLA Ops:
  7.2 42.2 %all-gather.8.cloned.1.call-start = ((), (), s32[]{:S(2)}) async-start(), calls=%async_computation | async-start | bytes 1966080 | tf_op jit(solution)/shard_map/all_gather | solution.py:33
  7.9 87.8 %all-gather.10.cloned.1.call-start = ((), (), s32[]{:S(2)}) async-start(), calls=%async_computation.1 | async-start | bytes 7077888 | tf_op jit(solution)/shard_map/all_gather | solution.py:37
  8.6 138.0 %all-gather.12.cloned.1.call-start = ((), (), s32[]{:S(2)}) async-start(), calls=%async_computation.2 | async-start | bytes 3538944 | tf_op jit(solution)/shard_map/all_gather | solution.py:79
  51.2 55.1 %copy-start.2 = (f32[2048]{0:T(1024)S(1)}, f32[2048]{0:T(1024)}, u32[]{:S(2)}) copy-start(f32[2048]{0:T(1024)} %param.8) | copy-start | bytes 24580
  113.6 68.1 %all-gather.18.cloned.1.call-start = ((), (), s32[]{:S(2)}) async-start(), calls=%async_computation.5 | async-start | bytes 3538944 | tf_op jit(solution)/shard_map/all_gather | solution.py:80
  114.5 122.0 %all-gather.16.cloned.1.call-start = ((), (), s32[]{:S(2)}) async-start(), calls=%async_computation.4 | async-start | bytes 2359296 | tf_op jit(solution)/shard_map/all_gather | solution.py:96
  115.1 156.6 %all-gather.14.cloned.1.call-start = ((), (), s32[]{:S(2)}) async-start(), calls=%async_computation.3 | async-start | bytes 1966080 | tf_op jit(solution)/shard_map/all_gather | solution.py:93
  186.5 3.8 %copy-start = (f32[4,768,384]{2,1,0:T(8,128)S(1)}, f32[4,768,384]{2,1,0:T(8,128)}, u32[]{:S(2)}) copy-start(f32[4,768,384]{2,1,0:T(8,128)} %get-tuple-element.333) | copy-start | bytes 14155780 | tf_op jit(solution)/shard_map/while
  198.9 4.1 %copy-start = (f32[4,768,384]{2,1,0:T(8,128)S(1)}, f32[4,768,384]{2,1,0:T(8,128)}, u32[]{:S(2)}) copy-start(f32[4,768,384]{2,1,0:T(8,128)} %get-tuple-element.333) | copy-start | bytes 14155780 | tf_op jit(solution)/shard_map/while
  211.8 3.8 %copy-start = (f32[4,768,384]{2,1,0:T(8,128)S(1)}, f32[4,768,384]{2,1,0:T(8,128)}, u32[]{:S(2)}) copy-start(f32[4,768,384]{2,1,0:T(8,128)} %get-tuple-element.333) | copy-start | bytes 14155780 | tf_op jit(solution)/shard_map/while
  224.4 3.8 %copy-start = (f32[4,768,384]{2,1,0:T(8,128)S(1)}, f32[4,768,384]{2,1,0:T(8,128)}, u32[]{:S(2)}) copy-start(f32[4,768,384]{2,1,0:T(8,128)} %get-tuple-element.333) | copy-start | bytes 14155780 | tf_op jit(solution)/shard_map/while
  232.2 2.3 copy-start.1
Sparse Core Ops, SparseCore 0:
  9.6 39.7 all-gather.7
  51.3 44.3 all-gather.9
  113.8 32.8 all-gather.11
  148.9 32.8 all-gather.17
  183.5 27.8 all-gather.15
  234.6 37.0 all-gather.13
where the time goes:
time: 283 us; the launch traced here: 282 us
  waiting for transfers between devices  187 us (66%)
  matrix products  43.8 us (15%)
  other arithmetic  21.6 us (8%)
  local copies, waits for them, and re-layouts  15.9 us (6%)
  between operations  14.2 us (5%)
    all_gather x1, waiting for transfers between devices, local(): piece = lax.all_gather(w_qkv, 'gx', axis=0, tiled=True)  44.5 us
    all_gather x1, waiting for transfers between devices, local(): whole = lax.all_gather(tokens, 'gy', axis=1, tiled=True)  38.7 us
    all_gather x1, waiting for transfers between devices, local(): all_heads = lax.all_gather(attended, 'gy', axis=1, tiled=True)  35.2 us
    all_gather x1, waiting for transfers between devices, local(): vals_piece = lax.all_gather(vals_own, 'gx', axis=0, tiled=True)  35.1 us
    all_gather x1, waiting for transfers between devices, local(): keys_piece = lax.all_gather(keys_own, 'gx', axis=0, tiled=True)  31.2 us
    dot_general x4, matrix products, tile_step(): jnp.einsum('qhd,khd->hqk', query, keys_blk, preferred_element_type=jnp.fl...  17.7 us
    dot_general x4, matrix products, tile_step(): jnp.einsum('hqk,khd->hqd', weight.astype(jnp.bfloat16), vals_blk, preferr...  16.1 us
    reduce_sum x4, other arithmetic, tile_step(): totals = totals * factor + jnp.sum(weight, axis=-1)  14.6 us
  transfers between devices with their start and end apart: 6, of which 5 were waited for; matrix products, arithmetic and copies ran while one was open for 21% of the time, Pallas kernels for 0%

commit v1 on v0

v1 whole, which is shorter than its diff:
```python
import functools
import math

import jax
import jax.numpy as jnp
from jax import lax
from jax.experimental import pallas as pl
from jax.experimental.pallas import tpu as pltpu
from jax.sharding import PartitionSpec as P


def tables(position, hsize):
    half = hsize // 2
    freq = 10000.0 ** (-(2.0 * jnp.arange(half, dtype=jnp.float32)) / hsize)
    angle = position.astype(jnp.float32)[:, None] * freq[None, :]
    return jnp.cos(angle), jnp.sin(angle)


def rotate(vectors, position):
    half = vectors.shape[-1] // 2
    cosine, sine = tables(position, vectors.shape[-1])
    cosine, sine = cosine[:, None, :], sine[:, None, :]
    first = vectors[..., :half]
    second = vectors[..., half:]
    return jnp.concatenate(
        [first * cosine - second * sine, second * cosine + first * sine], axis=-1
    )


def begins(lengths, glob):
    doc_start = jnp.cumsum(lengths) - lengths
    return jnp.max(jnp.where(doc_start[None, :] <= glob[:, None], doc_start[None, :], 0), axis=1)


def block_rows(count):
    size = count
    while size > 1024 and size % 2 == 0:
        size = size // 2
    return size


def general(tokens, gain, w_qkv, w_out, lengths):
    tok_dev = tokens.shape[0]
    hloc = w_qkv.shape[2]
    hsize = w_qkv.shape[3]
    whole = lax.all_gather(tokens, "gy", axis=1, tiled=True)
    wide = whole.astype(jnp.float32)
    meansq = jnp.mean(wide * wide, axis=-1, keepdims=True)
    normed = (wide * lax.rsqrt(meansq + 1e-06) * gain[None, :]).astype(jnp.bfloat16)
    piece = lax.all_gather(w_qkv, "gx", axis=0, tiled=True)
    projected = jnp.dot(
        normed, piece.reshape(piece.shape[0], -1), preferred_element_type=jnp.float32
    )
    projected = projected.reshape(tok_dev, 3, hloc, hsize)
    mine = lax.axis_index("gx")
    glob = mine * tok_dev + jnp.arange(tok_dev, dtype=jnp.int32)
    begin = begins(lengths, glob)
    position = glob - begin
    query = rotate(projected[:, 0], position).astype(jnp.bfloat16)
    keys_own = rotate(projected[:, 1], position).astype(jnp.bfloat16)
    vals_own = projected[:, 2].astype(jnp.bfloat16)
    scale = 1.0 / math.sqrt(hsize)
    initial = (
        jnp.full((hloc, tok_dev), -1e30, jnp.float32),
        jnp.zeros((hloc, tok_dev), jnp.float32),
        jnp.zeros((hloc, tok_dev, hsize), jnp.float32),
    )
    keys_piece = lax.all_gather(keys_own, "gx", axis=0, tiled=True)
    vals_piece = lax.all_gather(vals_own, "gx", axis=0, tiled=True)
    count = keys_piece.shape[0]
    size = block_rows(count)

    def one_tile(number, state):
        running, totals, accum = state
        first = (number * size).astype(jnp.int32)
        keys_blk = lax.dynamic_slice_in_dim(keys_piece, first, size, 0)
        vals_blk = lax.dynamic_slice_in_dim(vals_piece, first, size, 0)
        kidx = first + jnp.arange(size, dtype=jnp.int32)
        score = (
            jnp.einsum("qhd,khd->hqk", query, keys_blk, preferred_element_type=jnp.float32) * scale
        )
        keep = (kidx[None, :] >= begin[:, None]) & (kidx[None, :] <= glob[:, None])
        score = jnp.where(keep[None], score, -1e30)
        newmax = jnp.maximum(running, jnp.max(score, axis=-1))
        weight = jnp.where(keep[None], jnp.exp(score - newmax[..., None]), 0.0)
        factor = jnp.exp(running - newmax)
        totals = totals * factor + jnp.sum(weight, axis=-1)
        update = jnp.einsum(
            "hqk,khd->hqd",
            weight.astype(jnp.bfloat16),
            vals_blk,
            preferred_element_type=jnp.float32,
        )
        accum = accum * factor[..., None] + update
        return (newmax, totals, accum)

    running, totals, accum = lax.fori_loop(0, count // size, one_tile, initial)
    attended = (accum / totals[..., None]).astype(jnp.bfloat16)
    attended = jnp.transpose(attended, (1, 0, 2)).reshape(tok_dev, hloc * hsize)
    all_heads = lax.all_gather(attended, "gy", axis=1, tiled=True)
    mixed = jnp.dot(
        all_heads, lax.all_gather(w_out, "gx", axis=0, tiled=True),
        preferred_element_type=jnp.float32,
    ).astype(jnp.bfloat16)
    return (mixed, keys_own, vals_own)


LINE = 4
CHIPS = 4


def swap(x, mask):
    return lax.ppermute(x, "gx", [(i, i ^ mask) for i in range(2 * CHIPS)])


def up(x, least):
    return lax.ppermute(x, "gy", [(i, i + 1) for i in range(least, LINE - 1)])


def down(x, most):
    return lax.ppermute(x, "gy", [(i, i - 1) for i in range(most, 0, -1)])


def along_line(x):
    u1, d1 = up(x, 0), down(x, 3)
    u2, d2 = up(u1, 1), down(d1, 2)
    u3, d3 = up(u2, 2), down(d2, 1)
    return (u1, u2, u3), (d1, d2, d3)


def vmem():
    return pl.BlockSpec(memory_space=pltpu.VMEM)


def project_kernel(
    where_ref, own, u1, u2, u3, d1, d2, d3, gain_ref, cos_ref, sin_ref,
    wa0, wa1, wa2, wa3, wa4, wb0, wb1, wb2, wb3, wb4,
    o0, o1, o2, o3, key_ref, val_ref,
    x_ref, slot_ref,
):
    step = pl.program_id(0)
    chip, core, line = where_ref[0], where_ref[1], where_ref[2]
    wide = own.shape[1]

    @pl.when(step == 0)
    def _():
        raw = [
            own[...].astype(jnp.float32),
            jnp.where(line >= 1, u1[...], d3[...]).astype(jnp.float32),
            jnp.where(line >= 2, u2[...], d2[...]).astype(jnp.float32),
            jnp.where(line >= 3, u3[...], d1[...]).astype(jnp.float32),
        ]
        square = sum(jnp.sum(r * r, axis=1, keepdims=True) for r in raw)
        scale = lax.rsqrt(square * (1.0 / (LINE * wide)) + 1e-06)
        for d in range(LINE):
            feature = (line - d) & 3
            normed = (raw[d] * scale * gain_ref[feature]).astype(jnp.bfloat16)
            x_ref[2 * d] = normed[:, : wide // 2]
            x_ref[2 * d + 1] = normed[:, wide // 2 :]

    total = None
    for half, refs in ((core, (wa0, wa1, wa2, wa3, wa4)), (1 - core, (wb0, wb1, wb2, wb3, wb4))):
        for m in range(CHIPS):
            x = x_ref[2 * ((line - (chip ^ m)) & 3) + half]
            if m < 3:
                parts = [(x, refs[m])]
            else:
                parts = [(x[:, : wide // 4], refs[3]), (x[:, wide // 4 :], refs[4])]
            for left, right in parts:
                part = jnp.dot(left, right[...], preferred_element_type=jnp.float32)
                total = part if total is None else total + part

    hsize = cos_ref.shape[1]

    @pl.when(step < 2)
    def _():
        for h in range(CHIPS):
            u = total[:, h * hsize : (h + 1) * hsize]
            u = u * cos_ref[...] + pltpu.roll(u, hsize // 2, 1) * sin_ref[...]
            slot_ref[h] = u.astype(jnp.bfloat16)

    @pl.when(step == 2)
    def _():
        for h in range(CHIPS):
            slot_ref[h] = total[:, h * hsize : (h + 1) * hsize].astype(jnp.bfloat16)

    for m, out in enumerate((o0, o1, o2, o3)):
        out[0] = slot_ref[chip ^ m]

    @pl.when(step == 1)
    def _():
        for h in range(CHIPS):
            key_ref[:, h * hsize : (h + 1) * hsize] = slot_ref[h]

    @pl.when(step == 2)
    def _():
        for h in range(CHIPS):
            val_ref[:, h * hsize : (h + 1) * hsize] = slot_ref[h]


def project(where, raw, gain, cosine, sine, weights):
    rows, wide = raw[0].shape
    hsize = cosine.shape[1]
    whole = lambda a: pl.BlockSpec(a.shape, lambda j, s: (0,) * a.ndim)
    cols = weights[0].shape[1] // 3
    return pl.pallas_call(
        project_kernel,
        grid_spec=pltpu.PrefetchScalarGridSpec(
            num_scalar_prefetch=1,
            grid=(3,),
            in_specs=[whole(a) for a in (*raw, gain, cosine, sine)]
            + [pl.BlockSpec((w.shape[0], cols), lambda j, s: (0, j)) for w in weights],
            out_specs=[pl.BlockSpec((1, rows, hsize), lambda j, s: (j, 0, 0))] * CHIPS
            + [pl.BlockSpec((rows, cols), lambda j, s: (0, 0))] * 2,
            scratch_shapes=[
                pltpu.VMEM((2 * LINE, rows, wide // 2), jnp.bfloat16),
                pltpu.VMEM((CHIPS, rows, hsize), jnp.bfloat16),
            ],
        ),
        out_shape=[jax.ShapeDtypeStruct((3, rows, hsize), jnp.bfloat16)] * CHIPS
        + [jax.ShapeDtypeStruct((rows, cols), jnp.bfloat16)] * 2,
        compiler_params=pltpu.CompilerParams(vmem_limit_bytes=48 << 20),
        name="project",
    )(where, *raw, gain, cosine, sine, *weights)


def attend_kernel(
    where_ref, start_ref, low_ref, a0, a1, a2, a3, b0, b1, b2, b3, o0, o1, o2, o3,
    keys, vals, sem, *, scale,
):
    chip, core = where_ref[0], where_ref[1]
    rows, hsize = a0.shape[1], a0.shape[2]
    copies = []
    for part, refs in ((0, (a0, a1, a2, a3)), (1, (b0, b1, b2, b3))):
        for m, ref in enumerate(refs):
            block = 2 * (chip ^ m) + (core if part == 0 else 1 - core)
            keys[block] = ref[1]
            vals[block] = ref[2]
    docs = start_ref.shape[0]
    for m, (ref, out) in enumerate(((a0, o0), (a1, o1), (a2, o2), (a3, o3))):
        block = 2 * (chip ^ m) + core
        query = ref[0]
        qpos = block * rows + lax.broadcasted_iota(jnp.int32, (rows, 1), 0)
        begin = jnp.zeros((rows, 1), jnp.int32)
        for d in range(docs):
            begin = jnp.where(start_ref[d] <= qpos, start_ref[d], begin)

        def tile(number, state, block=block, query=query, qpos=qpos, begin=begin):
            running, totals, accum = state
            kv = block - number
            kpos = kv * rows + lax.broadcasted_iota(jnp.int32, (1, rows), 1)
            score = scale * lax.dot_general(
                query, keys[kv], (((1,), (1,)), ((), ())), preferred_element_type=jnp.float32
            )
            keep = (kpos >= begin) & (kpos <= qpos)
            score = jnp.where(keep, score, -1e30)
            newmax = jnp.maximum(running, jnp.max(score, axis=1, keepdims=True))
            weight = jnp.exp(score - newmax)
            factor = jnp.exp(running - newmax)
            totals = totals * factor + jnp.sum(weight, axis=1, keepdims=True)
            accum = accum * factor + jnp.dot(
                weight.astype(jnp.bfloat16), vals[kv], preferred_element_type=jnp.float32
            )
            return newmax, totals, accum

        state = (
            jnp.full((rows, 1), -1e30, jnp.float32),
            jnp.zeros((rows, 1), jnp.float32),
            jnp.zeros((rows, hsize), jnp.float32),
        )
        running, totals, accum = lax.fori_loop(0, block - low_ref[block] + 1, tile, state)
        out[...] = (accum / totals).astype(jnp.bfloat16)


def attend(where, starts, low, own, sibling, scale):
    rows, hsize = own[0].shape[1:]
    smem = pl.BlockSpec(memory_space=pltpu.SMEM)
    return pl.pallas_call(
        functools.partial(attend_kernel, scale=scale),
        in_specs=[smem] * 3 + [vmem()] * (2 * CHIPS),
        out_specs=[vmem()] * CHIPS,
        out_shape=[jax.ShapeDtypeStruct((rows, hsize), jnp.bfloat16)] * CHIPS,
        scratch_shapes=[
            pltpu.VMEM((2 * CHIPS, rows, hsize), jnp.bfloat16),
            pltpu.VMEM((2 * CHIPS, rows, hsize), jnp.bfloat16),
            pltpu.SemaphoreType.DMA,
        ],
        compiler_params=pltpu.CompilerParams(vmem_limit_bytes=48 << 20),
        name="attend",
    )(where, starts, low, *own, *sibling)


def mix_kernel(where_ref, own, u1, u2, u3, d1, d2, d3, w_ref, out_ref):
    line = where_ref[2]
    blocks = [
        own[...],
        jnp.where(line >= 1, u1[...], d3[...]),
        jnp.where(line >= 2, u2[...], d2[...]),
        jnp.where(line >= 3, u3[...], d1[...]),
    ]
    total = None
    for d in range(LINE):
        part = jnp.dot(blocks[d], w_ref[(line - d) & 3], preferred_element_type=jnp.float32)
        total = part if total is None else total + part
    out_ref[...] = total.astype(jnp.bfloat16)


def mix(where, raw, w_all):
    return pl.pallas_call(
        mix_kernel,
        in_specs=[pl.BlockSpec(memory_space=pltpu.SMEM)] + [vmem()] * 8,
        out_specs=vmem(),
        out_shape=jax.ShapeDtypeStruct((raw[0].shape[0], w_all.shape[2]), jnp.bfloat16),
        compiler_params=pltpu.CompilerParams(vmem_limit_bytes=48 << 20),
        name="mix",
    )(where, *raw, w_all)


def blocks_plan(tokens, gain, w_qkv, w_out, lengths):
    rows, wide = tokens.shape
    depth, _, heads, hsize = w_qkv.shape
    mine = lax.axis_index("gx")
    line = lax.axis_index("gy")
    chip, core = mine // 2, mine % 2
    where = jnp.stack([chip, core, line]).astype(jnp.int32)

    ups, downs = along_line(tokens)

    flat = w_qkv.reshape(depth, 3 * heads * hsize)
    across, along = swap(flat, 2), swap(flat, 4)
    half = depth // 2
    far = (swap(along[:half], 2), swap(across[half:], 4))
    held = (flat, across, along, *far)
    weights = held + tuple(swap(w, 1) for w in held)

    glob = mine * rows + jnp.arange(rows, dtype=jnp.int32)
    cosine, sine = tables(glob - begins(lengths, glob), hsize)
    cosine = jnp.concatenate([cosine, cosine], axis=1)
    sine = jnp.concatenate([-sine, sine], axis=1)
    starts = (jnp.cumsum(lengths) - lengths).astype(jnp.int32)
    firsts = jnp.arange(2 * CHIPS, dtype=jnp.int32) * rows
    low = (begins(lengths, firsts) // rows).astype(jnp.int32)

    *sent, keys, vals = project(
        where, (tokens, *ups, *downs), gain.reshape(LINE, 1, wide), cosine, sine, weights
    )
    own = [sent[0]] + [swap(sent[m], 2 * m) for m in range(1, CHIPS)]
    sibling = [swap(a, 1) for a in own]
    heads_out = attend(where, starts, low, own, sibling, 1.0 / math.sqrt(hsize))
    back = [heads_out[0]] + [swap(heads_out[m], 2 * m) for m in range(1, CHIPS)]

    odd, high = (chip & 1) == 1, (chip & 2) == 2
    pairs = []
    for a, b in ((back[0], back[1]), (back[2], back[3])):
        pairs.append(jnp.concatenate([jnp.where(odd, b, a), jnp.where(odd, a, b)], axis=1))
    attended = jnp.concatenate(
        [jnp.where(high, pairs[1], pairs[0]), jnp.where(high, pairs[0], pairs[1])], axis=1
    )
    w_late, attended = lax.optimization_barrier((w_out, attended))
    w_all = lax.all_gather(w_late, "gx", axis=0, tiled=True)
    ups, downs = along_line(attended)
    mixed = mix(where, (attended, *ups, *downs), w_all.reshape(LINE, wide, w_out.shape[1]))
    return (mixed, keys.reshape(rows, heads, hsize), vals.reshape(rows, heads, hsize))


def local(sizes, tokens, gain, w_qkv, w_out, lengths):
    heads = w_qkv.shape[2]
    fits = sizes == (2 * CHIPS, LINE) and heads == CHIPS and tokens.shape[1] == 2 * w_qkv.shape[0]
    plan = blocks_plan if fits else general
    return plan(tokens, gain, w_qkv, w_out, lengths)


def solution(mesh):
    sizes = (mesh.shape["gx"], mesh.shape["gy"])
    return jax.shard_map(
        functools.partial(local, sizes),
        mesh=mesh,
        in_specs=(P("gx", "gy"), P(), P("gx", None, "gy", None), P("gx", "gy"), P()),
        out_specs=(P("gx", "gy"), P("gx", "gy", None), P("gx", "gy", None)),
        check_vma=False,
    )
```

time: 283 us -> 146 us (0.52)
  waiting for transfers between devices: 187 us -> 69.8 us
  matrix products: 43.8 us -> 0 us
  starting transfers between devices: 0.24 us -> 29.2 us
  Pallas kernels: 0 us -> 18.1 us
  other arithmetic: 21.6 us -> 4.24 us
  local copies, waits for them, and re-layouts: 15.9 us -> 10.5 us
    all_gather x6 -> x1, waiting for transfers between devices: 185 us -> 0.01 us  [blocks_plan(): w_all = lax.all_gather(w_late, 'gx', axis=0, tiled=True)]
    ppermute x0 -> x31, waiting for transfers between devices: none -> 69.8 us  [the longest x6 36.9 us: down(): return lax.ppermute(x, 'gy', [(i, i - 1) for i in range(most, 0, -1)])]
    dot_general x10 -> x0, matrix products: 43.8 us -> none  [the longest x4 17.7 us: tile_step(): jnp.einsum('qhd,khd->hqk', query, keys_blk, preferred_element_type=jnp.fl...]
    ppermute x0 -> x31, starting transfers between devices: none -> 29.1 us  [the longest x19 13.7 us: swap(): return lax.ppermute(x, 'gx', [(i, i ^ mask) for i in range(2 * CHIPS)])]
    pallas_call x0 -> x3, Pallas kernels: none -> 18.1 us  [the longest x1 8.69 us: attend(): pl.pallas_call(functools.partial(attend_kernel, scale=scale), in_specs=[s...]
    reduce_sum x5 -> x0, other arithmetic: 16.4 us -> none  [the longest x4 14.6 us: tile_step(): totals = totals * factor + jnp.sum(weight, axis=-1)]
    reshape x1 -> x3, local copies, waits for them, and re-layouts: 10.6 us -> 4.08 us  [the longest x1 2.4 us: blocks_plan(): flat = w_qkv.reshape(depth, 3 * heads * hsize)]
  transfers between devices with their start and end apart: 6 -> 32, of which waited for: 5 -> 16; matrix products, arithmetic and copies ran while one was open for 21% -> 5% of each run, Pallas kernels for 0% -> 0%
where the time goes in v1:
time: 146 us
  waiting for transfers between devices  69.8 us (48%)
  starting transfers between devices  29.2 us (20%)
  Pallas kernels  18.1 us (12%)
  between operations  14.3 us (10%)
  local copies, waits for them, and re-layouts  10.5 us (7%)
  other arithmetic  4.24 us (3%)
    ppermute x6, waiting for transfers between devices, down(): return lax.ppermute(x, 'gy', [(i, i - 1) for i in range(most, 0, -1)])  36.9 us
    ppermute x19, waiting for transfers between devices, swap(): return lax.ppermute(x, 'gx', [(i, i ^ mask) for i in range(2 * CHIPS)])  18.6 us
    ppermute x6, waiting for transfers between devices, up(): return lax.ppermute(x, 'gy', [(i, i + 1) for i in range(least, LINE - 1)])  14.2 us
    ppermute x19, starting transfers between devices, swap(): return lax.ppermute(x, 'gx', [(i, i ^ mask) for i in range(2 * CHIPS)])  13.7 us
    pallas_call x1, Pallas kernels, attend(): pl.pallas_call(functools.partial(attend_kernel, scale=scale), in_specs=[s...  8.69 us
    ppermute x6, starting transfers between devices, down(): return lax.ppermute(x, 'gy', [(i, i - 1) for i in range(most, 0, -1)])  7.71 us
    ppermute x6, starting transfers between devices, up(): return lax.ppermute(x, 'gy', [(i, i + 1) for i in range(least, LINE - 1)])  7.68 us
    pallas_call x1, Pallas kernels, project(): pl.pallas_call(project_kernel, grid_spec=pltpu.PrefetchScalarGridSpec(num...  7.14 us
  transfers between devices with their start and end apart: 32, of which 16 were waited for; matrix products, arithmetic and copies ran while one was open for 5% of the time, Pallas kernels for 0%

profile of v1, /device:TPU:0, one launch (start us, length us, event | category | flops | bytes accessed | tf_op | source)
XLA Modules:
  0.0 146.1 jit_solution(10940998420172143170)
XLA Ops:
  7.2 2.4 %reshape.72.wa0 = bf16[256,1536]{1,0:T(8,128)(2,1)} reshape(bf16[256,3,4,128]{3,2,1,0:T(4,128)(2,1)} %param.7) | data formatting | bytes 1572864 | tf_op jit(solution)/shard_map/reshape | solution.py:329
  9.6 3.0 %collective-permute-start.7 = (bf16[256,1536]{1,0:T(8,128)(2,1)}, bf16[256,1536]{1,0:T(8,128)(2,1)S(1)}, u32[]{:S(2)}, u32[]{:S(2)}) collective-permute-start(bf16[256,1536]{1,0:T(8,128)(2,1)} %reshape.72.wa0), channel_id=1, source_target_pairs={{0,16},{4,20},{8,24},{12,28},{16,0},{20,4},{24,8},{28,12},{1,17},{... | collective-permute-start | bytes 2359304 | tf_op jit(solution)/shard_map/ppermute | solution.py:113
  12.6 1.5 %collective-permute-start.6 = (bf16[256,1536]{1,0:T(8,128)(2,1)}, bf16[256,1536]{1,0:T(8,128)(2,1)}, u32[]{:S(2)}, u32[]{:S(2)}) collective-permute-start(bf16[256,1536]{1,0:T(8,128)(2,1)} %reshape.72.wa0), channel_id=1, source_target_pairs={{0,8},{4,12},{8,0},{12,4},{16,24},{20,28},{24,16},{28,20},{1,9},{5... | collective-permute-start | bytes 2359304 | tf_op jit(solution)/shard_map/ppermute | solution.py:113
  14.1 3.5 %collective-permute-start = (bf16[384,512]{1,0:T(8,128)(2,1)}, bf16[384,512]{1,0:T(8,128)(2,1)S(1)}, u32[]{:S(2)}, u32[]{:S(2)}) collective-permute-start(bf16[384,512]{1,0:T(8,128)(2,1)} %own.1), channel_id=1, source_target_pairs={{0,1},{1,2},{2,3},{4,5},{5,6},{6,7},{8,9},{9,10},{10,11},{12,13},{... | collective-permute-start | bytes 1179656 | tf_op jit(solution)/shard_map/ppermute | solution.py:117
  17.6 1.3 collective-permute-start.3
  18.9 0.1 collective-permute-start.10
  19.0 6.7 %collective-permute-done.u1 = bf16[384,512]{1,0:T(8,128)(2,1)S(1)} collective-permute-done((bf16[384,512]{1,0:T(8,128)(2,1)}, bf16[384,512]{1,0:T(8,128)(2,1)S(1)}, u32[]{:S(2)}, u32[]{:S(2)}) %collective-permute-start) | collective-permute-done | bytes 393248 | tf_op jit(solution)/shard_map/ppermute | solution.py:117
  25.7 0.7 collective-permute-start.1
  26.4 3.3 %collective-permute-done.3.d1 = bf16[384,512]{1,0:T(8,128)(2,1)S(1)} collective-permute-done((bf16[384,512]{1,0:T(8,128)(2,1)}, bf16[384,512]{1,0:T(8,128)(2,1)S(1)}, u32[]{:S(2)}, u32[]{:S(2)}) %collective-permute-start.3) | collective-permute-done | bytes 393248 | tf_op jit(solution)/shard_map/ppermute | solution.py:121
  29.7 1.3 collective-permute-start.4
  31.0 0.8 reduce-window.9
  31.9 0.7 bitcast_subtract_fusion.start_ref
  32.5 0.9 copy-done.5
  33.4 0.6 collective-permute-start.8
  34.0 1.8 %slice.9 = bf16[128,1536]{1,0:T(8,128)(2,1)} slice(bf16[256,1536]{1,0:T(8,128)(2,1)} %collective-permute-done.6.wa1), slice={[128:256], [0:1536]} | slice | bytes 786432 | tf_op jit(solution)/shard_map/slice | solution.py:332
  35.8 0.5 collective-permute-start.9
  36.3 0.7 collective-permute-start.2
  37.0 0.7 select_reduce_fusion
  37.7 3.2 %collective-permute-done.4.d2 = bf16[384,512]{1,0:T(8,128)(2,1)S(1)} collective-permute-done((bf16[384,512]{1,0:T(8,128)(2,1)S(1)}, bf16[384,512]{1,0:T(8,128)(2,1)S(1)}, u32[]{:S(2)}, u32[]{:S(2)}) %collective-permute-start.4) | collective-permute-done | bytes 393248 | tf_op jit(solution)/shard_map/ppermute | solution.py:121
  40.9 0.7 subtract_convert_fusion
  41.6 1.0 collective-permute-done.8.wa3
  42.7 1.3 collective-permute-start.5
  44.0 0.9 collective-permute-done.9.wa4
  44.9 0.5 collective-permute-start.14
  45.4 0.1 pad_add_fusion.where_ref
  45.5 0.8 fusion
  46.3 0.2 pad_maximum_fusion.1
  46.5 8.6 %collective-permute-done.5.d3 = bf16[384,512]{1,0:T(8,128)(2,1)S(1)} collective-permute-done((bf16[384,512]{1,0:T(8,128)(2,1)S(1)}, bf16[384,512]{1,0:T(8,128)(2,1)S(1)}, u32[]{:S(2)}, u32[]{:S(2)}) %collective-permute-start.5) | collective-permute-done | bytes 393248 | tf_op jit(solution)/shard_map/ppermute | solution.py:121
  55.1 0.7 copy-done.8
  55.8 0.1 copy-done.9
  55.9 0.3 copy-done.6
  56.2 0.3 copy-done.7
  56.5 7.1 %project.1 = (bf16[3,384,128]{2,1,0:T(8,128)(2,1)S(1)}, bf16[3,384,128]{2,1,0:T(8,128)(2,1)S(1)}, bf16[3,384,128]{2,1,0:T(8,128)(2,1)S(1)}, bf16[3,384,128]{2,1,...) custom-call(s32[3]{0:T(128)S(1)} %pad_add_fusion.where_ref, ...), custom_call_target="tpu_custom_call" | custom-call | tf_op jit(solution)/shard_map/project/pallas_call | solution.py:206
  63.6 0.7 copy-done.2
  64.4 0.5 collective-permute-start.15
  64.9 0.5 collective-permute-start.16
  65.4 2.4 %collective-permute-start.17 = (bf16[3,384,128]{2,1,0:T(8,128)(2,1)S(1)}, bf16[3,384,128]{2,1,0:T(8,128)(2,1)S(1)}, u32[]{:S(2)}, u32[]{:S(2)}) collective-permute-start(bf16[3,384,128]{2,1,0:T(8,128)(2,1)S(1)} %get-tuple-element.18), channel_id=1, source_target_pairs={{0,24},{4,28},{8,16},{12,20},{16,8},{20,12},{24,0},{28,4},{1,25},{... | collective-permute-start | bytes 884744 | tf_op jit(solution)/shard_map/ppermute | solution.py:113
  67.9 6.5 %collective-permute-done.15.a1 = bf16[3,384,128]{2,1,0:T(8,128)(2,1)S(1)} collective-permute-done((bf16[3,384,128]{2,1,0:T(8,128)(2,1)S(1)}, bf16[3,384,128]{2,1,0:T(8,128)(2,1)S(1)}, u32[]{:S(2)}, u32[]{:S(2)}) %collective-permute-start.15) | collective-permute-done | bytes 294944 | tf_op jit(solution)/shard_map/ppermute | solution.py:113
  74.3 4.1 %collective-permute-done.16.a2 = bf16[3,384,128]{2,1,0:T(8,128)(2,1)S(1)} collective-permute-done((bf16[3,384,128]{2,1,0:T(8,128)(2,1)S(1)}, bf16[3,384,128]{2,1,0:T(8,128)(2,1)S(1)}, u32[]{:S(2)}, u32[]{:S(2)}) %collective-permute-start.16) | collective-permute-done | bytes 294944 | tf_op jit(solution)/shard_map/ppermute | solution.py:113
  78.4 0.5 collective-permute-start.21
  78.9 0.2 select_reduce_fusion.1
  79.1 0.8 collective-permute-done.20.b2
  80.0 0.4 collective-permute-done.21.b3
  80.4 8.7 %attend.1 = (bf16[384,128]{1,0:T(8,128)(2,1)S(1)}, bf16[384,128]{1,0:T(8,128)(2,1)S(1)}, bf16[384,128]{1,0:T(8,128)(2,1)S(1)}, bf16[384,128]{1,0:T(8,128)(2,1)S(1)}) custom-call(s32[3]{0:T(128)S(1)} %pad_add_fusion.where_ref, s32[6]{0:T(128)S(1)} %bitcast_subtract_fusion.start_ref, s32[8]{0:T(128)S(1)} %and_select_fusion.low_ref, ...), custom_call_target="tpu_custom_call" | custom-call | tf_op jit(solution)/shard_map/attend/pallas_call | solution.py:278
  89.1 1.5 %collective-permute-start.22 = (bf16[384,128]{1,0:T(8,128)(2,1)S(1)}, bf16[384,128]{1,0:T(8,128)(2,1)S(1)}, u32[]{:S(2)}, u32[]{:S(2)}) collective-permute-start(bf16[384,128]{1,0:T(8,128)(2,1)S(1)} %get-tuple-element.19), channel_id=1, source_target_pairs={{0,24},{4,28},{8,16},{12,20},{16,8},{20,12},{24,0},{28,4},{1,25},{... | collective-permute-start | bytes 294920 | tf_op jit(solution)/shard_map/ppermute | solution.py:113
  90.6 1.5 %collective-permute-start.23 = (bf16[384,128]{1,0:T(8,128)(2,1)S(1)}, bf16[384,128]{1,0:T(8,128)(2,1)S(1)}, u32[]{:S(2)}, u32[]{:S(2)}) collective-permute-start(bf16[384,128]{1,0:T(8,128)(2,1)S(1)} %get-tuple-element.20), channel_id=1, source_target_pairs={{0,16},{4,20},{8,24},{12,28},{16,0},{20,4},{24,8},{28,12},{1,17},{... | collective-permute-start | bytes 294920 | tf_op jit(solution)/shard_map/ppermute | solution.py:113
  92.1 0.5 collective-permute-start.24
  92.6 2.1 %collective-permute-done.22 = bf16[384,128]{1,0:T(8,128)(2,1)S(1)} collective-permute-done((bf16[384,128]{1,0:T(8,128)(2,1)S(1)}, bf16[384,128]{1,0:T(8,128)(2,1)S(1)}, u32[]{:S(2)}, u32[]{:S(2)}) %collective-permute-start.22) | collective-permute-done | bytes 98336 | tf_op jit(solution)/shard_map/ppermute | solution.py:113
  94.7 2.7 %collective-permute-done.23 = bf16[384,128]{1,0:T(8,128)(2,1)S(1)} collective-permute-done((bf16[384,128]{1,0:T(8,128)(2,1)S(1)}, bf16[384,128]{1,0:T(8,128)(2,1)S(1)}, u32[]{:S(2)}, u32[]{:S(2)}) %collective-permute-start.23) | collective-permute-done | bytes 98336 | tf_op jit(solution)/shard_map/ppermute | solution.py:113
  97.5 0.1 broadcast_select_fusion.1
  97.7 1.5 %collective-permute-start.25 = (bf16[384,512]{1,0:T(8,128)(2,1)S(1)}, bf16[384,512]{1,0:T(8,128)(2,1)S(1)}, u32[]{:S(2)}, u32[]{:S(2)}) collective-permute-start(bf16[384,512]{1,0:T(8,128)(2,1)S(1)} %pad_maximum_fusion.own), channel_id=1, source_target_pairs={{0,1},{1,2},{2,3},{4,5},{5,6},{6,7},{8,9},{9,10},{10,11},{12,13},{... | collective-permute-start | bytes 1179656 | tf_op jit(solution)/shard_map/ppermute | solution.py:117
  99.2 1.3 collective-permute-start.28
  100.5 7.5 %collective-permute-done.25.u1 = bf16[384,512]{1,0:T(8,128)(2,1)S(1)} collective-permute-done((bf16[384,512]{1,0:T(8,128)(2,1)S(1)}, bf16[384,512]{1,0:T(8,128)(2,1)S(1)}, u32[]{:S(2)}, u32[]{:S(2)}) %collective-permute-start.25) | collective-permute-done | bytes 393248 | tf_op jit(solution)/shard_map/ppermute | solution.py:117
  108.0 0.7 collective-permute-start.26
  108.7 3.5 %collective-permute-done.28.d1 = bf16[384,512]{1,0:T(8,128)(2,1)S(1)} collective-permute-done((bf16[384,512]{1,0:T(8,128)(2,1)S(1)}, bf16[384,512]{1,0:T(8,128)(2,1)S(1)}, u32[]{:S(2)}, u32[]{:S(2)}) %collective-permute-start.28) | collective-permute-done | bytes 393248 | tf_op jit(solution)/shard_map/ppermute | solution.py:121
  112.1 1.3 collective-permute-start.29
  113.4 0.7 collective-permute-start.27
  114.1 10.1 %collective-permute-done.29.d2 = bf16[384,512]{1,0:T(8,128)(2,1)S(1)} collective-permute-done((bf16[384,512]{1,0:T(8,128)(2,1)S(1)}, bf16[384,512]{1,0:T(8,128)(2,1)S(1)}, u32[]{:S(2)}, u32[]{:S(2)}) %collective-permute-start.29) | collective-permute-done | bytes 393248 | tf_op jit(solution)/shard_map/ppermute | solution.py:121
  124.2 1.3 collective-permute-start.30
  125.5 0.8 reshape.74
  126.4 0.8 reshape.75
  127.2 8.2 %collective-permute-done.30.d3 = bf16[384,512]{1,0:T(8,128)(2,1)S(1)} collective-permute-done((bf16[384,512]{1,0:T(8,128)(2,1)S(1)}, bf16[384,512]{1,0:T(8,128)(2,1)S(1)}, u32[]{:S(2)}, u32[]{:S(2)}) %collective-permute-start.30) | collective-permute-done | bytes 393248 | tf_op jit(solution)/shard_map/ppermute | solution.py:121
  135.4 1.6 %copy-done = bf16[2048,512]{1,0:T(8,128)(2,1)S(1)} copy-done((bf16[2048,512]{1,0:T(8,128)(2,1)S(1)}, bf16[2048,512]{1,0:T(8,128)(2,1)}, u32[]{:S(2)}) %copy-start) | copy-done | bytes 2097176
  137.0 2.3 %mix.1 = bf16[384,512]{1,0:T(8,128)(2,1)} custom-call(s32[3]{0:T(128)S(1)} %pad_add_fusion.where_ref, bf16[384,512]{1,0:T(8,128)(2,1)S(1)} %pad_maximum_fusion.own, bf16[384,512]{1,0:T(8,128)(2,1)S(1)} %collective-permute-done.25.u1, bf16[384,512]{1,0:T(8,128)(2,1)S(1)} %collective-permute-done.26.u2, bf16[384,512]{1,0:T(8,128)(2,1)S(1)} %collective-permute-done.27.u3, ...), custom_call_target="tpu_custom_call" | custom-call | tf_op jit(solution)/shard_map/mix/pallas_call | solution.py:309
  (45 shorter events, 0.3 us)
Async XLA Ops:
  7.2 128.2 %all-gather.2.cloned.1.call-start = ((), (), s32[]{:S(2)}) async-start(), calls=%async_computation | async-start | bytes 2359296 | tf_op jit(solution)/shard_map/all_gather | solution.py:360
  7.2 49.2 %copy-start.1 = (bf16[384,512]{1,0:T(8,128)(2,1)S(1)}, bf16[384,512]{1,0:T(8,128)(2,1)}, u32[]{:S(2)}) copy-start(bf16[384,512]{1,0:T(8,128)(2,1)} %own.1) | copy-start | bytes 1179652
  7.2 49.2 %copy-start.4 = (f32[2048]{0:T(1024)S(1)}, f32[2048]{0:T(1024)}, u32[]{:S(2)}) copy-start(f32[2048]{0:T(1024)} %param.6) | copy-start | bytes 24580
  9.6 22.9 %collective-permute-start.7 = (bf16[256,1536]{1,0:T(8,128)(2,1)}, bf16[256,1536]{1,0:T(8,128)(2,1)S(1)}, u32[]{:S(2)}, u32[]{:S(2)}) collective-permute-start(bf16[256,1536]{1,0:T(8,128)(2,1)} %reshape.72.wa0), channel_id=1, source_target_pairs={{0,16},{4,20},{8,24},{12,28},{16,0},{20,4},{24,8},{28,12},{1,17},{... | collective-permute-start | bytes 2359304 | tf_op jit(solution)/shard_map/ppermute | solution.py:113
  12.6 21.4 %collective-permute-start.6 = (bf16[256,1536]{1,0:T(8,128)(2,1)}, bf16[256,1536]{1,0:T(8,128)(2,1)}, u32[]{:S(2)}, u32[]{:S(2)}) collective-permute-start(bf16[256,1536]{1,0:T(8,128)(2,1)} %reshape.72.wa0), channel_id=1, source_target_pairs={{0,8},{4,12},{8,0},{12,4},{16,24},{20,28},{24,16},{28,20},{1,9},{5... | collective-permute-start | bytes 2359304 | tf_op jit(solution)/shard_map/ppermute | solution.py:113
  14.1 11.6 %collective-permute-start = (bf16[384,512]{1,0:T(8,128)(2,1)}, bf16[384,512]{1,0:T(8,128)(2,1)S(1)}, u32[]{:S(2)}, u32[]{:S(2)}) collective-permute-start(bf16[384,512]{1,0:T(8,128)(2,1)} %own.1), channel_id=1, source_target_pairs={{0,1},{1,2},{2,3},{4,5},{5,6},{6,7},{8,9},{9,10},{10,11},{12,13},{... | collective-permute-start | bytes 1179656 | tf_op jit(solution)/shard_map/ppermute | solution.py:117
  17.6 12.1 %collective-permute-start.3 = (bf16[384,512]{1,0:T(8,128)(2,1)}, bf16[384,512]{1,0:T(8,128)(2,1)S(1)}, u32[]{:S(2)}, u32[]{:S(2)}) collective-permute-start(bf16[384,512]{1,0:T(8,128)(2,1)} %own.1), channel_id=1, source_target_pairs={{3,2},{2,1},{1,0},{7,6},{6,5},{5,4},{11,10},{10,9},{9,8},{15,14},{... | collective-permute-start | bytes 1179656 | tf_op jit(solution)/shard_map/ppermute | solution.py:121
  18.9 18.8 %collective-permute-start.10 = (bf16[256,1536]{1,0:T(8,128)(2,1)}, bf16[256,1536]{1,0:T(8,128)(2,1)}, u32[]{:S(2)}, u32[]{:S(2)}) collective-permute-start(bf16[256,1536]{1,0:T(8,128)(2,1)} %reshape.72.wa0), channel_id=1, source_target_pairs={{0,4},{4,0},{8,12},{12,8},{16,20},{20,16},{24,28},{28,24},{1,5},{5... | collective-permute-start | bytes 2359304 | tf_op jit(solution)/shard_map/ppermute | solution.py:113
  25.7 10.7 %collective-permute-start.1 = (bf16[384,512]{1,0:T(8,128)(2,1)S(1)}, bf16[384,512]{1,0:T(8,128)(2,1)S(1)}, u32[]{:S(2)}, u32[]{:S(2)}) collective-permute-start(bf16[384,512]{1,0:T(8,128)(2,1)S(1)} %collective-permute-done.u1), channel_id=1, source_target_pairs={{1,2},{2,3},{5,6},{6,7},{9,10},{10,11},{13,14},{14,15},{17,18},{18... | collective-permute-start | bytes 1179656 | tf_op jit(solution)/shard_map/ppermute | solution.py:117
  29.7 11.2 %collective-permute-start.4 = (bf16[384,512]{1,0:T(8,128)(2,1)S(1)}, bf16[384,512]{1,0:T(8,128)(2,1)S(1)}, u32[]{:S(2)}, u32[]{:S(2)}) collective-permute-start(bf16[384,512]{1,0:T(8,128)(2,1)S(1)} %collective-permute-done.3.d1), channel_id=1, source_target_pairs={{2,1},{1,0},{6,5},{5,4},{10,9},{9,8},{14,13},{13,12},{18,17},{17,1... | collective-permute-start | bytes 1179656 | tf_op jit(solution)/shard_map/ppermute | solution.py:121
  32.5 0.9 copy-start.5
  33.4 9.3 %collective-permute-start.8 = (bf16[128,1536]{1,0:T(8,128)(2,1)S(1)}, bf16[128,1536]{1,0:T(8,128)(2,1)S(1)}, u32[]{:S(2)}, u32[]{:S(2)}) collective-permute-start(bf16[128,1536]{1,0:T(8,128)(2,1)S(1)} %slice.8), channel_id=1, source_target_pairs={{0,8},{4,12},{8,0},{12,4},{16,24},{20,28},{24,16},{28,20},{1,9},{5... | collective-permute-start | bytes 1179656 | tf_op jit(solution)/shard_map/ppermute | solution.py:113
  35.8 9.1 %collective-permute-start.9 = (bf16[128,1536]{1,0:T(8,128)(2,1)}, bf16[128,1536]{1,0:T(8,128)(2,1)S(1)}, u32[]{:S(2)}, u32[]{:S(2)}) collective-permute-start(bf16[128,1536]{1,0:T(8,128)(2,1)} %slice.9), channel_id=1, source_target_pairs={{0,16},{4,20},{8,24},{12,28},{16,0},{20,4},{24,8},{28,12},{1,17},{... | collective-permute-start | bytes 1179656 | tf_op jit(solution)/shard_map/ppermute | solution.py:113
  36.3 8.6 %collective-permute-start.2 = (bf16[384,512]{1,0:T(8,128)(2,1)S(1)}, bf16[384,512]{1,0:T(8,128)(2,1)S(1)}, u32[]{:S(2)}, u32[]{:S(2)}) collective-permute-start(bf16[384,512]{1,0:T(8,128)(2,1)S(1)} %collective-permute-done.1.u2), channel_id=1, source_target_pairs={{2,3},{6,7},{10,11},{14,15},{18,19},{22,23},{26,27},{30,31}} | collective-permute-start | bytes 1179656 | tf_op jit(solution)/shard_map/ppermute | solution.py:117
  37.7 17.4 %collective-permute-start.11 = (bf16[256,1536]{1,0:T(8,128)(2,1)}, bf16[256,1536]{1,0:T(8,128)(2,1)S(1)}, u32[]{:S(2)}, u32[]{:S(2)}) collective-permute-start(bf16[256,1536]{1,0:T(8,128)(2,1)} %collective-permute-done.6.wa1), channel_id=1, source_target_pairs={{0,4},{4,0},{8,12},{12,8},{16,20},{20,16},{24,28},{28,24},{1,5},{5... | collective-permute-start | bytes 2359304 | tf_op jit(solution)/shard_map/ppermute | solution.py:113
  40.9 14.2 %collective-permute-start.12 = (bf16[256,1536]{1,0:T(8,128)(2,1)}, bf16[256,1536]{1,0:T(8,128)(2,1)S(1)}, u32[]{:S(2)}, u32[]{:S(2)}) collective-permute-start(bf16[256,1536]{1,0:T(8,128)(2,1)} %copy-done.5), channel_id=1, source_target_pairs={{0,4},{4,0},{8,12},{12,8},{16,20},{20,16},{24,28},{28,24},{1,5},{5... | collective-permute-start | bytes 2359304 | tf_op jit(solution)/shard_map/ppermute | solution.py:113
  42.7 12.4 %collective-permute-start.5 = (bf16[384,512]{1,0:T(8,128)(2,1)S(1)}, bf16[384,512]{1,0:T(8,128)(2,1)S(1)}, u32[]{:S(2)}, u32[]{:S(2)}) collective-permute-start(bf16[384,512]{1,0:T(8,128)(2,1)S(1)} %collective-permute-done.4.d2), channel_id=1, source_target_pairs={{1,0},{5,4},{9,8},{13,12},{17,16},{21,20},{25,24},{29,28}} | collective-permute-start | bytes 1179656 | tf_op jit(solution)/shard_map/ppermute | solution.py:121
  44.9 10.1 %collective-permute-start.13 = (bf16[128,1536]{1,0:T(8,128)(2,1)S(1)}, bf16[128,1536]{1,0:T(8,128)(2,1)S(1)}, u32[]{:S(2)}, u32[]{:S(2)}) collective-permute-start(bf16[128,1536]{1,0:T(8,128)(2,1)S(1)} %collective-permute-done.8.wa3), channel_id=1, source_target_pairs={{0,4},{4,0},{8,12},{12,8},{16,20},{20,16},{24,28},{28,24},{1,5},{5... | collective-permute-start | bytes 1179656 | tf_op jit(solution)/shard_map/ppermute | solution.py:113
  44.9 10.1 %collective-permute-start.14 = (bf16[128,1536]{1,0:T(8,128)(2,1)S(1)}, bf16[128,1536]{1,0:T(8,128)(2,1)S(1)}, u32[]{:S(2)}, u32[]{:S(2)}) collective-permute-start(bf16[128,1536]{1,0:T(8,128)(2,1)S(1)} %collective-permute-done.9.wa4), channel_id=1, source_target_pairs={{0,4},{4,0},{8,12},{12,8},{16,20},{20,16},{24,28},{28,24},{1,5},{5... | collective-permute-start | bytes 1179656 | tf_op jit(solution)/shard_map/ppermute | solution.py:113
  55.1 0.7 copy-start.8
  55.1 0.9 copy-start.9
  55.1 1.1 copy-start.6
  55.1 1.3 copy-start.7
  63.6 0.7 copy-start.2
  64.4 9.9 %collective-permute-start.15 = (bf16[3,384,128]{2,1,0:T(8,128)(2,1)S(1)}, bf16[3,384,128]{2,1,0:T(8,128)(2,1)S(1)}, u32[]{:S(2)}, u32[]{:S(2)}) collective-permute-start(bf16[3,384,128]{2,1,0:T(8,128)(2,1)S(1)} %get-tuple-element.16), channel_id=1, source_target_pairs={{0,8},{4,12},{8,0},{12,4},{16,24},{20,28},{24,16},{28,20},{1,9},{5... | collective-permute-start | bytes 884744 | tf_op jit(solution)/shard_map/ppermute | solution.py:113
  64.9 13.5 %collective-permute-start.16 = (bf16[3,384,128]{2,1,0:T(8,128)(2,1)S(1)}, bf16[3,384,128]{2,1,0:T(8,128)(2,1)S(1)}, u32[]{:S(2)}, u32[]{:S(2)}) collective-permute-start(bf16[3,384,128]{2,1,0:T(8,128)(2,1)S(1)} %get-tuple-element.17), channel_id=1, source_target_pairs={{0,16},{4,20},{8,24},{12,28},{16,0},{20,4},{24,8},{28,12},{1,17},{... | collective-permute-start | bytes 884744 | tf_op jit(solution)/shard_map/ppermute | solution.py:113
  65.4 13.0 %collective-permute-start.17 = (bf16[3,384,128]{2,1,0:T(8,128)(2,1)S(1)}, bf16[3,384,128]{2,1,0:T(8,128)(2,1)S(1)}, u32[]{:S(2)}, u32[]{:S(2)}) collective-permute-start(bf16[3,384,128]{2,1,0:T(8,128)(2,1)S(1)} %get-tuple-element.18), channel_id=1, source_target_pairs={{0,24},{4,28},{8,16},{12,20},{16,8},{20,12},{24,0},{28,4},{1,25},{... | collective-permute-start | bytes 884744 | tf_op jit(solution)/shard_map/ppermute | solution.py:113
  67.9 11.3 %collective-permute-start.18 = (bf16[3,384,128]{2,1,0:T(8,128)(2,1)S(1)}, bf16[3,384,128]{2,1,0:T(8,128)(2,1)S(1)}, u32[]{:S(2)}, u32[]{:S(2)}) collective-permute-start(bf16[3,384,128]{2,1,0:T(8,128)(2,1)S(1)} %get-tuple-element.15.a0), channel_id=1, source_target_pairs={{0,4},{4,0},{8,12},{12,8},{16,20},{20,16},{24,28},{28,24},{1,5},{5... | collective-permute-start | bytes 884744 | tf_op jit(solution)/shard_map/ppermute | solution.py:113
  74.3 4.8 %collective-permute-start.19 = (bf16[3,384,128]{2,1,0:T(8,128)(2,1)S(1)}, bf16[3,384,128]{2,1,0:T(8,128)(2,1)S(1)}, u32[]{:S(2)}, u32[]{:S(2)}) collective-permute-start(bf16[3,384,128]{2,1,0:T(8,128)(2,1)S(1)} %collective-permute-done.15.a1), channel_id=1, source_target_pairs={{0,4},{4,0},{8,12},{12,8},{16,20},{20,16},{24,28},{28,24},{1,5},{5... | collective-permute-start | bytes 884744 | tf_op jit(solution)/shard_map/ppermute | solution.py:113
  78.4 1.6 %collective-permute-start.20 = (bf16[3,384,128]{2,1,0:T(8,128)(2,1)S(1)}, bf16[3,384,128]{2,1,0:T(8,128)(2,1)S(1)}, u32[]{:S(2)}, u32[]{:S(2)}) collective-permute-start(bf16[3,384,128]{2,1,0:T(8,128)(2,1)S(1)} %collective-permute-done.16.a2), channel_id=1, source_target_pairs={{0,4},{4,0},{8,12},{12,8},{16,20},{20,16},{24,28},{28,24},{1,5},{5... | collective-permute-start | bytes 884744 | tf_op jit(solution)/shard_map/ppermute | solution.py:113
  78.4 2.0 %collective-permute-start.21 = (bf16[3,384,128]{2,1,0:T(8,128)(2,1)S(1)}, bf16[3,384,128]{2,1,0:T(8,128)(2,1)S(1)}, u32[]{:S(2)}, u32[]{:S(2)}) collective-permute-start(bf16[3,384,128]{2,1,0:T(8,128)(2,1)S(1)} %collective-permute-done.17.a3), channel_id=1, source_target_pairs={{0,4},{4,0},{8,12},{12,8},{16,20},{20,16},{24,28},{28,24},{1,5},{5... | collective-permute-start | bytes 884744 | tf_op jit(solution)/shard_map/ppermute | solution.py:113
  79.1 46.4 %copy-start.3 = (bf16[384,512]{1,0:T(8,128)(2,1)S(1)}, bf16[384,512]{1,0:T(8,128)(2,1)}, u32[]{:S(2)}) copy-start(bf16[384,512]{1,0:T(8,128)(2,1)} %copy-done.2) | copy-start | bytes 1179652
  89.1 5.6 %collective-permute-start.22 = (bf16[384,128]{1,0:T(8,128)(2,1)S(1)}, bf16[384,128]{1,0:T(8,128)(2,1)S(1)}, u32[]{:S(2)}, u32[]{:S(2)}) collective-permute-start(bf16[384,128]{1,0:T(8,128)(2,1)S(1)} %get-tuple-element.19), channel_id=1, source_target_pairs={{0,24},{4,28},{8,16},{12,20},{16,8},{20,12},{24,0},{28,4},{1,25},{... | collective-permute-start | bytes 294920 | tf_op jit(solution)/shard_map/ppermute | solution.py:113
  90.6 6.9 %collective-permute-start.23 = (bf16[384,128]{1,0:T(8,128)(2,1)S(1)}, bf16[384,128]{1,0:T(8,128)(2,1)S(1)}, u32[]{:S(2)}, u32[]{:S(2)}) collective-permute-start(bf16[384,128]{1,0:T(8,128)(2,1)S(1)} %get-tuple-element.20), channel_id=1, source_target_pairs={{0,16},{4,20},{8,24},{12,28},{16,0},{20,4},{24,8},{28,12},{1,17},{... | collective-permute-start | bytes 294920 | tf_op jit(solution)/shard_map/ppermute | solution.py:113
  92.1 5.4 %collective-permute-start.24 = (bf16[384,128]{1,0:T(8,128)(2,1)S(1)}, bf16[384,128]{1,0:T(8,128)(2,1)S(1)}, u32[]{:S(2)}, u32[]{:S(2)}) collective-permute-start(bf16[384,128]{1,0:T(8,128)(2,1)S(1)} %get-tuple-element.21), channel_id=1, source_target_pairs={{0,8},{4,12},{8,0},{12,4},{16,24},{20,28},{24,16},{28,20},{1,9},{5... | collective-permute-start | bytes 294920 | tf_op jit(solution)/shard_map/ppermute | solution.py:113
  97.7 10.3 %collective-permute-start.25 = (bf16[384,512]{1,0:T(8,128)(2,1)S(1)}, bf16[384,512]{1,0:T(8,128)(2,1)S(1)}, u32[]{:S(2)}, u32[]{:S(2)}) collective-permute-start(bf16[384,512]{1,0:T(8,128)(2,1)S(1)} %pad_maximum_fusion.own), channel_id=1, source_target_pairs={{0,1},{1,2},{2,3},{4,5},{5,6},{6,7},{8,9},{9,10},{10,11},{12,13},{... | collective-permute-start | bytes 1179656 | tf_op jit(solution)/shard_map/ppermute | solution.py:117
  99.2 13.0 %collective-permute-start.28 = (bf16[384,512]{1,0:T(8,128)(2,1)S(1)}, bf16[384,512]{1,0:T(8,128)(2,1)S(1)}, u32[]{:S(2)}, u32[]{:S(2)}) collective-permute-start(bf16[384,512]{1,0:T(8,128)(2,1)S(1)} %pad_maximum_fusion.own), channel_id=1, source_target_pairs={{3,2},{2,1},{1,0},{7,6},{6,5},{5,4},{11,10},{10,9},{9,8},{15,14},{... | collective-permute-start | bytes 1179656 | tf_op jit(solution)/shard_map/ppermute | solution.py:121
  108.0 5.4 %collective-permute-start.26 = (bf16[384,512]{1,0:T(8,128)(2,1)S(1)}, bf16[384,512]{1,0:T(8,128)(2,1)S(1)}, u32[]{:S(2)}, u32[]{:S(2)}) collective-permute-start(bf16[384,512]{1,0:T(8,128)(2,1)S(1)} %collective-permute-done.25.u1), channel_id=1, source_target_pairs={{1,2},{2,3},{5,6},{6,7},{9,10},{10,11},{13,14},{14,15},{17,18},{18... | collective-permute-start | bytes 1179656 | tf_op jit(solution)/shard_map/ppermute | solution.py:117
  112.1 12.1 %collective-permute-start.29 = (bf16[384,512]{1,0:T(8,128)(2,1)S(1)}, bf16[384,512]{1,0:T(8,128)(2,1)S(1)}, u32[]{:S(2)}, u32[]{:S(2)}) collective-permute-start(bf16[384,512]{1,0:T(8,128)(2,1)S(1)} %collective-permute-done.28.d1), channel_id=1, source_target_pairs={{2,1},{1,0},{6,5},{5,4},{10,9},{9,8},{14,13},{13,12},{18,17},{17,1... | collective-permute-start | bytes 1179656 | tf_op jit(solution)/shard_map/ppermute | solution.py:121
  113.4 13.8 %collective-permute-start.27 = (bf16[384,512]{1,0:T(8,128)(2,1)S(1)}, bf16[384,512]{1,0:T(8,128)(2,1)S(1)}, u32[]{:S(2)}, u32[]{:S(2)}) collective-permute-start(bf16[384,512]{1,0:T(8,128)(2,1)S(1)} %collective-permute-done.26.u2), channel_id=1, source_target_pairs={{2,3},{6,7},{10,11},{14,15},{18,19},{22,23},{26,27},{30,31}} | collective-permute-start | bytes 1179656 | tf_op jit(solution)/shard_map/ppermute | solution.py:117
  124.2 11.2 %collective-permute-start.30 = (bf16[384,512]{1,0:T(8,128)(2,1)S(1)}, bf16[384,512]{1,0:T(8,128)(2,1)S(1)}, u32[]{:S(2)}, u32[]{:S(2)}) collective-permute-start(bf16[384,512]{1,0:T(8,128)(2,1)S(1)} %collective-permute-done.29.d2), channel_id=1, source_target_pairs={{1,0},{5,4},{9,8},{13,12},{17,16},{21,20},{25,24},{29,28}} | collective-permute-start | bytes 1179656 | tf_op jit(solution)/shard_map/ppermute | solution.py:121
  135.4 1.6 %copy-start = (bf16[2048,512]{1,0:T(8,128)(2,1)S(1)}, bf16[2048,512]{1,0:T(8,128)(2,1)}, u32[]{:S(2)}) copy-start(bf16[2048,512]{1,0:T(8,128)(2,1)} %all-gather.2.cloned.1.call-done) | copy-start | bytes 6291460
Sparse Core Ops, SparseCore 0:
  97.8 25.2 all-gather.1

commit v2 on v1

v2 whole, which is shorter than its diff:
```python
import functools
import math

import jax
import jax.numpy as jnp
from jax import lax
from jax.experimental import pallas as pl
from jax.experimental.pallas import tpu as pltpu
from jax.sharding import PartitionSpec as P


def tables(position, hsize):
    half = hsize // 2
    freq = 10000.0 ** (-(2.0 * jnp.arange(half, dtype=jnp.float32)) / hsize)
    angle = position.astype(jnp.float32)[:, None] * freq[None, :]
    return jnp.cos(angle), jnp.sin(angle)


def rotate(vectors, position):
    half = vectors.shape[-1] // 2
    cosine, sine = tables(position, vectors.shape[-1])
    cosine, sine = cosine[:, None, :], sine[:, None, :]
    first = vectors[..., :half]
    second = vectors[..., half:]
    return jnp.concatenate(
        [first * cosine - second * sine, second * cosine + first * sine], axis=-1
    )


def begins(lengths, glob):
    doc_start = jnp.cumsum(lengths) - lengths
    return jnp.max(jnp.where(doc_start[None, :] <= glob[:, None], doc_start[None, :], 0), axis=1)


def block_rows(count):
    size = count
    while size > 1024 and size % 2 == 0:
        size = size // 2
    return size


def general(tokens, gain, w_qkv, w_out, lengths):
    tok_dev = tokens.shape[0]
    hloc = w_qkv.shape[2]
    hsize = w_qkv.shape[3]
    whole = lax.all_gather(tokens, "gy", axis=1, tiled=True)
    wide = whole.astype(jnp.float32)
    meansq = jnp.mean(wide * wide, axis=-1, keepdims=True)
    normed = (wide * lax.rsqrt(meansq + 1e-06) * gain[None, :]).astype(jnp.bfloat16)
    piece = lax.all_gather(w_qkv, "gx", axis=0, tiled=True)
    projected = jnp.dot(
        normed, piece.reshape(piece.shape[0], -1), preferred_element_type=jnp.float32
    )
    projected = projected.reshape(tok_dev, 3, hloc, hsize)
    mine = lax.axis_index("gx")
    glob = mine * tok_dev + jnp.arange(tok_dev, dtype=jnp.int32)
    begin = begins(lengths, glob)
    position = glob - begin
    query = rotate(projected[:, 0], position).astype(jnp.bfloat16)
    keys_own = rotate(projected[:, 1], position).astype(jnp.bfloat16)
    vals_own = projected[:, 2].astype(jnp.bfloat16)
    scale = 1.0 / math.sqrt(hsize)
    initial = (
        jnp.full((hloc, tok_dev), -1e30, jnp.float32),
        jnp.zeros((hloc, tok_dev), jnp.float32),
        jnp.zeros((hloc, tok_dev, hsize), jnp.float32),
    )
    keys_piece = lax.all_gather(keys_own, "gx", axis=0, tiled=True)
    vals_piece = lax.all_gather(vals_own, "gx", axis=0, tiled=True)
    count = keys_piece.shape[0]
    size = block_rows(count)

    def one_tile(number, state):
        running, totals, accum = state
        first = (number * size).astype(jnp.int32)
        keys_blk = lax.dynamic_slice_in_dim(keys_piece, first, size, 0)
        vals_blk = lax.dynamic_slice_in_dim(vals_piece, first, size, 0)
        kidx = first + jnp.arange(size, dtype=jnp.int32)
        score = (
            jnp.einsum("qhd,khd->hqk", query, keys_blk, preferred_element_type=jnp.float32) * scale
        )
        keep = (kidx[None, :] >= begin[:, None]) & (kidx[None, :] <= glob[:, None])
        score = jnp.where(keep[None], score, -1e30)
        newmax = jnp.maximum(running, jnp.max(score, axis=-1))
        weight = jnp.where(keep[None], jnp.exp(score - newmax[..., None]), 0.0)
        factor = jnp.exp(running - newmax)
        totals = totals * factor + jnp.sum(weight, axis=-1)
        update = jnp.einsum(
            "hqk,khd->hqd",
            weight.astype(jnp.bfloat16),
            vals_blk,
            preferred_element_type=jnp.float32,
        )
        accum = accum * factor[..., None] + update
        return (newmax, totals, accum)

    running, totals, accum = lax.fori_loop(0, count // size, one_tile, initial)
    attended = (accum / totals[..., None]).astype(jnp.bfloat16)
    attended = jnp.transpose(attended, (1, 0, 2)).reshape(tok_dev, hloc * hsize)
    all_heads = lax.all_gather(attended, "gy", axis=1, tiled=True)
    mixed = jnp.dot(
        all_heads, lax.all_gather(w_out, "gx", axis=0, tiled=True),
        preferred_element_type=jnp.float32,
    ).astype(jnp.bfloat16)
    return (mixed, keys_own, vals_own)


LINE = 4
CHIPS = 4
NORM_EFFORT = 8 << 30
EARLY_EFFORT = 16 << 30


def swap(x, mask):
    return lax.ppermute(x, "gx", [(i, i ^ mask) for i in range(2 * CHIPS)])


def outer(x):
    return lax.ppermute(x, "gy", [(0, 1), (1, 0), (2, 3), (3, 2)])


def inner(x):
    return lax.ppermute(x, "gy", [(1, 2), (2, 1)])


def outward(x):
    return lax.ppermute(x, "gy", [(1, 0), (2, 3)])


def order(line):
    low = line < 2
    return line ^ 1, jnp.where(low, 2, 1), jnp.where(low, 3, 0), (line == 0) | (line == LINE - 1)


def vmem():
    return pl.BlockSpec(memory_space=pltpu.VMEM)


def smem():
    return pl.BlockSpec(memory_space=pltpu.SMEM)


def hbm():
    return pl.BlockSpec(memory_space=pl.ANY)


def full(array):
    return pl.BlockSpec(array.shape, lambda *_: (0,) * array.ndim)


def effort(flops):
    return pl.CostEstimate(flops=flops, transcendentals=0, bytes_accessed=8 << 20)


def normalize_kernel(where_ref, own, near, q1, p2, q2, p3, gain_ref, x_ref):
    line = where_ref[2]
    wide = own.shape[1]
    second, third, fourth, end = order(line)
    raw = [
        own[...].astype(jnp.float32),
        near[...].astype(jnp.float32),
        jnp.where(end, p2[...], q1[...]).astype(jnp.float32),
        jnp.where(end, p3[...], q2[...]).astype(jnp.float32),
    ]
    square = sum(jnp.sum(r * r, axis=1, keepdims=True) for r in raw)
    scale = lax.rsqrt(square * (1.0 / (LINE * wide)) + 1e-06)
    for r, feature in zip(raw, (line, second, third, fourth)):
        normed = (r * scale * gain_ref[feature]).astype(jnp.bfloat16)
        x_ref[2 * feature] = normed[:, : wide // 2]
        x_ref[2 * feature + 1] = normed[:, wide // 2 :]


def normalize(where, blocks, gain):
    rows, wide = blocks[0].shape
    return pl.pallas_call(
        normalize_kernel,
        in_specs=[smem()] + [vmem()] * 7,
        out_specs=vmem(),
        out_shape=jax.ShapeDtypeStruct((2 * LINE, rows, wide // 2), jnp.bfloat16),
        compiler_params=pltpu.CompilerParams(vmem_limit_bytes=20 << 20),
        cost_estimate=effort(NORM_EFFORT),
        name="normalize",
    )(where, *blocks, gain)


def project_kernel(where_ref, x_ref, cos_ref, sin_ref, *refs):
    weights, outs, (slot_ref,) = refs[:10], refs[10:16], refs[16:]
    sent, key_ref, val_ref = outs[:CHIPS], outs[CHIPS], outs[CHIPS + 1]
    step = pl.program_id(0)
    chip, core = where_ref[0], where_ref[1]
    wide = 2 * x_ref.shape[2]
    hsize = cos_ref.shape[1]

    total = None
    for side in range(2):
        half = core if side == 0 else 1 - core
        for m in range(CHIPS):
            x = x_ref[2 * (chip ^ m) + half]
            if m < 3:
                parts = [(x, weights[5 * side + m])]
            else:
                parts = [
                    (x[:, : wide // 4], weights[5 * side + 3]),
                    (x[:, wide // 4 :], weights[5 * side + 4]),
                ]
            for left, right in parts:
                part = jnp.dot(left, right[...], preferred_element_type=jnp.float32)
                total = part if total is None else total + part

    @pl.when(step < 2)
    def _():
        for h in range(CHIPS):
            u = total[:, h * hsize : (h + 1) * hsize]
            u = u * cos_ref[...] + pltpu.roll(u, hsize // 2, 1) * sin_ref[...]
            slot_ref[h] = u.astype(jnp.bfloat16)

    @pl.when(step == 2)
    def _():
        for h in range(CHIPS):
            slot_ref[h] = total[:, h * hsize : (h + 1) * hsize].astype(jnp.bfloat16)

    for m in range(CHIPS):
        sent[m][0] = slot_ref[chip ^ m]

    @pl.when(step == 1)
    def _():
        for h in range(CHIPS):
            key_ref[:, h * hsize : (h + 1) * hsize] = slot_ref[h]

    @pl.when(step == 2)
    def _():
        for h in range(CHIPS):
            val_ref[:, h * hsize : (h + 1) * hsize] = slot_ref[h]


def project(where, x, cosine, sine, weights):
    rows, hsize = cosine.shape
    wide = 2 * x.shape[2]
    cols = weights[0].shape[1] // 3
    return pl.pallas_call(
        project_kernel,
        grid=(3,),
        in_specs=[smem()]
        + [full(a) for a in (x, cosine, sine)]
        + [pl.BlockSpec((w.shape[0], cols), lambda j: (0, j)) for w in weights],
        out_specs=[pl.BlockSpec((1, rows, hsize), lambda j: (j, 0, 0))] * CHIPS
        + [pl.BlockSpec((rows, cols), lambda j: (0, 0))] * 2,
        out_shape=[jax.ShapeDtypeStruct((3, rows, hsize), jnp.bfloat16)] * CHIPS
        + [jax.ShapeDtypeStruct((rows, cols), jnp.bfloat16)] * 2,
        scratch_shapes=[
            pltpu.VMEM((CHIPS, rows, hsize), jnp.bfloat16),
        ],
        compiler_params=pltpu.CompilerParams(vmem_limit_bytes=24 << 20),
        cost_estimate=effort(2 * rows * LINE * wide * 3 * cols),
        name="project",
    )(where, x, cosine, sine, *weights)


def attend_kernel(where_ref, start_ref, *refs, scale):
    pieces, outs, (keys, vals) = refs[:8], refs[8:12], refs[12:]
    chip, core = where_ref[0], where_ref[1]
    _, rows, hsize = pieces[0].shape
    for side in range(2):
        for n in range(CHIPS):
            block = 2 * (chip ^ n) + (core if side == 0 else 1 - core)
            keys[block] = pieces[CHIPS * side + n][1]
            vals[block] = pieces[CHIPS * side + n][2]
    for m in range(CHIPS):
        block = 2 * (chip ^ m) + core
        query = pieces[m][0]
        qpos = block * rows + lax.broadcasted_iota(jnp.int32, (rows, 1), 0)
        begin = jnp.zeros((rows, 1), jnp.int32)
        lowest = jnp.int32(0)
        for d in range(start_ref.shape[0]):
            begin = jnp.where(start_ref[d] <= qpos, start_ref[d], begin)
            lowest = jnp.where(start_ref[d] <= block * rows, start_ref[d], lowest)

        def tile(number, state, block=block, query=query, qpos=qpos, begin=begin):
            running, totals, accum = state
            kv = block - number
            kpos = kv * rows + lax.broadcasted_iota(jnp.int32, (1, rows), 1)
            score = scale * lax.dot_general(
                query, keys[kv], (((1,), (1,)), ((), ())), preferred_element_type=jnp.float32
            )
            keep = (kpos >= begin) & (kpos <= qpos)
            score = jnp.where(keep, score, -1e30)
            newmax = jnp.maximum(running, jnp.max(score, axis=1, keepdims=True))
            weight = jnp.exp(score - newmax)
            factor = jnp.exp(running - newmax)
            totals = totals * factor + jnp.sum(weight, axis=1, keepdims=True)
            accum = accum * factor + jnp.dot(
                weight.astype(jnp.bfloat16), vals[kv], preferred_element_type=jnp.float32
            )
            return newmax, totals, accum

        state = (
            jnp.full((rows, 1), -1e30, jnp.float32),
            jnp.zeros((rows, 1), jnp.float32),
            jnp.zeros((rows, hsize), jnp.float32),
        )
        running, totals, accum = lax.fori_loop(0, block - lax.div(lowest, rows) + 1, tile, state)
        outs[m][...] = (accum / totals).astype(jnp.bfloat16)


def attend(where, starts, pieces, scale):
    _, rows, hsize = pieces[0].shape
    return pl.pallas_call(
        functools.partial(attend_kernel, scale=scale),
        in_specs=[smem()] * 2 + [vmem()] * len(pieces),
        out_specs=[vmem()] * CHIPS,
        out_shape=[jax.ShapeDtypeStruct((rows, hsize), jnp.bfloat16)] * CHIPS,
        scratch_shapes=[pltpu.VMEM((2 * CHIPS, rows, hsize), jnp.bfloat16)] * 2,
        compiler_params=pltpu.CompilerParams(vmem_limit_bytes=16 << 20),
        cost_estimate=effort(16 * 2 * rows * LINE * rows * hsize),
        name="attend",
    )(where, starts, *pieces)


def early_kernel(where_ref, own, near, q1, p2, *refs):
    pieces, total_ref, last_ref, w_ref = refs[:10], refs[10], refs[11], refs[12]
    chip, core, line = where_ref[0], where_ref[1], where_ref[2]
    depth = pieces[0].shape[0]
    for side in range(2):
        for m in range(CHIPS):
            block = 2 * (chip ^ m) + (core if side == 0 else 1 - core)
            if m < 3:
                w_ref[block] = pieces[5 * side + m][...]
            else:
                w_ref[block, : depth // 2] = pieces[5 * side + 3][...]
                w_ref[block, depth // 2 :] = pieces[5 * side + 4][...]

    def term(block, feature):
        return jnp.dot(
            block[:, :depth], w_ref[2 * feature], preferred_element_type=jnp.float32
        ) + jnp.dot(block[:, depth:], w_ref[2 * feature + 1], preferred_element_type=jnp.float32)

    second, third, fourth, end = order(line)
    total = term(own[...], line) + term(near[...], second)
    total_ref[...] = total + term(jnp.where(end, p2[...], q1[...]), third)
    last_ref[:depth] = w_ref[2 * fourth]
    last_ref[depth:] = w_ref[2 * fourth + 1]


def early(where, blocks, pieces):
    rows, wide = blocks[0].shape
    depth, cols = pieces[0].shape
    return pl.pallas_call(
        early_kernel,
        in_specs=[smem()] + [vmem()] * (len(blocks) + len(pieces)),
        out_specs=[vmem()] * 2,
        out_shape=[
            jax.ShapeDtypeStruct((rows, cols), jnp.float32),
            jax.ShapeDtypeStruct((wide, cols), jnp.bfloat16),
        ],
        scratch_shapes=[pltpu.VMEM((2 * CHIPS, depth, cols), jnp.bfloat16)],
        compiler_params=pltpu.CompilerParams(vmem_limit_bytes=16 << 20),
        cost_estimate=effort(EARLY_EFFORT),
        name="early",
    )(where, *blocks, *pieces)


def last_kernel(where_ref, q2, p3, total_ref, w_ref, out_ref):
    end = order(where_ref[2])[3]
    block = jnp.where(end, p3[...], q2[...])
    total = total_ref[...] + jnp.dot(block, w_ref[...], preferred_element_type=jnp.float32)
    out_ref[...] = total.astype(jnp.bfloat16)


def last(where, q2, p3, total, w_last):
    return pl.pallas_call(
        last_kernel,
        in_specs=[smem()] + [vmem()] * 4,
        out_specs=vmem(),
        out_shape=jax.ShapeDtypeStruct(total.shape, jnp.bfloat16),
        compiler_params=pltpu.CompilerParams(vmem_limit_bytes=8 << 20),
        cost_estimate=effort(2 * total.shape[0] * w_last.size),
        name="last",
    )(where, q2, p3, total, w_last)


def heads_in_order(back, chip):
    odd, high = (chip & 1) == 1, (chip & 2) == 2
    low, top = [
        jnp.concatenate([jnp.where(odd, b, a), jnp.where(odd, a, b)], axis=1)
        for a, b in (back[:2], back[2:])
    ]
    return jnp.concatenate([jnp.where(high, top, low), jnp.where(high, low, top)], axis=1)


def together(*arrays):
    return lax.optimization_barrier(arrays)


def blocks_plan(tokens, gain, w_qkv, w_out, lengths):
    rows, wide = tokens.shape
    depth, _, heads, hsize = w_qkv.shape
    half = depth // 2
    mine = lax.axis_index("gx")
    line = lax.axis_index("gy")
    chip, core = mine // 2, mine % 2
    where = jnp.stack([chip, core, line]).astype(jnp.int32)
    starts = (jnp.cumsum(lengths) - lengths).astype(jnp.int32)
    glob = mine * rows + jnp.arange(rows, dtype=jnp.int32)
    cosine, sine = tables(glob - begins(lengths, glob), hsize)
    cosine = jnp.concatenate([cosine, cosine], axis=1)
    sine = jnp.concatenate([-sine, sine], axis=1)

    flat = w_qkv.reshape(depth, -1)
    near, q1 = outer(tokens), inner(tokens)
    q2, p2 = inner(near), outward(q1)
    w_x, w_y = swap(flat, 2), swap(flat, 4)
    q2, p2, w_x, w_y = together(q2, p2, w_x, w_y)
    p3, far_a, far_b = outward(q2), swap(w_y[:half], 2), swap(w_x[half:], 4)
    held = (flat, w_x, w_y, far_a, far_b)
    weights = held + tuple(swap(w, 1) for w in held)
    x = normalize(where, (tokens, near, q1, p2, q2, p3), gain.reshape(LINE, 1, wide))
    *sent, keys, vals = project(where, x, cosine, sine, weights)

    pieces = [sent[0]] + [swap(sent[m], 2 * m) for m in range(1, CHIPS)]
    *pieces, w_late = together(*pieces, w_out)
    w_x, w_y = swap(w_late, 2), swap(w_late, 4)
    heads_out = attend(
        where, starts, pieces + [swap(a, 1) for a in pieces], 1.0 / math.sqrt(hsize)
    )
    *heads_out, w_x, w_y = together(*heads_out, w_x, w_y)
    back = [heads_out[0]] + [swap(heads_out[m], 2 * m) for m in range(1, CHIPS)]
    attended = heads_in_order(back, chip)
    attended, w_x, w_y = together(attended, w_x, w_y)
    near, q1, far_a, far_b = together(
        outer(attended), inner(attended), swap(w_y[:half], 2), swap(w_x[half:], 4)
    )
    pieces = (w_late, w_x, w_y, far_a, far_b)
    q2, p2 = inner(near), outward(q1)
    q2, *others = together(q2, *[swap(w, 1) for w in pieces])
    p3 = outward(q2)
    total, w_last = early(where, (attended, near, q1, p2), (*pieces, *others))
    mixed = last(where, q2, p3, total, w_last)
    return (mixed, keys.reshape(rows, heads, hsize), vals.reshape(rows, heads, hsize))


def local(sizes, tokens, gain, w_qkv, w_out, lengths):
    heads = w_qkv.shape[2]
    fits = sizes == (2 * CHIPS, LINE) and heads == CHIPS and tokens.shape[1] == 2 * w_qkv.shape[0]
    plan = blocks_plan if fits else general
    return plan(tokens, gain, w_qkv, w_out, lengths)


def solution(mesh):
    sizes = (mesh.shape["gx"], mesh.shape["gy"])
    return jax.shard_map(
        functools.partial(local, sizes),
        mesh=mesh,
        in_specs=(P("gx", "gy"), P(), P("gx", None, "gy", None), P("gx", "gy"), P()),
        out_specs=(P("gx", "gy"), P("gx", "gy", None), P("gx", "gy", None)),
        check_vma=False,
    )
```

time: 146 us -> 125 us (0.86)
  between operations: 14.3 us -> 0.96 us
  waiting for transfers between devices: 69.8 us -> 61.5 us
  starting transfers between devices: 29.2 us -> 34.6 us
  local copies, waits for them, and re-layouts: 10.5 us -> 7.1 us
  other arithmetic: 4.24 us -> 1.47 us
    ppermute x12 -> x10, waiting for transfers between devices: 51.2 us -> 28 us  [the longest x4 22.2 us: outward(): return lax.ppermute(x, 'gy', [(1, 0), (2, 3)])]
    ppermute x19 -> x28, waiting for transfers between devices: 18.6 us -> 33.5 us  [swap(): return lax.ppermute(x, 'gx', [(i, i ^ mask) for i in range(2 * CHIPS)])]
    ppermute x19 -> x28, starting transfers between devices: 13.7 us -> 19.8 us  [swap(): return lax.ppermute(x, 'gx', [(i, i ^ mask) for i in range(2 * CHIPS)])]
    slice x2 -> x4, local copies, waits for them, and re-layouts: 1.79 us -> 0.07 us  [the longest x2 0.05 us: blocks_plan(): p3, far_a, far_b = (outward(q2), swap(w_y[:half], 2), swap(w_x[half:], 4))]
    pallas_call x2 -> x4, Pallas kernels: 9.42 us -> 11.1 us  [the longest x1 5.36 us: project(): pl.pallas_call(project_kernel, grid=(3,), in_specs=[smem()] + [full(a) fo...]
    unnamed x20 -> x14, local copies, waits for them, and re-layouts: 4.58 us -> 3.69 us
    ppermute x12 -> x10, starting transfers between devices: 15.4 us -> 14.8 us  [the longest x2 5.53 us: outer(): return lax.ppermute(x, 'gy', [(0, 1), (1, 0), (2, 3), (3, 2)])]
  transfers between devices with their start and end apart: 32 -> 38, of which waited for: 16 -> 14; matrix products, arithmetic and copies ran while one was open for 5% -> 4% of each run, Pallas kernels for 0% -> 9%
where the time goes in v2:
time: 125 us; the launch traced here: 124 us
  waiting for transfers between devices  61.5 us (49%)
  starting transfers between devices  34.6 us (28%)
  Pallas kernels  18.6 us (15%)
  local copies, waits for them, and re-layouts  7.1 us (6%)
  other arithmetic  1.47 us (1%)
    ppermute x28, waiting for transfers between devices, swap(): return lax.ppermute(x, 'gx', [(i, i ^ mask) for i in range(2 * CHIPS)])  33.5 us
    ppermute x4, waiting for transfers between devices, outward(): return lax.ppermute(x, 'gy', [(1, 0), (2, 3)])  22.2 us
    ppermute x28, starting transfers between devices, swap(): return lax.ppermute(x, 'gx', [(i, i ^ mask) for i in range(2 * CHIPS)])  19.8 us
    pallas_call x1, Pallas kernels, attend(): pl.pallas_call(functools.partial(attend_kernel, scale=scale), in_specs=[s...  7.52 us
    ppermute x2, waiting for transfers between devices, outer(): return lax.ppermute(x, 'gy', [(0, 1), (1, 0), (2, 3), (3, 2)])  5.82 us
    ppermute x2, starting transfers between devices, outer(): return lax.ppermute(x, 'gy', [(0, 1), (1, 0), (2, 3), (3, 2)])  5.53 us
    pallas_call x1, Pallas kernels, project(): pl.pallas_call(project_kernel, grid=(3,), in_specs=[smem()] + [full(a) fo...  5.36 us
    ppermute x4, starting transfers between devices, outward(): return lax.ppermute(x, 'gy', [(1, 0), (2, 3)])  5.15 us
  transfers between devices with their start and end apart: 38, of which 14 were waited for; matrix products, arithmetic and copies ran while one was open for 4% of the time, Pallas kernels for 9%

profile of v2, /device:TPU:0, one launch (start us, length us, event | category | flops | bytes accessed | tf_op | source)
XLA Modules:
  0.0 124.3 jit_solution(5130980351549043145)
XLA Ops:
  0.6 3.1 %collective-permute-start = (bf16[384,512]{1,0:T(8,128)(2,1)}, bf16[384,512]{1,0:T(8,128)(2,1)S(1)}, u32[]{:S(2)}, u32[]{:S(2)}) collective-permute-start(bf16[384,512]{1,0:T(8,128)(2,1)} %own.1), channel_id=1, source_target_pairs={{0,1},{1,0},{2,3},{3,2},{4,5},{5,4},{6,7},{7,6},{8,9},{9,8},{10,11... | collective-permute-start | bytes 1179656 | tf_op jit(solution)/shard_map/ppermute | solution.py:119
  3.7 1.4 %collective-permute-start.1 = (bf16[384,512]{1,0:T(8,128)(2,1)}, bf16[384,512]{1,0:T(8,128)(2,1)}, u32[]{:S(2)}, u32[]{:S(2)}) collective-permute-start(bf16[384,512]{1,0:T(8,128)(2,1)} %own.1), channel_id=1, source_target_pairs={{1,2},{2,1},{5,6},{6,5},{9,10},{10,9},{13,14},{14,13},{17,18},{18,... | collective-permute-start | bytes 1179656 | tf_op jit(solution)/shard_map/ppermute | solution.py:123
  5.1 1.7 %reshape.64.refs_0_ = bf16[256,1536]{1,0:T(8,128)(2,1)S(1)} reshape(bf16[256,3,4,128]{3,2,1,0:T(4,128)(2,1)} %param.7) | data formatting | bytes 1572864 | tf_op jit(solution)/shard_map/reshape | solution.py:408
  6.8 1.6 %collective-permute-start.4 = (bf16[256,1536]{1,0:T(8,128)(2,1)S(1)}, bf16[256,1536]{1,0:T(8,128)(2,1)S(1)}, u32[]{:S(2)}, u32[]{:S(2)}) collective-permute-start(bf16[256,1536]{1,0:T(8,128)(2,1)S(1)} %reshape.64.refs_0_), channel_id=1, source_target_pairs={{0,8},{4,12},{8,0},{12,4},{16,24},{20,28},{24,16},{28,20},{1,9},{5... | collective-permute-start | bytes 2359304 | tf_op jit(solution)/shard_map/ppermute | solution.py:115
  8.4 1.5 %collective-permute-start.5 = (bf16[256,1536]{1,0:T(8,128)(2,1)S(1)}, bf16[256,1536]{1,0:T(8,128)(2,1)S(1)}, u32[]{:S(2)}, u32[]{:S(2)}) collective-permute-start(bf16[256,1536]{1,0:T(8,128)(2,1)S(1)} %reshape.64.refs_0_), channel_id=1, source_target_pairs={{0,16},{4,20},{8,24},{12,28},{16,0},{20,4},{24,8},{28,12},{1,17},{... | collective-permute-start | bytes 2359304 | tf_op jit(solution)/shard_map/ppermute | solution.py:115
  9.9 0.2 reduce-window.9
  10.1 3.0 %collective-permute-done.near = bf16[384,512]{1,0:T(8,128)(2,1)S(1)} collective-permute-done((bf16[384,512]{1,0:T(8,128)(2,1)}, bf16[384,512]{1,0:T(8,128)(2,1)S(1)}, u32[]{:S(2)}, u32[]{:S(2)}) %collective-permute-start) | collective-permute-done | bytes 393248 | tf_op jit(solution)/shard_map/ppermute | solution.py:119
  13.1 1.4 %collective-permute-start.2 = (bf16[384,512]{1,0:T(8,128)(2,1)S(1)}, bf16[384,512]{1,0:T(8,128)(2,1)}, u32[]{:S(2)}, u32[]{:S(2)}) collective-permute-start(bf16[384,512]{1,0:T(8,128)(2,1)S(1)} %collective-permute-done.near), channel_id=1, source_target_pairs={{1,2},{2,1},{5,6},{6,5},{9,10},{10,9},{13,14},{14,13},{17,18},{18,... | collective-permute-start | bytes 1179656 | tf_op jit(solution)/shard_map/ppermute | solution.py:123
  14.5 1.3 %collective-permute-start.3 = (bf16[384,512]{1,0:T(8,128)(2,1)}, bf16[384,512]{1,0:T(8,128)(2,1)}, u32[]{:S(2)}, u32[]{:S(2)}) collective-permute-start(bf16[384,512]{1,0:T(8,128)(2,1)} %collective-permute-done.1.q1), channel_id=1, source_target_pairs={{1,0},{2,3},{5,4},{6,7},{9,8},{10,11},{13,12},{14,15},{17,16},{18,... | collective-permute-start | bytes 1179656 | tf_op jit(solution)/shard_map/ppermute | solution.py:127
  15.8 0.1 select_reduce_fusion
  15.9 10.0 %collective-permute-done.4.refs_1_ = bf16[256,1536]{1,0:T(8,128)(2,1)S(1)} collective-permute-done((bf16[256,1536]{1,0:T(8,128)(2,1)S(1)}, bf16[256,1536]{1,0:T(8,128)(2,1)S(1)}, u32[]{:S(2)}, u32[]{:S(2)}) %collective-permute-start.4) | collective-permute-done | bytes 786464 | tf_op jit(solution)/shard_map/ppermute | solution.py:115
  25.9 1.2 collective-permute-done.5.refs_2_
  27.1 0.9 collective-permute-done.3.p2
  27.9 1.3 %collective-permute-start.6 = (bf16[384,512]{1,0:T(8,128)(2,1)}, bf16[384,512]{1,0:T(8,128)(2,1)S(1)}, u32[]{:S(2)}, u32[]{:S(2)}) collective-permute-start(bf16[384,512]{1,0:T(8,128)(2,1)} %collective-permute-done.2.q2), channel_id=1, source_target_pairs={{1,0},{2,3},{5,4},{6,7},{9,8},{10,11},{13,12},{14,15},{17,16},{18,... | collective-permute-start | bytes 1179656 | tf_op jit(solution)/shard_map/ppermute | solution.py:127
  29.3 1.6 %collective-permute-start.7 = (bf16[128,1536]{1,0:T(8,128)(2,1)S(1)}, bf16[128,1536]{1,0:T(8,128)(2,1)S(1)}, u32[]{:S(2)}, u32[]{:S(2)}) collective-permute-start(bf16[128,1536]{1,0:T(8,128)(2,1)S(1)} %slice.12), channel_id=1, source_target_pairs={{0,8},{4,12},{8,0},{12,4},{16,24},{20,28},{24,16},{28,20},{1,9},{5... | collective-permute-start | bytes 1179656 | tf_op jit(solution)/shard_map/ppermute | solution.py:115
  30.9 1.6 %collective-permute-start.8 = (bf16[128,1536]{1,0:T(8,128)(2,1)S(1)}, bf16[128,1536]{1,0:T(8,128)(2,1)S(1)}, u32[]{:S(2)}, u32[]{:S(2)}) collective-permute-start(bf16[128,1536]{1,0:T(8,128)(2,1)S(1)} %slice.13), channel_id=1, source_target_pairs={{0,16},{4,20},{8,24},{12,28},{16,0},{20,4},{24,8},{28,12},{1,17},{... | collective-permute-start | bytes 1179656 | tf_op jit(solution)/shard_map/ppermute | solution.py:115
  32.4 0.1 pad_add_fusion.where_ref
  32.5 0.8 fusion
  33.3 0.2 pad_maximum_fusion.1
  33.5 0.1 collective-permute-start.10
  33.5 5.7 %collective-permute-done.6.p3 = bf16[384,512]{1,0:T(8,128)(2,1)S(1)} collective-permute-done((bf16[384,512]{1,0:T(8,128)(2,1)}, bf16[384,512]{1,0:T(8,128)(2,1)S(1)}, u32[]{:S(2)}, u32[]{:S(2)}) %collective-permute-start.6) | collective-permute-done | bytes 393248 | tf_op jit(solution)/shard_map/ppermute | solution.py:127
  39.3 0.5 collective-permute-start.12
  39.8 0.1 collective-permute-start.13
  39.9 2.0 %normalize.1.x_ref = bf16[8,384,256]{2,1,0:T(8,128)(2,1)S(1)} custom-call(s32[3]{0:T(128)S(1)} %pad_add_fusion.where_ref, bf16[384,512]{1,0:T(8,128)(2,1)S(1)} %copy-done.2, bf16[384,512]{1,0:T(8,128)(2,1)S(1)} %collective-permute-done.near, bf16[384,512]{1,0:T(8,128)(2,1)} %collective-permute-done.1.q1, bf16[384,512]{1,0:T(8,128)(2,1)} %collective-permute-done.3.p2, ...), custom_call_target="tpu_custom_call" | custom-call | flops 8589934592 | bytes 8388608 | tf_op jit(solution)/shard_map/normalize/pallas_call | solution.py:175
  41.9 0.9 copy-done
  42.8 1.1 copy-done.1
  43.9 5.4 %project.1 = (bf16[3,384,128]{2,1,0:T(8,128)(2,1)S(1)}, bf16[3,384,128]{2,1,0:T(8,128)(2,1)S(1)}, bf16[3,384,128]{2,1,0:T(8,128)(2,1)S(1)}, bf16[3,384,128]{2,1,...) custom-call(s32[3]{0:T(128)S(1)} %pad_add_fusion.where_ref, ...), custom_call_target="tpu_custom_call" | custom-call | flops 2415919104 | bytes 8388608 | tf_op jit(solution)/shard_map/project/pallas_call | solution.py:240
  49.3 1.5 %collective-permute-start.14 = (bf16[3,384,128]{2,1,0:T(8,128)(2,1)S(1)}, bf16[3,384,128]{2,1,0:T(8,128)(2,1)S(1)}, u32[]{:S(2)}, u32[]{:S(2)}) collective-permute-start(bf16[3,384,128]{2,1,0:T(8,128)(2,1)S(1)} %get-tuple-element.48), channel_id=1, source_target_pairs={{0,8},{4,12},{8,0},{12,4},{16,24},{20,28},{24,16},{28,20},{1,9},{5... | collective-permute-start | bytes 884744 | tf_op jit(solution)/shard_map/ppermute | solution.py:115
  50.8 1.5 %collective-permute-start.15 = (bf16[3,384,128]{2,1,0:T(8,128)(2,1)S(1)}, bf16[3,384,128]{2,1,0:T(8,128)(2,1)S(1)}, u32[]{:S(2)}, u32[]{:S(2)}) collective-permute-start(bf16[3,384,128]{2,1,0:T(8,128)(2,1)S(1)} %get-tuple-element.49), channel_id=1, source_target_pairs={{0,16},{4,20},{8,24},{12,28},{16,0},{20,4},{24,8},{28,12},{1,17},{... | collective-permute-start | bytes 884744 | tf_op jit(solution)/shard_map/ppermute | solution.py:115
  52.3 0.6 collective-permute-start.16
  52.9 6.3 %collective-permute-done.14.refs_1_ = bf16[3,384,128]{2,1,0:T(8,128)(2,1)S(1)} collective-permute-done((bf16[3,384,128]{2,1,0:T(8,128)(2,1)S(1)}, bf16[3,384,128]{2,1,0:T(8,128)(2,1)S(1)}, u32[]{:S(2)}, u32[]{:S(2)}) %collective-permute-start.14) | collective-permute-done | bytes 294944 | tf_op jit(solution)/shard_map/ppermute | solution.py:115
  59.2 7.0 %collective-permute-done.15.refs_2_ = bf16[3,384,128]{2,1,0:T(8,128)(2,1)S(1)} collective-permute-done((bf16[3,384,128]{2,1,0:T(8,128)(2,1)S(1)}, bf16[3,384,128]{2,1,0:T(8,128)(2,1)S(1)}, u32[]{:S(2)}, u32[]{:S(2)}) %collective-permute-start.15) | collective-permute-done | bytes 294944 | tf_op jit(solution)/shard_map/ppermute | solution.py:115
  66.2 0.5 collective-permute-start.18
  66.7 0.5 collective-permute-start.20
  67.2 1.2 collective-permute-start.21
  68.4 0.9 collective-permute-start.22
  69.3 7.5 %attend.1 = (bf16[384,128]{1,0:T(8,128)(2,1)S(1)}, bf16[384,128]{1,0:T(8,128)(2,1)S(1)}, bf16[384,128]{1,0:T(8,128)(2,1)S(1)}, bf16[384,128]{1,0:T(8,128)(2,1)S(1)}) custom-call(s32[3]{0:T(128)S(1)} %pad_add_fusion.where_ref, s32[6]{0:T(128)S(1)} %bitcast_subtract_fusion.start_ref, bf16[3,384,128]{2,1,0:T(8,128)(2,1)S(1)} %get-tuple-element.51.refs_0_, ...), custom_call_target="tpu_custom_call" | custom-call | flops 2415919104 | bytes 8388608 | tf_op jit(solution)/shard_map/attend/pallas_call | solution.py:307
  76.9 1.4 %collective-permute-start.23 = (bf16[384,128]{1,0:T(8,128)(2,1)S(1)}, bf16[384,128]{1,0:T(8,128)(2,1)S(1)}, u32[]{:S(2)}, u32[]{:S(2)}) collective-permute-start(bf16[384,128]{1,0:T(8,128)(2,1)S(1)} %get-tuple-element.60), channel_id=1, source_target_pairs={{0,24},{4,28},{8,16},{12,20},{16,8},{20,12},{24,0},{28,4},{1,25},{... | collective-permute-start | bytes 294920 | tf_op jit(solution)/shard_map/ppermute | solution.py:115
  78.3 1.5 %collective-permute-start.24 = (bf16[384,128]{1,0:T(8,128)(2,1)S(1)}, bf16[384,128]{1,0:T(8,128)(2,1)S(1)}, u32[]{:S(2)}, u32[]{:S(2)}) collective-permute-start(bf16[384,128]{1,0:T(8,128)(2,1)S(1)} %get-tuple-element.61), channel_id=1, source_target_pairs={{0,16},{4,20},{8,24},{12,28},{16,0},{20,4},{24,8},{28,12},{1,17},{... | collective-permute-start | bytes 294920 | tf_op jit(solution)/shard_map/ppermute | solution.py:115
  79.9 0.6 collective-permute-start.25
  80.5 2.8 %collective-permute-done.23 = bf16[384,128]{1,0:T(8,128)(2,1)S(1)} collective-permute-done((bf16[384,128]{1,0:T(8,128)(2,1)S(1)}, bf16[384,128]{1,0:T(8,128)(2,1)S(1)}, u32[]{:S(2)}, u32[]{:S(2)}) %collective-permute-start.23) | collective-permute-done | bytes 98336 | tf_op jit(solution)/shard_map/ppermute | solution.py:115
  83.2 2.4 %collective-permute-done.24 = bf16[384,128]{1,0:T(8,128)(2,1)S(1)} collective-permute-done((bf16[384,128]{1,0:T(8,128)(2,1)S(1)}, bf16[384,128]{1,0:T(8,128)(2,1)S(1)}, u32[]{:S(2)}, u32[]{:S(2)}) %collective-permute-start.24) | collective-permute-done | bytes 98336 | tf_op jit(solution)/shard_map/ppermute | solution.py:115
  85.7 0.1 broadcast_select_fusion.1
  85.8 2.4 %collective-permute-start.26 = (bf16[384,512]{1,0:T(8,128)(2,1)S(1)}, bf16[384,512]{1,0:T(8,128)(2,1)S(1)}, u32[]{:S(2)}, u32[]{:S(2)}) collective-permute-start(bf16[384,512]{1,0:T(8,128)(2,1)S(1)} %pad_maximum_fusion.own), channel_id=1, source_target_pairs={{0,1},{1,0},{2,3},{3,2},{4,5},{5,4},{6,7},{7,6},{8,9},{9,8},{10,11... | collective-permute-start | bytes 1179656 | tf_op jit(solution)/shard_map/ppermute | solution.py:119
  88.2 0.7 collective-permute-start.27
  88.9 0.7 collective-permute-start.28
  89.7 1.3 %collective-permute-start.29 = (bf16[128,512]{1,0:T(8,128)(2,1)S(1)}, bf16[128,512]{1,0:T(8,128)(2,1)}, u32[]{:S(2)}, u32[]{:S(2)}) collective-permute-start(bf16[128,512]{1,0:T(8,128)(2,1)S(1)} %slice.15), channel_id=1, source_target_pairs={{0,16},{4,20},{8,24},{12,28},{16,0},{20,4},{24,8},{28,12},{1,17},{... | collective-permute-start | bytes 393224 | tf_op jit(solution)/shard_map/ppermute | solution.py:115
  90.9 3.4 %collective-permute-done.28.refs_3_ = bf16[128,512]{1,0:T(8,128)(2,1)} collective-permute-done((bf16[128,512]{1,0:T(8,128)(2,1)S(1)}, bf16[128,512]{1,0:T(8,128)(2,1)}, u32[]{:S(2)}, u32[]{:S(2)}) %collective-permute-start.28) | collective-permute-done | bytes 131104 | tf_op jit(solution)/shard_map/ppermute | solution.py:115
  94.4 0.5 collective-permute-done.29.refs_4_
  94.8 2.8 %collective-permute-done.26.near = bf16[384,512]{1,0:T(8,128)(2,1)S(1)} collective-permute-done((bf16[384,512]{1,0:T(8,128)(2,1)S(1)}, bf16[384,512]{1,0:T(8,128)(2,1)S(1)}, u32[]{:S(2)}, u32[]{:S(2)}) %collective-permute-start.26) | collective-permute-done | bytes 393248 | tf_op jit(solution)/shard_map/ppermute | solution.py:119
  97.6 0.7 collective-permute-start.30
  98.3 1.3 %collective-permute-start.37 = (bf16[384,512]{1,0:T(8,128)(2,1)S(1)}, bf16[384,512]{1,0:T(8,128)(2,1)S(1)}, u32[]{:S(2)}, u32[]{:S(2)}) collective-permute-start(bf16[384,512]{1,0:T(8,128)(2,1)S(1)} %collective-permute-done.27.q1), channel_id=1, source_target_pairs={{1,0},{2,3},{5,4},{6,7},{9,8},{10,11},{13,12},{14,15},{17,16},{18,... | collective-permute-start | bytes 1179656 | tf_op jit(solution)/shard_map/ppermute | solution.py:127
  99.6 0.1 collective-permute-start.33
  99.7 0.5 collective-permute-start.34
  100.2 0.7 copy-done.3
  100.9 0.1 collective-permute-start.35
  101.0 0.8 reshape.66
  101.8 0.8 reshape.67
  102.7 1.3 %collective-permute-start.36 = (bf16[384,512]{1,0:T(8,128)(2,1)S(1)}, bf16[384,512]{1,0:T(8,128)(2,1)S(1)}, u32[]{:S(2)}, u32[]{:S(2)}) collective-permute-start(bf16[384,512]{1,0:T(8,128)(2,1)S(1)} %collective-permute-done.30.q2), channel_id=1, source_target_pairs={{1,0},{2,3},{5,4},{6,7},{9,8},{10,11},{13,12},{14,15},{17,16},{18,... | collective-permute-start | bytes 1179656 | tf_op jit(solution)/shard_map/ppermute | solution.py:127
  104.0 10.4 %collective-permute-done.37.p2 = bf16[384,512]{1,0:T(8,128)(2,1)S(1)} collective-permute-done((bf16[384,512]{1,0:T(8,128)(2,1)S(1)}, bf16[384,512]{1,0:T(8,128)(2,1)S(1)}, u32[]{:S(2)}, u32[]{:S(2)}) %collective-permute-start.37) | collective-permute-done | bytes 393248 | tf_op jit(solution)/shard_map/ppermute | solution.py:127
  114.4 0.9 copy-done.4
  115.3 2.1 %early.1 = (f32[384,512]{1,0:T(8,128)S(1)}, bf16[512,512]{1,0:T(8,128)(2,1)S(1)}) custom-call(s32[3]{0:T(128)S(1)} %pad_add_fusion.where_ref, bf16[384,512]{1,0:T(8,128)(2,1)S(1)} %pad_maximum_fusion.own, bf16[384,512]{1,0:T(8,128)(2,1)S(1)} %collective-permute-done.26.near, bf16[384,512]{1,0:T(8,128)(2,1)S(1)} %collective-permute-done.27.q1, ...), custom_call_target="tpu_custom_call" | custom-call | flops 17179869184 | bytes 8388608 | tf_op jit(solution)/shard_map/early/pallas_call | solution.py:347
  117.5 5.2 %collective-permute-done.36.p3 = bf16[384,512]{1,0:T(8,128)(2,1)S(1)} collective-permute-done((bf16[384,512]{1,0:T(8,128)(2,1)S(1)}, bf16[384,512]{1,0:T(8,128)(2,1)S(1)}, u32[]{:S(2)}, u32[]{:S(2)}) %collective-permute-start.36) | collective-permute-done | bytes 393248 | tf_op jit(solution)/shard_map/ppermute | solution.py:127
  122.6 1.7 %last.1 = bf16[384,512]{1,0:T(8,128)(2,1)} custom-call(s32[3]{0:T(128)S(1)} %pad_add_fusion.where_ref, bf16[384,512]{1,0:T(8,128)(2,1)S(1)} %collective-permute-done.30.q2, bf16[384,512]{1,0:T(8,128)(2,1)S(1)} %collective-permute-done.36.p3, f32[384,512]{1,0:T(8,128)S(1)} %get-tuple-element.79.total_ref, bf16[512,512]{1,0:T(8,128)(2,1)S(1)} %get-tuple-element.80.w_ref), custom_call_target="tpu_custom_call" | custom-call | flops 201326592 | bytes 8388608 | tf_op jit(solution)/shard_map/last/pallas_call | solution.py:370
  (51 shorter events, 0.3 us)
Async XLA Ops:
  0.6 9.2 %copy-start.6 = (s32[6]{0:T(128)S(1)}, s32[6]{0:T(128)}, u32[]{:S(2)}) copy-start(s32[6]{0:T(128)} %param.9) | copy-start | bytes 76
  0.6 12.4 %collective-permute-start = (bf16[384,512]{1,0:T(8,128)(2,1)}, bf16[384,512]{1,0:T(8,128)(2,1)S(1)}, u32[]{:S(2)}, u32[]{:S(2)}) collective-permute-start(bf16[384,512]{1,0:T(8,128)(2,1)} %own.1), channel_id=1, source_target_pairs={{0,1},{1,0},{2,3},{3,2},{4,5},{5,4},{6,7},{7,6},{8,9},{9,8},{10,11... | collective-permute-start | bytes 1179656 | tf_op jit(solution)/shard_map/ppermute | solution.py:119
  3.7 10.7 %collective-permute-start.1 = (bf16[384,512]{1,0:T(8,128)(2,1)}, bf16[384,512]{1,0:T(8,128)(2,1)}, u32[]{:S(2)}, u32[]{:S(2)}) collective-permute-start(bf16[384,512]{1,0:T(8,128)(2,1)} %own.1), channel_id=1, source_target_pairs={{1,2},{2,1},{5,6},{6,5},{9,10},{10,9},{13,14},{14,13},{17,18},{18,... | collective-permute-start | bytes 1179656 | tf_op jit(solution)/shard_map/ppermute | solution.py:123
  6.8 19.1 %collective-permute-start.4 = (bf16[256,1536]{1,0:T(8,128)(2,1)S(1)}, bf16[256,1536]{1,0:T(8,128)(2,1)S(1)}, u32[]{:S(2)}, u32[]{:S(2)}) collective-permute-start(bf16[256,1536]{1,0:T(8,128)(2,1)S(1)} %reshape.64.refs_0_), channel_id=1, source_target_pairs={{0,8},{4,12},{8,0},{12,4},{16,24},{20,28},{24,16},{28,20},{1,9},{5... | collective-permute-start | bytes 2359304 | tf_op jit(solution)/shard_map/ppermute | solution.py:115
  8.4 18.7 %collective-permute-start.5 = (bf16[256,1536]{1,0:T(8,128)(2,1)S(1)}, bf16[256,1536]{1,0:T(8,128)(2,1)S(1)}, u32[]{:S(2)}, u32[]{:S(2)}) collective-permute-start(bf16[256,1536]{1,0:T(8,128)(2,1)S(1)} %reshape.64.refs_0_), channel_id=1, source_target_pairs={{0,16},{4,20},{8,24},{12,28},{16,0},{20,4},{24,8},{28,12},{1,17},{... | collective-permute-start | bytes 2359304 | tf_op jit(solution)/shard_map/ppermute | solution.py:115
  9.9 32.0 %collective-permute-start.9 = (bf16[256,1536]{1,0:T(8,128)(2,1)S(1)}, bf16[256,1536]{1,0:T(8,128)(2,1)S(1)}, u32[]{:S(2)}, u32[]{:S(2)}) collective-permute-start(bf16[256,1536]{1,0:T(8,128)(2,1)S(1)} %reshape.64.refs_0_), channel_id=1, source_target_pairs={{0,4},{4,0},{8,12},{12,8},{16,20},{20,16},{24,28},{28,24},{1,5},{5... | collective-permute-start | bytes 2359304 | tf_op jit(solution)/shard_map/ppermute | solution.py:115
  13.1 14.0 %collective-permute-start.2 = (bf16[384,512]{1,0:T(8,128)(2,1)S(1)}, bf16[384,512]{1,0:T(8,128)(2,1)}, u32[]{:S(2)}, u32[]{:S(2)}) collective-permute-start(bf16[384,512]{1,0:T(8,128)(2,1)S(1)} %collective-permute-done.near), channel_id=1, source_target_pairs={{1,2},{2,1},{5,6},{6,5},{9,10},{10,9},{13,14},{14,13},{17,18},{18,... | collective-permute-start | bytes 1179656 | tf_op jit(solution)/shard_map/ppermute | solution.py:123
  14.5 13.5 %collective-permute-start.3 = (bf16[384,512]{1,0:T(8,128)(2,1)}, bf16[384,512]{1,0:T(8,128)(2,1)}, u32[]{:S(2)}, u32[]{:S(2)}) collective-permute-start(bf16[384,512]{1,0:T(8,128)(2,1)} %collective-permute-done.1.q1), channel_id=1, source_target_pairs={{1,0},{2,3},{5,4},{6,7},{9,8},{10,11},{13,12},{14,15},{17,16},{18,... | collective-permute-start | bytes 1179656 | tf_op jit(solution)/shard_map/ppermute | solution.py:127
  15.9 24.0 %copy-start.2 = (bf16[384,512]{1,0:T(8,128)(2,1)S(1)}, bf16[384,512]{1,0:T(8,128)(2,1)}, u32[]{:S(2)}) copy-start(bf16[384,512]{1,0:T(8,128)(2,1)} %own.1) | copy-start | bytes 1179652
  15.9 24.0 %copy-start.5 = (f32[2048]{0:T(1024)S(1)}, f32[2048]{0:T(1024)}, u32[]{:S(2)}) copy-start(f32[2048]{0:T(1024)} %param.6) | copy-start | bytes 24580
  27.9 11.3 %collective-permute-start.6 = (bf16[384,512]{1,0:T(8,128)(2,1)}, bf16[384,512]{1,0:T(8,128)(2,1)S(1)}, u32[]{:S(2)}, u32[]{:S(2)}) collective-permute-start(bf16[384,512]{1,0:T(8,128)(2,1)} %collective-permute-done.2.q2), channel_id=1, source_target_pairs={{1,0},{2,3},{5,4},{6,7},{9,8},{10,11},{13,12},{14,15},{17,16},{18,... | collective-permute-start | bytes 1179656 | tf_op jit(solution)/shard_map/ppermute | solution.py:127
  29.3 10.0 %collective-permute-start.7 = (bf16[128,1536]{1,0:T(8,128)(2,1)S(1)}, bf16[128,1536]{1,0:T(8,128)(2,1)S(1)}, u32[]{:S(2)}, u32[]{:S(2)}) collective-permute-start(bf16[128,1536]{1,0:T(8,128)(2,1)S(1)} %slice.12), channel_id=1, source_target_pairs={{0,8},{4,12},{8,0},{12,4},{16,24},{20,28},{24,16},{28,20},{1,9},{5... | collective-permute-start | bytes 1179656 | tf_op jit(solution)/shard_map/ppermute | solution.py:115
  30.9 9.0 %collective-permute-start.8 = (bf16[128,1536]{1,0:T(8,128)(2,1)S(1)}, bf16[128,1536]{1,0:T(8,128)(2,1)S(1)}, u32[]{:S(2)}, u32[]{:S(2)}) collective-permute-start(bf16[128,1536]{1,0:T(8,128)(2,1)S(1)} %slice.13), channel_id=1, source_target_pairs={{0,16},{4,20},{8,24},{12,28},{16,0},{20,4},{24,8},{28,12},{1,17},{... | collective-permute-start | bytes 1179656 | tf_op jit(solution)/shard_map/ppermute | solution.py:115
  33.5 9.3 %collective-permute-start.10 = (bf16[256,1536]{1,0:T(8,128)(2,1)S(1)}, bf16[256,1536]{1,0:T(8,128)(2,1)S(1)}, u32[]{:S(2)}, u32[]{:S(2)}) collective-permute-start(bf16[256,1536]{1,0:T(8,128)(2,1)S(1)} %collective-permute-done.4.refs_1_), channel_id=1, source_target_pairs={{0,4},{4,0},{8,12},{12,8},{16,20},{20,16},{24,28},{28,24},{1,5},{5... | collective-permute-start | bytes 2359304 | tf_op jit(solution)/shard_map/ppermute | solution.py:115
  39.3 3.5 %collective-permute-start.11 = (bf16[256,1536]{1,0:T(8,128)(2,1)S(1)}, bf16[256,1536]{1,0:T(8,128)(2,1)S(1)}, u32[]{:S(2)}, u32[]{:S(2)}) collective-permute-start(bf16[256,1536]{1,0:T(8,128)(2,1)S(1)} %collective-permute-done.5.refs_2_), channel_id=1, source_target_pairs={{0,4},{4,0},{8,12},{12,8},{16,20},{20,16},{24,28},{28,24},{1,5},{5... | collective-permute-start | bytes 2359304 | tf_op jit(solution)/shard_map/ppermute | solution.py:115
  39.3 3.5 %collective-permute-start.12 = (bf16[128,1536]{1,0:T(8,128)(2,1)S(1)}, bf16[128,1536]{1,0:T(8,128)(2,1)S(1)}, u32[]{:S(2)}, u32[]{:S(2)}) collective-permute-start(bf16[128,1536]{1,0:T(8,128)(2,1)S(1)} %collective-permute-done.7.refs_3_), channel_id=1, source_target_pairs={{0,4},{4,0},{8,12},{12,8},{16,20},{20,16},{24,28},{28,24},{1,5},{5... | collective-permute-start | bytes 1179656 | tf_op jit(solution)/shard_map/ppermute | solution.py:115
  39.8 3.0 %collective-permute-start.13 = (bf16[128,1536]{1,0:T(8,128)(2,1)S(1)}, bf16[128,1536]{1,0:T(8,128)(2,1)S(1)}, u32[]{:S(2)}, u32[]{:S(2)}) collective-permute-start(bf16[128,1536]{1,0:T(8,128)(2,1)S(1)} %collective-permute-done.8.refs_4_), channel_id=1, source_target_pairs={{0,4},{4,0},{8,12},{12,8},{16,20},{20,16},{24,28},{28,24},{1,5},{5... | collective-permute-start | bytes 1179656 | tf_op jit(solution)/shard_map/ppermute | solution.py:115
  41.9 0.9 copy-start
  42.8 1.1 copy-start.1
  49.3 9.9 %collective-permute-start.14 = (bf16[3,384,128]{2,1,0:T(8,128)(2,1)S(1)}, bf16[3,384,128]{2,1,0:T(8,128)(2,1)S(1)}, u32[]{:S(2)}, u32[]{:S(2)}) collective-permute-start(bf16[3,384,128]{2,1,0:T(8,128)(2,1)S(1)} %get-tuple-element.48), channel_id=1, source_target_pairs={{0,8},{4,12},{8,0},{12,4},{16,24},{20,28},{24,16},{28,20},{1,9},{5... | collective-permute-start | bytes 884744 | tf_op jit(solution)/shard_map/ppermute | solution.py:115
  50.8 15.4 %collective-permute-start.15 = (bf16[3,384,128]{2,1,0:T(8,128)(2,1)S(1)}, bf16[3,384,128]{2,1,0:T(8,128)(2,1)S(1)}, u32[]{:S(2)}, u32[]{:S(2)}) collective-permute-start(bf16[3,384,128]{2,1,0:T(8,128)(2,1)S(1)} %get-tuple-element.49), channel_id=1, source_target_pairs={{0,16},{4,20},{8,24},{12,28},{16,0},{20,4},{24,8},{28,12},{1,17},{... | collective-permute-start | bytes 884744 | tf_op jit(solution)/shard_map/ppermute | solution.py:115
  52.3 13.9 %collective-permute-start.16 = (bf16[3,384,128]{2,1,0:T(8,128)(2,1)S(1)}, bf16[3,384,128]{2,1,0:T(8,128)(2,1)S(1)}, u32[]{:S(2)}, u32[]{:S(2)}) collective-permute-start(bf16[3,384,128]{2,1,0:T(8,128)(2,1)S(1)} %get-tuple-element.50), channel_id=1, source_target_pairs={{0,24},{4,28},{8,16},{12,20},{16,8},{20,12},{24,0},{28,4},{1,25},{... | collective-permute-start | bytes 884744 | tf_op jit(solution)/shard_map/ppermute | solution.py:115
  66.2 2.3 %collective-permute-start.17 = (bf16[3,384,128]{2,1,0:T(8,128)(2,1)S(1)}, bf16[3,384,128]{2,1,0:T(8,128)(2,1)S(1)}, u32[]{:S(2)}, u32[]{:S(2)}) collective-permute-start(bf16[3,384,128]{2,1,0:T(8,128)(2,1)S(1)} %get-tuple-element.51.refs_0_), channel_id=1, source_target_pairs={{0,4},{4,0},{8,12},{12,8},{16,20},{20,16},{24,28},{28,24},{1,5},{5... | collective-permute-start | bytes 884744 | tf_op jit(solution)/shard_map/ppermute | solution.py:115
  66.2 3.2 %collective-permute-start.18 = (bf16[3,384,128]{2,1,0:T(8,128)(2,1)S(1)}, bf16[3,384,128]{2,1,0:T(8,128)(2,1)S(1)}, u32[]{:S(2)}, u32[]{:S(2)}) collective-permute-start(bf16[3,384,128]{2,1,0:T(8,128)(2,1)S(1)} %collective-permute-done.14.refs_1_), channel_id=1, source_target_pairs={{0,4},{4,0},{8,12},{12,8},{16,20},{20,16},{24,28},{28,24},{1,5},{5... | collective-permute-start | bytes 884744 | tf_op jit(solution)/shard_map/ppermute | solution.py:115
  66.7 2.7 %collective-permute-start.19 = (bf16[3,384,128]{2,1,0:T(8,128)(2,1)S(1)}, bf16[3,384,128]{2,1,0:T(8,128)(2,1)S(1)}, u32[]{:S(2)}, u32[]{:S(2)}) collective-permute-start(bf16[3,384,128]{2,1,0:T(8,128)(2,1)S(1)} %collective-permute-done.15.refs_2_), channel_id=1, source_target_pairs={{0,4},{4,0},{8,12},{12,8},{16,20},{20,16},{24,28},{28,24},{1,5},{5... | collective-permute-start | bytes 884744 | tf_op jit(solution)/shard_map/ppermute | solution.py:115
  66.7 2.7 %collective-permute-start.20 = (bf16[3,384,128]{2,1,0:T(8,128)(2,1)S(1)}, bf16[3,384,128]{2,1,0:T(8,128)(2,1)S(1)}, u32[]{:S(2)}, u32[]{:S(2)}) collective-permute-start(bf16[3,384,128]{2,1,0:T(8,128)(2,1)S(1)} %collective-permute-done.16.refs_3_), channel_id=1, source_target_pairs={{0,4},{4,0},{8,12},{12,8},{16,20},{20,16},{24,28},{28,24},{1,5},{5... | collective-permute-start | bytes 884744 | tf_op jit(solution)/shard_map/ppermute | solution.py:115
  67.2 9.7 %collective-permute-start.21 = (bf16[256,512]{1,0:T(8,128)(2,1)}, bf16[256,512]{1,0:T(8,128)(2,1)S(1)}, u32[]{:S(2)}, u32[]{:S(2)}) collective-permute-start(bf16[256,512]{1,0:T(8,128)(2,1)} %refs_0_), channel_id=1, source_target_pairs={{0,8},{4,12},{8,0},{12,4},{16,24},{20,28},{24,16},{28,20},{1,9},{5... | collective-permute-start | bytes 786440 | tf_op jit(solution)/shard_map/ppermute | solution.py:115
  68.4 8.5 %collective-permute-start.22 = (bf16[256,512]{1,0:T(8,128)(2,1)}, bf16[256,512]{1,0:T(8,128)(2,1)S(1)}, u32[]{:S(2)}, u32[]{:S(2)}) collective-permute-start(bf16[256,512]{1,0:T(8,128)(2,1)} %refs_0_), channel_id=1, source_target_pairs={{0,16},{4,20},{8,24},{12,28},{16,0},{20,4},{24,8},{28,12},{1,17},{... | collective-permute-start | bytes 786440 | tf_op jit(solution)/shard_map/ppermute | solution.py:115
  76.9 6.3 %collective-permute-start.23 = (bf16[384,128]{1,0:T(8,128)(2,1)S(1)}, bf16[384,128]{1,0:T(8,128)(2,1)S(1)}, u32[]{:S(2)}, u32[]{:S(2)}) collective-permute-start(bf16[384,128]{1,0:T(8,128)(2,1)S(1)} %get-tuple-element.60), channel_id=1, source_target_pairs={{0,24},{4,28},{8,16},{12,20},{16,8},{20,12},{24,0},{28,4},{1,25},{... | collective-permute-start | bytes 294920 | tf_op jit(solution)/shard_map/ppermute | solution.py:115
  78.3 7.3 %collective-permute-start.24 = (bf16[384,128]{1,0:T(8,128)(2,1)S(1)}, bf16[384,128]{1,0:T(8,128)(2,1)S(1)}, u32[]{:S(2)}, u32[]{:S(2)}) collective-permute-start(bf16[384,128]{1,0:T(8,128)(2,1)S(1)} %get-tuple-element.61), channel_id=1, source_target_pairs={{0,16},{4,20},{8,24},{12,28},{16,0},{20,4},{24,8},{28,12},{1,17},{... | collective-permute-start | bytes 294920 | tf_op jit(solution)/shard_map/ppermute | solution.py:115
  79.9 5.8 %collective-permute-start.25 = (bf16[384,128]{1,0:T(8,128)(2,1)S(1)}, bf16[384,128]{1,0:T(8,128)(2,1)S(1)}, u32[]{:S(2)}, u32[]{:S(2)}) collective-permute-start(bf16[384,128]{1,0:T(8,128)(2,1)S(1)} %get-tuple-element.62), channel_id=1, source_target_pairs={{0,8},{4,12},{8,0},{12,4},{16,24},{20,28},{24,16},{28,20},{1,9},{5... | collective-permute-start | bytes 294920 | tf_op jit(solution)/shard_map/ppermute | solution.py:115
  85.8 11.8 %collective-permute-start.26 = (bf16[384,512]{1,0:T(8,128)(2,1)S(1)}, bf16[384,512]{1,0:T(8,128)(2,1)S(1)}, u32[]{:S(2)}, u32[]{:S(2)}) collective-permute-start(bf16[384,512]{1,0:T(8,128)(2,1)S(1)} %pad_maximum_fusion.own), channel_id=1, source_target_pairs={{0,1},{1,0},{2,3},{3,2},{4,5},{5,4},{6,7},{7,6},{8,9},{9,8},{10,11... | collective-permute-start | bytes 1179656 | tf_op jit(solution)/shard_map/ppermute | solution.py:119
  88.2 9.4 %collective-permute-start.27 = (bf16[384,512]{1,0:T(8,128)(2,1)S(1)}, bf16[384,512]{1,0:T(8,128)(2,1)S(1)}, u32[]{:S(2)}, u32[]{:S(2)}) collective-permute-start(bf16[384,512]{1,0:T(8,128)(2,1)S(1)} %pad_maximum_fusion.own), channel_id=1, source_target_pairs={{1,2},{2,1},{5,6},{6,5},{9,10},{10,9},{13,14},{14,13},{17,18},{18,... | collective-permute-start | bytes 1179656 | tf_op jit(solution)/shard_map/ppermute | solution.py:123
  88.9 5.4 %collective-permute-start.28 = (bf16[128,512]{1,0:T(8,128)(2,1)S(1)}, bf16[128,512]{1,0:T(8,128)(2,1)}, u32[]{:S(2)}, u32[]{:S(2)}) collective-permute-start(bf16[128,512]{1,0:T(8,128)(2,1)S(1)} %slice.14), channel_id=1, source_target_pairs={{0,8},{4,12},{8,0},{12,4},{16,24},{20,28},{24,16},{28,20},{1,9},{5... | collective-permute-start | bytes 393224 | tf_op jit(solution)/shard_map/ppermute | solution.py:115
  89.7 5.1 %collective-permute-start.29 = (bf16[128,512]{1,0:T(8,128)(2,1)S(1)}, bf16[128,512]{1,0:T(8,128)(2,1)}, u32[]{:S(2)}, u32[]{:S(2)}) collective-permute-start(bf16[128,512]{1,0:T(8,128)(2,1)S(1)} %slice.15), channel_id=1, source_target_pairs={{0,16},{4,20},{8,24},{12,28},{16,0},{20,4},{24,8},{28,12},{1,17},{... | collective-permute-start | bytes 393224 | tf_op jit(solution)/shard_map/ppermute | solution.py:115
  90.9 8.8 %collective-permute-start.31 = (bf16[256,512]{1,0:T(8,128)(2,1)}, bf16[256,512]{1,0:T(8,128)(2,1)S(1)}, u32[]{:S(2)}, u32[]{:S(2)}) collective-permute-start(bf16[256,512]{1,0:T(8,128)(2,1)} %refs_0_), channel_id=1, source_target_pairs={{0,4},{4,0},{8,12},{12,8},{16,20},{20,16},{24,28},{28,24},{1,5},{5... | collective-permute-start | bytes 786440 | tf_op jit(solution)/shard_map/ppermute | solution.py:115
  94.4 5.9 %collective-permute-start.32 = (bf16[256,512]{1,0:T(8,128)(2,1)S(1)}, bf16[256,512]{1,0:T(8,128)(2,1)S(1)}, u32[]{:S(2)}, u32[]{:S(2)}) collective-permute-start(bf16[256,512]{1,0:T(8,128)(2,1)S(1)} %collective-permute-done.21.refs_1_), channel_id=1, source_target_pairs={{0,4},{4,0},{8,12},{12,8},{16,20},{20,16},{24,28},{28,24},{1,5},{5... | collective-permute-start | bytes 786440 | tf_op jit(solution)/shard_map/ppermute | solution.py:115
  97.6 5.0 %collective-permute-start.30 = (bf16[384,512]{1,0:T(8,128)(2,1)S(1)}, bf16[384,512]{1,0:T(8,128)(2,1)S(1)}, u32[]{:S(2)}, u32[]{:S(2)}) collective-permute-start(bf16[384,512]{1,0:T(8,128)(2,1)S(1)} %collective-permute-done.26.near), channel_id=1, source_target_pairs={{1,2},{2,1},{5,6},{6,5},{9,10},{10,9},{13,14},{14,13},{17,18},{18,... | collective-permute-start | bytes 1179656 | tf_op jit(solution)/shard_map/ppermute | solution.py:123
  98.3 16.1 %collective-permute-start.37 = (bf16[384,512]{1,0:T(8,128)(2,1)S(1)}, bf16[384,512]{1,0:T(8,128)(2,1)S(1)}, u32[]{:S(2)}, u32[]{:S(2)}) collective-permute-start(bf16[384,512]{1,0:T(8,128)(2,1)S(1)} %collective-permute-done.27.q1), channel_id=1, source_target_pairs={{1,0},{2,3},{5,4},{6,7},{9,8},{10,11},{13,12},{14,15},{17,16},{18,... | collective-permute-start | bytes 1179656 | tf_op jit(solution)/shard_map/ppermute | solution.py:127
  99.6 3.1 %collective-permute-start.33 = (bf16[256,512]{1,0:T(8,128)(2,1)S(1)}, bf16[256,512]{1,0:T(8,128)(2,1)}, u32[]{:S(2)}, u32[]{:S(2)}) collective-permute-start(bf16[256,512]{1,0:T(8,128)(2,1)S(1)} %collective-permute-done.22.refs_2_), channel_id=1, source_target_pairs={{0,4},{4,0},{8,12},{12,8},{16,20},{20,16},{24,28},{28,24},{1,5},{5... | collective-permute-start | bytes 786440 | tf_op jit(solution)/shard_map/ppermute | solution.py:115
  99.7 3.0 %collective-permute-start.34 = (bf16[128,512]{1,0:T(8,128)(2,1)}, bf16[128,512]{1,0:T(8,128)(2,1)}, u32[]{:S(2)}, u32[]{:S(2)}) collective-permute-start(bf16[128,512]{1,0:T(8,128)(2,1)} %collective-permute-done.28.refs_3_), channel_id=1, source_target_pairs={{0,4},{4,0},{8,12},{12,8},{16,20},{20,16},{24,28},{28,24},{1,5},{5... | collective-permute-start | bytes 393224 | tf_op jit(solution)/shard_map/ppermute | solution.py:115
  100.2 0.7 copy-start.3
  100.9 1.8 %collective-permute-start.35 = (bf16[128,512]{1,0:T(8,128)(2,1)}, bf16[128,512]{1,0:T(8,128)(2,1)}, u32[]{:S(2)}, u32[]{:S(2)}) collective-permute-start(bf16[128,512]{1,0:T(8,128)(2,1)} %collective-permute-done.29.refs_4_), channel_id=1, source_target_pairs={{0,4},{4,0},{8,12},{12,8},{16,20},{20,16},{24,28},{28,24},{1,5},{5... | collective-permute-start | bytes 393224 | tf_op jit(solution)/shard_map/ppermute | solution.py:115
  102.7 19.9 %collective-permute-start.36 = (bf16[384,512]{1,0:T(8,128)(2,1)S(1)}, bf16[384,512]{1,0:T(8,128)(2,1)S(1)}, u32[]{:S(2)}, u32[]{:S(2)}) collective-permute-start(bf16[384,512]{1,0:T(8,128)(2,1)S(1)} %collective-permute-done.30.q2), channel_id=1, source_target_pairs={{1,0},{2,3},{5,4},{6,7},{9,8},{10,11},{13,12},{14,15},{17,16},{18,... | collective-permute-start | bytes 1179656 | tf_op jit(solution)/shard_map/ppermute | solution.py:127
  114.4 1.0 copy-start.4

commit v3 on v2

--- a/solution.py
+++ b/solution.py
@@ -108,6 +108,7 @@
 LINE = 4
 CHIPS = 4
 NORM_EFFORT = 8 << 30
+PAIRS = ((1, 2), (3, 0))
 EARLY_EFFORT = 16 << 30
 
 
@@ -141,7 +142,7 @@
 
 
 def hbm():
-    return pl.BlockSpec(memory_space=pl.ANY)
+    return pl.BlockSpec(memory_space=pltpu.HBM)
 
 
 def full(array):
@@ -152,106 +153,103 @@
     return pl.CostEstimate(flops=flops, transcendentals=0, bytes_accessed=8 << 20)
 
 
-def normalize_kernel(where_ref, own, near, q1, p2, q2, p3, gain_ref, x_ref):
-    line = where_ref[2]
-    wide = own.shape[1]
+def halves_kernel(x_ref, y_ref, upper_ref, lower_ref):
+    upper_ref[...] = y_ref[...]
+    lower_ref[...] = x_ref[...]
+
+
+def halves(across, along):
+    rows, cols = across.shape[0] // 2, across.shape[1]
+    block = lambda half: pl.BlockSpec((rows, cols), lambda _: (half, 0))
+    return pl.pallas_call(
+        halves_kernel,
+        grid=(1,),
+        in_specs=[block(1), block(0)],
+        out_specs=[block(0)] * 2,
+        out_shape=[jax.ShapeDtypeStruct((rows, cols), across.dtype)] * 2,
+        compiler_params=pltpu.CompilerParams(vmem_limit_bytes=6 << 20),
+        name="halves",
+    )(across, along)
+
+
+def normalize_kernel(where_ref, *refs):
+    blocks, (gain_ref, x_ref, raw_ref, sems) = refs[:6], refs[6:]
+    chip, line = where_ref[0], where_ref[2]
+    wide = raw_ref.shape[2]
+    copies = [
+        pltpu.make_async_copy(block, raw_ref.at[n], sems.at[n]) for n, block in enumerate(blocks)
+    ]
+    for copy in copies:
+        copy.start()
+    for copy in copies:
+        copy.wait()
+    own, near, q1, p2, q2, p3 = [raw_ref[n] for n in range(6)]
     second, third, fourth, end = order(line)
     raw = [
-        own[...].astype(jnp.float32),
-        near[...].astype(jnp.float32),
-        jnp.where(end, p2[...], q1[...]).astype(jnp.float32),
-        jnp.where(end, p3[...], q2[...]).astype(jnp.float32),
+        own.astype(jnp.float32),
+        near.astype(jnp.float32),
+        jnp.where(end, p2, q1).astype(jnp.float32),
+        jnp.where(end, p3, q2).astype(jnp.float32),
     ]
     square = sum(jnp.sum(r * r, axis=1, keepdims=True) for r in raw)
     scale = lax.rsqrt(square * (1.0 / (LINE * wide)) + 1e-06)
     for r, feature in zip(raw, (line, second, third, fourth)):
         normed = (r * scale * gain_ref[feature]).astype(jnp.bfloat16)
-        x_ref[2 * feature] = normed[:, : wide // 2]
-        x_ref[2 * feature + 1] = normed[:, wide // 2 :]
+        x_ref[:, pl.ds(pl.multiple_of((feature ^ chip) * wide, wide), wide)] = normed
 
 
 def normalize(where, blocks, gain):
     rows, wide = blocks[0].shape
     return pl.pallas_call(
         normalize_kernel,
-        in_specs=[smem()] + [vmem()] * 7,
+        in_specs=[smem()] + [hbm()] * 6 + [vmem()],
         out_specs=vmem(),
-        out_shape=jax.ShapeDtypeStruct((2 * LINE, rows, wide // 2), jnp.bfloat16),
-        compiler_params=pltpu.CompilerParams(vmem_limit_bytes=20 << 20),
+        out_shape=jax.ShapeDtypeStruct((rows, LINE * wide), jnp.bfloat16),
+        scratch_shapes=[pltpu.VMEM((6, rows, wide), jnp.bfloat16), pltpu.SemaphoreType.DMA((6,))],
+        compiler_params=pltpu.CompilerParams(vmem_limit_bytes=12 << 20),
         cost_estimate=effort(NORM_EFFORT),
         name="normalize",
     )(where, *blocks, gain)
 
 
-def project_kernel(where_ref, x_ref, cos_ref, sin_ref, *refs):
-    weights, outs, (slot_ref,) = refs[:10], refs[10:16], refs[16:]
-    sent, key_ref, val_ref = outs[:CHIPS], outs[CHIPS], outs[CHIPS + 1]
-    step = pl.program_id(0)
+def head_columns(chip, pair, hsize):
+    for i, m in enumerate(pair):
+        for j in range(3):
+            source = pl.multiple_of((CHIPS * j + (chip ^ m)) * hsize, hsize)
+            yield pl.ds(source, hsize), slice((3 * i + j) * hsize, (3 * i + j + 1) * hsize)
+
+
+def project_kernel(where_ref, x_ref, cos_ref, sin_ref, *refs, pair):
+    weights, (out_a, out_b, w_ref) = refs[:10], refs[10:]
     chip, core = where_ref[0], where_ref[1]
-    wide = 2 * x_ref.shape[2]
     hsize = cos_ref.shape[1]
-
-    total = None
-    for side in range(2):
-        half = core if side == 0 else 1 - core
-        for m in range(CHIPS):
-            x = x_ref[2 * (chip ^ m) + half]
-            if m < 3:
-                parts = [(x, weights[5 * side + m])]
-            else:
-                parts = [
-                    (x[:, : wide // 4], weights[5 * side + 3]),
-                    (x[:, wide // 4 :], weights[5 * side + 4]),
-                ]
-            for left, right in parts:
-                part = jnp.dot(left, right[...], preferred_element_type=jnp.float32)
-                total = part if total is None else total + part
-
-    @pl.when(step < 2)
-    def _():
-        for h in range(CHIPS):
-            u = total[:, h * hsize : (h + 1) * hsize]
-            u = u * cos_ref[...] + pltpu.roll(u, hsize // 2, 1) * sin_ref[...]
-            slot_ref[h] = u.astype(jnp.bfloat16)
-
-    @pl.when(step == 2)
-    def _():
-        for h in range(CHIPS):
-            slot_ref[h] = total[:, h * hsize : (h + 1) * hsize].astype(jnp.bfloat16)
-
-    for m in range(CHIPS):
-        sent[m][0] = slot_ref[chip ^ m]
-
-    @pl.when(step == 1)
-    def _():
-        for h in range(CHIPS):
-            key_ref[:, h * hsize : (h + 1) * hsize] = slot_ref[h]
-
-    @pl.when(step == 2)
-    def _():
-        for h in range(CHIPS):
-            val_ref[:, h * hsize : (h + 1) * hsize] = slot_ref[h]
-
-
-def project(where, x, cosine, sine, weights):
+    depth = weights[0].shape[0]
+    for source, target in head_columns(chip, pair, hsize):
+        for side, half in ((0, core), (1, 1 - core)):
+            for m in range(5):
+                piece = weights[5 * side + m]
+                row = (2 * min(m, 3) + half) * depth + (depth // 2 if m == 4 else 0)
+                row = pl.multiple_of(row, depth // 2)
+                w_ref[pl.ds(row, piece.shape[0]), target] = piece[:, source]
+    total = jnp.dot(x_ref[...], w_ref[...], preferred_element_type=jnp.float32)
+    for i, out in enumerate((out_a, out_b)):
+        for j in range(3):
+            u = total[:, (3 * i + j) * hsize : (3 * i + j + 1) * hsize]
+            if j < 2:
+                u = u * cos_ref[...] + pltpu.roll(u, hsize // 2, 1) * sin_ref[...]
+            out[j] = u.astype(jnp.bfloat16)
+
+
+def project(where, pair, x, cosine, sine, weights):
     rows, hsize = cosine.shape
-    wide = 2 * x.shape[2]
-    cols = weights[0].shape[1] // 3
-    return pl.pallas_call(
-        project_kernel,
-        grid=(3,),
-        in_specs=[smem()]
-        + [full(a) for a in (x, cosine, sine)]
-        + [pl.BlockSpec((w.shape[0], cols), lambda j: (0, j)) for w in weights],
-        out_specs=[pl.BlockSpec((1, rows, hsize), lambda j: (j, 0, 0))] * CHIPS
-        + [pl.BlockSpec((rows, cols), lambda j: (0, 0))] * 2,
-        out_shape=[jax.ShapeDtypeStruct((3, rows, hsize), jnp.bfloat16)] * CHIPS
-        + [jax.ShapeDtypeStruct((rows, cols), jnp.bfloat16)] * 2,
-        scratch_shapes=[
-            pltpu.VMEM((CHIPS, rows, hsize), jnp.bfloat16),
-        ],
-        compiler_params=pltpu.CompilerParams(vmem_limit_bytes=24 << 20),
-        cost_estimate=effort(2 * rows * LINE * wide * 3 * cols),
+    return pl.pallas_call(
+        functools.partial(project_kernel, pair=pair),
+        in_specs=[smem()] + [vmem()] * (3 + len(weights)),
+        out_specs=[vmem()] * 2,
+        out_shape=[jax.ShapeDtypeStruct((3, rows, hsize), jnp.bfloat16)] * 2,
+        scratch_shapes=[pltpu.VMEM((x.shape[1], 6 * hsize), jnp.bfloat16)],
+        compiler_params=pltpu.CompilerParams(vmem_limit_bytes=20 << 20),
+        cost_estimate=effort(2 * x.size * 6 * hsize),
         name="project",
     )(where, x, cosine, sine, *weights)
 
@@ -406,15 +404,19 @@
     sine = jnp.concatenate([-sine, sine], axis=1)
 
     flat = w_qkv.reshape(depth, -1)
-    near, q1 = outer(tokens), inner(tokens)
+    near, q1, cosine, sine, where = together(outer(tokens), inner(tokens), cosine, sine, where)
     q2, p2 = inner(near), outward(q1)
     w_x, w_y = swap(flat, 2), swap(flat, 4)
-    q2, p2, w_x, w_y = together(q2, p2, w_x, w_y)
-    p3, far_a, far_b = outward(q2), swap(w_y[:half], 2), swap(w_x[half:], 4)
+
+    upper, lower = halves(w_x, w_y)
+    p3, far_a, far_b = outward(q2), swap(upper, 2), swap(lower, 4)
+    x = normalize(where, (tokens, near, q1, p2, q2, p3), gain.reshape(LINE, 1, wide))
     held = (flat, w_x, w_y, far_a, far_b)
     weights = held + tuple(swap(w, 1) for w in held)
-    x = normalize(where, (tokens, near, q1, p2, q2, p3), gain.reshape(LINE, 1, wide))
-    *sent, keys, vals = project(where, x, cosine, sine, weights)
+    sent = [None] * CHIPS
+    for pair in PAIRS:
+        sent[pair[0]], sent[pair[1]] = project(where, pair, x, cosine, sine, weights)
+    keys, vals = [heads_in_order([a[j] for a in sent], chip) for j in (1, 2)]
 
     pieces = [sent[0]] + [swap(sent[m], 2 * m) for m in range(1, CHIPS)]
     *pieces, w_late = together(*pieces, w_out)
@@ -426,12 +428,11 @@
     back = [heads_out[0]] + [swap(heads_out[m], 2 * m) for m in range(1, CHIPS)]
     attended = heads_in_order(back, chip)
     attended, w_x, w_y = together(attended, w_x, w_y)
-    near, q1, far_a, far_b = together(
-        outer(attended), inner(attended), swap(w_y[:half], 2), swap(w_x[half:], 4)
-    )
+    upper, lower = halves(w_x, w_y)
+    near, q1, far_a, far_b = outer(attended), inner(attended), swap(upper, 2), swap(lower, 4)
     pieces = (w_late, w_x, w_y, far_a, far_b)
     q2, p2 = inner(near), outward(q1)
-    q2, *others = together(q2, *[swap(w, 1) for w in pieces])
+    others = [swap(w, 1) for w in pieces]
     p3 = outward(q2)
     total, w_last = early(where, (attended, near, q1, p2), (*pieces, *others))
     mixed = last(where, q2, p3, total, w_last)

time: 125 us -> 120 us (0.960)
  local copies, waits for them, and re-layouts: 7.1 us -> 3.79 us
  waiting for transfers between devices: 61.5 us -> 59.3 us
    ppermute x28, waiting for transfers between devices: 33.5 us -> 25.5 us  [swap(): return lax.ppermute(x, 'gx', [(i, i ^ mask) for i in range(2 * CHIPS)])]
    ppermute x4, waiting for transfers between devices: 22.2 us -> 26.1 us  [outward(): return lax.ppermute(x, 'gy', [(1, 0), (2, 3)])]
    ppermute x2, waiting for transfers between devices: 5.82 us -> 7.67 us  [outer(): return lax.ppermute(x, 'gy', [(0, 1), (1, 0), (2, 3), (3, 2)])]
    reshape x2 -> x0, local copies, waits for them, and re-layouts: 1.68 us -> none  [the longest x1 0.84 us: blocks_plan(): keys.reshape(rows, heads, hsize)]
    unnamed x14 -> x12, local copies, waits for them, and re-layouts: 3.69 us -> 2.12 us
    ppermute x4, starting transfers between devices: 4.15 us -> 2.71 us  [inner(): return lax.ppermute(x, 'gy', [(1, 2), (2, 1)])]
    pallas_call x2 -> x5, Pallas kernels: 7.33 us -> 7.67 us  [the longest x2 5.16 us: project(): pl.pallas_call(functools.partial(project_kernel, pair=pair), in_specs=[sm...]
  transfers between devices with their start and end apart: 38 -> 38, of which waited for: 14 -> 14; matrix products, arithmetic and copies ran while one was open for 4% -> 5% of each run, Pallas kernels for 9% -> 13%
where the time goes in v3:
time: 120 us; the launch traced here: 119 us
  waiting for transfers between devices  59.3 us (49%)
  starting transfers between devices  33.4 us (28%)
  Pallas kernels  19.4 us (16%)
  local copies, waits for them, and re-layouts  3.79 us (3%)
  other arithmetic  1.69 us (1%)
    ppermute x4, waiting for transfers between devices, outward(): return lax.ppermute(x, 'gy', [(1, 0), (2, 3)])  26.1 us
    ppermute x28, waiting for transfers between devices, swap(): return lax.ppermute(x, 'gx', [(i, i ^ mask) for i in range(2 * CHIPS)])  25.5 us
    ppermute x28, starting transfers between devices, swap(): return lax.ppermute(x, 'gx', [(i, i ^ mask) for i in range(2 * CHIPS)])  19 us
    pallas_call x1, Pallas kernels, attend(): pl.pallas_call(functools.partial(attend_kernel, scale=scale), in_specs=[s...  8.66 us
    ppermute x2, waiting for transfers between devices, outer(): return lax.ppermute(x, 'gy', [(0, 1), (1, 0), (2, 3), (3, 2)])  7.67 us
    ppermute x2, starting transfers between devices, outer(): return lax.ppermute(x, 'gy', [(0, 1), (1, 0), (2, 3), (3, 2)])  6.62 us
    pallas_call x2, Pallas kernels, project(): pl.pallas_call(functools.partial(project_kernel, pair=pair), in_specs=[sm...  5.16 us
    ppermute x4, starting transfers between devices, outward(): return lax.ppermute(x, 'gy', [(1, 0), (2, 3)])  5.15 us
  transfers between devices with their start and end apart: 38, of which 14 were waited for; matrix products, arithmetic and copies ran while one was open for 5% of the time, Pallas kernels for 13%

profile of v3, /device:TPU:0, one launch (start us, length us, event | category | flops | bytes accessed | tf_op | source)
XLA Modules:
  0.0 118.6 jit_solution(17058112337381213700)
XLA Ops:
  0.6 3.1 %collective-permute-start = (bf16[384,512]{1,0:T(8,128)(2,1)}, bf16[384,512]{1,0:T(8,128)(2,1)S(1)}, u32[]{:S(2)}, u32[]{:S(2)}) collective-permute-start(bf16[384,512]{1,0:T(8,128)(2,1)} %refs_0_.1), channel_id=1, source_target_pairs={{0,1},{1,0},{2,3},{3,2},{4,5},{5,4},{6,7},{7,6},{8,9},{9,8},{10,11... | collective-permute-start | bytes 1179656 | tf_op jit(solution)/shard_map/ppermute | solution.py:120
  3.7 0.7 collective-permute-start.1
  4.4 1.7 %reshape.193.refs_0_ = bf16[256,1536]{1,0:T(8,128)(2,1)S(1)} reshape(bf16[256,3,4,128]{3,2,1,0:T(4,128)(2,1)} %param.7) | data formatting | bytes 1572864 | tf_op jit(solution)/shard_map/reshape | solution.py:406
  6.1 1.6 %collective-permute-start.5 = (bf16[256,1536]{1,0:T(8,128)(2,1)S(1)}, bf16[256,1536]{1,0:T(8,128)(2,1)S(1)}, u32[]{:S(2)}, u32[]{:S(2)}) collective-permute-start(bf16[256,1536]{1,0:T(8,128)(2,1)S(1)} %reshape.193.refs_0_), channel_id=1, source_target_pairs={{0,8},{4,12},{8,0},{12,4},{16,24},{20,28},{24,16},{28,20},{1,9},{5... | collective-permute-start | bytes 2359304 | tf_op jit(solution)/shard_map/ppermute | solution.py:116
  7.6 1.5 %collective-permute-start.6 = (bf16[256,1536]{1,0:T(8,128)(2,1)S(1)}, bf16[256,1536]{1,0:T(8,128)(2,1)S(1)}, u32[]{:S(2)}, u32[]{:S(2)}) collective-permute-start(bf16[256,1536]{1,0:T(8,128)(2,1)S(1)} %reshape.193.refs_0_), channel_id=1, source_target_pairs={{0,16},{4,20},{8,24},{12,28},{16,0},{20,4},{24,8},{28,12},{1,17},{... | collective-permute-start | bytes 2359304 | tf_op jit(solution)/shard_map/ppermute | solution.py:116
  9.2 0.2 reduce-window.9
  9.4 0.1 select_reduce_fusion
  9.5 0.1 pad_add_fusion.where_ref
  9.6 0.8 fusion
  10.3 0.2 pad_maximum_fusion.3
  10.5 2.5 %collective-permute-done.refs_1_ = bf16[384,512]{1,0:T(8,128)(2,1)S(1)} collective-permute-done((bf16[384,512]{1,0:T(8,128)(2,1)}, bf16[384,512]{1,0:T(8,128)(2,1)S(1)}, u32[]{:S(2)}, u32[]{:S(2)}) %collective-permute-start) | collective-permute-done | bytes 393248 | tf_op jit(solution)/shard_map/ppermute | solution.py:120
  13.1 0.0 collective-permute-done.1.refs_2_
  13.1 0.7 collective-permute-start.3
  13.7 1.3 %collective-permute-start.2 = (bf16[384,512]{1,0:T(8,128)(2,1)S(1)}, bf16[384,512]{1,0:T(8,128)(2,1)S(1)}, u32[]{:S(2)}, u32[]{:S(2)}) collective-permute-start(bf16[384,512]{1,0:T(8,128)(2,1)S(1)} %collective-permute-done.1.refs_2_), channel_id=1, source_target_pairs={{1,0},{2,3},{5,4},{6,7},{9,8},{10,11},{13,12},{14,15},{17,16},{18,... | collective-permute-start | bytes 1179656 | tf_op jit(solution)/shard_map/ppermute | solution.py:128
  15.1 1.3 %collective-permute-start.4 = (bf16[384,512]{1,0:T(8,128)(2,1)S(1)}, bf16[384,512]{1,0:T(8,128)(2,1)S(1)}, u32[]{:S(2)}, u32[]{:S(2)}) collective-permute-start(bf16[384,512]{1,0:T(8,128)(2,1)S(1)} %collective-permute-done.3.refs_4_), channel_id=1, source_target_pairs={{1,0},{2,3},{5,4},{6,7},{9,8},{10,11},{13,12},{14,15},{17,16},{18,... | collective-permute-start | bytes 1179656 | tf_op jit(solution)/shard_map/ppermute | solution.py:128
  16.4 8.8 %collective-permute-done.5.x_ref.refs_1_ = bf16[256,1536]{1,0:T(8,128)(2,1)S(1)} collective-permute-done((bf16[256,1536]{1,0:T(8,128)(2,1)S(1)}, bf16[256,1536]{1,0:T(8,128)(2,1)S(1)}, u32[]{:S(2)}, u32[]{:S(2)}) %collective-permute-start.5) | collective-permute-done | bytes 786464 | tf_op jit(solution)/shard_map/ppermute | solution.py:116
  25.1 1.2 %collective-permute-done.6.y_ref.refs_2_ = bf16[256,1536]{1,0:T(8,128)(2,1)S(1)} collective-permute-done((bf16[256,1536]{1,0:T(8,128)(2,1)S(1)}, bf16[256,1536]{1,0:T(8,128)(2,1)S(1)}, u32[]{:S(2)}, u32[]{:S(2)}) %collective-permute-start.6) | collective-permute-done | bytes 786464 | tf_op jit(solution)/shard_map/ppermute | solution.py:116
  26.4 0.1 halves.2
  26.4 0.6 collective-permute-start.7
  27.0 1.5 %collective-permute-start.8 = (bf16[128,1536]{1,0:T(8,128)(2,1)S(1)}, bf16[128,1536]{1,0:T(8,128)(2,1)S(1)}, u32[]{:S(2)}, u32[]{:S(2)}) collective-permute-start(bf16[128,1536]{1,0:T(8,128)(2,1)S(1)} %get-tuple-element.42), channel_id=1, source_target_pairs={{0,16},{4,20},{8,24},{12,28},{16,0},{20,4},{24,8},{28,12},{1,17},{... | collective-permute-start | bytes 1179656 | tf_op jit(solution)/shard_map/ppermute | solution.py:116
  28.5 2.3 %collective-permute-done.2.refs_3_ = bf16[384,512]{1,0:T(8,128)(2,1)S(1)} collective-permute-done((bf16[384,512]{1,0:T(8,128)(2,1)S(1)}, bf16[384,512]{1,0:T(8,128)(2,1)S(1)}, u32[]{:S(2)}, u32[]{:S(2)}) %collective-permute-start.2) | collective-permute-done | bytes 393248 | tf_op jit(solution)/shard_map/ppermute | solution.py:128
  30.8 8.0 %collective-permute-done.4.refs_5_ = bf16[384,512]{1,0:T(8,128)(2,1)S(1)} collective-permute-done((bf16[384,512]{1,0:T(8,128)(2,1)S(1)}, bf16[384,512]{1,0:T(8,128)(2,1)S(1)}, u32[]{:S(2)}, u32[]{:S(2)}) %collective-permute-start.4) | collective-permute-done | bytes 393248 | tf_op jit(solution)/shard_map/ppermute | solution.py:128
  38.8 0.5 collective-permute-start.12
  39.3 0.1 collective-permute-start.13
  39.4 2.4 %normalize.1.x_ref = bf16[384,2048]{1,0:T(8,128)(2,1)S(1)} custom-call(s32[3]{0:T(128)S(1)} %pad_add_fusion.where_ref, bf16[384,512]{1,0:T(8,128)(2,1)S(1)} %copy-done, bf16[384,512]{1,0:T(8,128)(2,1)S(1)} %collective-permute-done.refs_1_, bf16[384,512]{1,0:T(8,128)(2,1)S(1)} %collective-permute-done.1.refs_2_, ...), custom_call_target="tpu_custom_call" | custom-call | flops 8589934592 | bytes 8388608 | tf_op jit(solution)/shard_map/normalize/pallas_call | solution.py:203
  41.9 0.3 collective-permute-done.13.refs_9_
  42.2 2.6 %project.3 = (bf16[3,384,128]{2,1,0:T(8,128)(2,1)S(1)}, bf16[3,384,128]{2,1,0:T(8,128)(2,1)S(1)}) custom-call(s32[3]{0:T(128)S(1)} %pad_add_fusion.where_ref, bf16[384,2048]{1,0:T(8,128)(2,1)S(1)} %normalize.1.x_ref, f32[384,128]{1,0:T(8,128)S(1)} %get-tuple-element.39.cos_ref, f32[384,128]{1,0:T(8,128)S(1)} %get-tuple-element.40.sin_ref, ...), custom_call_target="tpu_custom_call" | custom-call | flops 1207959552 | bytes 8388608 | tf_op jit(solution)/shard_map/project/pallas_call | solution.py:245
  44.8 1.6 %collective-permute-start.14 = (bf16[3,384,128]{2,1,0:T(8,128)(2,1)S(1)}, bf16[3,384,128]{2,1,0:T(8,128)(2,1)S(1)}, u32[]{:S(2)}, u32[]{:S(2)}) collective-permute-start(bf16[3,384,128]{2,1,0:T(8,128)(2,1)S(1)} %get-tuple-element.44), channel_id=1, source_target_pairs={{0,8},{4,12},{8,0},{12,4},{16,24},{20,28},{24,16},{28,20},{1,9},{5... | collective-permute-start | bytes 884744 | tf_op jit(solution)/shard_map/ppermute | solution.py:116
  46.4 1.5 %collective-permute-start.15 = (bf16[3,384,128]{2,1,0:T(8,128)(2,1)S(1)}, bf16[3,384,128]{2,1,0:T(8,128)(2,1)S(1)}, u32[]{:S(2)}, u32[]{:S(2)}) collective-permute-start(bf16[3,384,128]{2,1,0:T(8,128)(2,1)S(1)} %get-tuple-element.45), channel_id=1, source_target_pairs={{0,16},{4,20},{8,24},{12,28},{16,0},{20,4},{24,8},{28,12},{1,17},{... | collective-permute-start | bytes 884744 | tf_op jit(solution)/shard_map/ppermute | solution.py:116
  47.9 2.6 %project.2 = (bf16[3,384,128]{2,1,0:T(8,128)(2,1)S(1)}, bf16[3,384,128]{2,1,0:T(8,128)(2,1)S(1)}) custom-call(s32[3]{0:T(128)S(1)} %pad_add_fusion.where_ref, bf16[384,2048]{1,0:T(8,128)(2,1)S(1)} %normalize.1.x_ref, f32[384,128]{1,0:T(8,128)S(1)} %get-tuple-element.39.cos_ref, f32[384,128]{1,0:T(8,128)S(1)} %get-tuple-element.40.sin_ref, ...), custom_call_target="tpu_custom_call" | custom-call | flops 1207959552 | bytes 8388608 | tf_op jit(solution)/shard_map/project/pallas_call | solution.py:245
  50.5 0.5 collective-permute-start.16
  51.0 3.7 %collective-permute-done.14.refs_1_ = bf16[3,384,128]{2,1,0:T(8,128)(2,1)S(1)} collective-permute-done((bf16[3,384,128]{2,1,0:T(8,128)(2,1)S(1)}, bf16[3,384,128]{2,1,0:T(8,128)(2,1)S(1)}, u32[]{:S(2)}, u32[]{:S(2)}) %collective-permute-start.14) | collective-permute-done | bytes 294944 | tf_op jit(solution)/shard_map/ppermute | solution.py:116
  54.7 6.7 %collective-permute-done.15.refs_2_ = bf16[3,384,128]{2,1,0:T(8,128)(2,1)S(1)} collective-permute-done((bf16[3,384,128]{2,1,0:T(8,128)(2,1)S(1)}, bf16[3,384,128]{2,1,0:T(8,128)(2,1)S(1)}, u32[]{:S(2)}, u32[]{:S(2)}) %collective-permute-start.15) | collective-permute-done | bytes 294944 | tf_op jit(solution)/shard_map/ppermute | solution.py:116
  61.5 0.5 collective-permute-start.18
  62.0 0.1 collective-permute-start.19
  62.0 0.4 collective-permute-start.20
  62.5 1.2 %collective-permute-start.21 = (bf16[256,512]{1,0:T(8,128)(2,1)S(1)}, bf16[256,512]{1,0:T(8,128)(2,1)S(1)}, u32[]{:S(2)}, u32[]{:S(2)}) collective-permute-start(bf16[256,512]{1,0:T(8,128)(2,1)S(1)} %copy-done.1), channel_id=1, source_target_pairs={{0,8},{4,12},{8,0},{12,4},{16,24},{20,28},{24,16},{28,20},{1,9},{5... | collective-permute-start | bytes 786440 | tf_op jit(solution)/shard_map/ppermute | solution.py:116
  63.7 0.8 collective-permute-start.22
  64.6 8.7 %attend.1 = (bf16[384,128]{1,0:T(8,128)(2,1)S(1)}, bf16[384,128]{1,0:T(8,128)(2,1)S(1)}, bf16[384,128]{1,0:T(8,128)(2,1)S(1)}, bf16[384,128]{1,0:T(8,128)(2,1)S(1)}) custom-call(s32[3]{0:T(128)S(1)} %pad_add_fusion.where_ref, s32[6]{0:T(128)S(1)} %bitcast_subtract_fusion.start_ref, bf16[3,384,128]{2,1,0:T(8,128)(2,1)S(1)} %get-tuple-element.47.refs_0_, ...), custom_call_target="tpu_custom_call" | custom-call | flops 2415919104 | bytes 8388608 | tf_op jit(solution)/shard_map/attend/pallas_call | solution.py:305
  73.3 1.5 %collective-permute-start.23 = (bf16[384,128]{1,0:T(8,128)(2,1)S(1)}, bf16[384,128]{1,0:T(8,128)(2,1)S(1)}, u32[]{:S(2)}, u32[]{:S(2)}) collective-permute-start(bf16[384,128]{1,0:T(8,128)(2,1)S(1)} %get-tuple-element.56), channel_id=1, source_target_pairs={{0,24},{4,28},{8,16},{12,20},{16,8},{20,12},{24,0},{28,4},{1,25},{... | collective-permute-start | bytes 294920 | tf_op jit(solution)/shard_map/ppermute | solution.py:116
  74.7 1.5 %collective-permute-start.24 = (bf16[384,128]{1,0:T(8,128)(2,1)S(1)}, bf16[384,128]{1,0:T(8,128)(2,1)S(1)}, u32[]{:S(2)}, u32[]{:S(2)}) collective-permute-start(bf16[384,128]{1,0:T(8,128)(2,1)S(1)} %get-tuple-element.57), channel_id=1, source_target_pairs={{0,16},{4,20},{8,24},{12,28},{16,0},{20,4},{24,8},{28,12},{1,17},{... | collective-permute-start | bytes 294920 | tf_op jit(solution)/shard_map/ppermute | solution.py:116
  76.2 0.6 collective-permute-start.25
  76.8 2.1 %collective-permute-done.23 = bf16[384,128]{1,0:T(8,128)(2,1)S(1)} collective-permute-done((bf16[384,128]{1,0:T(8,128)(2,1)S(1)}, bf16[384,128]{1,0:T(8,128)(2,1)S(1)}, u32[]{:S(2)}, u32[]{:S(2)}) %collective-permute-start.23) | collective-permute-done | bytes 98336 | tf_op jit(solution)/shard_map/ppermute | solution.py:116
  78.9 1.4 %collective-permute-done.24 = bf16[384,128]{1,0:T(8,128)(2,1)S(1)} collective-permute-done((bf16[384,128]{1,0:T(8,128)(2,1)S(1)}, bf16[384,128]{1,0:T(8,128)(2,1)S(1)}, u32[]{:S(2)}, u32[]{:S(2)}) %collective-permute-start.24) | collective-permute-done | bytes 98336 | tf_op jit(solution)/shard_map/ppermute | solution.py:116
  80.3 1.1 collective-permute-done.25
  81.5 0.1 broadcast_select_fusion.5
  81.6 0.7 collective-permute-start.29
  82.3 3.5 %collective-permute-start.26 = (bf16[384,512]{1,0:T(8,128)(2,1)S(1)}, bf16[384,512]{1,0:T(8,128)(2,1)S(1)}, u32[]{:S(2)}, u32[]{:S(2)}) collective-permute-start(bf16[384,512]{1,0:T(8,128)(2,1)S(1)} %pad_maximum_fusion.own), channel_id=1, source_target_pairs={{0,1},{1,0},{2,3},{3,2},{4,5},{5,4},{6,7},{7,6},{8,9},{9,8},{10,11... | collective-permute-start | bytes 1179656 | tf_op jit(solution)/shard_map/ppermute | solution.py:120
  85.9 0.1 collective-permute-start.34
  86.0 1.6 %collective-permute-start.31 = (bf16[128,512]{1,0:T(8,128)(2,1)S(1)}, bf16[128,512]{1,0:T(8,128)(2,1)S(1)}, u32[]{:S(2)}, u32[]{:S(2)}) collective-permute-start(bf16[128,512]{1,0:T(8,128)(2,1)S(1)} %get-tuple-element.65), channel_id=1, source_target_pairs={{0,8},{4,12},{8,0},{12,4},{16,24},{20,28},{24,16},{28,20},{1,9},{5... | collective-permute-start | bytes 393224 | tf_op jit(solution)/shard_map/ppermute | solution.py:116
  87.6 0.6 collective-permute-start.32
  88.1 1.3 %collective-permute-start.30 = (bf16[384,512]{1,0:T(8,128)(2,1)S(1)}, bf16[384,512]{1,0:T(8,128)(2,1)S(1)}, u32[]{:S(2)}, u32[]{:S(2)}) collective-permute-start(bf16[384,512]{1,0:T(8,128)(2,1)S(1)} %collective-permute-done.29.q1), channel_id=1, source_target_pairs={{1,0},{2,3},{5,4},{6,7},{9,8},{10,11},{13,12},{14,15},{17,16},{18,... | collective-permute-start | bytes 1179656 | tf_op jit(solution)/shard_map/ppermute | solution.py:128
  89.4 5.1 %collective-permute-done.26.near = bf16[384,512]{1,0:T(8,128)(2,1)S(1)} collective-permute-done((bf16[384,512]{1,0:T(8,128)(2,1)S(1)}, bf16[384,512]{1,0:T(8,128)(2,1)S(1)}, u32[]{:S(2)}, u32[]{:S(2)}) %collective-permute-start.26) | collective-permute-done | bytes 393248 | tf_op jit(solution)/shard_map/ppermute | solution.py:120
  94.6 0.7 collective-permute-start.27
  95.3 0.1 collective-permute-start.35
  95.4 0.6 collective-permute-start.36
  96.0 0.1 collective-permute-start.37
  96.1 1.1 copy.11
  97.2 1.1 copy.10
  98.3 1.3 %collective-permute-start.28 = (bf16[384,512]{1,0:T(8,128)(2,1)S(1)}, bf16[384,512]{1,0:T(8,128)(2,1)S(1)}, u32[]{:S(2)}, u32[]{:S(2)}) collective-permute-start(bf16[384,512]{1,0:T(8,128)(2,1)S(1)} %collective-permute-done.27.q2), channel_id=1, source_target_pairs={{1,0},{2,3},{5,4},{6,7},{9,8},{10,11},{13,12},{14,15},{17,16},{18,... | collective-permute-start | bytes 1179656 | tf_op jit(solution)/shard_map/ppermute | solution.py:128
  99.6 5.2 %collective-permute-done.30.p2 = bf16[384,512]{1,0:T(8,128)(2,1)S(1)} collective-permute-done((bf16[384,512]{1,0:T(8,128)(2,1)S(1)}, bf16[384,512]{1,0:T(8,128)(2,1)S(1)}, u32[]{:S(2)}, u32[]{:S(2)}) %collective-permute-start.30) | collective-permute-done | bytes 393248 | tf_op jit(solution)/shard_map/ppermute | solution.py:128
  104.8 1.5 %early.1 = (f32[384,512]{1,0:T(8,128)S(1)}, bf16[512,512]{1,0:T(8,128)(2,1)S(1)}) custom-call(s32[3]{0:T(128)S(1)} %pad_add_fusion.where_ref, bf16[384,512]{1,0:T(8,128)(2,1)S(1)} %pad_maximum_fusion.own, bf16[384,512]{1,0:T(8,128)(2,1)S(1)} %collective-permute-done.26.near, bf16[384,512]{1,0:T(8,128)(2,1)S(1)} %collective-permute-done.29.q1, ...), custom_call_target="tpu_custom_call" | custom-call | flops 17179869184 | bytes 8388608 | tf_op jit(solution)/shard_map/early/pallas_call | solution.py:345
  106.2 10.7 %collective-permute-done.28.p3 = bf16[384,512]{1,0:T(8,128)(2,1)S(1)} collective-permute-done((bf16[384,512]{1,0:T(8,128)(2,1)S(1)}, bf16[384,512]{1,0:T(8,128)(2,1)S(1)}, u32[]{:S(2)}, u32[]{:S(2)}) %collective-permute-start.28) | collective-permute-done | bytes 393248 | tf_op jit(solution)/shard_map/ppermute | solution.py:128
  116.9 1.7 %last.1 = bf16[384,512]{1,0:T(8,128)(2,1)} custom-call(s32[3]{0:T(128)S(1)} %pad_add_fusion.where_ref, bf16[384,512]{1,0:T(8,128)(2,1)S(1)} %collective-permute-done.27.q2, bf16[384,512]{1,0:T(8,128)(2,1)S(1)} %collective-permute-done.28.p3, f32[384,512]{1,0:T(8,128)S(1)} %get-tuple-element.67.total_ref, bf16[512,512]{1,0:T(8,128)(2,1)S(1)} %get-tuple-element.68.w_ref), custom_call_target="tpu_custom_call" | custom-call | flops 201326592 | bytes 8388608 | tf_op jit(solution)/shard_map/last/pallas_call | solution.py:368
  (52 shorter events, 0.4 us)
Async XLA Ops:
  0.6 8.5 %copy-start.4 = (s32[6]{0:T(128)S(1)}, s32[6]{0:T(128)}, u32[]{:S(2)}) copy-start(s32[6]{0:T(128)} %param.9) | copy-start | bytes 76
  0.6 12.4 %collective-permute-start = (bf16[384,512]{1,0:T(8,128)(2,1)}, bf16[384,512]{1,0:T(8,128)(2,1)S(1)}, u32[]{:S(2)}, u32[]{:S(2)}) collective-permute-start(bf16[384,512]{1,0:T(8,128)(2,1)} %refs_0_.1), channel_id=1, source_target_pairs={{0,1},{1,0},{2,3},{3,2},{4,5},{5,4},{6,7},{7,6},{8,9},{9,8},{10,11... | collective-permute-start | bytes 1179656 | tf_op jit(solution)/shard_map/ppermute | solution.py:120
  3.7 9.3 %collective-permute-start.1 = (bf16[384,512]{1,0:T(8,128)(2,1)}, bf16[384,512]{1,0:T(8,128)(2,1)S(1)}, u32[]{:S(2)}, u32[]{:S(2)}) collective-permute-start(bf16[384,512]{1,0:T(8,128)(2,1)} %refs_0_.1), channel_id=1, source_target_pairs={{1,2},{2,1},{5,6},{6,5},{9,10},{10,9},{13,14},{14,13},{17,18},{18,... | collective-permute-start | bytes 1179656 | tf_op jit(solution)/shard_map/ppermute | solution.py:124
  6.1 19.1 %collective-permute-start.5 = (bf16[256,1536]{1,0:T(8,128)(2,1)S(1)}, bf16[256,1536]{1,0:T(8,128)(2,1)S(1)}, u32[]{:S(2)}, u32[]{:S(2)}) collective-permute-start(bf16[256,1536]{1,0:T(8,128)(2,1)S(1)} %reshape.193.refs_0_), channel_id=1, source_target_pairs={{0,8},{4,12},{8,0},{12,4},{16,24},{20,28},{24,16},{28,20},{1,9},{5... | collective-permute-start | bytes 2359304 | tf_op jit(solution)/shard_map/ppermute | solution.py:116
  7.6 18.7 %collective-permute-start.6 = (bf16[256,1536]{1,0:T(8,128)(2,1)S(1)}, bf16[256,1536]{1,0:T(8,128)(2,1)S(1)}, u32[]{:S(2)}, u32[]{:S(2)}) collective-permute-start(bf16[256,1536]{1,0:T(8,128)(2,1)S(1)} %reshape.193.refs_0_), channel_id=1, source_target_pairs={{0,16},{4,20},{8,24},{12,28},{16,0},{20,4},{24,8},{28,12},{1,17},{... | collective-permute-start | bytes 2359304 | tf_op jit(solution)/shard_map/ppermute | solution.py:116
  9.6 29.8 %copy-start = (bf16[384,512]{1,0:T(8,128)(2,1)S(1)}, bf16[384,512]{1,0:T(8,128)(2,1)}, u32[]{:S(2)}) copy-start(bf16[384,512]{1,0:T(8,128)(2,1)} %refs_0_.1) | copy-start | bytes 1179652
  9.6 29.8 %copy-start.3 = (f32[2048]{0:T(1024)S(1)}, f32[2048]{0:T(1024)}, u32[]{:S(2)}) copy-start(f32[2048]{0:T(1024)} %param.6) | copy-start | bytes 24580
  13.1 2.0 %collective-permute-start.3 = (bf16[384,512]{1,0:T(8,128)(2,1)S(1)}, bf16[384,512]{1,0:T(8,128)(2,1)S(1)}, u32[]{:S(2)}, u32[]{:S(2)}) collective-permute-start(bf16[384,512]{1,0:T(8,128)(2,1)S(1)} %collective-permute-done.refs_1_), channel_id=1, source_target_pairs={{1,2},{2,1},{5,6},{6,5},{9,10},{10,9},{13,14},{14,13},{17,18},{18,... | collective-permute-start | bytes 1179656 | tf_op jit(solution)/shard_map/ppermute | solution.py:124
  13.7 17.1 %collective-permute-start.2 = (bf16[384,512]{1,0:T(8,128)(2,1)S(1)}, bf16[384,512]{1,0:T(8,128)(2,1)S(1)}, u32[]{:S(2)}, u32[]{:S(2)}) collective-permute-start(bf16[384,512]{1,0:T(8,128)(2,1)S(1)} %collective-permute-done.1.refs_2_), channel_id=1, source_target_pairs={{1,0},{2,3},{5,4},{6,7},{9,8},{10,11},{13,12},{14,15},{17,16},{18,... | collective-permute-start | bytes 1179656 | tf_op jit(solution)/shard_map/ppermute | solution.py:128
  15.1 23.7 %collective-permute-start.4 = (bf16[384,512]{1,0:T(8,128)(2,1)S(1)}, bf16[384,512]{1,0:T(8,128)(2,1)S(1)}, u32[]{:S(2)}, u32[]{:S(2)}) collective-permute-start(bf16[384,512]{1,0:T(8,128)(2,1)S(1)} %collective-permute-done.3.refs_4_), channel_id=1, source_target_pairs={{1,0},{2,3},{5,4},{6,7},{9,8},{10,11},{13,12},{14,15},{17,16},{18,... | collective-permute-start | bytes 1179656 | tf_op jit(solution)/shard_map/ppermute | solution.py:128
  26.4 12.4 %collective-permute-start.7 = (bf16[128,1536]{1,0:T(8,128)(2,1)S(1)}, bf16[128,1536]{1,0:T(8,128)(2,1)S(1)}, u32[]{:S(2)}, u32[]{:S(2)}) collective-permute-start(bf16[128,1536]{1,0:T(8,128)(2,1)S(1)} %get-tuple-element.41), channel_id=1, source_target_pairs={{0,8},{4,12},{8,0},{12,4},{16,24},{20,28},{24,16},{28,20},{1,9},{5... | collective-permute-start | bytes 1179656 | tf_op jit(solution)/shard_map/ppermute | solution.py:116
  27.0 12.3 %collective-permute-start.8 = (bf16[128,1536]{1,0:T(8,128)(2,1)S(1)}, bf16[128,1536]{1,0:T(8,128)(2,1)S(1)}, u32[]{:S(2)}, u32[]{:S(2)}) collective-permute-start(bf16[128,1536]{1,0:T(8,128)(2,1)S(1)} %get-tuple-element.42), channel_id=1, source_target_pairs={{0,16},{4,20},{8,24},{12,28},{16,0},{20,4},{24,8},{28,12},{1,17},{... | collective-permute-start | bytes 1179656 | tf_op jit(solution)/shard_map/ppermute | solution.py:116
  28.5 13.3 %collective-permute-start.9 = (bf16[256,1536]{1,0:T(8,128)(2,1)S(1)}, bf16[256,1536]{1,0:T(8,128)(2,1)S(1)}, u32[]{:S(2)}, u32[]{:S(2)}) collective-permute-start(bf16[256,1536]{1,0:T(8,128)(2,1)S(1)} %reshape.193.refs_0_), channel_id=1, source_target_pairs={{0,4},{4,0},{8,12},{12,8},{16,20},{20,16},{24,28},{28,24},{1,5},{5... | collective-permute-start | bytes 2359304 | tf_op jit(solution)/shard_map/ppermute | solution.py:116
  30.8 11.4 %collective-permute-start.10 = (bf16[256,1536]{1,0:T(8,128)(2,1)S(1)}, bf16[256,1536]{1,0:T(8,128)(2,1)S(1)}, u32[]{:S(2)}, u32[]{:S(2)}) collective-permute-start(bf16[256,1536]{1,0:T(8,128)(2,1)S(1)} %collective-permute-done.5.x_ref.refs_1_), channel_id=1, source_target_pairs={{0,4},{4,0},{8,12},{12,8},{16,20},{20,16},{24,28},{28,24},{1,5},{5... | collective-permute-start | bytes 2359304 | tf_op jit(solution)/shard_map/ppermute | solution.py:116
  38.8 3.4 %collective-permute-start.11 = (bf16[256,1536]{1,0:T(8,128)(2,1)S(1)}, bf16[256,1536]{1,0:T(8,128)(2,1)S(1)}, u32[]{:S(2)}, u32[]{:S(2)}) collective-permute-start(bf16[256,1536]{1,0:T(8,128)(2,1)S(1)} %collective-permute-done.6.y_ref.refs_2_), channel_id=1, source_target_pairs={{0,4},{4,0},{8,12},{12,8},{16,20},{20,16},{24,28},{28,24},{1,5},{5... | collective-permute-start | bytes 2359304 | tf_op jit(solution)/shard_map/ppermute | solution.py:116
  38.8 3.1 %collective-permute-start.12 = (bf16[128,1536]{1,0:T(8,128)(2,1)S(1)}, bf16[128,1536]{1,0:T(8,128)(2,1)S(1)}, u32[]{:S(2)}, u32[]{:S(2)}) collective-permute-start(bf16[128,1536]{1,0:T(8,128)(2,1)S(1)} %collective-permute-done.7.refs_3_), channel_id=1, source_target_pairs={{0,4},{4,0},{8,12},{12,8},{16,20},{20,16},{24,28},{28,24},{1,5},{5... | collective-permute-start | bytes 1179656 | tf_op jit(solution)/shard_map/ppermute | solution.py:116
  39.3 2.9 %collective-permute-start.13 = (bf16[128,1536]{1,0:T(8,128)(2,1)S(1)}, bf16[128,1536]{1,0:T(8,128)(2,1)S(1)}, u32[]{:S(2)}, u32[]{:S(2)}) collective-permute-start(bf16[128,1536]{1,0:T(8,128)(2,1)S(1)} %collective-permute-done.8.refs_4_), channel_id=1, source_target_pairs={{0,4},{4,0},{8,12},{12,8},{16,20},{20,16},{24,28},{28,24},{1,5},{5... | collective-permute-start | bytes 1179656 | tf_op jit(solution)/shard_map/ppermute | solution.py:116
  44.8 9.9 %collective-permute-start.14 = (bf16[3,384,128]{2,1,0:T(8,128)(2,1)S(1)}, bf16[3,384,128]{2,1,0:T(8,128)(2,1)S(1)}, u32[]{:S(2)}, u32[]{:S(2)}) collective-permute-start(bf16[3,384,128]{2,1,0:T(8,128)(2,1)S(1)} %get-tuple-element.44), channel_id=1, source_target_pairs={{0,8},{4,12},{8,0},{12,4},{16,24},{20,28},{24,16},{28,20},{1,9},{5... | collective-permute-start | bytes 884744 | tf_op jit(solution)/shard_map/ppermute | solution.py:116
  46.4 16.1 %copy-start.1 = (bf16[256,512]{1,0:T(8,128)(2,1)S(1)}, bf16[256,512]{1,0:T(8,128)(2,1)}, u32[]{:S(2)}) copy-start(bf16[256,512]{1,0:T(8,128)(2,1)} %refs_0_.2) | copy-start | bytes 786436
  46.4 15.1 %collective-permute-start.15 = (bf16[3,384,128]{2,1,0:T(8,128)(2,1)S(1)}, bf16[3,384,128]{2,1,0:T(8,128)(2,1)S(1)}, u32[]{:S(2)}, u32[]{:S(2)}) collective-permute-start(bf16[3,384,128]{2,1,0:T(8,128)(2,1)S(1)} %get-tuple-element.45), channel_id=1, source_target_pairs={{0,16},{4,20},{8,24},{12,28},{16,0},{20,4},{24,8},{28,12},{1,17},{... | collective-permute-start | bytes 884744 | tf_op jit(solution)/shard_map/ppermute | solution.py:116
  50.5 11.0 %collective-permute-start.16 = (bf16[3,384,128]{2,1,0:T(8,128)(2,1)S(1)}, bf16[3,384,128]{2,1,0:T(8,128)(2,1)S(1)}, u32[]{:S(2)}, u32[]{:S(2)}) collective-permute-start(bf16[3,384,128]{2,1,0:T(8,128)(2,1)S(1)} %get-tuple-element.46), channel_id=1, source_target_pairs={{0,24},{4,28},{8,16},{12,20},{16,8},{20,12},{24,0},{28,4},{1,25},{... | collective-permute-start | bytes 884744 | tf_op jit(solution)/shard_map/ppermute | solution.py:116
  61.5 14.8 %copy-start.2 = (bf16[256,512]{1,0:T(8,128)(2,1)S(1)}, bf16[256,512]{1,0:T(8,128)(2,1)}, u32[]{:S(2)}) copy-start(bf16[256,512]{1,0:T(8,128)(2,1)} %refs_0_.2) | copy-start | bytes 786436
  61.5 2.3 %collective-permute-start.17 = (bf16[3,384,128]{2,1,0:T(8,128)(2,1)S(1)}, bf16[3,384,128]{2,1,0:T(8,128)(2,1)S(1)}, u32[]{:S(2)}, u32[]{:S(2)}) collective-permute-start(bf16[3,384,128]{2,1,0:T(8,128)(2,1)S(1)} %get-tuple-element.47.refs_0_), channel_id=1, source_target_pairs={{0,4},{4,0},{8,12},{12,8},{16,20},{20,16},{24,28},{28,24},{1,5},{5... | collective-permute-start | bytes 884744 | tf_op jit(solution)/shard_map/ppermute | solution.py:116
  61.5 3.1 %collective-permute-start.18 = (bf16[3,384,128]{2,1,0:T(8,128)(2,1)S(1)}, bf16[3,384,128]{2,1,0:T(8,128)(2,1)S(1)}, u32[]{:S(2)}, u32[]{:S(2)}) collective-permute-start(bf16[3,384,128]{2,1,0:T(8,128)(2,1)S(1)} %collective-permute-done.14.refs_1_), channel_id=1, source_target_pairs={{0,4},{4,0},{8,12},{12,8},{16,20},{20,16},{24,28},{28,24},{1,5},{5... | collective-permute-start | bytes 884744 | tf_op jit(solution)/shard_map/ppermute | solution.py:116
  62.0 2.6 %collective-permute-start.19 = (bf16[3,384,128]{2,1,0:T(8,128)(2,1)S(1)}, bf16[3,384,128]{2,1,0:T(8,128)(2,1)S(1)}, u32[]{:S(2)}, u32[]{:S(2)}) collective-permute-start(bf16[3,384,128]{2,1,0:T(8,128)(2,1)S(1)} %collective-permute-done.15.refs_2_), channel_id=1, source_target_pairs={{0,4},{4,0},{8,12},{12,8},{16,20},{20,16},{24,28},{28,24},{1,5},{5... | collective-permute-start | bytes 884744 | tf_op jit(solution)/shard_map/ppermute | solution.py:116
  62.0 2.5 %collective-permute-start.20 = (bf16[3,384,128]{2,1,0:T(8,128)(2,1)S(1)}, bf16[3,384,128]{2,1,0:T(8,128)(2,1)S(1)}, u32[]{:S(2)}, u32[]{:S(2)}) collective-permute-start(bf16[3,384,128]{2,1,0:T(8,128)(2,1)S(1)} %collective-permute-done.16.refs_3_), channel_id=1, source_target_pairs={{0,4},{4,0},{8,12},{12,8},{16,20},{20,16},{24,28},{28,24},{1,5},{5... | collective-permute-start | bytes 884744 | tf_op jit(solution)/shard_map/ppermute | solution.py:116
  62.5 10.8 %collective-permute-start.21 = (bf16[256,512]{1,0:T(8,128)(2,1)S(1)}, bf16[256,512]{1,0:T(8,128)(2,1)S(1)}, u32[]{:S(2)}, u32[]{:S(2)}) collective-permute-start(bf16[256,512]{1,0:T(8,128)(2,1)S(1)} %copy-done.1), channel_id=1, source_target_pairs={{0,8},{4,12},{8,0},{12,4},{16,24},{20,28},{24,16},{28,20},{1,9},{5... | collective-permute-start | bytes 786440 | tf_op jit(solution)/shard_map/ppermute | solution.py:116
  63.7 9.5 %collective-permute-start.22 = (bf16[256,512]{1,0:T(8,128)(2,1)S(1)}, bf16[256,512]{1,0:T(8,128)(2,1)S(1)}, u32[]{:S(2)}, u32[]{:S(2)}) collective-permute-start(bf16[256,512]{1,0:T(8,128)(2,1)S(1)} %copy-done.1), channel_id=1, source_target_pairs={{0,16},{4,20},{8,24},{12,28},{16,0},{20,4},{24,8},{28,12},{1,17},{... | collective-permute-start | bytes 786440 | tf_op jit(solution)/shard_map/ppermute | solution.py:116
  73.3 5.7 %collective-permute-start.23 = (bf16[384,128]{1,0:T(8,128)(2,1)S(1)}, bf16[384,128]{1,0:T(8,128)(2,1)S(1)}, u32[]{:S(2)}, u32[]{:S(2)}) collective-permute-start(bf16[384,128]{1,0:T(8,128)(2,1)S(1)} %get-tuple-element.56), channel_id=1, source_target_pairs={{0,24},{4,28},{8,16},{12,20},{16,8},{20,12},{24,0},{28,4},{1,25},{... | collective-permute-start | bytes 294920 | tf_op jit(solution)/shard_map/ppermute | solution.py:116
  74.7 5.6 %collective-permute-start.24 = (bf16[384,128]{1,0:T(8,128)(2,1)S(1)}, bf16[384,128]{1,0:T(8,128)(2,1)S(1)}, u32[]{:S(2)}, u32[]{:S(2)}) collective-permute-start(bf16[384,128]{1,0:T(8,128)(2,1)S(1)} %get-tuple-element.57), channel_id=1, source_target_pairs={{0,16},{4,20},{8,24},{12,28},{16,0},{20,4},{24,8},{28,12},{1,17},{... | collective-permute-start | bytes 294920 | tf_op jit(solution)/shard_map/ppermute | solution.py:116
  76.2 11.3 %collective-permute-start.33 = (bf16[256,512]{1,0:T(8,128)(2,1)S(1)}, bf16[256,512]{1,0:T(8,128)(2,1)S(1)}, u32[]{:S(2)}, u32[]{:S(2)}) collective-permute-start(bf16[256,512]{1,0:T(8,128)(2,1)S(1)} %copy-done.2), channel_id=1, source_target_pairs={{0,4},{4,0},{8,12},{12,8},{16,20},{20,16},{24,28},{28,24},{1,5},{5... | collective-permute-start | bytes 786440 | tf_op jit(solution)/shard_map/ppermute | solution.py:116
  76.2 5.2 %collective-permute-start.25 = (bf16[384,128]{1,0:T(8,128)(2,1)S(1)}, bf16[384,128]{1,0:T(8,128)(2,1)S(1)}, u32[]{:S(2)}, u32[]{:S(2)}) collective-permute-start(bf16[384,128]{1,0:T(8,128)(2,1)S(1)} %get-tuple-element.58), channel_id=1, source_target_pairs={{0,8},{4,12},{8,0},{12,4},{16,24},{20,28},{24,16},{28,20},{1,9},{5... | collective-permute-start | bytes 294920 | tf_op jit(solution)/shard_map/ppermute | solution.py:116
  81.6 6.5 %collective-permute-start.29 = (bf16[384,512]{1,0:T(8,128)(2,1)S(1)}, bf16[384,512]{1,0:T(8,128)(2,1)S(1)}, u32[]{:S(2)}, u32[]{:S(2)}) collective-permute-start(bf16[384,512]{1,0:T(8,128)(2,1)S(1)} %pad_maximum_fusion.own), channel_id=1, source_target_pairs={{1,2},{2,1},{5,6},{6,5},{9,10},{10,9},{13,14},{14,13},{17,18},{18,... | collective-permute-start | bytes 1179656 | tf_op jit(solution)/shard_map/ppermute | solution.py:124
  82.3 12.3 %collective-permute-start.26 = (bf16[384,512]{1,0:T(8,128)(2,1)S(1)}, bf16[384,512]{1,0:T(8,128)(2,1)S(1)}, u32[]{:S(2)}, u32[]{:S(2)}) collective-permute-start(bf16[384,512]{1,0:T(8,128)(2,1)S(1)} %pad_maximum_fusion.own), channel_id=1, source_target_pairs={{0,1},{1,0},{2,3},{3,2},{4,5},{5,4},{6,7},{7,6},{8,9},{9,8},{10,11... | collective-permute-start | bytes 1179656 | tf_op jit(solution)/shard_map/ppermute | solution.py:120
  85.9 10.1 %collective-permute-start.34 = (bf16[256,512]{1,0:T(8,128)(2,1)S(1)}, bf16[256,512]{1,0:T(8,128)(2,1)S(1)}, u32[]{:S(2)}, u32[]{:S(2)}) collective-permute-start(bf16[256,512]{1,0:T(8,128)(2,1)S(1)} %collective-permute-done.21.x_ref.refs_1_), channel_id=1, source_target_pairs={{0,4},{4,0},{8,12},{12,8},{16,20},{20,16},{24,28},{28,24},{1,5},{5... | collective-permute-start | bytes 786440 | tf_op jit(solution)/shard_map/ppermute | solution.py:116
  86.0 9.3 %collective-permute-start.31 = (bf16[128,512]{1,0:T(8,128)(2,1)S(1)}, bf16[128,512]{1,0:T(8,128)(2,1)S(1)}, u32[]{:S(2)}, u32[]{:S(2)}) collective-permute-start(bf16[128,512]{1,0:T(8,128)(2,1)S(1)} %get-tuple-element.65), channel_id=1, source_target_pairs={{0,8},{4,12},{8,0},{12,4},{16,24},{20,28},{24,16},{28,20},{1,9},{5... | collective-permute-start | bytes 393224 | tf_op jit(solution)/shard_map/ppermute | solution.py:116
  87.6 7.8 %collective-permute-start.32 = (bf16[128,512]{1,0:T(8,128)(2,1)S(1)}, bf16[128,512]{1,0:T(8,128)(2,1)S(1)}, u32[]{:S(2)}, u32[]{:S(2)}) collective-permute-start(bf16[128,512]{1,0:T(8,128)(2,1)S(1)} %get-tuple-element.66), channel_id=1, source_target_pairs={{0,16},{4,20},{8,24},{12,28},{16,0},{20,4},{24,8},{28,12},{1,17},{... | collective-permute-start | bytes 393224 | tf_op jit(solution)/shard_map/ppermute | solution.py:116
  88.1 16.6 %collective-permute-start.30 = (bf16[384,512]{1,0:T(8,128)(2,1)S(1)}, bf16[384,512]{1,0:T(8,128)(2,1)S(1)}, u32[]{:S(2)}, u32[]{:S(2)}) collective-permute-start(bf16[384,512]{1,0:T(8,128)(2,1)S(1)} %collective-permute-done.29.q1), channel_id=1, source_target_pairs={{1,0},{2,3},{5,4},{6,7},{9,8},{10,11},{13,12},{14,15},{17,16},{18,... | collective-permute-start | bytes 1179656 | tf_op jit(solution)/shard_map/ppermute | solution.py:128
  94.6 3.7 %collective-permute-start.27 = (bf16[384,512]{1,0:T(8,128)(2,1)S(1)}, bf16[384,512]{1,0:T(8,128)(2,1)S(1)}, u32[]{:S(2)}, u32[]{:S(2)}) collective-permute-start(bf16[384,512]{1,0:T(8,128)(2,1)S(1)} %collective-permute-done.26.near), channel_id=1, source_target_pairs={{1,2},{2,1},{5,6},{6,5},{9,10},{10,9},{13,14},{14,13},{17,18},{18,... | collective-permute-start | bytes 1179656 | tf_op jit(solution)/shard_map/ppermute | solution.py:124
  95.3 4.3 %collective-permute-start.35 = (bf16[256,512]{1,0:T(8,128)(2,1)S(1)}, bf16[256,512]{1,0:T(8,128)(2,1)S(1)}, u32[]{:S(2)}, u32[]{:S(2)}) collective-permute-start(bf16[256,512]{1,0:T(8,128)(2,1)S(1)} %collective-permute-done.22.y_ref.refs_2_), channel_id=1, source_target_pairs={{0,4},{4,0},{8,12},{12,8},{16,20},{20,16},{24,28},{28,24},{1,5},{5... | collective-permute-start | bytes 786440 | tf_op jit(solution)/shard_map/ppermute | solution.py:116
  95.4 4.1 %collective-permute-start.36 = (bf16[128,512]{1,0:T(8,128)(2,1)S(1)}, bf16[128,512]{1,0:T(8,128)(2,1)S(1)}, u32[]{:S(2)}, u32[]{:S(2)}) collective-permute-start(bf16[128,512]{1,0:T(8,128)(2,1)S(1)} %collective-permute-done.31.refs_3_), channel_id=1, source_target_pairs={{0,4},{4,0},{8,12},{12,8},{16,20},{20,16},{24,28},{28,24},{1,5},{5... | collective-permute-start | bytes 393224 | tf_op jit(solution)/shard_map/ppermute | solution.py:116
  96.0 3.6 %collective-permute-start.37 = (bf16[128,512]{1,0:T(8,128)(2,1)S(1)}, bf16[128,512]{1,0:T(8,128)(2,1)S(1)}, u32[]{:S(2)}, u32[]{:S(2)}) collective-permute-start(bf16[128,512]{1,0:T(8,128)(2,1)S(1)} %collective-permute-done.32.refs_4_), channel_id=1, source_target_pairs={{0,4},{4,0},{8,12},{12,8},{16,20},{20,16},{24,28},{28,24},{1,5},{5... | collective-permute-start | bytes 393224 | tf_op jit(solution)/shard_map/ppermute | solution.py:116
  98.3 18.7 %collective-permute-start.28 = (bf16[384,512]{1,0:T(8,128)(2,1)S(1)}, bf16[384,512]{1,0:T(8,128)(2,1)S(1)}, u32[]{:S(2)}, u32[]{:S(2)}) collective-permute-start(bf16[384,512]{1,0:T(8,128)(2,1)S(1)} %collective-permute-done.27.q2), channel_id=1, source_target_pairs={{1,0},{2,3},{5,4},{6,7},{9,8},{10,11},{13,12},{14,15},{17,16},{18,... | collective-permute-start | bytes 1179656 | tf_op jit(solution)/shard_map/ppermute | solution.py:128

commit v4 on v3

--- a/solution.py
+++ b/solution.py
@@ -109,7 +109,8 @@
 CHIPS = 4
 NORM_EFFORT = 8 << 30
 PAIRS = ((1, 2), (3, 0))
-EARLY_EFFORT = 16 << 30
+KEYS = 512
+EARLY_EFFORT = 1 << 30
 
 
 def swap(x, mask):
@@ -258,13 +259,17 @@
     pieces, outs, (keys, vals) = refs[:8], refs[8:12], refs[12:]
     chip, core = where_ref[0], where_ref[1]
     _, rows, hsize = pieces[0].shape
+    for cache in (keys, vals):
+        cache[:KEYS] = jnp.zeros((KEYS, hsize), jnp.bfloat16)
     for side in range(2):
         for n in range(CHIPS):
             block = 2 * (chip ^ n) + (core if side == 0 else 1 - core)
-            keys[block] = pieces[CHIPS * side + n][1]
-            vals[block] = pieces[CHIPS * side + n][2]
+            place = pl.ds(pl.multiple_of(KEYS + block * rows, 128), rows)
+            keys[place, :] = pieces[CHIPS * side + n][1]
+            vals[place, :] = pieces[CHIPS * side + n][2]
     for m in range(CHIPS):
         block = 2 * (chip ^ m) + core
+        after = (block + 1) * rows
         query = pieces[m][0]
         qpos = block * rows + lax.broadcasted_iota(jnp.int32, (rows, 1), 0)
         begin = jnp.zeros((rows, 1), jnp.int32)
@@ -273,21 +278,22 @@
             begin = jnp.where(start_ref[d] <= qpos, start_ref[d], begin)
             lowest = jnp.where(start_ref[d] <= block * rows, start_ref[d], lowest)
 
-        def tile(number, state, block=block, query=query, qpos=qpos, begin=begin):
+        def tile(number, state, after=after, query=query, qpos=qpos, begin=begin):
             running, totals, accum = state
-            kv = block - number
-            kpos = kv * rows + lax.broadcasted_iota(jnp.int32, (1, rows), 1)
+            first = after - KEYS * (number + 1)
+            place = pl.ds(pl.multiple_of(KEYS + first, 128), KEYS)
+            kpos = first + lax.broadcasted_iota(jnp.int32, (1, KEYS), 1)
             score = scale * lax.dot_general(
-                query, keys[kv], (((1,), (1,)), ((), ())), preferred_element_type=jnp.float32
+                query, keys[place, :], (((1,), (1,)), ((), ())), preferred_element_type=jnp.float32
             )
             keep = (kpos >= begin) & (kpos <= qpos)
             score = jnp.where(keep, score, -1e30)
             newmax = jnp.maximum(running, jnp.max(score, axis=1, keepdims=True))
-            weight = jnp.exp(score - newmax)
-            factor = jnp.exp(running - newmax)
+            weight = jnp.exp2(score - newmax)
+            factor = jnp.exp2(running - newmax)
             totals = totals * factor + jnp.sum(weight, axis=1, keepdims=True)
             accum = accum * factor + jnp.dot(
-                weight.astype(jnp.bfloat16), vals[kv], preferred_element_type=jnp.float32
+                weight.astype(jnp.bfloat16), vals[place, :], preferred_element_type=jnp.float32
             )
             return newmax, totals, accum
 
@@ -296,18 +302,20 @@
             jnp.zeros((rows, 1), jnp.float32),
             jnp.zeros((rows, hsize), jnp.float32),
         )
-        running, totals, accum = lax.fori_loop(0, block - lax.div(lowest, rows) + 1, tile, state)
+        tiles = lax.div(after - lowest + KEYS - 1, KEYS)
+        running, totals, accum = lax.fori_loop(0, tiles, tile, state)
         outs[m][...] = (accum / totals).astype(jnp.bfloat16)
 
 
-def attend(where, starts, pieces, scale):
+def attend(where, starts, pieces):
     _, rows, hsize = pieces[0].shape
+    scale = math.log2(math.e) / math.sqrt(hsize)
     return pl.pallas_call(
         functools.partial(attend_kernel, scale=scale),
         in_specs=[smem()] * 2 + [vmem()] * len(pieces),
         out_specs=[vmem()] * CHIPS,
         out_shape=[jax.ShapeDtypeStruct((rows, hsize), jnp.bfloat16)] * CHIPS,
-        scratch_shapes=[pltpu.VMEM((2 * CHIPS, rows, hsize), jnp.bfloat16)] * 2,
+        scratch_shapes=[pltpu.VMEM((KEYS + 2 * CHIPS * rows, hsize), jnp.bfloat16)] * 2,
         compiler_params=pltpu.CompilerParams(vmem_limit_bytes=16 << 20),
         cost_estimate=effort(16 * 2 * rows * LINE * rows * hsize),
         name="attend",
@@ -392,7 +400,6 @@
 def blocks_plan(tokens, gain, w_qkv, w_out, lengths):
     rows, wide = tokens.shape
     depth, _, heads, hsize = w_qkv.shape
-    half = depth // 2
     mine = lax.axis_index("gx")
     line = lax.axis_index("gy")
     chip, core = mine // 2, mine % 2
@@ -421,18 +428,18 @@
     pieces = [sent[0]] + [swap(sent[m], 2 * m) for m in range(1, CHIPS)]
     *pieces, w_late = together(*pieces, w_out)
     w_x, w_y = swap(w_late, 2), swap(w_late, 4)
-    heads_out = attend(
-        where, starts, pieces + [swap(a, 1) for a in pieces], 1.0 / math.sqrt(hsize)
-    )
-    *heads_out, w_x, w_y = together(*heads_out, w_x, w_y)
+    heads_out = attend(where, starts, pieces + [swap(a, 1) for a in pieces])
+    *heads_out, w_x, w_y, w_other = together(*heads_out, w_x, w_y, swap(w_late, 1))
     back = [heads_out[0]] + [swap(heads_out[m], 2 * m) for m in range(1, CHIPS)]
     attended = heads_in_order(back, chip)
     attended, w_x, w_y = together(attended, w_x, w_y)
     upper, lower = halves(w_x, w_y)
-    near, q1, far_a, far_b = outer(attended), inner(attended), swap(upper, 2), swap(lower, 4)
+    near, q1 = outer(attended), inner(attended)
+    q1, upper, lower = together(q1, upper, lower)
+    far_a, far_b = swap(upper, 2), swap(lower, 4)
     pieces = (w_late, w_x, w_y, far_a, far_b)
     q2, p2 = inner(near), outward(q1)
-    others = [swap(w, 1) for w in pieces]
+    others = [w_other] + [swap(w, 1) for w in pieces[1:]]
     p3 = outward(q2)
     total, w_last = early(where, (attended, near, q1, p2), (*pieces, *others))
     mixed = last(where, q2, p3, total, w_last)

time: 120 us -> 118 us (0.983)
  waiting for transfers between devices: 59.3 us -> 62.3 us
  starting transfers between devices: 33.4 us -> 31.1 us
  Pallas kernels: 19.4 us -> 17.8 us
    ppermute x4, waiting for transfers between devices: 26.1 us -> 22 us  [outward(): return lax.ppermute(x, 'gy', [(1, 0), (2, 3)])]
    ppermute x28, waiting for transfers between devices: 25.5 us -> 29.1 us  [swap(): return lax.ppermute(x, 'gx', [(i, i ^ mask) for i in range(2 * CHIPS)])]
    ppermute x2, waiting for transfers between devices: 7.67 us -> 11.2 us  [outer(): return lax.ppermute(x, 'gy', [(0, 1), (1, 0), (2, 3), (3, 2)])]
    pallas_call x1, Pallas kernels: 8.66 us -> 6.99 us  [attend(): pl.pallas_call(functools.partial(attend_kernel, scale=scale), in_specs=[s...]
    ppermute x2, starting transfers between devices: 6.62 us -> 5.22 us  [outer(): return lax.ppermute(x, 'gy', [(0, 1), (1, 0), (2, 3), (3, 2)])]
  transfers between devices with their start and end apart: 38 -> 38, of which waited for: 14 -> 16; matrix products, arithmetic and copies ran while one was open for 5% -> 5% of each run, Pallas kernels for 13% -> 12%
where the time goes in v4:
time: 118 us
  waiting for transfers between devices  62.3 us (53%)
  starting transfers between devices  31.1 us (26%)
  Pallas kernels  17.8 us (15%)
  local copies, waits for them, and re-layouts  3.79 us (3%)
  other arithmetic  1.69 us (1%)
    ppermute x28, waiting for transfers between devices, swap(): return lax.ppermute(x, 'gx', [(i, i ^ mask) for i in range(2 * CHIPS)])  29.1 us
    ppermute x4, waiting for transfers between devices, outward(): return lax.ppermute(x, 'gy', [(1, 0), (2, 3)])  22 us
    ppermute x28, starting transfers between devices, swap(): return lax.ppermute(x, 'gx', [(i, i ^ mask) for i in range(2 * CHIPS)])  18 us
    ppermute x2, waiting for transfers between devices, outer(): return lax.ppermute(x, 'gy', [(0, 1), (1, 0), (2, 3), (3, 2)])  11.2 us
    pallas_call x1, Pallas kernels, attend(): pl.pallas_call(functools.partial(attend_kernel, scale=scale), in_specs=[s...  6.99 us
    ppermute x2, starting transfers between devices, outer(): return lax.ppermute(x, 'gy', [(0, 1), (1, 0), (2, 3), (3, 2)])  5.22 us
    ppermute x4, starting transfers between devices, outward(): return lax.ppermute(x, 'gy', [(1, 0), (2, 3)])  5.17 us
    pallas_call x2, Pallas kernels, project(): pl.pallas_call(functools.partial(project_kernel, pair=pair), in_specs=[sm...  5.16 us
  transfers between devices with their start and end apart: 38, of which 16 were waited for; matrix products, arithmetic and copies ran while one was open for 5% of the time, Pallas kernels for 12%

profile of v4, /device:TPU:0, one launch (start us, length us, event | category | flops | bytes accessed | tf_op | source)
XLA Modules:
  0.0 117.6 jit_solution(4284936820063852818)
XLA Ops:
  0.6 3.1 %collective-permute-start = (bf16[384,512]{1,0:T(8,128)(2,1)}, bf16[384,512]{1,0:T(8,128)(2,1)S(1)}, u32[]{:S(2)}, u32[]{:S(2)}) collective-permute-start(bf16[384,512]{1,0:T(8,128)(2,1)} %refs_0_.1), channel_id=1, source_target_pairs={{0,1},{1,0},{2,3},{3,2},{4,5},{5,4},{6,7},{7,6},{8,9},{9,8},{10,11... | collective-permute-start | bytes 1179656 | tf_op jit(solution)/shard_map/ppermute | solution.py:121
  3.7 0.7 collective-permute-start.1
  4.4 1.7 %reshape.193.refs_0_ = bf16[256,1536]{1,0:T(8,128)(2,1)S(1)} reshape(bf16[256,3,4,128]{3,2,1,0:T(4,128)(2,1)} %param.7) | data formatting | bytes 1572864 | tf_op jit(solution)/shard_map/reshape | solution.py:413
  6.1 1.6 %collective-permute-start.5 = (bf16[256,1536]{1,0:T(8,128)(2,1)S(1)}, bf16[256,1536]{1,0:T(8,128)(2,1)S(1)}, u32[]{:S(2)}, u32[]{:S(2)}) collective-permute-start(bf16[256,1536]{1,0:T(8,128)(2,1)S(1)} %reshape.193.refs_0_), channel_id=1, source_target_pairs={{0,8},{4,12},{8,0},{12,4},{16,24},{20,28},{24,16},{28,20},{1,9},{5... | collective-permute-start | bytes 2359304 | tf_op jit(solution)/shard_map/ppermute | solution.py:117
  7.6 1.5 %collective-permute-start.6 = (bf16[256,1536]{1,0:T(8,128)(2,1)S(1)}, bf16[256,1536]{1,0:T(8,128)(2,1)S(1)}, u32[]{:S(2)}, u32[]{:S(2)}) collective-permute-start(bf16[256,1536]{1,0:T(8,128)(2,1)S(1)} %reshape.193.refs_0_), channel_id=1, source_target_pairs={{0,16},{4,20},{8,24},{12,28},{16,0},{20,4},{24,8},{28,12},{1,17},{... | collective-permute-start | bytes 2359304 | tf_op jit(solution)/shard_map/ppermute | solution.py:117
  9.2 0.2 reduce-window.9
  9.4 0.1 select_reduce_fusion
  9.5 0.1 pad_add_fusion.where_ref
  9.6 0.8 fusion
  10.3 0.2 pad_maximum_fusion.3
  10.5 2.5 %collective-permute-done.refs_1_ = bf16[384,512]{1,0:T(8,128)(2,1)S(1)} collective-permute-done((bf16[384,512]{1,0:T(8,128)(2,1)}, bf16[384,512]{1,0:T(8,128)(2,1)S(1)}, u32[]{:S(2)}, u32[]{:S(2)}) %collective-permute-start) | collective-permute-done | bytes 393248 | tf_op jit(solution)/shard_map/ppermute | solution.py:121
  13.1 0.0 collective-permute-done.1.refs_2_
  13.1 0.7 collective-permute-start.3
  13.7 1.3 %collective-permute-start.2 = (bf16[384,512]{1,0:T(8,128)(2,1)S(1)}, bf16[384,512]{1,0:T(8,128)(2,1)S(1)}, u32[]{:S(2)}, u32[]{:S(2)}) collective-permute-start(bf16[384,512]{1,0:T(8,128)(2,1)S(1)} %collective-permute-done.1.refs_2_), channel_id=1, source_target_pairs={{1,0},{2,3},{5,4},{6,7},{9,8},{10,11},{13,12},{14,15},{17,16},{18,... | collective-permute-start | bytes 1179656 | tf_op jit(solution)/shard_map/ppermute | solution.py:129
  15.1 1.3 %collective-permute-start.4 = (bf16[384,512]{1,0:T(8,128)(2,1)S(1)}, bf16[384,512]{1,0:T(8,128)(2,1)S(1)}, u32[]{:S(2)}, u32[]{:S(2)}) collective-permute-start(bf16[384,512]{1,0:T(8,128)(2,1)S(1)} %collective-permute-done.3.refs_4_), channel_id=1, source_target_pairs={{1,0},{2,3},{5,4},{6,7},{9,8},{10,11},{13,12},{14,15},{17,16},{18,... | collective-permute-start | bytes 1179656 | tf_op jit(solution)/shard_map/ppermute | solution.py:129
  16.4 8.8 %collective-permute-done.5.x_ref.refs_1_ = bf16[256,1536]{1,0:T(8,128)(2,1)S(1)} collective-permute-done((bf16[256,1536]{1,0:T(8,128)(2,1)S(1)}, bf16[256,1536]{1,0:T(8,128)(2,1)S(1)}, u32[]{:S(2)}, u32[]{:S(2)}) %collective-permute-start.5) | collective-permute-done | bytes 786464 | tf_op jit(solution)/shard_map/ppermute | solution.py:117
  25.1 1.2 %collective-permute-done.6.y_ref.refs_2_ = bf16[256,1536]{1,0:T(8,128)(2,1)S(1)} collective-permute-done((bf16[256,1536]{1,0:T(8,128)(2,1)S(1)}, bf16[256,1536]{1,0:T(8,128)(2,1)S(1)}, u32[]{:S(2)}, u32[]{:S(2)}) %collective-permute-start.6) | collective-permute-done | bytes 786464 | tf_op jit(solution)/shard_map/ppermute | solution.py:117
  26.4 0.1 halves.2
  26.4 0.6 collective-permute-start.7
  27.0 1.5 %collective-permute-start.8 = (bf16[128,1536]{1,0:T(8,128)(2,1)S(1)}, bf16[128,1536]{1,0:T(8,128)(2,1)S(1)}, u32[]{:S(2)}, u32[]{:S(2)}) collective-permute-start(bf16[128,1536]{1,0:T(8,128)(2,1)S(1)} %get-tuple-element.46), channel_id=1, source_target_pairs={{0,16},{4,20},{8,24},{12,28},{16,0},{20,4},{24,8},{28,12},{1,17},{... | collective-permute-start | bytes 1179656 | tf_op jit(solution)/shard_map/ppermute | solution.py:117
  28.5 2.3 %collective-permute-done.2.refs_3_ = bf16[384,512]{1,0:T(8,128)(2,1)S(1)} collective-permute-done((bf16[384,512]{1,0:T(8,128)(2,1)S(1)}, bf16[384,512]{1,0:T(8,128)(2,1)S(1)}, u32[]{:S(2)}, u32[]{:S(2)}) %collective-permute-start.2) | collective-permute-done | bytes 393248 | tf_op jit(solution)/shard_map/ppermute | solution.py:129
  30.8 8.0 %collective-permute-done.4.refs_5_ = bf16[384,512]{1,0:T(8,128)(2,1)S(1)} collective-permute-done((bf16[384,512]{1,0:T(8,128)(2,1)S(1)}, bf16[384,512]{1,0:T(8,128)(2,1)S(1)}, u32[]{:S(2)}, u32[]{:S(2)}) %collective-permute-start.4) | collective-permute-done | bytes 393248 | tf_op jit(solution)/shard_map/ppermute | solution.py:129
  38.8 0.5 collective-permute-start.12
  39.3 0.1 collective-permute-start.13
  39.4 2.4 %normalize.1.x_ref = bf16[384,2048]{1,0:T(8,128)(2,1)S(1)} custom-call(s32[3]{0:T(128)S(1)} %pad_add_fusion.where_ref, bf16[384,512]{1,0:T(8,128)(2,1)S(1)} %copy-done, bf16[384,512]{1,0:T(8,128)(2,1)S(1)} %collective-permute-done.refs_1_, bf16[384,512]{1,0:T(8,128)(2,1)S(1)} %collective-permute-done.1.refs_2_, ...), custom_call_target="tpu_custom_call" | custom-call | flops 8589934592 | bytes 8388608 | tf_op jit(solution)/shard_map/normalize/pallas_call | solution.py:204
  41.9 0.3 collective-permute-done.13.refs_9_
  42.2 2.6 %project.3 = (bf16[3,384,128]{2,1,0:T(8,128)(2,1)S(1)}, bf16[3,384,128]{2,1,0:T(8,128)(2,1)S(1)}) custom-call(s32[3]{0:T(128)S(1)} %pad_add_fusion.where_ref, bf16[384,2048]{1,0:T(8,128)(2,1)S(1)} %normalize.1.x_ref, f32[384,128]{1,0:T(8,128)S(1)} %get-tuple-element.43.cos_ref, f32[384,128]{1,0:T(8,128)S(1)} %get-tuple-element.44.sin_ref, ...), custom_call_target="tpu_custom_call" | custom-call | flops 1207959552 | bytes 8388608 | tf_op jit(solution)/shard_map/project/pallas_call | solution.py:246
  44.8 1.6 %collective-permute-start.14 = (bf16[3,384,128]{2,1,0:T(8,128)(2,1)S(1)}, bf16[3,384,128]{2,1,0:T(8,128)(2,1)S(1)}, u32[]{:S(2)}, u32[]{:S(2)}) collective-permute-start(bf16[3,384,128]{2,1,0:T(8,128)(2,1)S(1)} %get-tuple-element.48), channel_id=1, source_target_pairs={{0,8},{4,12},{8,0},{12,4},{16,24},{20,28},{24,16},{28,20},{1,9},{5... | collective-permute-start | bytes 884744 | tf_op jit(solution)/shard_map/ppermute | solution.py:117
  46.4 1.5 %collective-permute-start.15 = (bf16[3,384,128]{2,1,0:T(8,128)(2,1)S(1)}, bf16[3,384,128]{2,1,0:T(8,128)(2,1)S(1)}, u32[]{:S(2)}, u32[]{:S(2)}) collective-permute-start(bf16[3,384,128]{2,1,0:T(8,128)(2,1)S(1)} %get-tuple-element.49), channel_id=1, source_target_pairs={{0,16},{4,20},{8,24},{12,28},{16,0},{20,4},{24,8},{28,12},{1,17},{... | collective-permute-start | bytes 884744 | tf_op jit(solution)/shard_map/ppermute | solution.py:117
  47.9 2.6 %project.2 = (bf16[3,384,128]{2,1,0:T(8,128)(2,1)S(1)}, bf16[3,384,128]{2,1,0:T(8,128)(2,1)S(1)}) custom-call(s32[3]{0:T(128)S(1)} %pad_add_fusion.where_ref, bf16[384,2048]{1,0:T(8,128)(2,1)S(1)} %normalize.1.x_ref, f32[384,128]{1,0:T(8,128)S(1)} %get-tuple-element.43.cos_ref, f32[384,128]{1,0:T(8,128)S(1)} %get-tuple-element.44.sin_ref, ...), custom_call_target="tpu_custom_call" | custom-call | flops 1207959552 | bytes 8388608 | tf_op jit(solution)/shard_map/project/pallas_call | solution.py:246
  50.5 0.5 collective-permute-start.16
  51.0 3.7 %collective-permute-done.14.refs_1_ = bf16[3,384,128]{2,1,0:T(8,128)(2,1)S(1)} collective-permute-done((bf16[3,384,128]{2,1,0:T(8,128)(2,1)S(1)}, bf16[3,384,128]{2,1,0:T(8,128)(2,1)S(1)}, u32[]{:S(2)}, u32[]{:S(2)}) %collective-permute-start.14) | collective-permute-done | bytes 294944 | tf_op jit(solution)/shard_map/ppermute | solution.py:117
  54.7 6.7 %collective-permute-done.15.refs_2_ = bf16[3,384,128]{2,1,0:T(8,128)(2,1)S(1)} collective-permute-done((bf16[3,384,128]{2,1,0:T(8,128)(2,1)S(1)}, bf16[3,384,128]{2,1,0:T(8,128)(2,1)S(1)}, u32[]{:S(2)}, u32[]{:S(2)}) %collective-permute-start.15) | collective-permute-done | bytes 294944 | tf_op jit(solution)/shard_map/ppermute | solution.py:117
  61.5 0.5 collective-permute-start.18
  62.0 0.0 collective-permute-start.19
  62.0 0.5 collective-permute-start.20
  62.5 1.2 %collective-permute-start.21 = (bf16[256,512]{1,0:T(8,128)(2,1)S(1)}, bf16[256,512]{1,0:T(8,128)(2,1)S(1)}, u32[]{:S(2)}, u32[]{:S(2)}) collective-permute-start(bf16[256,512]{1,0:T(8,128)(2,1)S(1)} %copy-done.1), channel_id=1, source_target_pairs={{0,8},{4,12},{8,0},{12,4},{16,24},{20,28},{24,16},{28,20},{1,9},{5... | collective-permute-start | bytes 786440 | tf_op jit(solution)/shard_map/ppermute | solution.py:117
  63.7 0.8 collective-permute-start.22
  64.6 7.0 %attend.1 = (bf16[384,128]{1,0:T(8,128)(2,1)S(1)}, bf16[384,128]{1,0:T(8,128)(2,1)S(1)}, bf16[384,128]{1,0:T(8,128)(2,1)S(1)}, bf16[384,128]{1,0:T(8,128)(2,1)S(1)}) custom-call(s32[3]{0:T(128)S(1)} %pad_add_fusion.where_ref, s32[6]{0:T(128)S(1)} %bitcast_subtract_fusion.start_ref, bf16[3,384,128]{2,1,0:T(8,128)(2,1)S(1)} %get-tuple-element.51.refs_0_, ...), custom_call_target="tpu_custom_call" | custom-call | flops 2415919104 | bytes 8388608 | tf_op jit(solution)/shard_map/attend/pallas_call | solution.py:313
  71.6 0.1 collective-permute-done.22.y_ref.refs_2_
  71.7 1.8 %collective-permute-start.24 = (bf16[384,128]{1,0:T(8,128)(2,1)S(1)}, bf16[384,128]{1,0:T(8,128)(2,1)S(1)}, u32[]{:S(2)}, u32[]{:S(2)}) collective-permute-start(bf16[384,128]{1,0:T(8,128)(2,1)S(1)} %get-tuple-element.60), channel_id=1, source_target_pairs={{0,24},{4,28},{8,16},{12,20},{16,8},{20,12},{24,0},{28,4},{1,25},{... | collective-permute-start | bytes 294920 | tf_op jit(solution)/shard_map/ppermute | solution.py:117
  73.4 1.2 %collective-permute-start.25 = (bf16[384,128]{1,0:T(8,128)(2,1)S(1)}, bf16[384,128]{1,0:T(8,128)(2,1)S(1)}, u32[]{:S(2)}, u32[]{:S(2)}) collective-permute-start(bf16[384,128]{1,0:T(8,128)(2,1)S(1)} %get-tuple-element.61), channel_id=1, source_target_pairs={{0,16},{4,20},{8,24},{12,28},{16,0},{20,4},{24,8},{28,12},{1,17},{... | collective-permute-start | bytes 294920 | tf_op jit(solution)/shard_map/ppermute | solution.py:117
  74.6 0.5 collective-permute-start.26
  75.2 3.0 %collective-permute-done.24 = bf16[384,128]{1,0:T(8,128)(2,1)S(1)} collective-permute-done((bf16[384,128]{1,0:T(8,128)(2,1)S(1)}, bf16[384,128]{1,0:T(8,128)(2,1)S(1)}, u32[]{:S(2)}, u32[]{:S(2)}) %collective-permute-start.24) | collective-permute-done | bytes 98336 | tf_op jit(solution)/shard_map/ppermute | solution.py:117
  78.2 1.7 %collective-permute-done.25 = bf16[384,128]{1,0:T(8,128)(2,1)S(1)} collective-permute-done((bf16[384,128]{1,0:T(8,128)(2,1)S(1)}, bf16[384,128]{1,0:T(8,128)(2,1)S(1)}, u32[]{:S(2)}, u32[]{:S(2)}) %collective-permute-start.25) | collective-permute-done | bytes 98336 | tf_op jit(solution)/shard_map/ppermute | solution.py:117
  79.9 0.1 broadcast_select_fusion.5
  80.1 2.1 %collective-permute-start.27 = (bf16[384,512]{1,0:T(8,128)(2,1)S(1)}, bf16[384,512]{1,0:T(8,128)(2,1)S(1)}, u32[]{:S(2)}, u32[]{:S(2)}) collective-permute-start(bf16[384,512]{1,0:T(8,128)(2,1)S(1)} %pad_maximum_fusion.own), channel_id=1, source_target_pairs={{0,1},{1,0},{2,3},{3,2},{4,5},{5,4},{6,7},{7,6},{8,9},{9,8},{10,11... | collective-permute-start | bytes 1179656 | tf_op jit(solution)/shard_map/ppermute | solution.py:121
  82.2 0.7 collective-permute-start.30
  82.9 8.6 %collective-permute-done.27.near = bf16[384,512]{1,0:T(8,128)(2,1)S(1)} collective-permute-done((bf16[384,512]{1,0:T(8,128)(2,1)S(1)}, bf16[384,512]{1,0:T(8,128)(2,1)S(1)}, u32[]{:S(2)}, u32[]{:S(2)}) %collective-permute-start.27) | collective-permute-done | bytes 393248 | tf_op jit(solution)/shard_map/ppermute | solution.py:121
  91.5 0.7 collective-permute-start.28
  92.2 0.1 collective-permute-start.34
  92.4 1.3 %collective-permute-start.31 = (bf16[384,512]{1,0:T(8,128)(2,1)S(1)}, bf16[384,512]{1,0:T(8,128)(2,1)S(1)}, u32[]{:S(2)}, u32[]{:S(2)}) collective-permute-start(bf16[384,512]{1,0:T(8,128)(2,1)S(1)} %collective-permute-done.30.q1), channel_id=1, source_target_pairs={{1,0},{2,3},{5,4},{6,7},{9,8},{10,11},{13,12},{14,15},{17,16},{18,... | collective-permute-start | bytes 1179656 | tf_op jit(solution)/shard_map/ppermute | solution.py:129
  93.7 1.2 collective-permute-start.32
  94.9 0.6 collective-permute-start.33
  95.6 0.1 collective-permute-start.35
  95.7 1.3 %collective-permute-start.29 = (bf16[384,512]{1,0:T(8,128)(2,1)S(1)}, bf16[384,512]{1,0:T(8,128)(2,1)S(1)}, u32[]{:S(2)}, u32[]{:S(2)}) collective-permute-start(bf16[384,512]{1,0:T(8,128)(2,1)S(1)} %collective-permute-done.28.q2), channel_id=1, source_target_pairs={{1,0},{2,3},{5,4},{6,7},{9,8},{10,11},{13,12},{14,15},{17,16},{18,... | collective-permute-start | bytes 1179656 | tf_op jit(solution)/shard_map/ppermute | solution.py:129
  97.0 2.6 %collective-permute-done.32.refs_3_ = bf16[128,512]{1,0:T(8,128)(2,1)S(1)} collective-permute-done((bf16[128,512]{1,0:T(8,128)(2,1)S(1)}, bf16[128,512]{1,0:T(8,128)(2,1)S(1)}, u32[]{:S(2)}, u32[]{:S(2)}) %collective-permute-start.32) | collective-permute-done | bytes 131104 | tf_op jit(solution)/shard_map/ppermute | solution.py:117
  99.7 0.8 collective-permute-done.33.refs_4_
  100.5 1.1 copy.11
  101.6 1.1 copy.10
  102.7 5.0 %collective-permute-done.31.p2 = bf16[384,512]{1,0:T(8,128)(2,1)S(1)} collective-permute-done((bf16[384,512]{1,0:T(8,128)(2,1)S(1)}, bf16[384,512]{1,0:T(8,128)(2,1)S(1)}, u32[]{:S(2)}, u32[]{:S(2)}) %collective-permute-start.31) | collective-permute-done | bytes 393248 | tf_op jit(solution)/shard_map/ppermute | solution.py:129
  107.7 1.5 %early.1 = (f32[384,512]{1,0:T(8,128)S(1)}, bf16[512,512]{1,0:T(8,128)(2,1)S(1)}) custom-call(s32[3]{0:T(128)S(1)} %pad_add_fusion.where_ref, bf16[384,512]{1,0:T(8,128)(2,1)S(1)} %pad_maximum_fusion.own, bf16[384,512]{1,0:T(8,128)(2,1)S(1)} %collective-permute-done.27.near, bf16[384,512]{1,0:T(8,128)(2,1)S(1)} %collective-permute-done.30.q1, ...), custom_call_target="tpu_custom_call" | custom-call | flops 1073741824 | bytes 8388608 | tf_op jit(solution)/shard_map/early/pallas_call | solution.py:353
  109.2 6.8 %collective-permute-done.29.p3 = bf16[384,512]{1,0:T(8,128)(2,1)S(1)} collective-permute-done((bf16[384,512]{1,0:T(8,128)(2,1)S(1)}, bf16[384,512]{1,0:T(8,128)(2,1)S(1)}, u32[]{:S(2)}, u32[]{:S(2)}) %collective-permute-start.29) | collective-permute-done | bytes 393248 | tf_op jit(solution)/shard_map/ppermute | solution.py:129
  115.9 1.7 %last.1 = bf16[384,512]{1,0:T(8,128)(2,1)} custom-call(s32[3]{0:T(128)S(1)} %pad_add_fusion.where_ref, bf16[384,512]{1,0:T(8,128)(2,1)S(1)} %collective-permute-done.28.q2, bf16[384,512]{1,0:T(8,128)(2,1)S(1)} %collective-permute-done.29.p3, f32[384,512]{1,0:T(8,128)S(1)} %get-tuple-element.75.total_ref, bf16[512,512]{1,0:T(8,128)(2,1)S(1)} %get-tuple-element.76.w_ref), custom_call_target="tpu_custom_call" | custom-call | flops 201326592 | bytes 8388608 | tf_op jit(solution)/shard_map/last/pallas_call | solution.py:376
  (52 shorter events, 0.4 us)
Async XLA Ops:
  0.6 8.5 %copy-start.4 = (s32[6]{0:T(128)S(1)}, s32[6]{0:T(128)}, u32[]{:S(2)}) copy-start(s32[6]{0:T(128)} %param.9) | copy-start | bytes 76
  0.6 12.4 %collective-permute-start = (bf16[384,512]{1,0:T(8,128)(2,1)}, bf16[384,512]{1,0:T(8,128)(2,1)S(1)}, u32[]{:S(2)}, u32[]{:S(2)}) collective-permute-start(bf16[384,512]{1,0:T(8,128)(2,1)} %refs_0_.1), channel_id=1, source_target_pairs={{0,1},{1,0},{2,3},{3,2},{4,5},{5,4},{6,7},{7,6},{8,9},{9,8},{10,11... | collective-permute-start | bytes 1179656 | tf_op jit(solution)/shard_map/ppermute | solution.py:121
  3.7 9.3 %collective-permute-start.1 = (bf16[384,512]{1,0:T(8,128)(2,1)}, bf16[384,512]{1,0:T(8,128)(2,1)S(1)}, u32[]{:S(2)}, u32[]{:S(2)}) collective-permute-start(bf16[384,512]{1,0:T(8,128)(2,1)} %refs_0_.1), channel_id=1, source_target_pairs={{1,2},{2,1},{5,6},{6,5},{9,10},{10,9},{13,14},{14,13},{17,18},{18,... | collective-permute-start | bytes 1179656 | tf_op jit(solution)/shard_map/ppermute | solution.py:125
  6.1 19.1 %collective-permute-start.5 = (bf16[256,1536]{1,0:T(8,128)(2,1)S(1)}, bf16[256,1536]{1,0:T(8,128)(2,1)S(1)}, u32[]{:S(2)}, u32[]{:S(2)}) collective-permute-start(bf16[256,1536]{1,0:T(8,128)(2,1)S(1)} %reshape.193.refs_0_), channel_id=1, source_target_pairs={{0,8},{4,12},{8,0},{12,4},{16,24},{20,28},{24,16},{28,20},{1,9},{5... | collective-permute-start | bytes 2359304 | tf_op jit(solution)/shard_map/ppermute | solution.py:117
  7.6 18.7 %collective-permute-start.6 = (bf16[256,1536]{1,0:T(8,128)(2,1)S(1)}, bf16[256,1536]{1,0:T(8,128)(2,1)S(1)}, u32[]{:S(2)}, u32[]{:S(2)}) collective-permute-start(bf16[256,1536]{1,0:T(8,128)(2,1)S(1)} %reshape.193.refs_0_), channel_id=1, source_target_pairs={{0,16},{4,20},{8,24},{12,28},{16,0},{20,4},{24,8},{28,12},{1,17},{... | collective-permute-start | bytes 2359304 | tf_op jit(solution)/shard_map/ppermute | solution.py:117
  9.6 29.8 %copy-start = (bf16[384,512]{1,0:T(8,128)(2,1)S(1)}, bf16[384,512]{1,0:T(8,128)(2,1)}, u32[]{:S(2)}) copy-start(bf16[384,512]{1,0:T(8,128)(2,1)} %refs_0_.1) | copy-start | bytes 1179652
  9.6 29.8 %copy-start.3 = (f32[2048]{0:T(1024)S(1)}, f32[2048]{0:T(1024)}, u32[]{:S(2)}) copy-start(f32[2048]{0:T(1024)} %param.6) | copy-start | bytes 24580
  13.1 2.0 %collective-permute-start.3 = (bf16[384,512]{1,0:T(8,128)(2,1)S(1)}, bf16[384,512]{1,0:T(8,128)(2,1)S(1)}, u32[]{:S(2)}, u32[]{:S(2)}) collective-permute-start(bf16[384,512]{1,0:T(8,128)(2,1)S(1)} %collective-permute-done.refs_1_), channel_id=1, source_target_pairs={{1,2},{2,1},{5,6},{6,5},{9,10},{10,9},{13,14},{14,13},{17,18},{18,... | collective-permute-start | bytes 1179656 | tf_op jit(solution)/shard_map/ppermute | solution.py:125
  13.7 17.1 %collective-permute-start.2 = (bf16[384,512]{1,0:T(8,128)(2,1)S(1)}, bf16[384,512]{1,0:T(8,128)(2,1)S(1)}, u32[]{:S(2)}, u32[]{:S(2)}) collective-permute-start(bf16[384,512]{1,0:T(8,128)(2,1)S(1)} %collective-permute-done.1.refs_2_), channel_id=1, source_target_pairs={{1,0},{2,3},{5,4},{6,7},{9,8},{10,11},{13,12},{14,15},{17,16},{18,... | collective-permute-start | bytes 1179656 | tf_op jit(solution)/shard_map/ppermute | solution.py:129
  15.1 23.7 %collective-permute-start.4 = (bf16[384,512]{1,0:T(8,128)(2,1)S(1)}, bf16[384,512]{1,0:T(8,128)(2,1)S(1)}, u32[]{:S(2)}, u32[]{:S(2)}) collective-permute-start(bf16[384,512]{1,0:T(8,128)(2,1)S(1)} %collective-permute-done.3.refs_4_), channel_id=1, source_target_pairs={{1,0},{2,3},{5,4},{6,7},{9,8},{10,11},{13,12},{14,15},{17,16},{18,... | collective-permute-start | bytes 1179656 | tf_op jit(solution)/shard_map/ppermute | solution.py:129
  26.4 12.4 %collective-permute-start.7 = (bf16[128,1536]{1,0:T(8,128)(2,1)S(1)}, bf16[128,1536]{1,0:T(8,128)(2,1)S(1)}, u32[]{:S(2)}, u32[]{:S(2)}) collective-permute-start(bf16[128,1536]{1,0:T(8,128)(2,1)S(1)} %get-tuple-element.45), channel_id=1, source_target_pairs={{0,8},{4,12},{8,0},{12,4},{16,24},{20,28},{24,16},{28,20},{1,9},{5... | collective-permute-start | bytes 1179656 | tf_op jit(solution)/shard_map/ppermute | solution.py:117
  27.0 12.3 %collective-permute-start.8 = (bf16[128,1536]{1,0:T(8,128)(2,1)S(1)}, bf16[128,1536]{1,0:T(8,128)(2,1)S(1)}, u32[]{:S(2)}, u32[]{:S(2)}) collective-permute-start(bf16[128,1536]{1,0:T(8,128)(2,1)S(1)} %get-tuple-element.46), channel_id=1, source_target_pairs={{0,16},{4,20},{8,24},{12,28},{16,0},{20,4},{24,8},{28,12},{1,17},{... | collective-permute-start | bytes 1179656 | tf_op jit(solution)/shard_map/ppermute | solution.py:117
  28.5 13.3 %collective-permute-start.9 = (bf16[256,1536]{1,0:T(8,128)(2,1)S(1)}, bf16[256,1536]{1,0:T(8,128)(2,1)S(1)}, u32[]{:S(2)}, u32[]{:S(2)}) collective-permute-start(bf16[256,1536]{1,0:T(8,128)(2,1)S(1)} %reshape.193.refs_0_), channel_id=1, source_target_pairs={{0,4},{4,0},{8,12},{12,8},{16,20},{20,16},{24,28},{28,24},{1,5},{5... | collective-permute-start | bytes 2359304 | tf_op jit(solution)/shard_map/ppermute | solution.py:117
  30.8 11.4 %collective-permute-start.10 = (bf16[256,1536]{1,0:T(8,128)(2,1)S(1)}, bf16[256,1536]{1,0:T(8,128)(2,1)S(1)}, u32[]{:S(2)}, u32[]{:S(2)}) collective-permute-start(bf16[256,1536]{1,0:T(8,128)(2,1)S(1)} %collective-permute-done.5.x_ref.refs_1_), channel_id=1, source_target_pairs={{0,4},{4,0},{8,12},{12,8},{16,20},{20,16},{24,28},{28,24},{1,5},{5... | collective-permute-start | bytes 2359304 | tf_op jit(solution)/shard_map/ppermute | solution.py:117
  38.8 3.4 %collective-permute-start.11 = (bf16[256,1536]{1,0:T(8,128)(2,1)S(1)}, bf16[256,1536]{1,0:T(8,128)(2,1)S(1)}, u32[]{:S(2)}, u32[]{:S(2)}) collective-permute-start(bf16[256,1536]{1,0:T(8,128)(2,1)S(1)} %collective-permute-done.6.y_ref.refs_2_), channel_id=1, source_target_pairs={{0,4},{4,0},{8,12},{12,8},{16,20},{20,16},{24,28},{28,24},{1,5},{5... | collective-permute-start | bytes 2359304 | tf_op jit(solution)/shard_map/ppermute | solution.py:117
  38.8 3.1 %collective-permute-start.12 = (bf16[128,1536]{1,0:T(8,128)(2,1)S(1)}, bf16[128,1536]{1,0:T(8,128)(2,1)S(1)}, u32[]{:S(2)}, u32[]{:S(2)}) collective-permute-start(bf16[128,1536]{1,0:T(8,128)(2,1)S(1)} %collective-permute-done.7.refs_3_), channel_id=1, source_target_pairs={{0,4},{4,0},{8,12},{12,8},{16,20},{20,16},{24,28},{28,24},{1,5},{5... | collective-permute-start | bytes 1179656 | tf_op jit(solution)/shard_map/ppermute | solution.py:117
  39.3 2.9 %collective-permute-start.13 = (bf16[128,1536]{1,0:T(8,128)(2,1)S(1)}, bf16[128,1536]{1,0:T(8,128)(2,1)S(1)}, u32[]{:S(2)}, u32[]{:S(2)}) collective-permute-start(bf16[128,1536]{1,0:T(8,128)(2,1)S(1)} %collective-permute-done.8.refs_4_), channel_id=1, source_target_pairs={{0,4},{4,0},{8,12},{12,8},{16,20},{20,16},{24,28},{28,24},{1,5},{5... | collective-permute-start | bytes 1179656 | tf_op jit(solution)/shard_map/ppermute | solution.py:117
  44.8 9.9 %collective-permute-start.14 = (bf16[3,384,128]{2,1,0:T(8,128)(2,1)S(1)}, bf16[3,384,128]{2,1,0:T(8,128)(2,1)S(1)}, u32[]{:S(2)}, u32[]{:S(2)}) collective-permute-start(bf16[3,384,128]{2,1,0:T(8,128)(2,1)S(1)} %get-tuple-element.48), channel_id=1, source_target_pairs={{0,8},{4,12},{8,0},{12,4},{16,24},{20,28},{24,16},{28,20},{1,9},{5... | collective-permute-start | bytes 884744 | tf_op jit(solution)/shard_map/ppermute | solution.py:117
  46.4 16.1 %copy-start.1 = (bf16[256,512]{1,0:T(8,128)(2,1)S(1)}, bf16[256,512]{1,0:T(8,128)(2,1)}, u32[]{:S(2)}) copy-start(bf16[256,512]{1,0:T(8,128)(2,1)} %refs_0_.2) | copy-start | bytes 786436
  46.4 15.1 %collective-permute-start.15 = (bf16[3,384,128]{2,1,0:T(8,128)(2,1)S(1)}, bf16[3,384,128]{2,1,0:T(8,128)(2,1)S(1)}, u32[]{:S(2)}, u32[]{:S(2)}) collective-permute-start(bf16[3,384,128]{2,1,0:T(8,128)(2,1)S(1)} %get-tuple-element.49), channel_id=1, source_target_pairs={{0,16},{4,20},{8,24},{12,28},{16,0},{20,4},{24,8},{28,12},{1,17},{... | collective-permute-start | bytes 884744 | tf_op jit(solution)/shard_map/ppermute | solution.py:117
  50.5 11.0 %collective-permute-start.16 = (bf16[3,384,128]{2,1,0:T(8,128)(2,1)S(1)}, bf16[3,384,128]{2,1,0:T(8,128)(2,1)S(1)}, u32[]{:S(2)}, u32[]{:S(2)}) collective-permute-start(bf16[3,384,128]{2,1,0:T(8,128)(2,1)S(1)} %get-tuple-element.50), channel_id=1, source_target_pairs={{0,24},{4,28},{8,16},{12,20},{16,8},{20,12},{24,0},{28,4},{1,25},{... | collective-permute-start | bytes 884744 | tf_op jit(solution)/shard_map/ppermute | solution.py:117
  61.5 2.3 %collective-permute-start.17 = (bf16[3,384,128]{2,1,0:T(8,128)(2,1)S(1)}, bf16[3,384,128]{2,1,0:T(8,128)(2,1)S(1)}, u32[]{:S(2)}, u32[]{:S(2)}) collective-permute-start(bf16[3,384,128]{2,1,0:T(8,128)(2,1)S(1)} %get-tuple-element.51.refs_0_), channel_id=1, source_target_pairs={{0,4},{4,0},{8,12},{12,8},{16,20},{20,16},{24,28},{28,24},{1,5},{5... | collective-permute-start | bytes 884744 | tf_op jit(solution)/shard_map/ppermute | solution.py:117
  61.5 3.1 %collective-permute-start.18 = (bf16[3,384,128]{2,1,0:T(8,128)(2,1)S(1)}, bf16[3,384,128]{2,1,0:T(8,128)(2,1)S(1)}, u32[]{:S(2)}, u32[]{:S(2)}) collective-permute-start(bf16[3,384,128]{2,1,0:T(8,128)(2,1)S(1)} %collective-permute-done.14.refs_1_), channel_id=1, source_target_pairs={{0,4},{4,0},{8,12},{12,8},{16,20},{20,16},{24,28},{28,24},{1,5},{5... | collective-permute-start | bytes 884744 | tf_op jit(solution)/shard_map/ppermute | solution.py:117
  62.0 2.6 %collective-permute-start.19 = (bf16[3,384,128]{2,1,0:T(8,128)(2,1)S(1)}, bf16[3,384,128]{2,1,0:T(8,128)(2,1)S(1)}, u32[]{:S(2)}, u32[]{:S(2)}) collective-permute-start(bf16[3,384,128]{2,1,0:T(8,128)(2,1)S(1)} %collective-permute-done.15.refs_2_), channel_id=1, source_target_pairs={{0,4},{4,0},{8,12},{12,8},{16,20},{20,16},{24,28},{28,24},{1,5},{5... | collective-permute-start | bytes 884744 | tf_op jit(solution)/shard_map/ppermute | solution.py:117
  62.0 2.6 %collective-permute-start.20 = (bf16[3,384,128]{2,1,0:T(8,128)(2,1)S(1)}, bf16[3,384,128]{2,1,0:T(8,128)(2,1)S(1)}, u32[]{:S(2)}, u32[]{:S(2)}) collective-permute-start(bf16[3,384,128]{2,1,0:T(8,128)(2,1)S(1)} %collective-permute-done.16.refs_3_), channel_id=1, source_target_pairs={{0,4},{4,0},{8,12},{12,8},{16,20},{20,16},{24,28},{28,24},{1,5},{5... | collective-permute-start | bytes 884744 | tf_op jit(solution)/shard_map/ppermute | solution.py:117
  62.5 9.1 %collective-permute-start.21 = (bf16[256,512]{1,0:T(8,128)(2,1)S(1)}, bf16[256,512]{1,0:T(8,128)(2,1)S(1)}, u32[]{:S(2)}, u32[]{:S(2)}) collective-permute-start(bf16[256,512]{1,0:T(8,128)(2,1)S(1)} %copy-done.1), channel_id=1, source_target_pairs={{0,8},{4,12},{8,0},{12,4},{16,24},{20,28},{24,16},{28,20},{1,9},{5... | collective-permute-start | bytes 786440 | tf_op jit(solution)/shard_map/ppermute | solution.py:117
  63.7 7.9 %collective-permute-start.22 = (bf16[256,512]{1,0:T(8,128)(2,1)S(1)}, bf16[256,512]{1,0:T(8,128)(2,1)S(1)}, u32[]{:S(2)}, u32[]{:S(2)}) collective-permute-start(bf16[256,512]{1,0:T(8,128)(2,1)S(1)} %copy-done.1), channel_id=1, source_target_pairs={{0,16},{4,20},{8,24},{12,28},{16,0},{20,4},{24,8},{28,12},{1,17},{... | collective-permute-start | bytes 786440 | tf_op jit(solution)/shard_map/ppermute | solution.py:117
  64.6 7.1 %collective-permute-start.23 = (bf16[256,512]{1,0:T(8,128)(2,1)S(1)}, bf16[256,512]{1,0:T(8,128)(2,1)S(1)}, u32[]{:S(2)}, u32[]{:S(2)}) collective-permute-start(bf16[256,512]{1,0:T(8,128)(2,1)S(1)} %copy-done.1), channel_id=1, source_target_pairs={{0,4},{4,0},{8,12},{12,8},{16,20},{20,16},{24,28},{28,24},{1,5},{5... | collective-permute-start | bytes 786440 | tf_op jit(solution)/shard_map/ppermute | solution.py:117
  71.7 6.5 %collective-permute-start.24 = (bf16[384,128]{1,0:T(8,128)(2,1)S(1)}, bf16[384,128]{1,0:T(8,128)(2,1)S(1)}, u32[]{:S(2)}, u32[]{:S(2)}) collective-permute-start(bf16[384,128]{1,0:T(8,128)(2,1)S(1)} %get-tuple-element.60), channel_id=1, source_target_pairs={{0,24},{4,28},{8,16},{12,20},{16,8},{20,12},{24,0},{28,4},{1,25},{... | collective-permute-start | bytes 294920 | tf_op jit(solution)/shard_map/ppermute | solution.py:117
  73.4 6.5 %collective-permute-start.25 = (bf16[384,128]{1,0:T(8,128)(2,1)S(1)}, bf16[384,128]{1,0:T(8,128)(2,1)S(1)}, u32[]{:S(2)}, u32[]{:S(2)}) collective-permute-start(bf16[384,128]{1,0:T(8,128)(2,1)S(1)} %get-tuple-element.61), channel_id=1, source_target_pairs={{0,16},{4,20},{8,24},{12,28},{16,0},{20,4},{24,8},{28,12},{1,17},{... | collective-permute-start | bytes 294920 | tf_op jit(solution)/shard_map/ppermute | solution.py:117
  74.6 5.3 %collective-permute-start.26 = (bf16[384,128]{1,0:T(8,128)(2,1)S(1)}, bf16[384,128]{1,0:T(8,128)(2,1)S(1)}, u32[]{:S(2)}, u32[]{:S(2)}) collective-permute-start(bf16[384,128]{1,0:T(8,128)(2,1)S(1)} %get-tuple-element.62), channel_id=1, source_target_pairs={{0,8},{4,12},{8,0},{12,4},{16,24},{20,28},{24,16},{28,20},{1,9},{5... | collective-permute-start | bytes 294920 | tf_op jit(solution)/shard_map/ppermute | solution.py:117
  80.1 11.4 %collective-permute-start.27 = (bf16[384,512]{1,0:T(8,128)(2,1)S(1)}, bf16[384,512]{1,0:T(8,128)(2,1)S(1)}, u32[]{:S(2)}, u32[]{:S(2)}) collective-permute-start(bf16[384,512]{1,0:T(8,128)(2,1)S(1)} %pad_maximum_fusion.own), channel_id=1, source_target_pairs={{0,1},{1,0},{2,3},{3,2},{4,5},{5,4},{6,7},{7,6},{8,9},{9,8},{10,11... | collective-permute-start | bytes 1179656 | tf_op jit(solution)/shard_map/ppermute | solution.py:121
  82.2 10.2 %collective-permute-start.30 = (bf16[384,512]{1,0:T(8,128)(2,1)S(1)}, bf16[384,512]{1,0:T(8,128)(2,1)S(1)}, u32[]{:S(2)}, u32[]{:S(2)}) collective-permute-start(bf16[384,512]{1,0:T(8,128)(2,1)S(1)} %pad_maximum_fusion.own), channel_id=1, source_target_pairs={{1,2},{2,1},{5,6},{6,5},{9,10},{10,9},{13,14},{14,13},{17,18},{18,... | collective-permute-start | bytes 1179656 | tf_op jit(solution)/shard_map/ppermute | solution.py:125
  91.5 4.1 %collective-permute-start.28 = (bf16[384,512]{1,0:T(8,128)(2,1)S(1)}, bf16[384,512]{1,0:T(8,128)(2,1)S(1)}, u32[]{:S(2)}, u32[]{:S(2)}) collective-permute-start(bf16[384,512]{1,0:T(8,128)(2,1)S(1)} %collective-permute-done.27.near), channel_id=1, source_target_pairs={{1,2},{2,1},{5,6},{6,5},{9,10},{10,9},{13,14},{14,13},{17,18},{18,... | collective-permute-start | bytes 1179656 | tf_op jit(solution)/shard_map/ppermute | solution.py:125
  92.2 3.3 %collective-permute-start.34 = (bf16[256,512]{1,0:T(8,128)(2,1)S(1)}, bf16[256,512]{1,0:T(8,128)(2,1)S(1)}, u32[]{:S(2)}, u32[]{:S(2)}) collective-permute-start(bf16[256,512]{1,0:T(8,128)(2,1)S(1)} %collective-permute-done.21.x_ref.refs_1_), channel_id=1, source_target_pairs={{0,4},{4,0},{8,12},{12,8},{16,20},{20,16},{24,28},{28,24},{1,5},{5... | collective-permute-start | bytes 786440 | tf_op jit(solution)/shard_map/ppermute | solution.py:117
  92.4 15.3 %collective-permute-start.31 = (bf16[384,512]{1,0:T(8,128)(2,1)S(1)}, bf16[384,512]{1,0:T(8,128)(2,1)S(1)}, u32[]{:S(2)}, u32[]{:S(2)}) collective-permute-start(bf16[384,512]{1,0:T(8,128)(2,1)S(1)} %collective-permute-done.30.q1), channel_id=1, source_target_pairs={{1,0},{2,3},{5,4},{6,7},{9,8},{10,11},{13,12},{14,15},{17,16},{18,... | collective-permute-start | bytes 1179656 | tf_op jit(solution)/shard_map/ppermute | solution.py:129
  93.7 6.0 %collective-permute-start.32 = (bf16[128,512]{1,0:T(8,128)(2,1)S(1)}, bf16[128,512]{1,0:T(8,128)(2,1)S(1)}, u32[]{:S(2)}, u32[]{:S(2)}) collective-permute-start(bf16[128,512]{1,0:T(8,128)(2,1)S(1)} %get-tuple-element.72), channel_id=1, source_target_pairs={{0,8},{4,12},{8,0},{12,4},{16,24},{20,28},{24,16},{28,20},{1,9},{5... | collective-permute-start | bytes 393224 | tf_op jit(solution)/shard_map/ppermute | solution.py:117
  94.9 5.6 %collective-permute-start.33 = (bf16[128,512]{1,0:T(8,128)(2,1)S(1)}, bf16[128,512]{1,0:T(8,128)(2,1)S(1)}, u32[]{:S(2)}, u32[]{:S(2)}) collective-permute-start(bf16[128,512]{1,0:T(8,128)(2,1)S(1)} %get-tuple-element.73), channel_id=1, source_target_pairs={{0,16},{4,20},{8,24},{12,28},{16,0},{20,4},{24,8},{28,12},{1,17},{... | collective-permute-start | bytes 393224 | tf_op jit(solution)/shard_map/ppermute | solution.py:117
  95.6 7.1 %collective-permute-start.35 = (bf16[256,512]{1,0:T(8,128)(2,1)S(1)}, bf16[256,512]{1,0:T(8,128)(2,1)S(1)}, u32[]{:S(2)}, u32[]{:S(2)}) collective-permute-start(bf16[256,512]{1,0:T(8,128)(2,1)S(1)} %collective-permute-done.22.y_ref.refs_2_), channel_id=1, source_target_pairs={{0,4},{4,0},{8,12},{12,8},{16,20},{20,16},{24,28},{28,24},{1,5},{5... | collective-permute-start | bytes 786440 | tf_op jit(solution)/shard_map/ppermute | solution.py:117
  95.7 20.3 %collective-permute-start.29 = (bf16[384,512]{1,0:T(8,128)(2,1)S(1)}, bf16[384,512]{1,0:T(8,128)(2,1)S(1)}, u32[]{:S(2)}, u32[]{:S(2)}) collective-permute-start(bf16[384,512]{1,0:T(8,128)(2,1)S(1)} %collective-permute-done.28.q2), channel_id=1, source_target_pairs={{1,0},{2,3},{5,4},{6,7},{9,8},{10,11},{13,12},{14,15},{17,16},{18,... | collective-permute-start | bytes 1179656 | tf_op jit(solution)/shard_map/ppermute | solution.py:129
  99.7 3.0 %collective-permute-start.36 = (bf16[128,512]{1,0:T(8,128)(2,1)S(1)}, bf16[128,512]{1,0:T(8,128)(2,1)S(1)}, u32[]{:S(2)}, u32[]{:S(2)}) collective-permute-start(bf16[128,512]{1,0:T(8,128)(2,1)S(1)} %collective-permute-done.32.refs_3_), channel_id=1, source_target_pairs={{0,4},{4,0},{8,12},{12,8},{16,20},{20,16},{24,28},{28,24},{1,5},{5... | collective-permute-start | bytes 393224 | tf_op jit(solution)/shard_map/ppermute | solution.py:117
  100.5 2.2 %collective-permute-start.37 = (bf16[128,512]{1,0:T(8,128)(2,1)S(1)}, bf16[128,512]{1,0:T(8,128)(2,1)S(1)}, u32[]{:S(2)}, u32[]{:S(2)}) collective-permute-start(bf16[128,512]{1,0:T(8,128)(2,1)S(1)} %collective-permute-done.33.refs_4_), channel_id=1, source_target_pairs={{0,4},{4,0},{8,12},{12,8},{16,20},{20,16},{24,28},{28,24},{1,5},{5... | collective-permute-start | bytes 393224 | tf_op jit(solution)/shard_map/ppermute | solution.py:117
  100.5 7.2 %copy-start.2 = (bf16[256,512]{1,0:T(8,128)(2,1)S(1)}, bf16[256,512]{1,0:T(8,128)(2,1)}, u32[]{:S(2)}) copy-start(bf16[256,512]{1,0:T(8,128)(2,1)} %refs_0_.2) | copy-start | bytes 786436

commit v5 on v4

--- a/solution.py
+++ b/solution.py
@@ -426,22 +426,20 @@
     keys, vals = [heads_in_order([a[j] for a in sent], chip) for j in (1, 2)]
 
     pieces = [sent[0]] + [swap(sent[m], 2 * m) for m in range(1, CHIPS)]
-    *pieces, w_late = together(*pieces, w_out)
+    heads_out = attend(where, starts, pieces + [swap(a, 1) for a in pieces])
+    back = [heads_out[0]] + [swap(heads_out[m], 2 * m) for m in range(1, CHIPS)]
+
+    attended, w_late = together(heads_in_order(back, chip), w_out)
+    near, q1 = outer(attended), inner(attended)
     w_x, w_y = swap(w_late, 2), swap(w_late, 4)
-    heads_out = attend(where, starts, pieces + [swap(a, 1) for a in pieces])
-    *heads_out, w_x, w_y, w_other = together(*heads_out, w_x, w_y, swap(w_late, 1))
-    back = [heads_out[0]] + [swap(heads_out[m], 2 * m) for m in range(1, CHIPS)]
-    attended = heads_in_order(back, chip)
-    attended, w_x, w_y = together(attended, w_x, w_y)
     upper, lower = halves(w_x, w_y)
-    near, q1 = outer(attended), inner(attended)
     q1, upper, lower = together(q1, upper, lower)
     far_a, far_b = swap(upper, 2), swap(lower, 4)
     pieces = (w_late, w_x, w_y, far_a, far_b)
     q2, p2 = inner(near), outward(q1)
-    others = [w_other] + [swap(w, 1) for w in pieces[1:]]
     p3 = outward(q2)
-    total, w_last = early(where, (attended, near, q1, p2), (*pieces, *others))
+    pieces = pieces + tuple(swap(w, 1) for w in pieces)
+    total, w_last = early(where, (attended, near, q1, p2), pieces)
     mixed = last(where, q2, p3, total, w_last)
     return (mixed, keys.reshape(rows, heads, hsize), vals.reshape(rows, heads, hsize))
 

time: 118 us -> 116 us (0.983); the launches traced: 118 us -> 114 us
  waiting for transfers between devices: 62.3 us -> 56.9 us
  Pallas kernels: 17.8 us -> 19 us
    ppermute x2, waiting for transfers between devices: 11.2 us -> 6.94 us  [outer(): return lax.ppermute(x, 'gy', [(0, 1), (1, 0), (2, 3), (3, 2)])]
    pallas_call x1, Pallas kernels: 6.99 us -> 8.22 us  [attend(): pl.pallas_call(functools.partial(attend_kernel, scale=scale), in_specs=[s...]
  transfers between devices with their start and end apart: 38 -> 38, of which waited for: 16 -> 17; matrix products, arithmetic and copies ran while one was open for 5% -> 5% of each run, Pallas kernels for 12% -> 6%
where the time goes in v5:
time: 116 us; the launch traced here: 114 us
  waiting for transfers between devices  56.9 us (49%)
  starting transfers between devices  31.8 us (27%)
  Pallas kernels  19 us (16%)
  local copies, waits for them, and re-layouts  3.79 us (3%)
  other arithmetic  1.68 us (1%)
    ppermute x28, waiting for transfers between devices, swap(): return lax.ppermute(x, 'gx', [(i, i ^ mask) for i in range(2 * CHIPS)])  28.1 us
    ppermute x4, waiting for transfers between devices, outward(): return lax.ppermute(x, 'gy', [(1, 0), (2, 3)])  21.8 us
    ppermute x28, starting transfers between devices, swap(): return lax.ppermute(x, 'gx', [(i, i ^ mask) for i in range(2 * CHIPS)])  19 us
    pallas_call x1, Pallas kernels, attend(): pl.pallas_call(functools.partial(attend_kernel, scale=scale), in_specs=[s...  8.22 us
    ppermute x2, waiting for transfers between devices, outer(): return lax.ppermute(x, 'gy', [(0, 1), (1, 0), (2, 3), (3, 2)])  6.94 us
    ppermute x4, starting transfers between devices, outward(): return lax.ppermute(x, 'gy', [(1, 0), (2, 3)])  5.17 us
    pallas_call x2, Pallas kernels, project(): pl.pallas_call(functools.partial(project_kernel, pair=pair), in_specs=[sm...  5.15 us
    ppermute x2, starting transfers between devices, outer(): return lax.ppermute(x, 'gy', [(0, 1), (1, 0), (2, 3), (3, 2)])  4.96 us
  transfers between devices with their start and end apart: 38, of which 17 were waited for; matrix products, arithmetic and copies ran while one was open for 5% of the time, Pallas kernels for 6%

profile of v5, /device:TPU:0, one launch (start us, length us, event | category | flops | bytes accessed | tf_op | source)
XLA Modules:
  0.0 114.1 jit_solution(2039934296714370336)
XLA Ops:
  0.6 3.1 %collective-permute-start = (bf16[384,512]{1,0:T(8,128)(2,1)}, bf16[384,512]{1,0:T(8,128)(2,1)S(1)}, u32[]{:S(2)}, u32[]{:S(2)}) collective-permute-start(bf16[384,512]{1,0:T(8,128)(2,1)} %refs_0_.1), channel_id=1, source_target_pairs={{0,1},{1,0},{2,3},{3,2},{4,5},{5,4},{6,7},{7,6},{8,9},{9,8},{10,11... | collective-permute-start | bytes 1179656 | tf_op jit(solution)/shard_map/ppermute | solution.py:121
  3.7 0.7 collective-permute-start.1
  4.4 1.7 %reshape.193.refs_0_ = bf16[256,1536]{1,0:T(8,128)(2,1)S(1)} reshape(bf16[256,3,4,128]{3,2,1,0:T(4,128)(2,1)} %param.7) | data formatting | bytes 1572864 | tf_op jit(solution)/shard_map/reshape | solution.py:413
  6.1 1.6 %collective-permute-start.5 = (bf16[256,1536]{1,0:T(8,128)(2,1)S(1)}, bf16[256,1536]{1,0:T(8,128)(2,1)S(1)}, u32[]{:S(2)}, u32[]{:S(2)}) collective-permute-start(bf16[256,1536]{1,0:T(8,128)(2,1)S(1)} %reshape.193.refs_0_), channel_id=1, source_target_pairs={{0,8},{4,12},{8,0},{12,4},{16,24},{20,28},{24,16},{28,20},{1,9},{5... | collective-permute-start | bytes 2359304 | tf_op jit(solution)/shard_map/ppermute | solution.py:117
  7.6 1.5 %collective-permute-start.6 = (bf16[256,1536]{1,0:T(8,128)(2,1)S(1)}, bf16[256,1536]{1,0:T(8,128)(2,1)S(1)}, u32[]{:S(2)}, u32[]{:S(2)}) collective-permute-start(bf16[256,1536]{1,0:T(8,128)(2,1)S(1)} %reshape.193.refs_0_), channel_id=1, source_target_pairs={{0,16},{4,20},{8,24},{12,28},{16,0},{20,4},{24,8},{28,12},{1,17},{... | collective-permute-start | bytes 2359304 | tf_op jit(solution)/shard_map/ppermute | solution.py:117
  9.2 0.2 reduce-window.9
  9.4 0.1 select_reduce_fusion
  9.5 0.1 pad_add_fusion.where_ref
  9.6 0.8 fusion
  10.3 0.2 pad_maximum_fusion.3
  10.5 2.5 %collective-permute-done.refs_1_ = bf16[384,512]{1,0:T(8,128)(2,1)S(1)} collective-permute-done((bf16[384,512]{1,0:T(8,128)(2,1)}, bf16[384,512]{1,0:T(8,128)(2,1)S(1)}, u32[]{:S(2)}, u32[]{:S(2)}) %collective-permute-start) | collective-permute-done | bytes 393248 | tf_op jit(solution)/shard_map/ppermute | solution.py:121
  13.1 0.7 collective-permute-start.3
  13.7 1.3 %collective-permute-start.2 = (bf16[384,512]{1,0:T(8,128)(2,1)S(1)}, bf16[384,512]{1,0:T(8,128)(2,1)S(1)}, u32[]{:S(2)}, u32[]{:S(2)}) collective-permute-start(bf16[384,512]{1,0:T(8,128)(2,1)S(1)} %collective-permute-done.1.refs_2_), channel_id=1, source_target_pairs={{1,0},{2,3},{5,4},{6,7},{9,8},{10,11},{13,12},{14,15},{17,16},{18,... | collective-permute-start | bytes 1179656 | tf_op jit(solution)/shard_map/ppermute | solution.py:129
  15.1 1.3 %collective-permute-start.4 = (bf16[384,512]{1,0:T(8,128)(2,1)S(1)}, bf16[384,512]{1,0:T(8,128)(2,1)S(1)}, u32[]{:S(2)}, u32[]{:S(2)}) collective-permute-start(bf16[384,512]{1,0:T(8,128)(2,1)S(1)} %collective-permute-done.3.refs_4_), channel_id=1, source_target_pairs={{1,0},{2,3},{5,4},{6,7},{9,8},{10,11},{13,12},{14,15},{17,16},{18,... | collective-permute-start | bytes 1179656 | tf_op jit(solution)/shard_map/ppermute | solution.py:129
  16.4 8.8 %collective-permute-done.5.x_ref.refs_1_ = bf16[256,1536]{1,0:T(8,128)(2,1)S(1)} collective-permute-done((bf16[256,1536]{1,0:T(8,128)(2,1)S(1)}, bf16[256,1536]{1,0:T(8,128)(2,1)S(1)}, u32[]{:S(2)}, u32[]{:S(2)}) %collective-permute-start.5) | collective-permute-done | bytes 786464 | tf_op jit(solution)/shard_map/ppermute | solution.py:117
  25.1 1.2 %collective-permute-done.6.y_ref.refs_2_ = bf16[256,1536]{1,0:T(8,128)(2,1)S(1)} collective-permute-done((bf16[256,1536]{1,0:T(8,128)(2,1)S(1)}, bf16[256,1536]{1,0:T(8,128)(2,1)S(1)}, u32[]{:S(2)}, u32[]{:S(2)}) %collective-permute-start.6) | collective-permute-done | bytes 786464 | tf_op jit(solution)/shard_map/ppermute | solution.py:117
  26.4 0.1 halves.2
  26.4 0.6 collective-permute-start.7
  27.0 1.5 %collective-permute-start.8 = (bf16[128,1536]{1,0:T(8,128)(2,1)S(1)}, bf16[128,1536]{1,0:T(8,128)(2,1)S(1)}, u32[]{:S(2)}, u32[]{:S(2)}) collective-permute-start(bf16[128,1536]{1,0:T(8,128)(2,1)S(1)} %get-tuple-element.33), channel_id=1, source_target_pairs={{0,16},{4,20},{8,24},{12,28},{16,0},{20,4},{24,8},{28,12},{1,17},{... | collective-permute-start | bytes 1179656 | tf_op jit(solution)/shard_map/ppermute | solution.py:117
  28.5 2.3 %collective-permute-done.2.refs_3_ = bf16[384,512]{1,0:T(8,128)(2,1)S(1)} collective-permute-done((bf16[384,512]{1,0:T(8,128)(2,1)S(1)}, bf16[384,512]{1,0:T(8,128)(2,1)S(1)}, u32[]{:S(2)}, u32[]{:S(2)}) %collective-permute-start.2) | collective-permute-done | bytes 393248 | tf_op jit(solution)/shard_map/ppermute | solution.py:129
  30.8 8.0 %collective-permute-done.4.refs_5_ = bf16[384,512]{1,0:T(8,128)(2,1)S(1)} collective-permute-done((bf16[384,512]{1,0:T(8,128)(2,1)S(1)}, bf16[384,512]{1,0:T(8,128)(2,1)S(1)}, u32[]{:S(2)}, u32[]{:S(2)}) %collective-permute-start.4) | collective-permute-done | bytes 393248 | tf_op jit(solution)/shard_map/ppermute | solution.py:129
  38.8 0.5 collective-permute-start.12
  39.3 0.1 collective-permute-start.13
  39.4 2.4 %normalize.1.x_ref = bf16[384,2048]{1,0:T(8,128)(2,1)S(1)} custom-call(s32[3]{0:T(128)S(1)} %pad_add_fusion.where_ref, bf16[384,512]{1,0:T(8,128)(2,1)S(1)} %copy-done, bf16[384,512]{1,0:T(8,128)(2,1)S(1)} %collective-permute-done.refs_1_, bf16[384,512]{1,0:T(8,128)(2,1)S(1)} %collective-permute-done.1.refs_2_, ...), custom_call_target="tpu_custom_call" | custom-call | flops 8589934592 | bytes 8388608 | tf_op jit(solution)/shard_map/normalize/pallas_call | solution.py:204
  41.9 0.3 collective-permute-done.13.refs_9_
  42.2 2.6 %project.3 = (bf16[3,384,128]{2,1,0:T(8,128)(2,1)S(1)}, bf16[3,384,128]{2,1,0:T(8,128)(2,1)S(1)}) custom-call(s32[3]{0:T(128)S(1)} %pad_add_fusion.where_ref, bf16[384,2048]{1,0:T(8,128)(2,1)S(1)} %normalize.1.x_ref, f32[384,128]{1,0:T(8,128)S(1)} %get-tuple-element.30.cos_ref, f32[384,128]{1,0:T(8,128)S(1)} %get-tuple-element.31.sin_ref, ...), custom_call_target="tpu_custom_call" | custom-call | flops 1207959552 | bytes 8388608 | tf_op jit(solution)/shard_map/project/pallas_call | solution.py:246
  44.8 1.6 %collective-permute-start.14 = (bf16[3,384,128]{2,1,0:T(8,128)(2,1)S(1)}, bf16[3,384,128]{2,1,0:T(8,128)(2,1)S(1)}, u32[]{:S(2)}, u32[]{:S(2)}) collective-permute-start(bf16[3,384,128]{2,1,0:T(8,128)(2,1)S(1)} %get-tuple-element.35), channel_id=1, source_target_pairs={{0,8},{4,12},{8,0},{12,4},{16,24},{20,28},{24,16},{28,20},{1,9},{5... | collective-permute-start | bytes 884744 | tf_op jit(solution)/shard_map/ppermute | solution.py:117
  46.4 1.5 %collective-permute-start.15 = (bf16[3,384,128]{2,1,0:T(8,128)(2,1)S(1)}, bf16[3,384,128]{2,1,0:T(8,128)(2,1)S(1)}, u32[]{:S(2)}, u32[]{:S(2)}) collective-permute-start(bf16[3,384,128]{2,1,0:T(8,128)(2,1)S(1)} %get-tuple-element.36), channel_id=1, source_target_pairs={{0,16},{4,20},{8,24},{12,28},{16,0},{20,4},{24,8},{28,12},{1,17},{... | collective-permute-start | bytes 884744 | tf_op jit(solution)/shard_map/ppermute | solution.py:117
  47.9 2.6 %project.2 = (bf16[3,384,128]{2,1,0:T(8,128)(2,1)S(1)}, bf16[3,384,128]{2,1,0:T(8,128)(2,1)S(1)}) custom-call(s32[3]{0:T(128)S(1)} %pad_add_fusion.where_ref, bf16[384,2048]{1,0:T(8,128)(2,1)S(1)} %normalize.1.x_ref, f32[384,128]{1,0:T(8,128)S(1)} %get-tuple-element.30.cos_ref, f32[384,128]{1,0:T(8,128)S(1)} %get-tuple-element.31.sin_ref, ...), custom_call_target="tpu_custom_call" | custom-call | flops 1207959552 | bytes 8388608 | tf_op jit(solution)/shard_map/project/pallas_call | solution.py:246
  50.5 0.5 collective-permute-start.16
  51.0 3.7 %collective-permute-done.14.refs_1_ = bf16[3,384,128]{2,1,0:T(8,128)(2,1)S(1)} collective-permute-done((bf16[3,384,128]{2,1,0:T(8,128)(2,1)S(1)}, bf16[3,384,128]{2,1,0:T(8,128)(2,1)S(1)}, u32[]{:S(2)}, u32[]{:S(2)}) %collective-permute-start.14) | collective-permute-done | bytes 294944 | tf_op jit(solution)/shard_map/ppermute | solution.py:117
  54.7 6.7 %collective-permute-done.15.refs_2_ = bf16[3,384,128]{2,1,0:T(8,128)(2,1)S(1)} collective-permute-done((bf16[3,384,128]{2,1,0:T(8,128)(2,1)S(1)}, bf16[3,384,128]{2,1,0:T(8,128)(2,1)S(1)}, u32[]{:S(2)}, u32[]{:S(2)}) %collective-permute-start.15) | collective-permute-done | bytes 294944 | tf_op jit(solution)/shard_map/ppermute | solution.py:117
  61.5 0.5 collective-permute-start.20
  62.0 1.1 collective-permute-done.19.refs_6_
  63.0 0.4 collective-permute-done.20.refs_7_
  63.5 8.2 %attend.1 = (bf16[384,128]{1,0:T(8,128)(2,1)S(1)}, bf16[384,128]{1,0:T(8,128)(2,1)S(1)}, bf16[384,128]{1,0:T(8,128)(2,1)S(1)}, bf16[384,128]{1,0:T(8,128)(2,1)S(1)}) custom-call(s32[3]{0:T(128)S(1)} %pad_add_fusion.where_ref, s32[6]{0:T(128)S(1)} %bitcast_subtract_fusion.start_ref, bf16[3,384,128]{2,1,0:T(8,128)(2,1)S(1)} %get-tuple-element.34.refs_0_, ...), custom_call_target="tpu_custom_call" | custom-call | flops 2415919104 | bytes 8388608 | tf_op jit(solution)/shard_map/attend/pallas_call | solution.py:313
  71.7 1.6 %collective-permute-start.21 = (bf16[384,128]{1,0:T(8,128)(2,1)S(1)}, bf16[384,128]{1,0:T(8,128)(2,1)S(1)}, u32[]{:S(2)}, u32[]{:S(2)}) collective-permute-start(bf16[384,128]{1,0:T(8,128)(2,1)S(1)} %get-tuple-element.38), channel_id=1, source_target_pairs={{0,24},{4,28},{8,16},{12,20},{16,8},{20,12},{24,0},{28,4},{1,25},{... | collective-permute-start | bytes 294920 | tf_op jit(solution)/shard_map/ppermute | solution.py:117
  73.3 0.8 collective-permute-start.22
  74.0 1.2 %collective-permute-start.23 = (bf16[384,128]{1,0:T(8,128)(2,1)S(1)}, bf16[384,128]{1,0:T(8,128)(2,1)S(1)}, u32[]{:S(2)}, u32[]{:S(2)}) collective-permute-start(bf16[384,128]{1,0:T(8,128)(2,1)S(1)} %get-tuple-element.40), channel_id=1, source_target_pairs={{0,8},{4,12},{8,0},{12,4},{16,24},{20,28},{24,16},{28,20},{1,9},{5... | collective-permute-start | bytes 294920 | tf_op jit(solution)/shard_map/ppermute | solution.py:117
  75.2 2.6 %collective-permute-done.21 = bf16[384,128]{1,0:T(8,128)(2,1)S(1)} collective-permute-done((bf16[384,128]{1,0:T(8,128)(2,1)S(1)}, bf16[384,128]{1,0:T(8,128)(2,1)S(1)}, u32[]{:S(2)}, u32[]{:S(2)}) %collective-permute-start.21) | collective-permute-done | bytes 98336 | tf_op jit(solution)/shard_map/ppermute | solution.py:117
  77.8 0.8 collective-permute-done.22
  78.6 0.0 collective-permute-done.23
  78.7 0.1 broadcast_select_fusion.5
  78.8 1.9 %collective-permute-start.24 = (bf16[384,512]{1,0:T(8,128)(2,1)S(1)}, bf16[384,512]{1,0:T(8,128)(2,1)S(1)}, u32[]{:S(2)}, u32[]{:S(2)}) collective-permute-start(bf16[384,512]{1,0:T(8,128)(2,1)S(1)} %pad_maximum_fusion.own), channel_id=1, source_target_pairs={{0,1},{1,0},{2,3},{3,2},{4,5},{5,4},{6,7},{7,6},{8,9},{9,8},{10,11... | collective-permute-start | bytes 1179656 | tf_op jit(solution)/shard_map/ppermute | solution.py:121
  80.7 0.8 collective-permute-start.28
  81.5 1.2 %collective-permute-start.29 = (bf16[256,512]{1,0:T(8,128)(2,1)S(1)}, bf16[256,512]{1,0:T(8,128)(2,1)S(1)}, u32[]{:S(2)}, u32[]{:S(2)}) collective-permute-start(bf16[256,512]{1,0:T(8,128)(2,1)S(1)} %copy-done.1), channel_id=1, source_target_pairs={{0,16},{4,20},{8,24},{12,28},{16,0},{20,4},{24,8},{28,12},{1,17},{... | collective-permute-start | bytes 786440 | tf_op jit(solution)/shard_map/ppermute | solution.py:117
  82.7 0.7 collective-permute-start.27
  83.4 0.1 collective-permute-start.33
  83.5 4.4 %collective-permute-done.24.near = bf16[384,512]{1,0:T(8,128)(2,1)S(1)} collective-permute-done((bf16[384,512]{1,0:T(8,128)(2,1)S(1)}, bf16[384,512]{1,0:T(8,128)(2,1)S(1)}, u32[]{:S(2)}, u32[]{:S(2)}) %collective-permute-start.24) | collective-permute-done | bytes 393248 | tf_op jit(solution)/shard_map/ppermute | solution.py:121
  87.9 0.7 collective-permute-start.25
  88.6 0.1 collective-permute-start.34
  88.8 1.3 %collective-permute-start.30 = (bf16[384,512]{1,0:T(8,128)(2,1)S(1)}, bf16[384,512]{1,0:T(8,128)(2,1)S(1)}, u32[]{:S(2)}, u32[]{:S(2)}) collective-permute-start(bf16[384,512]{1,0:T(8,128)(2,1)S(1)} %collective-permute-done.27.q1), channel_id=1, source_target_pairs={{1,0},{2,3},{5,4},{6,7},{9,8},{10,11},{13,12},{14,15},{17,16},{18,... | collective-permute-start | bytes 1179656 | tf_op jit(solution)/shard_map/ppermute | solution.py:129
  90.1 1.2 %collective-permute-start.31 = (bf16[128,512]{1,0:T(8,128)(2,1)S(1)}, bf16[128,512]{1,0:T(8,128)(2,1)S(1)}, u32[]{:S(2)}, u32[]{:S(2)}) collective-permute-start(bf16[128,512]{1,0:T(8,128)(2,1)S(1)} %get-tuple-element.47), channel_id=1, source_target_pairs={{0,8},{4,12},{8,0},{12,4},{16,24},{20,28},{24,16},{28,20},{1,9},{5... | collective-permute-start | bytes 393224 | tf_op jit(solution)/shard_map/ppermute | solution.py:117
  91.3 2.0 %collective-permute-start.32 = (bf16[128,512]{1,0:T(8,128)(2,1)S(1)}, bf16[128,512]{1,0:T(8,128)(2,1)S(1)}, u32[]{:S(2)}, u32[]{:S(2)}) collective-permute-start(bf16[128,512]{1,0:T(8,128)(2,1)S(1)} %get-tuple-element.48), channel_id=1, source_target_pairs={{0,16},{4,20},{8,24},{12,28},{16,0},{20,4},{24,8},{28,12},{1,17},{... | collective-permute-start | bytes 393224 | tf_op jit(solution)/shard_map/ppermute | solution.py:117
  93.4 0.1 collective-permute-start.35
  93.5 1.3 %collective-permute-start.26 = (bf16[384,512]{1,0:T(8,128)(2,1)S(1)}, bf16[384,512]{1,0:T(8,128)(2,1)S(1)}, u32[]{:S(2)}, u32[]{:S(2)}) collective-permute-start(bf16[384,512]{1,0:T(8,128)(2,1)S(1)} %collective-permute-done.25.q2), channel_id=1, source_target_pairs={{1,0},{2,3},{5,4},{6,7},{9,8},{10,11},{13,12},{14,15},{17,16},{18,... | collective-permute-start | bytes 1179656 | tf_op jit(solution)/shard_map/ppermute | solution.py:129
  94.8 1.2 %collective-permute-done.31.refs_3_ = bf16[128,512]{1,0:T(8,128)(2,1)S(1)} collective-permute-done((bf16[128,512]{1,0:T(8,128)(2,1)S(1)}, bf16[128,512]{1,0:T(8,128)(2,1)S(1)}, u32[]{:S(2)}, u32[]{:S(2)}) %collective-permute-start.31) | collective-permute-done | bytes 131104 | tf_op jit(solution)/shard_map/ppermute | solution.py:117
  96.1 1.1 %collective-permute-done.32.refs_4_ = bf16[128,512]{1,0:T(8,128)(2,1)S(1)} collective-permute-done((bf16[128,512]{1,0:T(8,128)(2,1)S(1)}, bf16[128,512]{1,0:T(8,128)(2,1)S(1)}, u32[]{:S(2)}, u32[]{:S(2)}) %collective-permute-start.32) | collective-permute-done | bytes 131104 | tf_op jit(solution)/shard_map/ppermute | solution.py:117
  97.3 1.1 copy.11
  98.4 1.1 copy.10
  99.4 6.7 %collective-permute-done.30.p2 = bf16[384,512]{1,0:T(8,128)(2,1)S(1)} collective-permute-done((bf16[384,512]{1,0:T(8,128)(2,1)S(1)}, bf16[384,512]{1,0:T(8,128)(2,1)S(1)}, u32[]{:S(2)}, u32[]{:S(2)}) %collective-permute-start.30) | collective-permute-done | bytes 393248 | tf_op jit(solution)/shard_map/ppermute | solution.py:129
  106.1 1.5 %early.1 = (f32[384,512]{1,0:T(8,128)S(1)}, bf16[512,512]{1,0:T(8,128)(2,1)S(1)}) custom-call(s32[3]{0:T(128)S(1)} %pad_add_fusion.where_ref, bf16[384,512]{1,0:T(8,128)(2,1)S(1)} %pad_maximum_fusion.own, bf16[384,512]{1,0:T(8,128)(2,1)S(1)} %collective-permute-done.24.near, bf16[384,512]{1,0:T(8,128)(2,1)S(1)} %collective-permute-done.27.q1, ...), custom_call_target="tpu_custom_call" | custom-call | flops 1073741824 | bytes 8388608 | tf_op jit(solution)/shard_map/early/pallas_call | solution.py:353
  107.6 4.9 %collective-permute-done.26.p3 = bf16[384,512]{1,0:T(8,128)(2,1)S(1)} collective-permute-done((bf16[384,512]{1,0:T(8,128)(2,1)S(1)}, bf16[384,512]{1,0:T(8,128)(2,1)S(1)}, u32[]{:S(2)}, u32[]{:S(2)}) %collective-permute-start.26) | collective-permute-done | bytes 393248 | tf_op jit(solution)/shard_map/ppermute | solution.py:129
  112.5 1.7 %last.1 = bf16[384,512]{1,0:T(8,128)(2,1)} custom-call(s32[3]{0:T(128)S(1)} %pad_add_fusion.where_ref, bf16[384,512]{1,0:T(8,128)(2,1)S(1)} %collective-permute-done.25.q2, bf16[384,512]{1,0:T(8,128)(2,1)S(1)} %collective-permute-done.26.p3, f32[384,512]{1,0:T(8,128)S(1)} %get-tuple-element.49.total_ref, bf16[512,512]{1,0:T(8,128)(2,1)S(1)} %get-tuple-element.50.w_ref), custom_call_target="tpu_custom_call" | custom-call | flops 201326592 | bytes 8388608 | tf_op jit(solution)/shard_map/last/pallas_call | solution.py:376
  (50 shorter events, 0.4 us)
Async XLA Ops:
  0.6 8.5 %copy-start.3 = (s32[6]{0:T(128)S(1)}, s32[6]{0:T(128)}, u32[]{:S(2)}) copy-start(s32[6]{0:T(128)} %param.9) | copy-start | bytes 76
  0.6 12.4 %collective-permute-start = (bf16[384,512]{1,0:T(8,128)(2,1)}, bf16[384,512]{1,0:T(8,128)(2,1)S(1)}, u32[]{:S(2)}, u32[]{:S(2)}) collective-permute-start(bf16[384,512]{1,0:T(8,128)(2,1)} %refs_0_.1), channel_id=1, source_target_pairs={{0,1},{1,0},{2,3},{3,2},{4,5},{5,4},{6,7},{7,6},{8,9},{9,8},{10,11... | collective-permute-start | bytes 1179656 | tf_op jit(solution)/shard_map/ppermute | solution.py:121
  3.7 9.3 %collective-permute-start.1 = (bf16[384,512]{1,0:T(8,128)(2,1)}, bf16[384,512]{1,0:T(8,128)(2,1)S(1)}, u32[]{:S(2)}, u32[]{:S(2)}) collective-permute-start(bf16[384,512]{1,0:T(8,128)(2,1)} %refs_0_.1), channel_id=1, source_target_pairs={{1,2},{2,1},{5,6},{6,5},{9,10},{10,9},{13,14},{14,13},{17,18},{18,... | collective-permute-start | bytes 1179656 | tf_op jit(solution)/shard_map/ppermute | solution.py:125
  6.1 19.1 %collective-permute-start.5 = (bf16[256,1536]{1,0:T(8,128)(2,1)S(1)}, bf16[256,1536]{1,0:T(8,128)(2,1)S(1)}, u32[]{:S(2)}, u32[]{:S(2)}) collective-permute-start(bf16[256,1536]{1,0:T(8,128)(2,1)S(1)} %reshape.193.refs_0_), channel_id=1, source_target_pairs={{0,8},{4,12},{8,0},{12,4},{16,24},{20,28},{24,16},{28,20},{1,9},{5... | collective-permute-start | bytes 2359304 | tf_op jit(solution)/shard_map/ppermute | solution.py:117
  7.6 18.7 %collective-permute-start.6 = (bf16[256,1536]{1,0:T(8,128)(2,1)S(1)}, bf16[256,1536]{1,0:T(8,128)(2,1)S(1)}, u32[]{:S(2)}, u32[]{:S(2)}) collective-permute-start(bf16[256,1536]{1,0:T(8,128)(2,1)S(1)} %reshape.193.refs_0_), channel_id=1, source_target_pairs={{0,16},{4,20},{8,24},{12,28},{16,0},{20,4},{24,8},{28,12},{1,17},{... | collective-permute-start | bytes 2359304 | tf_op jit(solution)/shard_map/ppermute | solution.py:117
  9.6 29.8 %copy-start = (bf16[384,512]{1,0:T(8,128)(2,1)S(1)}, bf16[384,512]{1,0:T(8,128)(2,1)}, u32[]{:S(2)}) copy-start(bf16[384,512]{1,0:T(8,128)(2,1)} %refs_0_.1) | copy-start | bytes 1179652
  9.6 29.8 %copy-start.2 = (f32[2048]{0:T(1024)S(1)}, f32[2048]{0:T(1024)}, u32[]{:S(2)}) copy-start(f32[2048]{0:T(1024)} %param.6) | copy-start | bytes 24580
  13.1 2.0 %collective-permute-start.3 = (bf16[384,512]{1,0:T(8,128)(2,1)S(1)}, bf16[384,512]{1,0:T(8,128)(2,1)S(1)}, u32[]{:S(2)}, u32[]{:S(2)}) collective-permute-start(bf16[384,512]{1,0:T(8,128)(2,1)S(1)} %collective-permute-done.refs_1_), channel_id=1, source_target_pairs={{1,2},{2,1},{5,6},{6,5},{9,10},{10,9},{13,14},{14,13},{17,18},{18,... | collective-permute-start | bytes 1179656 | tf_op jit(solution)/shard_map/ppermute | solution.py:125
  13.7 17.1 %collective-permute-start.2 = (bf16[384,512]{1,0:T(8,128)(2,1)S(1)}, bf16[384,512]{1,0:T(8,128)(2,1)S(1)}, u32[]{:S(2)}, u32[]{:S(2)}) collective-permute-start(bf16[384,512]{1,0:T(8,128)(2,1)S(1)} %collective-permute-done.1.refs_2_), channel_id=1, source_target_pairs={{1,0},{2,3},{5,4},{6,7},{9,8},{10,11},{13,12},{14,15},{17,16},{18,... | collective-permute-start | bytes 1179656 | tf_op jit(solution)/shard_map/ppermute | solution.py:129
  15.1 23.7 %collective-permute-start.4 = (bf16[384,512]{1,0:T(8,128)(2,1)S(1)}, bf16[384,512]{1,0:T(8,128)(2,1)S(1)}, u32[]{:S(2)}, u32[]{:S(2)}) collective-permute-start(bf16[384,512]{1,0:T(8,128)(2,1)S(1)} %collective-permute-done.3.refs_4_), channel_id=1, source_target_pairs={{1,0},{2,3},{5,4},{6,7},{9,8},{10,11},{13,12},{14,15},{17,16},{18,... | collective-permute-start | bytes 1179656 | tf_op jit(solution)/shard_map/ppermute | solution.py:129
  26.4 12.4 %collective-permute-start.7 = (bf16[128,1536]{1,0:T(8,128)(2,1)S(1)}, bf16[128,1536]{1,0:T(8,128)(2,1)S(1)}, u32[]{:S(2)}, u32[]{:S(2)}) collective-permute-start(bf16[128,1536]{1,0:T(8,128)(2,1)S(1)} %get-tuple-element.32), channel_id=1, source_target_pairs={{0,8},{4,12},{8,0},{12,4},{16,24},{20,28},{24,16},{28,20},{1,9},{5... | collective-permute-start | bytes 1179656 | tf_op jit(solution)/shard_map/ppermute | solution.py:117
  27.0 12.3 %collective-permute-start.8 = (bf16[128,1536]{1,0:T(8,128)(2,1)S(1)}, bf16[128,1536]{1,0:T(8,128)(2,1)S(1)}, u32[]{:S(2)}, u32[]{:S(2)}) collective-permute-start(bf16[128,1536]{1,0:T(8,128)(2,1)S(1)} %get-tuple-element.33), channel_id=1, source_target_pairs={{0,16},{4,20},{8,24},{12,28},{16,0},{20,4},{24,8},{28,12},{1,17},{... | collective-permute-start | bytes 1179656 | tf_op jit(solution)/shard_map/ppermute | solution.py:117
  28.5 13.3 %collective-permute-start.9 = (bf16[256,1536]{1,0:T(8,128)(2,1)S(1)}, bf16[256,1536]{1,0:T(8,128)(2,1)S(1)}, u32[]{:S(2)}, u32[]{:S(2)}) collective-permute-start(bf16[256,1536]{1,0:T(8,128)(2,1)S(1)} %reshape.193.refs_0_), channel_id=1, source_target_pairs={{0,4},{4,0},{8,12},{12,8},{16,20},{20,16},{24,28},{28,24},{1,5},{5... | collective-permute-start | bytes 2359304 | tf_op jit(solution)/shard_map/ppermute | solution.py:117
  30.8 11.4 %collective-permute-start.10 = (bf16[256,1536]{1,0:T(8,128)(2,1)S(1)}, bf16[256,1536]{1,0:T(8,128)(2,1)S(1)}, u32[]{:S(2)}, u32[]{:S(2)}) collective-permute-start(bf16[256,1536]{1,0:T(8,128)(2,1)S(1)} %collective-permute-done.5.x_ref.refs_1_), channel_id=1, source_target_pairs={{0,4},{4,0},{8,12},{12,8},{16,20},{20,16},{24,28},{28,24},{1,5},{5... | collective-permute-start | bytes 2359304 | tf_op jit(solution)/shard_map/ppermute | solution.py:117
  38.8 3.4 %collective-permute-start.11 = (bf16[256,1536]{1,0:T(8,128)(2,1)S(1)}, bf16[256,1536]{1,0:T(8,128)(2,1)S(1)}, u32[]{:S(2)}, u32[]{:S(2)}) collective-permute-start(bf16[256,1536]{1,0:T(8,128)(2,1)S(1)} %collective-permute-done.6.y_ref.refs_2_), channel_id=1, source_target_pairs={{0,4},{4,0},{8,12},{12,8},{16,20},{20,16},{24,28},{28,24},{1,5},{5... | collective-permute-start | bytes 2359304 | tf_op jit(solution)/shard_map/ppermute | solution.py:117
  38.8 3.1 %collective-permute-start.12 = (bf16[128,1536]{1,0:T(8,128)(2,1)S(1)}, bf16[128,1536]{1,0:T(8,128)(2,1)S(1)}, u32[]{:S(2)}, u32[]{:S(2)}) collective-permute-start(bf16[128,1536]{1,0:T(8,128)(2,1)S(1)} %collective-permute-done.7.refs_3_), channel_id=1, source_target_pairs={{0,4},{4,0},{8,12},{12,8},{16,20},{20,16},{24,28},{28,24},{1,5},{5... | collective-permute-start | bytes 1179656 | tf_op jit(solution)/shard_map/ppermute | solution.py:117
  39.3 2.9 %collective-permute-start.13 = (bf16[128,1536]{1,0:T(8,128)(2,1)S(1)}, bf16[128,1536]{1,0:T(8,128)(2,1)S(1)}, u32[]{:S(2)}, u32[]{:S(2)}) collective-permute-start(bf16[128,1536]{1,0:T(8,128)(2,1)S(1)} %collective-permute-done.8.refs_4_), channel_id=1, source_target_pairs={{0,4},{4,0},{8,12},{12,8},{16,20},{20,16},{24,28},{28,24},{1,5},{5... | collective-permute-start | bytes 1179656 | tf_op jit(solution)/shard_map/ppermute | solution.py:117
  44.8 9.9 %collective-permute-start.14 = (bf16[3,384,128]{2,1,0:T(8,128)(2,1)S(1)}, bf16[3,384,128]{2,1,0:T(8,128)(2,1)S(1)}, u32[]{:S(2)}, u32[]{:S(2)}) collective-permute-start(bf16[3,384,128]{2,1,0:T(8,128)(2,1)S(1)} %get-tuple-element.35), channel_id=1, source_target_pairs={{0,8},{4,12},{8,0},{12,4},{16,24},{20,28},{24,16},{28,20},{1,9},{5... | collective-permute-start | bytes 884744 | tf_op jit(solution)/shard_map/ppermute | solution.py:117
  46.4 15.1 %collective-permute-start.15 = (bf16[3,384,128]{2,1,0:T(8,128)(2,1)S(1)}, bf16[3,384,128]{2,1,0:T(8,128)(2,1)S(1)}, u32[]{:S(2)}, u32[]{:S(2)}) collective-permute-start(bf16[3,384,128]{2,1,0:T(8,128)(2,1)S(1)} %get-tuple-element.36), channel_id=1, source_target_pairs={{0,16},{4,20},{8,24},{12,28},{16,0},{20,4},{24,8},{28,12},{1,17},{... | collective-permute-start | bytes 884744 | tf_op jit(solution)/shard_map/ppermute | solution.py:117
  50.5 11.0 %collective-permute-start.16 = (bf16[3,384,128]{2,1,0:T(8,128)(2,1)S(1)}, bf16[3,384,128]{2,1,0:T(8,128)(2,1)S(1)}, u32[]{:S(2)}, u32[]{:S(2)}) collective-permute-start(bf16[3,384,128]{2,1,0:T(8,128)(2,1)S(1)} %get-tuple-element.37), channel_id=1, source_target_pairs={{0,24},{4,28},{8,16},{12,20},{16,8},{20,12},{24,0},{28,4},{1,25},{... | collective-permute-start | bytes 884744 | tf_op jit(solution)/shard_map/ppermute | solution.py:117
  51.0 11.0 %collective-permute-start.17 = (bf16[3,384,128]{2,1,0:T(8,128)(2,1)S(1)}, bf16[3,384,128]{2,1,0:T(8,128)(2,1)S(1)}, u32[]{:S(2)}, u32[]{:S(2)}) collective-permute-start(bf16[3,384,128]{2,1,0:T(8,128)(2,1)S(1)} %get-tuple-element.34.refs_0_), channel_id=1, source_target_pairs={{0,4},{4,0},{8,12},{12,8},{16,20},{20,16},{24,28},{28,24},{1,5},{5... | collective-permute-start | bytes 884744 | tf_op jit(solution)/shard_map/ppermute | solution.py:117
  54.7 7.3 %collective-permute-start.18 = (bf16[3,384,128]{2,1,0:T(8,128)(2,1)S(1)}, bf16[3,384,128]{2,1,0:T(8,128)(2,1)S(1)}, u32[]{:S(2)}, u32[]{:S(2)}) collective-permute-start(bf16[3,384,128]{2,1,0:T(8,128)(2,1)S(1)} %collective-permute-done.14.refs_1_), channel_id=1, source_target_pairs={{0,4},{4,0},{8,12},{12,8},{16,20},{20,16},{24,28},{28,24},{1,5},{5... | collective-permute-start | bytes 884744 | tf_op jit(solution)/shard_map/ppermute | solution.py:117
  61.5 1.6 %collective-permute-start.19 = (bf16[3,384,128]{2,1,0:T(8,128)(2,1)S(1)}, bf16[3,384,128]{2,1,0:T(8,128)(2,1)S(1)}, u32[]{:S(2)}, u32[]{:S(2)}) collective-permute-start(bf16[3,384,128]{2,1,0:T(8,128)(2,1)S(1)} %collective-permute-done.15.refs_2_), channel_id=1, source_target_pairs={{0,4},{4,0},{8,12},{12,8},{16,20},{20,16},{24,28},{28,24},{1,5},{5... | collective-permute-start | bytes 884744 | tf_op jit(solution)/shard_map/ppermute | solution.py:117
  61.5 2.0 %collective-permute-start.20 = (bf16[3,384,128]{2,1,0:T(8,128)(2,1)S(1)}, bf16[3,384,128]{2,1,0:T(8,128)(2,1)S(1)}, u32[]{:S(2)}, u32[]{:S(2)}) collective-permute-start(bf16[3,384,128]{2,1,0:T(8,128)(2,1)S(1)} %collective-permute-done.16.refs_3_), channel_id=1, source_target_pairs={{0,4},{4,0},{8,12},{12,8},{16,20},{20,16},{24,28},{28,24},{1,5},{5... | collective-permute-start | bytes 884744 | tf_op jit(solution)/shard_map/ppermute | solution.py:117
  71.7 9.0 %copy-start.1 = (bf16[256,512]{1,0:T(8,128)(2,1)S(1)}, bf16[256,512]{1,0:T(8,128)(2,1)}, u32[]{:S(2)}) copy-start(bf16[256,512]{1,0:T(8,128)(2,1)} %refs_0_.2) | copy-start | bytes 786436
  71.7 6.1 %collective-permute-start.21 = (bf16[384,128]{1,0:T(8,128)(2,1)S(1)}, bf16[384,128]{1,0:T(8,128)(2,1)S(1)}, u32[]{:S(2)}, u32[]{:S(2)}) collective-permute-start(bf16[384,128]{1,0:T(8,128)(2,1)S(1)} %get-tuple-element.38), channel_id=1, source_target_pairs={{0,24},{4,28},{8,16},{12,20},{16,8},{20,12},{24,0},{28,4},{1,25},{... | collective-permute-start | bytes 294920 | tf_op jit(solution)/shard_map/ppermute | solution.py:117
  73.3 5.3 %collective-permute-start.22 = (bf16[384,128]{1,0:T(8,128)(2,1)S(1)}, bf16[384,128]{1,0:T(8,128)(2,1)S(1)}, u32[]{:S(2)}, u32[]{:S(2)}) collective-permute-start(bf16[384,128]{1,0:T(8,128)(2,1)S(1)} %get-tuple-element.39), channel_id=1, source_target_pairs={{0,16},{4,20},{8,24},{12,28},{16,0},{20,4},{24,8},{28,12},{1,17},{... | collective-permute-start | bytes 294920 | tf_op jit(solution)/shard_map/ppermute | solution.py:117
  74.0 4.6 %collective-permute-start.23 = (bf16[384,128]{1,0:T(8,128)(2,1)S(1)}, bf16[384,128]{1,0:T(8,128)(2,1)S(1)}, u32[]{:S(2)}, u32[]{:S(2)}) collective-permute-start(bf16[384,128]{1,0:T(8,128)(2,1)S(1)} %get-tuple-element.40), channel_id=1, source_target_pairs={{0,8},{4,12},{8,0},{12,4},{16,24},{20,28},{24,16},{28,20},{1,9},{5... | collective-permute-start | bytes 294920 | tf_op jit(solution)/shard_map/ppermute | solution.py:117
  78.8 9.1 %collective-permute-start.24 = (bf16[384,512]{1,0:T(8,128)(2,1)S(1)}, bf16[384,512]{1,0:T(8,128)(2,1)S(1)}, u32[]{:S(2)}, u32[]{:S(2)}) collective-permute-start(bf16[384,512]{1,0:T(8,128)(2,1)S(1)} %pad_maximum_fusion.own), channel_id=1, source_target_pairs={{0,1},{1,0},{2,3},{3,2},{4,5},{5,4},{6,7},{7,6},{8,9},{9,8},{10,11... | collective-permute-start | bytes 1179656 | tf_op jit(solution)/shard_map/ppermute | solution.py:121
  80.7 7.9 %collective-permute-start.28 = (bf16[256,512]{1,0:T(8,128)(2,1)S(1)}, bf16[256,512]{1,0:T(8,128)(2,1)S(1)}, u32[]{:S(2)}, u32[]{:S(2)}) collective-permute-start(bf16[256,512]{1,0:T(8,128)(2,1)S(1)} %copy-done.1), channel_id=1, source_target_pairs={{0,8},{4,12},{8,0},{12,4},{16,24},{20,28},{24,16},{28,20},{1,9},{5... | collective-permute-start | bytes 786440 | tf_op jit(solution)/shard_map/ppermute | solution.py:117
  81.5 7.3 %collective-permute-start.29 = (bf16[256,512]{1,0:T(8,128)(2,1)S(1)}, bf16[256,512]{1,0:T(8,128)(2,1)S(1)}, u32[]{:S(2)}, u32[]{:S(2)}) collective-permute-start(bf16[256,512]{1,0:T(8,128)(2,1)S(1)} %copy-done.1), channel_id=1, source_target_pairs={{0,16},{4,20},{8,24},{12,28},{16,0},{20,4},{24,8},{28,12},{1,17},{... | collective-permute-start | bytes 786440 | tf_op jit(solution)/shard_map/ppermute | solution.py:117
  82.7 6.1 %collective-permute-start.27 = (bf16[384,512]{1,0:T(8,128)(2,1)S(1)}, bf16[384,512]{1,0:T(8,128)(2,1)S(1)}, u32[]{:S(2)}, u32[]{:S(2)}) collective-permute-start(bf16[384,512]{1,0:T(8,128)(2,1)S(1)} %pad_maximum_fusion.own), channel_id=1, source_target_pairs={{1,2},{2,1},{5,6},{6,5},{9,10},{10,9},{13,14},{14,13},{17,18},{18,... | collective-permute-start | bytes 1179656 | tf_op jit(solution)/shard_map/ppermute | solution.py:125
  83.4 7.9 %collective-permute-start.33 = (bf16[256,512]{1,0:T(8,128)(2,1)S(1)}, bf16[256,512]{1,0:T(8,128)(2,1)S(1)}, u32[]{:S(2)}, u32[]{:S(2)}) collective-permute-start(bf16[256,512]{1,0:T(8,128)(2,1)S(1)} %copy-done.1), channel_id=1, source_target_pairs={{0,4},{4,0},{8,12},{12,8},{16,20},{20,16},{24,28},{28,24},{1,5},{5... | collective-permute-start | bytes 786440 | tf_op jit(solution)/shard_map/ppermute | solution.py:117
  87.9 5.6 %collective-permute-start.25 = (bf16[384,512]{1,0:T(8,128)(2,1)S(1)}, bf16[384,512]{1,0:T(8,128)(2,1)S(1)}, u32[]{:S(2)}, u32[]{:S(2)}) collective-permute-start(bf16[384,512]{1,0:T(8,128)(2,1)S(1)} %collective-permute-done.24.near), channel_id=1, source_target_pairs={{1,2},{2,1},{5,6},{6,5},{9,10},{10,9},{13,14},{14,13},{17,18},{18,... | collective-permute-start | bytes 1179656 | tf_op jit(solution)/shard_map/ppermute | solution.py:125
  88.6 4.7 %collective-permute-start.34 = (bf16[256,512]{1,0:T(8,128)(2,1)S(1)}, bf16[256,512]{1,0:T(8,128)(2,1)S(1)}, u32[]{:S(2)}, u32[]{:S(2)}) collective-permute-start(bf16[256,512]{1,0:T(8,128)(2,1)S(1)} %collective-permute-done.28.x_ref.refs_1_), channel_id=1, source_target_pairs={{0,4},{4,0},{8,12},{12,8},{16,20},{20,16},{24,28},{28,24},{1,5},{5... | collective-permute-start | bytes 786440 | tf_op jit(solution)/shard_map/ppermute | solution.py:117
  88.8 17.3 %collective-permute-start.30 = (bf16[384,512]{1,0:T(8,128)(2,1)S(1)}, bf16[384,512]{1,0:T(8,128)(2,1)S(1)}, u32[]{:S(2)}, u32[]{:S(2)}) collective-permute-start(bf16[384,512]{1,0:T(8,128)(2,1)S(1)} %collective-permute-done.27.q1), channel_id=1, source_target_pairs={{1,0},{2,3},{5,4},{6,7},{9,8},{10,11},{13,12},{14,15},{17,16},{18,... | collective-permute-start | bytes 1179656 | tf_op jit(solution)/shard_map/ppermute | solution.py:129
  90.1 6.0 %collective-permute-start.31 = (bf16[128,512]{1,0:T(8,128)(2,1)S(1)}, bf16[128,512]{1,0:T(8,128)(2,1)S(1)}, u32[]{:S(2)}, u32[]{:S(2)}) collective-permute-start(bf16[128,512]{1,0:T(8,128)(2,1)S(1)} %get-tuple-element.47), channel_id=1, source_target_pairs={{0,8},{4,12},{8,0},{12,4},{16,24},{20,28},{24,16},{28,20},{1,9},{5... | collective-permute-start | bytes 393224 | tf_op jit(solution)/shard_map/ppermute | solution.py:117
  91.3 5.9 %collective-permute-start.32 = (bf16[128,512]{1,0:T(8,128)(2,1)S(1)}, bf16[128,512]{1,0:T(8,128)(2,1)S(1)}, u32[]{:S(2)}, u32[]{:S(2)}) collective-permute-start(bf16[128,512]{1,0:T(8,128)(2,1)S(1)} %get-tuple-element.48), channel_id=1, source_target_pairs={{0,16},{4,20},{8,24},{12,28},{16,0},{20,4},{24,8},{28,12},{1,17},{... | collective-permute-start | bytes 393224 | tf_op jit(solution)/shard_map/ppermute | solution.py:117
  93.4 6.0 %collective-permute-start.35 = (bf16[256,512]{1,0:T(8,128)(2,1)S(1)}, bf16[256,512]{1,0:T(8,128)(2,1)S(1)}, u32[]{:S(2)}, u32[]{:S(2)}) collective-permute-start(bf16[256,512]{1,0:T(8,128)(2,1)S(1)} %collective-permute-done.29.y_ref.refs_2_), channel_id=1, source_target_pairs={{0,4},{4,0},{8,12},{12,8},{16,20},{20,16},{24,28},{28,24},{1,5},{5... | collective-permute-start | bytes 786440 | tf_op jit(solution)/shard_map/ppermute | solution.py:117
  93.5 19.0 %collective-permute-start.26 = (bf16[384,512]{1,0:T(8,128)(2,1)S(1)}, bf16[384,512]{1,0:T(8,128)(2,1)S(1)}, u32[]{:S(2)}, u32[]{:S(2)}) collective-permute-start(bf16[384,512]{1,0:T(8,128)(2,1)S(1)} %collective-permute-done.25.q2), channel_id=1, source_target_pairs={{1,0},{2,3},{5,4},{6,7},{9,8},{10,11},{13,12},{14,15},{17,16},{18,... | collective-permute-start | bytes 1179656 | tf_op jit(solution)/shard_map/ppermute | solution.py:129
  96.1 3.3 %collective-permute-start.36 = (bf16[128,512]{1,0:T(8,128)(2,1)S(1)}, bf16[128,512]{1,0:T(8,128)(2,1)S(1)}, u32[]{:S(2)}, u32[]{:S(2)}) collective-permute-start(bf16[128,512]{1,0:T(8,128)(2,1)S(1)} %collective-permute-done.31.refs_3_), channel_id=1, source_target_pairs={{0,4},{4,0},{8,12},{12,8},{16,20},{20,16},{24,28},{28,24},{1,5},{5... | collective-permute-start | bytes 393224 | tf_op jit(solution)/shard_map/ppermute | solution.py:117
  97.2 2.2 %collective-permute-start.37 = (bf16[128,512]{1,0:T(8,128)(2,1)S(1)}, bf16[128,512]{1,0:T(8,128)(2,1)S(1)}, u32[]{:S(2)}, u32[]{:S(2)}) collective-permute-start(bf16[128,512]{1,0:T(8,128)(2,1)S(1)} %collective-permute-done.32.refs_4_), channel_id=1, source_target_pairs={{0,4},{4,0},{8,12},{12,8},{16,20},{20,16},{24,28},{28,24},{1,5},{5... | collective-permute-start | bytes 393224 | tf_op jit(solution)/shard_map/ppermute | solution.py:117

commit v6 on v5

--- a/solution.py
+++ b/solution.py
@@ -174,17 +174,10 @@
 
 
 def normalize_kernel(where_ref, *refs):
-    blocks, (gain_ref, x_ref, raw_ref, sems) = refs[:6], refs[6:]
+    blocks, (gain_ref, x_ref) = refs[:6], refs[6:]
     chip, line = where_ref[0], where_ref[2]
-    wide = raw_ref.shape[2]
-    copies = [
-        pltpu.make_async_copy(block, raw_ref.at[n], sems.at[n]) for n, block in enumerate(blocks)
-    ]
-    for copy in copies:
-        copy.start()
-    for copy in copies:
-        copy.wait()
-    own, near, q1, p2, q2, p3 = [raw_ref[n] for n in range(6)]
+    wide = blocks[0].shape[1]
+    own, near, q1, p2, q2, p3 = [block[...] for block in blocks]
     second, third, fourth, end = order(line)
     raw = [
         own.astype(jnp.float32),
@@ -203,10 +196,9 @@
     rows, wide = blocks[0].shape
     return pl.pallas_call(
         normalize_kernel,
-        in_specs=[smem()] + [hbm()] * 6 + [vmem()],
+        in_specs=[smem()] + [vmem()] * 7,
         out_specs=vmem(),
         out_shape=jax.ShapeDtypeStruct((rows, LINE * wide), jnp.bfloat16),
-        scratch_shapes=[pltpu.VMEM((6, rows, wide), jnp.bfloat16), pltpu.SemaphoreType.DMA((6,))],
         compiler_params=pltpu.CompilerParams(vmem_limit_bytes=12 << 20),
         cost_estimate=effort(NORM_EFFORT),
         name="normalize",
@@ -411,7 +403,8 @@
     sine = jnp.concatenate([-sine, sine], axis=1)
 
     flat = w_qkv.reshape(depth, -1)
-    near, q1, cosine, sine, where = together(outer(tokens), inner(tokens), cosine, sine, where)
+    near, cosine, sine, where = together(outer(tokens), cosine, sine, where)
+    q1 = inner(tokens)
     q2, p2 = inner(near), outward(q1)
     w_x, w_y = swap(flat, 2), swap(flat, 4)
 

time: 116 us -> 113 us (0.974); the launches traced: 114 us -> 113 us
  Pallas kernels: 19 us -> 16 us
  waiting for transfers between devices: 56.9 us -> 58.7 us
    ppermute x4, waiting for transfers between devices: 21.8 us -> 18.3 us  [outward(): return lax.ppermute(x, 'gy', [(1, 0), (2, 3)])]
    ppermute x28, waiting for transfers between devices: 28.1 us -> 31.5 us  [swap(): return lax.ppermute(x, 'gx', [(i, i ^ mask) for i in range(2 * CHIPS)])]
    ppermute x2, waiting for transfers between devices: 6.94 us -> 8.95 us  [outer(): return lax.ppermute(x, 'gy', [(0, 1), (1, 0), (2, 3), (3, 2)])]
    pallas_call x1, Pallas kernels: 8.22 us -> 6.37 us  [attend(): pl.pallas_call(functools.partial(attend_kernel, scale=scale), in_specs=[s...]
    pallas_call x1, Pallas kernels: 2.44 us -> 1.27 us  [normalize(): pl.pallas_call(normalize_kernel, in_specs=[smem()] + [vmem()] * 7, out_sp...]
  transfers between devices with their start and end apart: 38 -> 38, of which waited for: 17 -> 17; matrix products, arithmetic and copies ran while one was open for 5% -> 5% of each run, Pallas kernels for 6% -> 5%
where the time goes in v6:
time: 113 us
  waiting for transfers between devices  58.7 us (52%)
  starting transfers between devices  31.8 us (28%)
  Pallas kernels  16 us (14%)
  local copies, waits for them, and re-layouts  3.79 us (3%)
  other arithmetic  1.68 us (1%)
    ppermute x28, waiting for transfers between devices, swap(): return lax.ppermute(x, 'gx', [(i, i ^ mask) for i in range(2 * CHIPS)])  31.5 us
    ppermute x28, starting transfers between devices, swap(): return lax.ppermute(x, 'gx', [(i, i ^ mask) for i in range(2 * CHIPS)])  18.9 us
    ppermute x4, waiting for transfers between devices, outward(): return lax.ppermute(x, 'gy', [(1, 0), (2, 3)])  18.3 us
    ppermute x2, waiting for transfers between devices, outer(): return lax.ppermute(x, 'gy', [(0, 1), (1, 0), (2, 3), (3, 2)])  8.95 us
    pallas_call x1, Pallas kernels, attend(): pl.pallas_call(functools.partial(attend_kernel, scale=scale), in_specs=[s...  6.37 us
    ppermute x4, starting transfers between devices, outward(): return lax.ppermute(x, 'gy', [(1, 0), (2, 3)])  5.17 us
    pallas_call x2, Pallas kernels, project(): pl.pallas_call(functools.partial(project_kernel, pair=pair), in_specs=[sm...  5.16 us
    ppermute x2, starting transfers between devices, outer(): return lax.ppermute(x, 'gy', [(0, 1), (1, 0), (2, 3), (3, 2)])  5.08 us
  transfers between devices with their start and end apart: 38, of which 17 were waited for; matrix products, arithmetic and copies ran while one was open for 5% of the time, Pallas kernels for 5%

profile of v6, /device:TPU:0, one launch (start us, length us, event | category | flops | bytes accessed | tf_op | source)
XLA Modules:
  0.0 113.0 jit_solution(14486920792643444888)
XLA Ops:
  0.6 3.1 %collective-permute-start = (bf16[384,512]{1,0:T(8,128)(2,1)}, bf16[384,512]{1,0:T(8,128)(2,1)S(1)}, u32[]{:S(2)}, u32[]{:S(2)}) collective-permute-start(bf16[384,512]{1,0:T(8,128)(2,1)} %refs_0_.1), channel_id=1, source_target_pairs={{0,1},{1,0},{2,3},{3,2},{4,5},{5,4},{6,7},{7,6},{8,9},{9,8},{10,11... | collective-permute-start | bytes 1179656 | tf_op jit(solution)/shard_map/ppermute | solution.py:121
  3.7 0.7 collective-permute-start.1
  4.4 1.7 %reshape.193.refs_0_ = bf16[256,1536]{1,0:T(8,128)(2,1)S(1)} reshape(bf16[256,3,4,128]{3,2,1,0:T(4,128)(2,1)} %param.7) | data formatting | bytes 1572864 | tf_op jit(solution)/shard_map/reshape | solution.py:405
  6.1 1.6 %collective-permute-start.5 = (bf16[256,1536]{1,0:T(8,128)(2,1)S(1)}, bf16[256,1536]{1,0:T(8,128)(2,1)S(1)}, u32[]{:S(2)}, u32[]{:S(2)}) collective-permute-start(bf16[256,1536]{1,0:T(8,128)(2,1)S(1)} %reshape.193.refs_0_), channel_id=1, source_target_pairs={{0,8},{4,12},{8,0},{12,4},{16,24},{20,28},{24,16},{28,20},{1,9},{5... | collective-permute-start | bytes 2359304 | tf_op jit(solution)/shard_map/ppermute | solution.py:117
  7.6 1.5 %collective-permute-start.6 = (bf16[256,1536]{1,0:T(8,128)(2,1)S(1)}, bf16[256,1536]{1,0:T(8,128)(2,1)S(1)}, u32[]{:S(2)}, u32[]{:S(2)}) collective-permute-start(bf16[256,1536]{1,0:T(8,128)(2,1)S(1)} %reshape.193.refs_0_), channel_id=1, source_target_pairs={{0,16},{4,20},{8,24},{12,28},{16,0},{20,4},{24,8},{28,12},{1,17},{... | collective-permute-start | bytes 2359304 | tf_op jit(solution)/shard_map/ppermute | solution.py:117
  9.2 0.2 reduce-window.9
  9.4 0.1 select_reduce_fusion
  9.5 0.1 pad_add_fusion.where_ref
  9.6 0.8 fusion
  10.3 0.2 pad_maximum_fusion.3
  10.5 2.5 %collective-permute-done.refs_1_ = bf16[384,512]{1,0:T(8,128)(2,1)S(1)} collective-permute-done((bf16[384,512]{1,0:T(8,128)(2,1)}, bf16[384,512]{1,0:T(8,128)(2,1)S(1)}, u32[]{:S(2)}, u32[]{:S(2)}) %collective-permute-start) | collective-permute-done | bytes 393248 | tf_op jit(solution)/shard_map/ppermute | solution.py:121
  13.1 0.7 collective-permute-start.3
  13.7 1.3 %collective-permute-start.2 = (bf16[384,512]{1,0:T(8,128)(2,1)S(1)}, bf16[384,512]{1,0:T(8,128)(2,1)S(1)}, u32[]{:S(2)}, u32[]{:S(2)}) collective-permute-start(bf16[384,512]{1,0:T(8,128)(2,1)S(1)} %collective-permute-done.1.refs_2_), channel_id=1, source_target_pairs={{1,0},{2,3},{5,4},{6,7},{9,8},{10,11},{13,12},{14,15},{17,16},{18,... | collective-permute-start | bytes 1179656 | tf_op jit(solution)/shard_map/ppermute | solution.py:129
  15.1 1.3 %collective-permute-start.4 = (bf16[384,512]{1,0:T(8,128)(2,1)S(1)}, bf16[384,512]{1,0:T(8,128)(2,1)S(1)}, u32[]{:S(2)}, u32[]{:S(2)}) collective-permute-start(bf16[384,512]{1,0:T(8,128)(2,1)S(1)} %collective-permute-done.3.refs_4_), channel_id=1, source_target_pairs={{1,0},{2,3},{5,4},{6,7},{9,8},{10,11},{13,12},{14,15},{17,16},{18,... | collective-permute-start | bytes 1179656 | tf_op jit(solution)/shard_map/ppermute | solution.py:129
  16.4 8.8 %collective-permute-done.5.x_ref.refs_1_ = bf16[256,1536]{1,0:T(8,128)(2,1)S(1)} collective-permute-done((bf16[256,1536]{1,0:T(8,128)(2,1)S(1)}, bf16[256,1536]{1,0:T(8,128)(2,1)S(1)}, u32[]{:S(2)}, u32[]{:S(2)}) %collective-permute-start.5) | collective-permute-done | bytes 786464 | tf_op jit(solution)/shard_map/ppermute | solution.py:117
  25.1 1.2 %collective-permute-done.6.y_ref.refs_2_ = bf16[256,1536]{1,0:T(8,128)(2,1)S(1)} collective-permute-done((bf16[256,1536]{1,0:T(8,128)(2,1)S(1)}, bf16[256,1536]{1,0:T(8,128)(2,1)S(1)}, u32[]{:S(2)}, u32[]{:S(2)}) %collective-permute-start.6) | collective-permute-done | bytes 786464 | tf_op jit(solution)/shard_map/ppermute | solution.py:117
  26.4 0.1 halves.2
  26.4 0.6 collective-permute-start.7
  27.0 1.5 %collective-permute-start.8 = (bf16[128,1536]{1,0:T(8,128)(2,1)S(1)}, bf16[128,1536]{1,0:T(8,128)(2,1)S(1)}, u32[]{:S(2)}, u32[]{:S(2)}) collective-permute-start(bf16[128,1536]{1,0:T(8,128)(2,1)S(1)} %get-tuple-element.31), channel_id=1, source_target_pairs={{0,16},{4,20},{8,24},{12,28},{16,0},{20,4},{24,8},{28,12},{1,17},{... | collective-permute-start | bytes 1179656 | tf_op jit(solution)/shard_map/ppermute | solution.py:117
  28.5 0.5 collective-permute-start.10
  29.1 6.9 %collective-permute-done.4.refs_5_ = bf16[384,512]{1,0:T(8,128)(2,1)S(1)} collective-permute-done((bf16[384,512]{1,0:T(8,128)(2,1)S(1)}, bf16[384,512]{1,0:T(8,128)(2,1)S(1)}, u32[]{:S(2)}, u32[]{:S(2)}) %collective-permute-start.4) | collective-permute-done | bytes 393248 | tf_op jit(solution)/shard_map/ppermute | solution.py:129
  36.0 0.5 collective-permute-start.12
  36.5 0.1 collective-permute-start.13
  36.5 1.3 %normalize.1.x_ref = bf16[384,2048]{1,0:T(8,128)(2,1)S(1)} custom-call(s32[3]{0:T(128)S(1)} %pad_add_fusion.where_ref, bf16[384,512]{1,0:T(8,128)(2,1)S(1)} %copy-done, bf16[384,512]{1,0:T(8,128)(2,1)S(1)} %collective-permute-done.refs_1_, bf16[384,512]{1,0:T(8,128)(2,1)S(1)} %collective-permute-done.1.refs_2_, ...), custom_call_target="tpu_custom_call" | custom-call | flops 8589934592 | bytes 8388608 | tf_op jit(solution)/shard_map/normalize/pallas_call | solution.py:197
  37.8 1.0 collective-permute-done.12.refs_8_
  38.8 0.6 collective-permute-done.13.refs_9_
  39.4 2.6 %project.3 = (bf16[3,384,128]{2,1,0:T(8,128)(2,1)S(1)}, bf16[3,384,128]{2,1,0:T(8,128)(2,1)S(1)}) custom-call(s32[3]{0:T(128)S(1)} %pad_add_fusion.where_ref, bf16[384,2048]{1,0:T(8,128)(2,1)S(1)} %normalize.1.x_ref, f32[384,128]{1,0:T(8,128)S(1)} %get-tuple-element.28.cos_ref, f32[384,128]{1,0:T(8,128)S(1)} %get-tuple-element.29.sin_ref, ...), custom_call_target="tpu_custom_call" | custom-call | flops 1207959552 | bytes 8388608 | tf_op jit(solution)/shard_map/project/pallas_call | solution.py:238
  42.0 1.6 %collective-permute-start.14 = (bf16[3,384,128]{2,1,0:T(8,128)(2,1)S(1)}, bf16[3,384,128]{2,1,0:T(8,128)(2,1)S(1)}, u32[]{:S(2)}, u32[]{:S(2)}) collective-permute-start(bf16[3,384,128]{2,1,0:T(8,128)(2,1)S(1)} %get-tuple-element.33), channel_id=1, source_target_pairs={{0,8},{4,12},{8,0},{12,4},{16,24},{20,28},{24,16},{28,20},{1,9},{5... | collective-permute-start | bytes 884744 | tf_op jit(solution)/shard_map/ppermute | solution.py:117
  43.5 1.5 %collective-permute-start.15 = (bf16[3,384,128]{2,1,0:T(8,128)(2,1)S(1)}, bf16[3,384,128]{2,1,0:T(8,128)(2,1)S(1)}, u32[]{:S(2)}, u32[]{:S(2)}) collective-permute-start(bf16[3,384,128]{2,1,0:T(8,128)(2,1)S(1)} %get-tuple-element.34), channel_id=1, source_target_pairs={{0,16},{4,20},{8,24},{12,28},{16,0},{20,4},{24,8},{28,12},{1,17},{... | collective-permute-start | bytes 884744 | tf_op jit(solution)/shard_map/ppermute | solution.py:117
  45.0 2.6 %project.2 = (bf16[3,384,128]{2,1,0:T(8,128)(2,1)S(1)}, bf16[3,384,128]{2,1,0:T(8,128)(2,1)S(1)}) custom-call(s32[3]{0:T(128)S(1)} %pad_add_fusion.where_ref, bf16[384,2048]{1,0:T(8,128)(2,1)S(1)} %normalize.1.x_ref, f32[384,128]{1,0:T(8,128)S(1)} %get-tuple-element.28.cos_ref, f32[384,128]{1,0:T(8,128)S(1)} %get-tuple-element.29.sin_ref, ...), custom_call_target="tpu_custom_call" | custom-call | flops 1207959552 | bytes 8388608 | tf_op jit(solution)/shard_map/project/pallas_call | solution.py:238
  47.6 0.5 collective-permute-start.16
  48.2 3.7 %collective-permute-done.14.refs_1_ = bf16[3,384,128]{2,1,0:T(8,128)(2,1)S(1)} collective-permute-done((bf16[3,384,128]{2,1,0:T(8,128)(2,1)S(1)}, bf16[3,384,128]{2,1,0:T(8,128)(2,1)S(1)}, u32[]{:S(2)}, u32[]{:S(2)}) %collective-permute-start.14) | collective-permute-done | bytes 294944 | tf_op jit(solution)/shard_map/ppermute | solution.py:117
  51.9 6.7 %collective-permute-done.15.refs_2_ = bf16[3,384,128]{2,1,0:T(8,128)(2,1)S(1)} collective-permute-done((bf16[3,384,128]{2,1,0:T(8,128)(2,1)S(1)}, bf16[3,384,128]{2,1,0:T(8,128)(2,1)S(1)}, u32[]{:S(2)}, u32[]{:S(2)}) %collective-permute-start.15) | collective-permute-done | bytes 294944 | tf_op jit(solution)/shard_map/ppermute | solution.py:117
  58.6 0.5 collective-permute-start.20
  59.1 1.1 collective-permute-done.19.refs_6_
  60.2 0.4 collective-permute-done.20.refs_7_
  60.6 6.4 %attend.1 = (bf16[384,128]{1,0:T(8,128)(2,1)S(1)}, bf16[384,128]{1,0:T(8,128)(2,1)S(1)}, bf16[384,128]{1,0:T(8,128)(2,1)S(1)}, bf16[384,128]{1,0:T(8,128)(2,1)S(1)}) custom-call(s32[3]{0:T(128)S(1)} %pad_add_fusion.where_ref, s32[6]{0:T(128)S(1)} %bitcast_subtract_fusion.start_ref, bf16[3,384,128]{2,1,0:T(8,128)(2,1)S(1)} %get-tuple-element.32.refs_0_, ...), custom_call_target="tpu_custom_call" | custom-call | flops 2415919104 | bytes 8388608 | tf_op jit(solution)/shard_map/attend/pallas_call | solution.py:305
  67.0 1.6 %collective-permute-start.21 = (bf16[384,128]{1,0:T(8,128)(2,1)S(1)}, bf16[384,128]{1,0:T(8,128)(2,1)S(1)}, u32[]{:S(2)}, u32[]{:S(2)}) collective-permute-start(bf16[384,128]{1,0:T(8,128)(2,1)S(1)} %get-tuple-element.36), channel_id=1, source_target_pairs={{0,24},{4,28},{8,16},{12,20},{16,8},{20,12},{24,0},{28,4},{1,25},{... | collective-permute-start | bytes 294920 | tf_op jit(solution)/shard_map/ppermute | solution.py:117
  68.6 0.8 collective-permute-start.22
  69.3 1.2 %collective-permute-start.23 = (bf16[384,128]{1,0:T(8,128)(2,1)S(1)}, bf16[384,128]{1,0:T(8,128)(2,1)S(1)}, u32[]{:S(2)}, u32[]{:S(2)}) collective-permute-start(bf16[384,128]{1,0:T(8,128)(2,1)S(1)} %get-tuple-element.38), channel_id=1, source_target_pairs={{0,8},{4,12},{8,0},{12,4},{16,24},{20,28},{24,16},{28,20},{1,9},{5... | collective-permute-start | bytes 294920 | tf_op jit(solution)/shard_map/ppermute | solution.py:117
  70.5 2.1 %collective-permute-done.21 = bf16[384,128]{1,0:T(8,128)(2,1)S(1)} collective-permute-done((bf16[384,128]{1,0:T(8,128)(2,1)S(1)}, bf16[384,128]{1,0:T(8,128)(2,1)S(1)}, u32[]{:S(2)}, u32[]{:S(2)}) %collective-permute-start.21) | collective-permute-done | bytes 98336 | tf_op jit(solution)/shard_map/ppermute | solution.py:117
  72.7 3.0 %collective-permute-done.22 = bf16[384,128]{1,0:T(8,128)(2,1)S(1)} collective-permute-done((bf16[384,128]{1,0:T(8,128)(2,1)S(1)}, bf16[384,128]{1,0:T(8,128)(2,1)S(1)}, u32[]{:S(2)}, u32[]{:S(2)}) %collective-permute-start.22) | collective-permute-done | bytes 98336 | tf_op jit(solution)/shard_map/ppermute | solution.py:117
  75.7 0.1 broadcast_select_fusion.5
  75.9 2.0 %collective-permute-start.24 = (bf16[384,512]{1,0:T(8,128)(2,1)S(1)}, bf16[384,512]{1,0:T(8,128)(2,1)S(1)}, u32[]{:S(2)}, u32[]{:S(2)}) collective-permute-start(bf16[384,512]{1,0:T(8,128)(2,1)S(1)} %pad_maximum_fusion.own), channel_id=1, source_target_pairs={{0,1},{1,0},{2,3},{3,2},{4,5},{5,4},{6,7},{7,6},{8,9},{9,8},{10,11... | collective-permute-start | bytes 1179656 | tf_op jit(solution)/shard_map/ppermute | solution.py:121
  77.9 1.2 %collective-permute-start.28 = (bf16[256,512]{1,0:T(8,128)(2,1)S(1)}, bf16[256,512]{1,0:T(8,128)(2,1)S(1)}, u32[]{:S(2)}, u32[]{:S(2)}) collective-permute-start(bf16[256,512]{1,0:T(8,128)(2,1)S(1)} %copy-done.1), channel_id=1, source_target_pairs={{0,8},{4,12},{8,0},{12,4},{16,24},{20,28},{24,16},{28,20},{1,9},{5... | collective-permute-start | bytes 786440 | tf_op jit(solution)/shard_map/ppermute | solution.py:117
  79.0 1.2 %collective-permute-start.29 = (bf16[256,512]{1,0:T(8,128)(2,1)S(1)}, bf16[256,512]{1,0:T(8,128)(2,1)S(1)}, u32[]{:S(2)}, u32[]{:S(2)}) collective-permute-start(bf16[256,512]{1,0:T(8,128)(2,1)S(1)} %copy-done.1), channel_id=1, source_target_pairs={{0,16},{4,20},{8,24},{12,28},{16,0},{20,4},{24,8},{28,12},{1,17},{... | collective-permute-start | bytes 786440 | tf_op jit(solution)/shard_map/ppermute | solution.py:117
  80.3 0.7 collective-permute-start.27
  81.0 0.1 collective-permute-start.33
  81.0 6.4 %collective-permute-done.24.near = bf16[384,512]{1,0:T(8,128)(2,1)S(1)} collective-permute-done((bf16[384,512]{1,0:T(8,128)(2,1)S(1)}, bf16[384,512]{1,0:T(8,128)(2,1)S(1)}, u32[]{:S(2)}, u32[]{:S(2)}) %collective-permute-start.24) | collective-permute-done | bytes 393248 | tf_op jit(solution)/shard_map/ppermute | solution.py:121
  87.4 0.7 collective-permute-start.25
  88.2 0.1 collective-permute-start.34
  88.3 1.3 %collective-permute-start.30 = (bf16[384,512]{1,0:T(8,128)(2,1)S(1)}, bf16[384,512]{1,0:T(8,128)(2,1)S(1)}, u32[]{:S(2)}, u32[]{:S(2)}) collective-permute-start(bf16[384,512]{1,0:T(8,128)(2,1)S(1)} %collective-permute-done.27.q1), channel_id=1, source_target_pairs={{1,0},{2,3},{5,4},{6,7},{9,8},{10,11},{13,12},{14,15},{17,16},{18,... | collective-permute-start | bytes 1179656 | tf_op jit(solution)/shard_map/ppermute | solution.py:129
  89.6 1.0 collective-permute-start.31
  90.7 1.2 %collective-permute-start.32 = (bf16[128,512]{1,0:T(8,128)(2,1)S(1)}, bf16[128,512]{1,0:T(8,128)(2,1)S(1)}, u32[]{:S(2)}, u32[]{:S(2)}) collective-permute-start(bf16[128,512]{1,0:T(8,128)(2,1)S(1)} %get-tuple-element.46), channel_id=1, source_target_pairs={{0,16},{4,20},{8,24},{12,28},{16,0},{20,4},{24,8},{28,12},{1,17},{... | collective-permute-start | bytes 393224 | tf_op jit(solution)/shard_map/ppermute | solution.py:117
  92.0 0.1 collective-permute-start.35
  92.1 1.3 %collective-permute-start.26 = (bf16[384,512]{1,0:T(8,128)(2,1)S(1)}, bf16[384,512]{1,0:T(8,128)(2,1)S(1)}, u32[]{:S(2)}, u32[]{:S(2)}) collective-permute-start(bf16[384,512]{1,0:T(8,128)(2,1)S(1)} %collective-permute-done.25.q2), channel_id=1, source_target_pairs={{1,0},{2,3},{5,4},{6,7},{9,8},{10,11},{13,12},{14,15},{17,16},{18,... | collective-permute-start | bytes 1179656 | tf_op jit(solution)/shard_map/ppermute | solution.py:129
  93.4 2.2 %collective-permute-done.31.refs_3_ = bf16[128,512]{1,0:T(8,128)(2,1)S(1)} collective-permute-done((bf16[128,512]{1,0:T(8,128)(2,1)S(1)}, bf16[128,512]{1,0:T(8,128)(2,1)S(1)}, u32[]{:S(2)}, u32[]{:S(2)}) %collective-permute-start.31) | collective-permute-done | bytes 131104 | tf_op jit(solution)/shard_map/ppermute | solution.py:117
  95.6 0.7 collective-permute-done.32.refs_4_
  96.3 1.1 copy.11
  97.4 1.1 copy.10
  98.5 5.0 %collective-permute-done.30.p2 = bf16[384,512]{1,0:T(8,128)(2,1)S(1)} collective-permute-done((bf16[384,512]{1,0:T(8,128)(2,1)S(1)}, bf16[384,512]{1,0:T(8,128)(2,1)S(1)}, u32[]{:S(2)}, u32[]{:S(2)}) %collective-permute-start.30) | collective-permute-done | bytes 393248 | tf_op jit(solution)/shard_map/ppermute | solution.py:129
  103.5 1.5 %early.1 = (f32[384,512]{1,0:T(8,128)S(1)}, bf16[512,512]{1,0:T(8,128)(2,1)S(1)}) custom-call(s32[3]{0:T(128)S(1)} %pad_add_fusion.where_ref, bf16[384,512]{1,0:T(8,128)(2,1)S(1)} %pad_maximum_fusion.own, bf16[384,512]{1,0:T(8,128)(2,1)S(1)} %collective-permute-done.24.near, bf16[384,512]{1,0:T(8,128)(2,1)S(1)} %collective-permute-done.27.q1, ...), custom_call_target="tpu_custom_call" | custom-call | flops 1073741824 | bytes 8388608 | tf_op jit(solution)/shard_map/early/pallas_call | solution.py:345
  104.9 6.4 %collective-permute-done.26.p3 = bf16[384,512]{1,0:T(8,128)(2,1)S(1)} collective-permute-done((bf16[384,512]{1,0:T(8,128)(2,1)S(1)}, bf16[384,512]{1,0:T(8,128)(2,1)S(1)}, u32[]{:S(2)}, u32[]{:S(2)}) %collective-permute-start.26) | collective-permute-done | bytes 393248 | tf_op jit(solution)/shard_map/ppermute | solution.py:129
  111.3 1.7 %last.1 = bf16[384,512]{1,0:T(8,128)(2,1)} custom-call(s32[3]{0:T(128)S(1)} %pad_add_fusion.where_ref, bf16[384,512]{1,0:T(8,128)(2,1)S(1)} %collective-permute-done.25.q2, bf16[384,512]{1,0:T(8,128)(2,1)S(1)} %collective-permute-done.26.p3, f32[384,512]{1,0:T(8,128)S(1)} %get-tuple-element.47.total_ref, bf16[512,512]{1,0:T(8,128)(2,1)S(1)} %get-tuple-element.48.w_ref), custom_call_target="tpu_custom_call" | custom-call | flops 201326592 | bytes 8388608 | tf_op jit(solution)/shard_map/last/pallas_call | solution.py:368
  (50 shorter events, 0.4 us)
Async XLA Ops:
  0.6 8.5 %copy-start.3 = (s32[6]{0:T(128)S(1)}, s32[6]{0:T(128)}, u32[]{:S(2)}) copy-start(s32[6]{0:T(128)} %param.9) | copy-start | bytes 76
  0.6 12.4 %collective-permute-start = (bf16[384,512]{1,0:T(8,128)(2,1)}, bf16[384,512]{1,0:T(8,128)(2,1)S(1)}, u32[]{:S(2)}, u32[]{:S(2)}) collective-permute-start(bf16[384,512]{1,0:T(8,128)(2,1)} %refs_0_.1), channel_id=1, source_target_pairs={{0,1},{1,0},{2,3},{3,2},{4,5},{5,4},{6,7},{7,6},{8,9},{9,8},{10,11... | collective-permute-start | bytes 1179656 | tf_op jit(solution)/shard_map/ppermute | solution.py:121
  3.7 10.0 %collective-permute-start.1 = (bf16[384,512]{1,0:T(8,128)(2,1)}, bf16[384,512]{1,0:T(8,128)(2,1)S(1)}, u32[]{:S(2)}, u32[]{:S(2)}) collective-permute-start(bf16[384,512]{1,0:T(8,128)(2,1)} %refs_0_.1), channel_id=1, source_target_pairs={{1,2},{2,1},{5,6},{6,5},{9,10},{10,9},{13,14},{14,13},{17,18},{18,... | collective-permute-start | bytes 1179656 | tf_op jit(solution)/shard_map/ppermute | solution.py:125
  6.1 19.1 %collective-permute-start.5 = (bf16[256,1536]{1,0:T(8,128)(2,1)S(1)}, bf16[256,1536]{1,0:T(8,128)(2,1)S(1)}, u32[]{:S(2)}, u32[]{:S(2)}) collective-permute-start(bf16[256,1536]{1,0:T(8,128)(2,1)S(1)} %reshape.193.refs_0_), channel_id=1, source_target_pairs={{0,8},{4,12},{8,0},{12,4},{16,24},{20,28},{24,16},{28,20},{1,9},{5... | collective-permute-start | bytes 2359304 | tf_op jit(solution)/shard_map/ppermute | solution.py:117
  7.6 18.7 %collective-permute-start.6 = (bf16[256,1536]{1,0:T(8,128)(2,1)S(1)}, bf16[256,1536]{1,0:T(8,128)(2,1)S(1)}, u32[]{:S(2)}, u32[]{:S(2)}) collective-permute-start(bf16[256,1536]{1,0:T(8,128)(2,1)S(1)} %reshape.193.refs_0_), channel_id=1, source_target_pairs={{0,16},{4,20},{8,24},{12,28},{16,0},{20,4},{24,8},{28,12},{1,17},{... | collective-permute-start | bytes 2359304 | tf_op jit(solution)/shard_map/ppermute | solution.py:117
  9.6 27.0 %copy-start = (bf16[384,512]{1,0:T(8,128)(2,1)S(1)}, bf16[384,512]{1,0:T(8,128)(2,1)}, u32[]{:S(2)}) copy-start(bf16[384,512]{1,0:T(8,128)(2,1)} %refs_0_.1) | copy-start | bytes 1179652
  9.6 27.0 %copy-start.2 = (f32[2048]{0:T(1024)S(1)}, f32[2048]{0:T(1024)}, u32[]{:S(2)}) copy-start(f32[2048]{0:T(1024)} %param.6) | copy-start | bytes 24580
  13.1 2.0 %collective-permute-start.3 = (bf16[384,512]{1,0:T(8,128)(2,1)S(1)}, bf16[384,512]{1,0:T(8,128)(2,1)S(1)}, u32[]{:S(2)}, u32[]{:S(2)}) collective-permute-start(bf16[384,512]{1,0:T(8,128)(2,1)S(1)} %collective-permute-done.refs_1_), channel_id=1, source_target_pairs={{1,2},{2,1},{5,6},{6,5},{9,10},{10,9},{13,14},{14,13},{17,18},{18,... | collective-permute-start | bytes 1179656 | tf_op jit(solution)/shard_map/ppermute | solution.py:125
  13.7 14.8 %collective-permute-start.2 = (bf16[384,512]{1,0:T(8,128)(2,1)S(1)}, bf16[384,512]{1,0:T(8,128)(2,1)S(1)}, u32[]{:S(2)}, u32[]{:S(2)}) collective-permute-start(bf16[384,512]{1,0:T(8,128)(2,1)S(1)} %collective-permute-done.1.refs_2_), channel_id=1, source_target_pairs={{1,0},{2,3},{5,4},{6,7},{9,8},{10,11},{13,12},{14,15},{17,16},{18,... | collective-permute-start | bytes 1179656 | tf_op jit(solution)/shard_map/ppermute | solution.py:129
  15.1 20.9 %collective-permute-start.4 = (bf16[384,512]{1,0:T(8,128)(2,1)S(1)}, bf16[384,512]{1,0:T(8,128)(2,1)S(1)}, u32[]{:S(2)}, u32[]{:S(2)}) collective-permute-start(bf16[384,512]{1,0:T(8,128)(2,1)S(1)} %collective-permute-done.3.refs_4_), channel_id=1, source_target_pairs={{1,0},{2,3},{5,4},{6,7},{9,8},{10,11},{13,12},{14,15},{17,16},{18,... | collective-permute-start | bytes 1179656 | tf_op jit(solution)/shard_map/ppermute | solution.py:129
  26.4 9.5 %collective-permute-start.7 = (bf16[128,1536]{1,0:T(8,128)(2,1)S(1)}, bf16[128,1536]{1,0:T(8,128)(2,1)S(1)}, u32[]{:S(2)}, u32[]{:S(2)}) collective-permute-start(bf16[128,1536]{1,0:T(8,128)(2,1)S(1)} %get-tuple-element.30), channel_id=1, source_target_pairs={{0,8},{4,12},{8,0},{12,4},{16,24},{20,28},{24,16},{28,20},{1,9},{5... | collective-permute-start | bytes 1179656 | tf_op jit(solution)/shard_map/ppermute | solution.py:117
  27.0 9.4 %collective-permute-start.8 = (bf16[128,1536]{1,0:T(8,128)(2,1)S(1)}, bf16[128,1536]{1,0:T(8,128)(2,1)S(1)}, u32[]{:S(2)}, u32[]{:S(2)}) collective-permute-start(bf16[128,1536]{1,0:T(8,128)(2,1)S(1)} %get-tuple-element.31), channel_id=1, source_target_pairs={{0,16},{4,20},{8,24},{12,28},{16,0},{20,4},{24,8},{28,12},{1,17},{... | collective-permute-start | bytes 1179656 | tf_op jit(solution)/shard_map/ppermute | solution.py:117
  28.5 9.3 %collective-permute-start.9 = (bf16[256,1536]{1,0:T(8,128)(2,1)S(1)}, bf16[256,1536]{1,0:T(8,128)(2,1)S(1)}, u32[]{:S(2)}, u32[]{:S(2)}) collective-permute-start(bf16[256,1536]{1,0:T(8,128)(2,1)S(1)} %reshape.193.refs_0_), channel_id=1, source_target_pairs={{0,4},{4,0},{8,12},{12,8},{16,20},{20,16},{24,28},{28,24},{1,5},{5... | collective-permute-start | bytes 2359304 | tf_op jit(solution)/shard_map/ppermute | solution.py:117
  28.5 10.8 %collective-permute-start.10 = (bf16[256,1536]{1,0:T(8,128)(2,1)S(1)}, bf16[256,1536]{1,0:T(8,128)(2,1)S(1)}, u32[]{:S(2)}, u32[]{:S(2)}) collective-permute-start(bf16[256,1536]{1,0:T(8,128)(2,1)S(1)} %collective-permute-done.5.x_ref.refs_1_), channel_id=1, source_target_pairs={{0,4},{4,0},{8,12},{12,8},{16,20},{20,16},{24,28},{28,24},{1,5},{5... | collective-permute-start | bytes 2359304 | tf_op jit(solution)/shard_map/ppermute | solution.py:117
  36.0 3.4 %collective-permute-start.11 = (bf16[256,1536]{1,0:T(8,128)(2,1)S(1)}, bf16[256,1536]{1,0:T(8,128)(2,1)S(1)}, u32[]{:S(2)}, u32[]{:S(2)}) collective-permute-start(bf16[256,1536]{1,0:T(8,128)(2,1)S(1)} %collective-permute-done.6.y_ref.refs_2_), channel_id=1, source_target_pairs={{0,4},{4,0},{8,12},{12,8},{16,20},{20,16},{24,28},{28,24},{1,5},{5... | collective-permute-start | bytes 2359304 | tf_op jit(solution)/shard_map/ppermute | solution.py:117
  36.0 2.8 %collective-permute-start.12 = (bf16[128,1536]{1,0:T(8,128)(2,1)S(1)}, bf16[128,1536]{1,0:T(8,128)(2,1)S(1)}, u32[]{:S(2)}, u32[]{:S(2)}) collective-permute-start(bf16[128,1536]{1,0:T(8,128)(2,1)S(1)} %collective-permute-done.7.refs_3_), channel_id=1, source_target_pairs={{0,4},{4,0},{8,12},{12,8},{16,20},{20,16},{24,28},{28,24},{1,5},{5... | collective-permute-start | bytes 1179656 | tf_op jit(solution)/shard_map/ppermute | solution.py:117
  36.5 2.9 %collective-permute-start.13 = (bf16[128,1536]{1,0:T(8,128)(2,1)S(1)}, bf16[128,1536]{1,0:T(8,128)(2,1)S(1)}, u32[]{:S(2)}, u32[]{:S(2)}) collective-permute-start(bf16[128,1536]{1,0:T(8,128)(2,1)S(1)} %collective-permute-done.8.refs_4_), channel_id=1, source_target_pairs={{0,4},{4,0},{8,12},{12,8},{16,20},{20,16},{24,28},{28,24},{1,5},{5... | collective-permute-start | bytes 1179656 | tf_op jit(solution)/shard_map/ppermute | solution.py:117
  42.0 9.9 %collective-permute-start.14 = (bf16[3,384,128]{2,1,0:T(8,128)(2,1)S(1)}, bf16[3,384,128]{2,1,0:T(8,128)(2,1)S(1)}, u32[]{:S(2)}, u32[]{:S(2)}) collective-permute-start(bf16[3,384,128]{2,1,0:T(8,128)(2,1)S(1)} %get-tuple-element.33), channel_id=1, source_target_pairs={{0,8},{4,12},{8,0},{12,4},{16,24},{20,28},{24,16},{28,20},{1,9},{5... | collective-permute-start | bytes 884744 | tf_op jit(solution)/shard_map/ppermute | solution.py:117
  43.5 15.1 %collective-permute-start.15 = (bf16[3,384,128]{2,1,0:T(8,128)(2,1)S(1)}, bf16[3,384,128]{2,1,0:T(8,128)(2,1)S(1)}, u32[]{:S(2)}, u32[]{:S(2)}) collective-permute-start(bf16[3,384,128]{2,1,0:T(8,128)(2,1)S(1)} %get-tuple-element.34), channel_id=1, source_target_pairs={{0,16},{4,20},{8,24},{12,28},{16,0},{20,4},{24,8},{28,12},{1,17},{... | collective-permute-start | bytes 884744 | tf_op jit(solution)/shard_map/ppermute | solution.py:117
  47.6 11.0 %collective-permute-start.16 = (bf16[3,384,128]{2,1,0:T(8,128)(2,1)S(1)}, bf16[3,384,128]{2,1,0:T(8,128)(2,1)S(1)}, u32[]{:S(2)}, u32[]{:S(2)}) collective-permute-start(bf16[3,384,128]{2,1,0:T(8,128)(2,1)S(1)} %get-tuple-element.35), channel_id=1, source_target_pairs={{0,24},{4,28},{8,16},{12,20},{16,8},{20,12},{24,0},{28,4},{1,25},{... | collective-permute-start | bytes 884744 | tf_op jit(solution)/shard_map/ppermute | solution.py:117
  48.2 11.0 %collective-permute-start.17 = (bf16[3,384,128]{2,1,0:T(8,128)(2,1)S(1)}, bf16[3,384,128]{2,1,0:T(8,128)(2,1)S(1)}, u32[]{:S(2)}, u32[]{:S(2)}) collective-permute-start(bf16[3,384,128]{2,1,0:T(8,128)(2,1)S(1)} %get-tuple-element.32.refs_0_), channel_id=1, source_target_pairs={{0,4},{4,0},{8,12},{12,8},{16,20},{20,16},{24,28},{28,24},{1,5},{5... | collective-permute-start | bytes 884744 | tf_op jit(solution)/shard_map/ppermute | solution.py:117
  51.9 7.2 %collective-permute-start.18 = (bf16[3,384,128]{2,1,0:T(8,128)(2,1)S(1)}, bf16[3,384,128]{2,1,0:T(8,128)(2,1)S(1)}, u32[]{:S(2)}, u32[]{:S(2)}) collective-permute-start(bf16[3,384,128]{2,1,0:T(8,128)(2,1)S(1)} %collective-permute-done.14.refs_1_), channel_id=1, source_target_pairs={{0,4},{4,0},{8,12},{12,8},{16,20},{20,16},{24,28},{28,24},{1,5},{5... | collective-permute-start | bytes 884744 | tf_op jit(solution)/shard_map/ppermute | solution.py:117
  58.6 1.6 %collective-permute-start.19 = (bf16[3,384,128]{2,1,0:T(8,128)(2,1)S(1)}, bf16[3,384,128]{2,1,0:T(8,128)(2,1)S(1)}, u32[]{:S(2)}, u32[]{:S(2)}) collective-permute-start(bf16[3,384,128]{2,1,0:T(8,128)(2,1)S(1)} %collective-permute-done.15.refs_2_), channel_id=1, source_target_pairs={{0,4},{4,0},{8,12},{12,8},{16,20},{20,16},{24,28},{28,24},{1,5},{5... | collective-permute-start | bytes 884744 | tf_op jit(solution)/shard_map/ppermute | solution.py:117
  58.6 2.0 %collective-permute-start.20 = (bf16[3,384,128]{2,1,0:T(8,128)(2,1)S(1)}, bf16[3,384,128]{2,1,0:T(8,128)(2,1)S(1)}, u32[]{:S(2)}, u32[]{:S(2)}) collective-permute-start(bf16[3,384,128]{2,1,0:T(8,128)(2,1)S(1)} %collective-permute-done.16.refs_3_), channel_id=1, source_target_pairs={{0,4},{4,0},{8,12},{12,8},{16,20},{20,16},{24,28},{28,24},{1,5},{5... | collective-permute-start | bytes 884744 | tf_op jit(solution)/shard_map/ppermute | solution.py:117
  67.0 10.9 %copy-start.1 = (bf16[256,512]{1,0:T(8,128)(2,1)S(1)}, bf16[256,512]{1,0:T(8,128)(2,1)}, u32[]{:S(2)}) copy-start(bf16[256,512]{1,0:T(8,128)(2,1)} %refs_0_.2) | copy-start | bytes 786436
  67.0 5.7 %collective-permute-start.21 = (bf16[384,128]{1,0:T(8,128)(2,1)S(1)}, bf16[384,128]{1,0:T(8,128)(2,1)S(1)}, u32[]{:S(2)}, u32[]{:S(2)}) collective-permute-start(bf16[384,128]{1,0:T(8,128)(2,1)S(1)} %get-tuple-element.36), channel_id=1, source_target_pairs={{0,24},{4,28},{8,16},{12,20},{16,8},{20,12},{24,0},{28,4},{1,25},{... | collective-permute-start | bytes 294920 | tf_op jit(solution)/shard_map/ppermute | solution.py:117
  68.6 7.1 %collective-permute-start.22 = (bf16[384,128]{1,0:T(8,128)(2,1)S(1)}, bf16[384,128]{1,0:T(8,128)(2,1)S(1)}, u32[]{:S(2)}, u32[]{:S(2)}) collective-permute-start(bf16[384,128]{1,0:T(8,128)(2,1)S(1)} %get-tuple-element.37), channel_id=1, source_target_pairs={{0,16},{4,20},{8,24},{12,28},{16,0},{20,4},{24,8},{28,12},{1,17},{... | collective-permute-start | bytes 294920 | tf_op jit(solution)/shard_map/ppermute | solution.py:117
  69.3 6.4 %collective-permute-start.23 = (bf16[384,128]{1,0:T(8,128)(2,1)S(1)}, bf16[384,128]{1,0:T(8,128)(2,1)S(1)}, u32[]{:S(2)}, u32[]{:S(2)}) collective-permute-start(bf16[384,128]{1,0:T(8,128)(2,1)S(1)} %get-tuple-element.38), channel_id=1, source_target_pairs={{0,8},{4,12},{8,0},{12,4},{16,24},{20,28},{24,16},{28,20},{1,9},{5... | collective-permute-start | bytes 294920 | tf_op jit(solution)/shard_map/ppermute | solution.py:117
  75.9 11.6 %collective-permute-start.24 = (bf16[384,512]{1,0:T(8,128)(2,1)S(1)}, bf16[384,512]{1,0:T(8,128)(2,1)S(1)}, u32[]{:S(2)}, u32[]{:S(2)}) collective-permute-start(bf16[384,512]{1,0:T(8,128)(2,1)S(1)} %pad_maximum_fusion.own), channel_id=1, source_target_pairs={{0,1},{1,0},{2,3},{3,2},{4,5},{5,4},{6,7},{7,6},{8,9},{9,8},{10,11... | collective-permute-start | bytes 1179656 | tf_op jit(solution)/shard_map/ppermute | solution.py:121
  77.9 10.3 %collective-permute-start.28 = (bf16[256,512]{1,0:T(8,128)(2,1)S(1)}, bf16[256,512]{1,0:T(8,128)(2,1)S(1)}, u32[]{:S(2)}, u32[]{:S(2)}) collective-permute-start(bf16[256,512]{1,0:T(8,128)(2,1)S(1)} %copy-done.1), channel_id=1, source_target_pairs={{0,8},{4,12},{8,0},{12,4},{16,24},{20,28},{24,16},{28,20},{1,9},{5... | collective-permute-start | bytes 786440 | tf_op jit(solution)/shard_map/ppermute | solution.py:117
  79.0 9.3 %collective-permute-start.29 = (bf16[256,512]{1,0:T(8,128)(2,1)S(1)}, bf16[256,512]{1,0:T(8,128)(2,1)S(1)}, u32[]{:S(2)}, u32[]{:S(2)}) collective-permute-start(bf16[256,512]{1,0:T(8,128)(2,1)S(1)} %copy-done.1), channel_id=1, source_target_pairs={{0,16},{4,20},{8,24},{12,28},{16,0},{20,4},{24,8},{28,12},{1,17},{... | collective-permute-start | bytes 786440 | tf_op jit(solution)/shard_map/ppermute | solution.py:117
  80.3 8.1 %collective-permute-start.27 = (bf16[384,512]{1,0:T(8,128)(2,1)S(1)}, bf16[384,512]{1,0:T(8,128)(2,1)S(1)}, u32[]{:S(2)}, u32[]{:S(2)}) collective-permute-start(bf16[384,512]{1,0:T(8,128)(2,1)S(1)} %pad_maximum_fusion.own), channel_id=1, source_target_pairs={{1,2},{2,1},{5,6},{6,5},{9,10},{10,9},{13,14},{14,13},{17,18},{18,... | collective-permute-start | bytes 1179656 | tf_op jit(solution)/shard_map/ppermute | solution.py:125
  81.0 9.7 %collective-permute-start.33 = (bf16[256,512]{1,0:T(8,128)(2,1)S(1)}, bf16[256,512]{1,0:T(8,128)(2,1)S(1)}, u32[]{:S(2)}, u32[]{:S(2)}) collective-permute-start(bf16[256,512]{1,0:T(8,128)(2,1)S(1)} %copy-done.1), channel_id=1, source_target_pairs={{0,4},{4,0},{8,12},{12,8},{16,20},{20,16},{24,28},{28,24},{1,5},{5... | collective-permute-start | bytes 786440 | tf_op jit(solution)/shard_map/ppermute | solution.py:117
  87.4 4.6 %collective-permute-start.25 = (bf16[384,512]{1,0:T(8,128)(2,1)S(1)}, bf16[384,512]{1,0:T(8,128)(2,1)S(1)}, u32[]{:S(2)}, u32[]{:S(2)}) collective-permute-start(bf16[384,512]{1,0:T(8,128)(2,1)S(1)} %collective-permute-done.24.near), channel_id=1, source_target_pairs={{1,2},{2,1},{5,6},{6,5},{9,10},{10,9},{13,14},{14,13},{17,18},{18,... | collective-permute-start | bytes 1179656 | tf_op jit(solution)/shard_map/ppermute | solution.py:125
  88.2 3.8 %collective-permute-start.34 = (bf16[256,512]{1,0:T(8,128)(2,1)S(1)}, bf16[256,512]{1,0:T(8,128)(2,1)S(1)}, u32[]{:S(2)}, u32[]{:S(2)}) collective-permute-start(bf16[256,512]{1,0:T(8,128)(2,1)S(1)} %collective-permute-done.28.x_ref.refs_1_), channel_id=1, source_target_pairs={{0,4},{4,0},{8,12},{12,8},{16,20},{20,16},{24,28},{28,24},{1,5},{5... | collective-permute-start | bytes 786440 | tf_op jit(solution)/shard_map/ppermute | solution.py:117
  88.3 15.1 %collective-permute-start.30 = (bf16[384,512]{1,0:T(8,128)(2,1)S(1)}, bf16[384,512]{1,0:T(8,128)(2,1)S(1)}, u32[]{:S(2)}, u32[]{:S(2)}) collective-permute-start(bf16[384,512]{1,0:T(8,128)(2,1)S(1)} %collective-permute-done.27.q1), channel_id=1, source_target_pairs={{1,0},{2,3},{5,4},{6,7},{9,8},{10,11},{13,12},{14,15},{17,16},{18,... | collective-permute-start | bytes 1179656 | tf_op jit(solution)/shard_map/ppermute | solution.py:129
  89.6 6.0 %collective-permute-start.31 = (bf16[128,512]{1,0:T(8,128)(2,1)S(1)}, bf16[128,512]{1,0:T(8,128)(2,1)S(1)}, u32[]{:S(2)}, u32[]{:S(2)}) collective-permute-start(bf16[128,512]{1,0:T(8,128)(2,1)S(1)} %get-tuple-element.45), channel_id=1, source_target_pairs={{0,8},{4,12},{8,0},{12,4},{16,24},{20,28},{24,16},{28,20},{1,9},{5... | collective-permute-start | bytes 393224 | tf_op jit(solution)/shard_map/ppermute | solution.py:117
  90.7 5.6 %collective-permute-start.32 = (bf16[128,512]{1,0:T(8,128)(2,1)S(1)}, bf16[128,512]{1,0:T(8,128)(2,1)S(1)}, u32[]{:S(2)}, u32[]{:S(2)}) collective-permute-start(bf16[128,512]{1,0:T(8,128)(2,1)S(1)} %get-tuple-element.46), channel_id=1, source_target_pairs={{0,16},{4,20},{8,24},{12,28},{16,0},{20,4},{24,8},{28,12},{1,17},{... | collective-permute-start | bytes 393224 | tf_op jit(solution)/shard_map/ppermute | solution.py:117
  92.0 6.5 %collective-permute-start.35 = (bf16[256,512]{1,0:T(8,128)(2,1)S(1)}, bf16[256,512]{1,0:T(8,128)(2,1)S(1)}, u32[]{:S(2)}, u32[]{:S(2)}) collective-permute-start(bf16[256,512]{1,0:T(8,128)(2,1)S(1)} %collective-permute-done.29.y_ref.refs_2_), channel_id=1, source_target_pairs={{0,4},{4,0},{8,12},{12,8},{16,20},{20,16},{24,28},{28,24},{1,5},{5... | collective-permute-start | bytes 786440 | tf_op jit(solution)/shard_map/ppermute | solution.py:117
  92.1 19.3 %collective-permute-start.26 = (bf16[384,512]{1,0:T(8,128)(2,1)S(1)}, bf16[384,512]{1,0:T(8,128)(2,1)S(1)}, u32[]{:S(2)}, u32[]{:S(2)}) collective-permute-start(bf16[384,512]{1,0:T(8,128)(2,1)S(1)} %collective-permute-done.25.q2), channel_id=1, source_target_pairs={{1,0},{2,3},{5,4},{6,7},{9,8},{10,11},{13,12},{14,15},{17,16},{18,... | collective-permute-start | bytes 1179656 | tf_op jit(solution)/shard_map/ppermute | solution.py:129
  95.6 2.9 %collective-permute-start.36 = (bf16[128,512]{1,0:T(8,128)(2,1)S(1)}, bf16[128,512]{1,0:T(8,128)(2,1)S(1)}, u32[]{:S(2)}, u32[]{:S(2)}) collective-permute-start(bf16[128,512]{1,0:T(8,128)(2,1)S(1)} %collective-permute-done.31.refs_3_), channel_id=1, source_target_pairs={{0,4},{4,0},{8,12},{12,8},{16,20},{20,16},{24,28},{28,24},{1,5},{5... | collective-permute-start | bytes 393224 | tf_op jit(solution)/shard_map/ppermute | solution.py:117
  96.3 2.2 %collective-permute-start.37 = (bf16[128,512]{1,0:T(8,128)(2,1)S(1)}, bf16[128,512]{1,0:T(8,128)(2,1)S(1)}, u32[]{:S(2)}, u32[]{:S(2)}) collective-permute-start(bf16[128,512]{1,0:T(8,128)(2,1)S(1)} %collective-permute-done.32.refs_4_), channel_id=1, source_target_pairs={{0,4},{4,0},{8,12},{12,8},{16,20},{20,16},{24,28},{28,24},{1,5},{5... | collective-permute-start | bytes 393224 | tf_op jit(solution)/shard_map/ppermute | solution.py:117

commit v7 on v6

--- a/solution.py
+++ b/solution.py
@@ -270,32 +270,36 @@
             begin = jnp.where(start_ref[d] <= qpos, start_ref[d], begin)
             lowest = jnp.where(start_ref[d] <= block * rows, start_ref[d], lowest)
 
-        def tile(number, state, after=after, query=query, qpos=qpos, begin=begin):
-            running, totals, accum = state
+        def scores(number, after=after, query=query, begin=begin):
             first = after - KEYS * (number + 1)
             place = pl.ds(pl.multiple_of(KEYS + first, 128), KEYS)
             kpos = first + lax.broadcasted_iota(jnp.int32, (1, KEYS), 1)
             score = scale * lax.dot_general(
                 query, keys[place, :], (((1,), (1,)), ((), ())), preferred_element_type=jnp.float32
             )
-            keep = (kpos >= begin) & (kpos <= qpos)
+            return score, kpos, kpos >= begin, vals[place, :]
+
+        def tile(number, state, scores=scores):
+            running, totals, accum = state
+            score, _, keep, values = scores(number)
             score = jnp.where(keep, score, -1e30)
             newmax = jnp.maximum(running, jnp.max(score, axis=1, keepdims=True))
             weight = jnp.exp2(score - newmax)
             factor = jnp.exp2(running - newmax)
             totals = totals * factor + jnp.sum(weight, axis=1, keepdims=True)
             accum = accum * factor + jnp.dot(
-                weight.astype(jnp.bfloat16), vals[place, :], preferred_element_type=jnp.float32
+                weight.astype(jnp.bfloat16), values, preferred_element_type=jnp.float32
             )
             return newmax, totals, accum
 
-        state = (
-            jnp.full((rows, 1), -1e30, jnp.float32),
-            jnp.zeros((rows, 1), jnp.float32),
-            jnp.zeros((rows, hsize), jnp.float32),
-        )
+        score, kpos, keep, values = scores(0)
+        score = jnp.where(keep & (kpos <= qpos), score, -1e30)
+        running = jnp.max(score, axis=1, keepdims=True)
+        weight = jnp.exp2(score - running)
+        totals = jnp.sum(weight, axis=1, keepdims=True)
+        accum = jnp.dot(weight.astype(jnp.bfloat16), values, preferred_element_type=jnp.float32)
         tiles = lax.div(after - lowest + KEYS - 1, KEYS)
-        running, totals, accum = lax.fori_loop(0, tiles, tile, state)
+        running, totals, accum = lax.fori_loop(1, tiles, tile, (running, totals, accum))
         outs[m][...] = (accum / totals).astype(jnp.bfloat16)
 
 
@@ -440,6 +444,7 @@
 def local(sizes, tokens, gain, w_qkv, w_out, lengths):
     heads = w_qkv.shape[2]
     fits = sizes == (2 * CHIPS, LINE) and heads == CHIPS and tokens.shape[1] == 2 * w_qkv.shape[0]
+    fits = fits and tokens.shape[0] <= KEYS
     plan = blocks_plan if fits else general
     return plan(tokens, gain, w_qkv, w_out, lengths)
 

time: 113 us -> 113 us (level)
  waiting for transfers between devices: 58.7 us -> 55.9 us
  Pallas kernels: 16 us -> 17.4 us
    pallas_call x1, Pallas kernels: 6.37 us -> 7.82 us  [attend(): pl.pallas_call(functools.partial(attend_kernel, scale=scale), in_specs=[s...]
    ppermute x28, waiting for transfers between devices: 31.5 us -> 30.1 us  [swap(): return lax.ppermute(x, 'gx', [(i, i ^ mask) for i in range(2 * CHIPS)])]
    ppermute x2, waiting for transfers between devices: 8.95 us -> 7.78 us  [outer(): return lax.ppermute(x, 'gy', [(0, 1), (1, 0), (2, 3), (3, 2)])]
  transfers between devices with their start and end apart: 38 -> 38, of which waited for: 17 -> 18; matrix products, arithmetic and copies ran while one was open for 5% -> 5% of each run, Pallas kernels for 5% -> 5%
where the time goes in v7:
time: 113 us; the launch traced here: 112 us
  waiting for transfers between devices  55.9 us (49%)
  starting transfers between devices  32.4 us (29%)
  Pallas kernels  17.4 us (15%)
  local copies, waits for them, and re-layouts  3.79 us (3%)
  other arithmetic  1.68 us (1%)
    ppermute x28, waiting for transfers between devices, swap(): return lax.ppermute(x, 'gx', [(i, i ^ mask) for i in range(2 * CHIPS)])  30.1 us
    ppermute x28, starting transfers between devices, swap(): return lax.ppermute(x, 'gx', [(i, i ^ mask) for i in range(2 * CHIPS)])  19.1 us
    ppermute x4, waiting for transfers between devices, outward(): return lax.ppermute(x, 'gy', [(1, 0), (2, 3)])  18.1 us
    pallas_call x1, Pallas kernels, attend(): pl.pallas_call(functools.partial(attend_kernel, scale=scale), in_specs=[s...  7.82 us
    ppermute x2, waiting for transfers between devices, outer(): return lax.ppermute(x, 'gy', [(0, 1), (1, 0), (2, 3), (3, 2)])  7.78 us
    ppermute x2, starting transfers between devices, outer(): return lax.ppermute(x, 'gy', [(0, 1), (1, 0), (2, 3), (3, 2)])  5.43 us
    ppermute x4, starting transfers between devices, outward(): return lax.ppermute(x, 'gy', [(1, 0), (2, 3)])  5.17 us
    pallas_call x2, Pallas kernels, project(): pl.pallas_call(functools.partial(project_kernel, pair=pair), in_specs=[sm...  5.15 us
  transfers between devices with their start and end apart: 38, of which 18 were waited for; matrix products, arithmetic and copies ran while one was open for 5% of the time, Pallas kernels for 5%

profile of v7, /device:TPU:0, one launch (start us, length us, event | category | flops | bytes accessed | tf_op | source)
XLA Modules:
  0.0 112.2 jit_solution(1922362555169065331)
XLA Ops:
  0.6 3.1 %collective-permute-start = (bf16[384,512]{1,0:T(8,128)(2,1)}, bf16[384,512]{1,0:T(8,128)(2,1)S(1)}, u32[]{:S(2)}, u32[]{:S(2)}) collective-permute-start(bf16[384,512]{1,0:T(8,128)(2,1)} %refs_0_.1), channel_id=1, source_target_pairs={{0,1},{1,0},{2,3},{3,2},{4,5},{5,4},{6,7},{7,6},{8,9},{9,8},{10,11... | collective-permute-start | bytes 1179656 | tf_op jit(solution)/shard_map/ppermute | solution.py:121
  3.7 0.7 collective-permute-start.1
  4.4 1.7 %reshape.193.refs_0_ = bf16[256,1536]{1,0:T(8,128)(2,1)S(1)} reshape(bf16[256,3,4,128]{3,2,1,0:T(4,128)(2,1)} %param.7) | data formatting | bytes 1572864 | tf_op jit(solution)/shard_map/reshape | solution.py:409
  6.1 1.6 %collective-permute-start.5 = (bf16[256,1536]{1,0:T(8,128)(2,1)S(1)}, bf16[256,1536]{1,0:T(8,128)(2,1)S(1)}, u32[]{:S(2)}, u32[]{:S(2)}) collective-permute-start(bf16[256,1536]{1,0:T(8,128)(2,1)S(1)} %reshape.193.refs_0_), channel_id=1, source_target_pairs={{0,8},{4,12},{8,0},{12,4},{16,24},{20,28},{24,16},{28,20},{1,9},{5... | collective-permute-start | bytes 2359304 | tf_op jit(solution)/shard_map/ppermute | solution.py:117
  7.6 1.5 %collective-permute-start.6 = (bf16[256,1536]{1,0:T(8,128)(2,1)S(1)}, bf16[256,1536]{1,0:T(8,128)(2,1)S(1)}, u32[]{:S(2)}, u32[]{:S(2)}) collective-permute-start(bf16[256,1536]{1,0:T(8,128)(2,1)S(1)} %reshape.193.refs_0_), channel_id=1, source_target_pairs={{0,16},{4,20},{8,24},{12,28},{16,0},{20,4},{24,8},{28,12},{1,17},{... | collective-permute-start | bytes 2359304 | tf_op jit(solution)/shard_map/ppermute | solution.py:117
  9.2 0.2 reduce-window.9
  9.4 0.1 select_reduce_fusion
  9.5 0.1 pad_add_fusion.where_ref
  9.6 0.8 fusion
  10.3 0.2 pad_maximum_fusion.3
  10.5 2.5 %collective-permute-done.refs_1_ = bf16[384,512]{1,0:T(8,128)(2,1)S(1)} collective-permute-done((bf16[384,512]{1,0:T(8,128)(2,1)}, bf16[384,512]{1,0:T(8,128)(2,1)S(1)}, u32[]{:S(2)}, u32[]{:S(2)}) %collective-permute-start) | collective-permute-done | bytes 393248 | tf_op jit(solution)/shard_map/ppermute | solution.py:121
  13.1 0.7 collective-permute-start.3
  13.7 1.3 %collective-permute-start.2 = (bf16[384,512]{1,0:T(8,128)(2,1)S(1)}, bf16[384,512]{1,0:T(8,128)(2,1)S(1)}, u32[]{:S(2)}, u32[]{:S(2)}) collective-permute-start(bf16[384,512]{1,0:T(8,128)(2,1)S(1)} %collective-permute-done.1.refs_2_), channel_id=1, source_target_pairs={{1,0},{2,3},{5,4},{6,7},{9,8},{10,11},{13,12},{14,15},{17,16},{18,... | collective-permute-start | bytes 1179656 | tf_op jit(solution)/shard_map/ppermute | solution.py:129
  15.1 1.3 %collective-permute-start.4 = (bf16[384,512]{1,0:T(8,128)(2,1)S(1)}, bf16[384,512]{1,0:T(8,128)(2,1)S(1)}, u32[]{:S(2)}, u32[]{:S(2)}) collective-permute-start(bf16[384,512]{1,0:T(8,128)(2,1)S(1)} %collective-permute-done.3.refs_4_), channel_id=1, source_target_pairs={{1,0},{2,3},{5,4},{6,7},{9,8},{10,11},{13,12},{14,15},{17,16},{18,... | collective-permute-start | bytes 1179656 | tf_op jit(solution)/shard_map/ppermute | solution.py:129
  16.4 8.8 %collective-permute-done.5.x_ref.refs_1_ = bf16[256,1536]{1,0:T(8,128)(2,1)S(1)} collective-permute-done((bf16[256,1536]{1,0:T(8,128)(2,1)S(1)}, bf16[256,1536]{1,0:T(8,128)(2,1)S(1)}, u32[]{:S(2)}, u32[]{:S(2)}) %collective-permute-start.5) | collective-permute-done | bytes 786464 | tf_op jit(solution)/shard_map/ppermute | solution.py:117
  25.1 1.2 %collective-permute-done.6.y_ref.refs_2_ = bf16[256,1536]{1,0:T(8,128)(2,1)S(1)} collective-permute-done((bf16[256,1536]{1,0:T(8,128)(2,1)S(1)}, bf16[256,1536]{1,0:T(8,128)(2,1)S(1)}, u32[]{:S(2)}, u32[]{:S(2)}) %collective-permute-start.6) | collective-permute-done | bytes 786464 | tf_op jit(solution)/shard_map/ppermute | solution.py:117
  26.4 0.6 collective-permute-start.7
  27.0 1.5 %collective-permute-start.8 = (bf16[128,1536]{1,0:T(8,128)(2,1)S(1)}, bf16[128,1536]{1,0:T(8,128)(2,1)S(1)}, u32[]{:S(2)}, u32[]{:S(2)}) collective-permute-start(bf16[128,1536]{1,0:T(8,128)(2,1)S(1)} %get-tuple-element.31), channel_id=1, source_target_pairs={{0,16},{4,20},{8,24},{12,28},{16,0},{20,4},{24,8},{28,12},{1,17},{... | collective-permute-start | bytes 1179656 | tf_op jit(solution)/shard_map/ppermute | solution.py:117
  28.5 0.5 collective-permute-start.10
  29.1 6.9 %collective-permute-done.4.refs_5_ = bf16[384,512]{1,0:T(8,128)(2,1)S(1)} collective-permute-done((bf16[384,512]{1,0:T(8,128)(2,1)S(1)}, bf16[384,512]{1,0:T(8,128)(2,1)S(1)}, u32[]{:S(2)}, u32[]{:S(2)}) %collective-permute-start.4) | collective-permute-done | bytes 393248 | tf_op jit(solution)/shard_map/ppermute | solution.py:129
  36.0 0.5 collective-permute-start.12
  36.5 0.1 collective-permute-start.13
  36.5 1.3 %normalize.1.x_ref = bf16[384,2048]{1,0:T(8,128)(2,1)S(1)} custom-call(s32[3]{0:T(128)S(1)} %pad_add_fusion.where_ref, bf16[384,512]{1,0:T(8,128)(2,1)S(1)} %copy-done, bf16[384,512]{1,0:T(8,128)(2,1)S(1)} %collective-permute-done.refs_1_, bf16[384,512]{1,0:T(8,128)(2,1)S(1)} %collective-permute-done.1.refs_2_, ...), custom_call_target="tpu_custom_call" | custom-call | flops 8589934592 | bytes 8388608 | tf_op jit(solution)/shard_map/normalize/pallas_call | solution.py:197
  37.8 1.0 collective-permute-done.12.refs_8_
  38.8 0.6 collective-permute-done.13.refs_9_
  39.4 2.6 %project.3 = (bf16[3,384,128]{2,1,0:T(8,128)(2,1)S(1)}, bf16[3,384,128]{2,1,0:T(8,128)(2,1)S(1)}) custom-call(s32[3]{0:T(128)S(1)} %pad_add_fusion.where_ref, bf16[384,2048]{1,0:T(8,128)(2,1)S(1)} %normalize.1.x_ref, f32[384,128]{1,0:T(8,128)S(1)} %get-tuple-element.28.cos_ref, f32[384,128]{1,0:T(8,128)S(1)} %get-tuple-element.29.sin_ref, ...), custom_call_target="tpu_custom_call" | custom-call | flops 1207959552 | bytes 8388608 | tf_op jit(solution)/shard_map/project/pallas_call | solution.py:238
  42.0 1.6 %collective-permute-start.14 = (bf16[3,384,128]{2,1,0:T(8,128)(2,1)S(1)}, bf16[3,384,128]{2,1,0:T(8,128)(2,1)S(1)}, u32[]{:S(2)}, u32[]{:S(2)}) collective-permute-start(bf16[3,384,128]{2,1,0:T(8,128)(2,1)S(1)} %get-tuple-element.33), channel_id=1, source_target_pairs={{0,8},{4,12},{8,0},{12,4},{16,24},{20,28},{24,16},{28,20},{1,9},{5... | collective-permute-start | bytes 884744 | tf_op jit(solution)/shard_map/ppermute | solution.py:117
  43.5 1.5 %collective-permute-start.15 = (bf16[3,384,128]{2,1,0:T(8,128)(2,1)S(1)}, bf16[3,384,128]{2,1,0:T(8,128)(2,1)S(1)}, u32[]{:S(2)}, u32[]{:S(2)}) collective-permute-start(bf16[3,384,128]{2,1,0:T(8,128)(2,1)S(1)} %get-tuple-element.34), channel_id=1, source_target_pairs={{0,16},{4,20},{8,24},{12,28},{16,0},{20,4},{24,8},{28,12},{1,17},{... | collective-permute-start | bytes 884744 | tf_op jit(solution)/shard_map/ppermute | solution.py:117
  45.0 2.6 %project.2 = (bf16[3,384,128]{2,1,0:T(8,128)(2,1)S(1)}, bf16[3,384,128]{2,1,0:T(8,128)(2,1)S(1)}) custom-call(s32[3]{0:T(128)S(1)} %pad_add_fusion.where_ref, bf16[384,2048]{1,0:T(8,128)(2,1)S(1)} %normalize.1.x_ref, f32[384,128]{1,0:T(8,128)S(1)} %get-tuple-element.28.cos_ref, f32[384,128]{1,0:T(8,128)S(1)} %get-tuple-element.29.sin_ref, ...), custom_call_target="tpu_custom_call" | custom-call | flops 1207959552 | bytes 8388608 | tf_op jit(solution)/shard_map/project/pallas_call | solution.py:238
  47.6 0.5 collective-permute-start.16
  48.2 3.7 %collective-permute-done.14.refs_1_ = bf16[3,384,128]{2,1,0:T(8,128)(2,1)S(1)} collective-permute-done((bf16[3,384,128]{2,1,0:T(8,128)(2,1)S(1)}, bf16[3,384,128]{2,1,0:T(8,128)(2,1)S(1)}, u32[]{:S(2)}, u32[]{:S(2)}) %collective-permute-start.14) | collective-permute-done | bytes 294944 | tf_op jit(solution)/shard_map/ppermute | solution.py:117
  51.9 6.7 %collective-permute-done.15.refs_2_ = bf16[3,384,128]{2,1,0:T(8,128)(2,1)S(1)} collective-permute-done((bf16[3,384,128]{2,1,0:T(8,128)(2,1)S(1)}, bf16[3,384,128]{2,1,0:T(8,128)(2,1)S(1)}, u32[]{:S(2)}, u32[]{:S(2)}) %collective-permute-start.15) | collective-permute-done | bytes 294944 | tf_op jit(solution)/shard_map/ppermute | solution.py:117
  58.6 0.5 collective-permute-start.20
  59.1 1.1 collective-permute-done.19.refs_6_
  60.2 0.4 collective-permute-done.20.refs_7_
  60.6 7.8 %attend.1 = (bf16[384,128]{1,0:T(8,128)(2,1)S(1)}, bf16[384,128]{1,0:T(8,128)(2,1)S(1)}, bf16[384,128]{1,0:T(8,128)(2,1)S(1)}, bf16[384,128]{1,0:T(8,128)(2,1)S(1)}) custom-call(s32[3]{0:T(128)S(1)} %pad_add_fusion.where_ref, s32[6]{0:T(128)S(1)} %bitcast_subtract_fusion.start_ref, bf16[3,384,128]{2,1,0:T(8,128)(2,1)S(1)} %get-tuple-element.32.refs_0_, ...), custom_call_target="tpu_custom_call" | custom-call | flops 2415919104 | bytes 8388608 | tf_op jit(solution)/shard_map/attend/pallas_call | solution.py:309
  68.4 1.5 %collective-permute-start.21 = (bf16[384,128]{1,0:T(8,128)(2,1)S(1)}, bf16[384,128]{1,0:T(8,128)(2,1)S(1)}, u32[]{:S(2)}, u32[]{:S(2)}) collective-permute-start(bf16[384,128]{1,0:T(8,128)(2,1)S(1)} %get-tuple-element.36), channel_id=1, source_target_pairs={{0,24},{4,28},{8,16},{12,20},{16,8},{20,12},{24,0},{28,4},{1,25},{... | collective-permute-start | bytes 294920 | tf_op jit(solution)/shard_map/ppermute | solution.py:117
  70.0 0.8 collective-permute-start.22
  70.8 1.2 %collective-permute-start.23 = (bf16[384,128]{1,0:T(8,128)(2,1)S(1)}, bf16[384,128]{1,0:T(8,128)(2,1)S(1)}, u32[]{:S(2)}, u32[]{:S(2)}) collective-permute-start(bf16[384,128]{1,0:T(8,128)(2,1)S(1)} %get-tuple-element.38), channel_id=1, source_target_pairs={{0,8},{4,12},{8,0},{12,4},{16,24},{20,28},{24,16},{28,20},{1,9},{5... | collective-permute-start | bytes 294920 | tf_op jit(solution)/shard_map/ppermute | solution.py:117
  72.0 3.0 %collective-permute-done.21 = bf16[384,128]{1,0:T(8,128)(2,1)S(1)} collective-permute-done((bf16[384,128]{1,0:T(8,128)(2,1)S(1)}, bf16[384,128]{1,0:T(8,128)(2,1)S(1)}, u32[]{:S(2)}, u32[]{:S(2)}) %collective-permute-start.21) | collective-permute-done | bytes 98336 | tf_op jit(solution)/shard_map/ppermute | solution.py:117
  75.0 0.8 collective-permute-done.22
  75.8 0.1 collective-permute-done.23
  75.9 0.1 broadcast_select_fusion.5
  76.0 2.3 %collective-permute-start.24 = (bf16[384,512]{1,0:T(8,128)(2,1)S(1)}, bf16[384,512]{1,0:T(8,128)(2,1)S(1)}, u32[]{:S(2)}, u32[]{:S(2)}) collective-permute-start(bf16[384,512]{1,0:T(8,128)(2,1)S(1)} %pad_maximum_fusion.own), channel_id=1, source_target_pairs={{0,1},{1,0},{2,3},{3,2},{4,5},{5,4},{6,7},{7,6},{8,9},{9,8},{10,11... | collective-permute-start | bytes 1179656 | tf_op jit(solution)/shard_map/ppermute | solution.py:121
  78.4 0.9 collective-permute-start.28
  79.2 1.4 %collective-permute-start.29 = (bf16[256,512]{1,0:T(8,128)(2,1)S(1)}, bf16[256,512]{1,0:T(8,128)(2,1)S(1)}, u32[]{:S(2)}, u32[]{:S(2)}) collective-permute-start(bf16[256,512]{1,0:T(8,128)(2,1)S(1)} %copy-done.1), channel_id=1, source_target_pairs={{0,16},{4,20},{8,24},{12,28},{16,0},{20,4},{24,8},{28,12},{1,17},{... | collective-permute-start | bytes 786440 | tf_op jit(solution)/shard_map/ppermute | solution.py:117
  80.6 0.7 collective-permute-start.27
  81.3 0.1 collective-permute-start.33
  81.4 5.2 %collective-permute-done.24.near = bf16[384,512]{1,0:T(8,128)(2,1)S(1)} collective-permute-done((bf16[384,512]{1,0:T(8,128)(2,1)S(1)}, bf16[384,512]{1,0:T(8,128)(2,1)S(1)}, u32[]{:S(2)}, u32[]{:S(2)}) %collective-permute-start.24) | collective-permute-done | bytes 393248 | tf_op jit(solution)/shard_map/ppermute | solution.py:121
  86.6 0.7 collective-permute-start.25
  87.4 0.1 collective-permute-start.34
  87.5 1.3 %collective-permute-start.30 = (bf16[384,512]{1,0:T(8,128)(2,1)S(1)}, bf16[384,512]{1,0:T(8,128)(2,1)S(1)}, u32[]{:S(2)}, u32[]{:S(2)}) collective-permute-start(bf16[384,512]{1,0:T(8,128)(2,1)S(1)} %collective-permute-done.27.q1), channel_id=1, source_target_pairs={{1,0},{2,3},{5,4},{6,7},{9,8},{10,11},{13,12},{14,15},{17,16},{18,... | collective-permute-start | bytes 1179656 | tf_op jit(solution)/shard_map/ppermute | solution.py:129
  88.8 1.3 %collective-permute-start.31 = (bf16[128,512]{1,0:T(8,128)(2,1)S(1)}, bf16[128,512]{1,0:T(8,128)(2,1)S(1)}, u32[]{:S(2)}, u32[]{:S(2)}) collective-permute-start(bf16[128,512]{1,0:T(8,128)(2,1)S(1)} %get-tuple-element.45), channel_id=1, source_target_pairs={{0,8},{4,12},{8,0},{12,4},{16,24},{20,28},{24,16},{28,20},{1,9},{5... | collective-permute-start | bytes 393224 | tf_op jit(solution)/shard_map/ppermute | solution.py:117
  90.1 1.4 %collective-permute-start.32 = (bf16[128,512]{1,0:T(8,128)(2,1)S(1)}, bf16[128,512]{1,0:T(8,128)(2,1)S(1)}, u32[]{:S(2)}, u32[]{:S(2)}) collective-permute-start(bf16[128,512]{1,0:T(8,128)(2,1)S(1)} %get-tuple-element.46), channel_id=1, source_target_pairs={{0,16},{4,20},{8,24},{12,28},{16,0},{20,4},{24,8},{28,12},{1,17},{... | collective-permute-start | bytes 393224 | tf_op jit(solution)/shard_map/ppermute | solution.py:117
  91.6 0.1 collective-permute-start.35
  91.6 1.3 %collective-permute-start.26 = (bf16[384,512]{1,0:T(8,128)(2,1)S(1)}, bf16[384,512]{1,0:T(8,128)(2,1)S(1)}, u32[]{:S(2)}, u32[]{:S(2)}) collective-permute-start(bf16[384,512]{1,0:T(8,128)(2,1)S(1)} %collective-permute-done.25.q2), channel_id=1, source_target_pairs={{1,0},{2,3},{5,4},{6,7},{9,8},{10,11},{13,12},{14,15},{17,16},{18,... | collective-permute-start | bytes 1179656 | tf_op jit(solution)/shard_map/ppermute | solution.py:129
  93.0 1.8 %collective-permute-done.31.refs_3_ = bf16[128,512]{1,0:T(8,128)(2,1)S(1)} collective-permute-done((bf16[128,512]{1,0:T(8,128)(2,1)S(1)}, bf16[128,512]{1,0:T(8,128)(2,1)S(1)}, u32[]{:S(2)}, u32[]{:S(2)}) %collective-permute-start.31) | collective-permute-done | bytes 131104 | tf_op jit(solution)/shard_map/ppermute | solution.py:117
  94.8 0.9 collective-permute-done.32.refs_4_
  95.8 1.1 copy.11
  96.9 1.1 copy.10
  97.9 4.7 %collective-permute-done.30.p2 = bf16[384,512]{1,0:T(8,128)(2,1)S(1)} collective-permute-done((bf16[384,512]{1,0:T(8,128)(2,1)S(1)}, bf16[384,512]{1,0:T(8,128)(2,1)S(1)}, u32[]{:S(2)}, u32[]{:S(2)}) %collective-permute-start.30) | collective-permute-done | bytes 393248 | tf_op jit(solution)/shard_map/ppermute | solution.py:129
  102.7 1.5 %early.1 = (f32[384,512]{1,0:T(8,128)S(1)}, bf16[512,512]{1,0:T(8,128)(2,1)S(1)}) custom-call(s32[3]{0:T(128)S(1)} %pad_add_fusion.where_ref, bf16[384,512]{1,0:T(8,128)(2,1)S(1)} %pad_maximum_fusion.own, bf16[384,512]{1,0:T(8,128)(2,1)S(1)} %collective-permute-done.24.near, bf16[384,512]{1,0:T(8,128)(2,1)S(1)} %collective-permute-done.27.q1, ...), custom_call_target="tpu_custom_call" | custom-call | flops 1073741824 | bytes 8388608 | tf_op jit(solution)/shard_map/early/pallas_call | solution.py:349
  104.1 6.4 %collective-permute-done.26.p3 = bf16[384,512]{1,0:T(8,128)(2,1)S(1)} collective-permute-done((bf16[384,512]{1,0:T(8,128)(2,1)S(1)}, bf16[384,512]{1,0:T(8,128)(2,1)S(1)}, u32[]{:S(2)}, u32[]{:S(2)}) %collective-permute-start.26) | collective-permute-done | bytes 393248 | tf_op jit(solution)/shard_map/ppermute | solution.py:129
  110.6 1.7 %last.1 = bf16[384,512]{1,0:T(8,128)(2,1)} custom-call(s32[3]{0:T(128)S(1)} %pad_add_fusion.where_ref, bf16[384,512]{1,0:T(8,128)(2,1)S(1)} %collective-permute-done.25.q2, bf16[384,512]{1,0:T(8,128)(2,1)S(1)} %collective-permute-done.26.p3, f32[384,512]{1,0:T(8,128)S(1)} %get-tuple-element.47.total_ref, bf16[512,512]{1,0:T(8,128)(2,1)S(1)} %get-tuple-element.48.w_ref), custom_call_target="tpu_custom_call" | custom-call | flops 201326592 | bytes 8388608 | tf_op jit(solution)/shard_map/last/pallas_call | solution.py:372
  (50 shorter events, 0.5 us)
Async XLA Ops:
  0.6 8.5 %copy-start.3 = (s32[6]{0:T(128)S(1)}, s32[6]{0:T(128)}, u32[]{:S(2)}) copy-start(s32[6]{0:T(128)} %param.9) | copy-start | bytes 76
  0.6 12.4 %collective-permute-start = (bf16[384,512]{1,0:T(8,128)(2,1)}, bf16[384,512]{1,0:T(8,128)(2,1)S(1)}, u32[]{:S(2)}, u32[]{:S(2)}) collective-permute-start(bf16[384,512]{1,0:T(8,128)(2,1)} %refs_0_.1), channel_id=1, source_target_pairs={{0,1},{1,0},{2,3},{3,2},{4,5},{5,4},{6,7},{7,6},{8,9},{9,8},{10,11... | collective-permute-start | bytes 1179656 | tf_op jit(solution)/shard_map/ppermute | solution.py:121
  3.7 10.0 %collective-permute-start.1 = (bf16[384,512]{1,0:T(8,128)(2,1)}, bf16[384,512]{1,0:T(8,128)(2,1)S(1)}, u32[]{:S(2)}, u32[]{:S(2)}) collective-permute-start(bf16[384,512]{1,0:T(8,128)(2,1)} %refs_0_.1), channel_id=1, source_target_pairs={{1,2},{2,1},{5,6},{6,5},{9,10},{10,9},{13,14},{14,13},{17,18},{18,... | collective-permute-start | bytes 1179656 | tf_op jit(solution)/shard_map/ppermute | solution.py:125
  6.1 19.1 %collective-permute-start.5 = (bf16[256,1536]{1,0:T(8,128)(2,1)S(1)}, bf16[256,1536]{1,0:T(8,128)(2,1)S(1)}, u32[]{:S(2)}, u32[]{:S(2)}) collective-permute-start(bf16[256,1536]{1,0:T(8,128)(2,1)S(1)} %reshape.193.refs_0_), channel_id=1, source_target_pairs={{0,8},{4,12},{8,0},{12,4},{16,24},{20,28},{24,16},{28,20},{1,9},{5... | collective-permute-start | bytes 2359304 | tf_op jit(solution)/shard_map/ppermute | solution.py:117
  7.6 18.7 %collective-permute-start.6 = (bf16[256,1536]{1,0:T(8,128)(2,1)S(1)}, bf16[256,1536]{1,0:T(8,128)(2,1)S(1)}, u32[]{:S(2)}, u32[]{:S(2)}) collective-permute-start(bf16[256,1536]{1,0:T(8,128)(2,1)S(1)} %reshape.193.refs_0_), channel_id=1, source_target_pairs={{0,16},{4,20},{8,24},{12,28},{16,0},{20,4},{24,8},{28,12},{1,17},{... | collective-permute-start | bytes 2359304 | tf_op jit(solution)/shard_map/ppermute | solution.py:117
  9.6 27.0 %copy-start = (bf16[384,512]{1,0:T(8,128)(2,1)S(1)}, bf16[384,512]{1,0:T(8,128)(2,1)}, u32[]{:S(2)}) copy-start(bf16[384,512]{1,0:T(8,128)(2,1)} %refs_0_.1) | copy-start | bytes 1179652
  9.6 27.0 %copy-start.2 = (f32[2048]{0:T(1024)S(1)}, f32[2048]{0:T(1024)}, u32[]{:S(2)}) copy-start(f32[2048]{0:T(1024)} %param.6) | copy-start | bytes 24580
  13.1 2.0 %collective-permute-start.3 = (bf16[384,512]{1,0:T(8,128)(2,1)S(1)}, bf16[384,512]{1,0:T(8,128)(2,1)S(1)}, u32[]{:S(2)}, u32[]{:S(2)}) collective-permute-start(bf16[384,512]{1,0:T(8,128)(2,1)S(1)} %collective-permute-done.refs_1_), channel_id=1, source_target_pairs={{1,2},{2,1},{5,6},{6,5},{9,10},{10,9},{13,14},{14,13},{17,18},{18,... | collective-permute-start | bytes 1179656 | tf_op jit(solution)/shard_map/ppermute | solution.py:125
  13.7 14.8 %collective-permute-start.2 = (bf16[384,512]{1,0:T(8,128)(2,1)S(1)}, bf16[384,512]{1,0:T(8,128)(2,1)S(1)}, u32[]{:S(2)}, u32[]{:S(2)}) collective-permute-start(bf16[384,512]{1,0:T(8,128)(2,1)S(1)} %collective-permute-done.1.refs_2_), channel_id=1, source_target_pairs={{1,0},{2,3},{5,4},{6,7},{9,8},{10,11},{13,12},{14,15},{17,16},{18,... | collective-permute-start | bytes 1179656 | tf_op jit(solution)/shard_map/ppermute | solution.py:129
  15.1 20.9 %collective-permute-start.4 = (bf16[384,512]{1,0:T(8,128)(2,1)S(1)}, bf16[384,512]{1,0:T(8,128)(2,1)S(1)}, u32[]{:S(2)}, u32[]{:S(2)}) collective-permute-start(bf16[384,512]{1,0:T(8,128)(2,1)S(1)} %collective-permute-done.3.refs_4_), channel_id=1, source_target_pairs={{1,0},{2,3},{5,4},{6,7},{9,8},{10,11},{13,12},{14,15},{17,16},{18,... | collective-permute-start | bytes 1179656 | tf_op jit(solution)/shard_map/ppermute | solution.py:129
  26.4 9.5 %collective-permute-start.7 = (bf16[128,1536]{1,0:T(8,128)(2,1)S(1)}, bf16[128,1536]{1,0:T(8,128)(2,1)S(1)}, u32[]{:S(2)}, u32[]{:S(2)}) collective-permute-start(bf16[128,1536]{1,0:T(8,128)(2,1)S(1)} %get-tuple-element.30), channel_id=1, source_target_pairs={{0,8},{4,12},{8,0},{12,4},{16,24},{20,28},{24,16},{28,20},{1,9},{5... | collective-permute-start | bytes 1179656 | tf_op jit(solution)/shard_map/ppermute | solution.py:117
  27.0 9.4 %collective-permute-start.8 = (bf16[128,1536]{1,0:T(8,128)(2,1)S(1)}, bf16[128,1536]{1,0:T(8,128)(2,1)S(1)}, u32[]{:S(2)}, u32[]{:S(2)}) collective-permute-start(bf16[128,1536]{1,0:T(8,128)(2,1)S(1)} %get-tuple-element.31), channel_id=1, source_target_pairs={{0,16},{4,20},{8,24},{12,28},{16,0},{20,4},{24,8},{28,12},{1,17},{... | collective-permute-start | bytes 1179656 | tf_op jit(solution)/shard_map/ppermute | solution.py:117
  28.5 9.3 %collective-permute-start.9 = (bf16[256,1536]{1,0:T(8,128)(2,1)S(1)}, bf16[256,1536]{1,0:T(8,128)(2,1)S(1)}, u32[]{:S(2)}, u32[]{:S(2)}) collective-permute-start(bf16[256,1536]{1,0:T(8,128)(2,1)S(1)} %reshape.193.refs_0_), channel_id=1, source_target_pairs={{0,4},{4,0},{8,12},{12,8},{16,20},{20,16},{24,28},{28,24},{1,5},{5... | collective-permute-start | bytes 2359304 | tf_op jit(solution)/shard_map/ppermute | solution.py:117
  28.5 10.8 %collective-permute-start.10 = (bf16[256,1536]{1,0:T(8,128)(2,1)S(1)}, bf16[256,1536]{1,0:T(8,128)(2,1)S(1)}, u32[]{:S(2)}, u32[]{:S(2)}) collective-permute-start(bf16[256,1536]{1,0:T(8,128)(2,1)S(1)} %collective-permute-done.5.x_ref.refs_1_), channel_id=1, source_target_pairs={{0,4},{4,0},{8,12},{12,8},{16,20},{20,16},{24,28},{28,24},{1,5},{5... | collective-permute-start | bytes 2359304 | tf_op jit(solution)/shard_map/ppermute | solution.py:117
  36.0 3.4 %collective-permute-start.11 = (bf16[256,1536]{1,0:T(8,128)(2,1)S(1)}, bf16[256,1536]{1,0:T(8,128)(2,1)S(1)}, u32[]{:S(2)}, u32[]{:S(2)}) collective-permute-start(bf16[256,1536]{1,0:T(8,128)(2,1)S(1)} %collective-permute-done.6.y_ref.refs_2_), channel_id=1, source_target_pairs={{0,4},{4,0},{8,12},{12,8},{16,20},{20,16},{24,28},{28,24},{1,5},{5... | collective-permute-start | bytes 2359304 | tf_op jit(solution)/shard_map/ppermute | solution.py:117
  36.0 2.8 %collective-permute-start.12 = (bf16[128,1536]{1,0:T(8,128)(2,1)S(1)}, bf16[128,1536]{1,0:T(8,128)(2,1)S(1)}, u32[]{:S(2)}, u32[]{:S(2)}) collective-permute-start(bf16[128,1536]{1,0:T(8,128)(2,1)S(1)} %collective-permute-done.7.refs_3_), channel_id=1, source_target_pairs={{0,4},{4,0},{8,12},{12,8},{16,20},{20,16},{24,28},{28,24},{1,5},{5... | collective-permute-start | bytes 1179656 | tf_op jit(solution)/shard_map/ppermute | solution.py:117
  36.5 2.9 %collective-permute-start.13 = (bf16[128,1536]{1,0:T(8,128)(2,1)S(1)}, bf16[128,1536]{1,0:T(8,128)(2,1)S(1)}, u32[]{:S(2)}, u32[]{:S(2)}) collective-permute-start(bf16[128,1536]{1,0:T(8,128)(2,1)S(1)} %collective-permute-done.8.refs_4_), channel_id=1, source_target_pairs={{0,4},{4,0},{8,12},{12,8},{16,20},{20,16},{24,28},{28,24},{1,5},{5... | collective-permute-start | bytes 1179656 | tf_op jit(solution)/shard_map/ppermute | solution.py:117
  42.0 9.9 %collective-permute-start.14 = (bf16[3,384,128]{2,1,0:T(8,128)(2,1)S(1)}, bf16[3,384,128]{2,1,0:T(8,128)(2,1)S(1)}, u32[]{:S(2)}, u32[]{:S(2)}) collective-permute-start(bf16[3,384,128]{2,1,0:T(8,128)(2,1)S(1)} %get-tuple-element.33), channel_id=1, source_target_pairs={{0,8},{4,12},{8,0},{12,4},{16,24},{20,28},{24,16},{28,20},{1,9},{5... | collective-permute-start | bytes 884744 | tf_op jit(solution)/shard_map/ppermute | solution.py:117
  43.5 15.1 %collective-permute-start.15 = (bf16[3,384,128]{2,1,0:T(8,128)(2,1)S(1)}, bf16[3,384,128]{2,1,0:T(8,128)(2,1)S(1)}, u32[]{:S(2)}, u32[]{:S(2)}) collective-permute-start(bf16[3,384,128]{2,1,0:T(8,128)(2,1)S(1)} %get-tuple-element.34), channel_id=1, source_target_pairs={{0,16},{4,20},{8,24},{12,28},{16,0},{20,4},{24,8},{28,12},{1,17},{... | collective-permute-start | bytes 884744 | tf_op jit(solution)/shard_map/ppermute | solution.py:117
  47.6 11.0 %collective-permute-start.16 = (bf16[3,384,128]{2,1,0:T(8,128)(2,1)S(1)}, bf16[3,384,128]{2,1,0:T(8,128)(2,1)S(1)}, u32[]{:S(2)}, u32[]{:S(2)}) collective-permute-start(bf16[3,384,128]{2,1,0:T(8,128)(2,1)S(1)} %get-tuple-element.35), channel_id=1, source_target_pairs={{0,24},{4,28},{8,16},{12,20},{16,8},{20,12},{24,0},{28,4},{1,25},{... | collective-permute-start | bytes 884744 | tf_op jit(solution)/shard_map/ppermute | solution.py:117
  48.2 11.0 %collective-permute-start.17 = (bf16[3,384,128]{2,1,0:T(8,128)(2,1)S(1)}, bf16[3,384,128]{2,1,0:T(8,128)(2,1)S(1)}, u32[]{:S(2)}, u32[]{:S(2)}) collective-permute-start(bf16[3,384,128]{2,1,0:T(8,128)(2,1)S(1)} %get-tuple-element.32.refs_0_), channel_id=1, source_target_pairs={{0,4},{4,0},{8,12},{12,8},{16,20},{20,16},{24,28},{28,24},{1,5},{5... | collective-permute-start | bytes 884744 | tf_op jit(solution)/shard_map/ppermute | solution.py:117
  51.9 7.2 %collective-permute-start.18 = (bf16[3,384,128]{2,1,0:T(8,128)(2,1)S(1)}, bf16[3,384,128]{2,1,0:T(8,128)(2,1)S(1)}, u32[]{:S(2)}, u32[]{:S(2)}) collective-permute-start(bf16[3,384,128]{2,1,0:T(8,128)(2,1)S(1)} %collective-permute-done.14.refs_1_), channel_id=1, source_target_pairs={{0,4},{4,0},{8,12},{12,8},{16,20},{20,16},{24,28},{28,24},{1,5},{5... | collective-permute-start | bytes 884744 | tf_op jit(solution)/shard_map/ppermute | solution.py:117
  58.6 1.6 %collective-permute-start.19 = (bf16[3,384,128]{2,1,0:T(8,128)(2,1)S(1)}, bf16[3,384,128]{2,1,0:T(8,128)(2,1)S(1)}, u32[]{:S(2)}, u32[]{:S(2)}) collective-permute-start(bf16[3,384,128]{2,1,0:T(8,128)(2,1)S(1)} %collective-permute-done.15.refs_2_), channel_id=1, source_target_pairs={{0,4},{4,0},{8,12},{12,8},{16,20},{20,16},{24,28},{28,24},{1,5},{5... | collective-permute-start | bytes 884744 | tf_op jit(solution)/shard_map/ppermute | solution.py:117
  58.6 2.0 %collective-permute-start.20 = (bf16[3,384,128]{2,1,0:T(8,128)(2,1)S(1)}, bf16[3,384,128]{2,1,0:T(8,128)(2,1)S(1)}, u32[]{:S(2)}, u32[]{:S(2)}) collective-permute-start(bf16[3,384,128]{2,1,0:T(8,128)(2,1)S(1)} %collective-permute-done.16.refs_3_), channel_id=1, source_target_pairs={{0,4},{4,0},{8,12},{12,8},{16,20},{20,16},{24,28},{28,24},{1,5},{5... | collective-permute-start | bytes 884744 | tf_op jit(solution)/shard_map/ppermute | solution.py:117
  68.4 9.9 %copy-start.1 = (bf16[256,512]{1,0:T(8,128)(2,1)S(1)}, bf16[256,512]{1,0:T(8,128)(2,1)}, u32[]{:S(2)}) copy-start(bf16[256,512]{1,0:T(8,128)(2,1)} %refs_0_.2) | copy-start | bytes 786436
  68.4 6.6 %collective-permute-start.21 = (bf16[384,128]{1,0:T(8,128)(2,1)S(1)}, bf16[384,128]{1,0:T(8,128)(2,1)S(1)}, u32[]{:S(2)}, u32[]{:S(2)}) collective-permute-start(bf16[384,128]{1,0:T(8,128)(2,1)S(1)} %get-tuple-element.36), channel_id=1, source_target_pairs={{0,24},{4,28},{8,16},{12,20},{16,8},{20,12},{24,0},{28,4},{1,25},{... | collective-permute-start | bytes 294920 | tf_op jit(solution)/shard_map/ppermute | solution.py:117
  70.0 5.8 %collective-permute-start.22 = (bf16[384,128]{1,0:T(8,128)(2,1)S(1)}, bf16[384,128]{1,0:T(8,128)(2,1)S(1)}, u32[]{:S(2)}, u32[]{:S(2)}) collective-permute-start(bf16[384,128]{1,0:T(8,128)(2,1)S(1)} %get-tuple-element.37), channel_id=1, source_target_pairs={{0,16},{4,20},{8,24},{12,28},{16,0},{20,4},{24,8},{28,12},{1,17},{... | collective-permute-start | bytes 294920 | tf_op jit(solution)/shard_map/ppermute | solution.py:117
  70.8 5.1 %collective-permute-start.23 = (bf16[384,128]{1,0:T(8,128)(2,1)S(1)}, bf16[384,128]{1,0:T(8,128)(2,1)S(1)}, u32[]{:S(2)}, u32[]{:S(2)}) collective-permute-start(bf16[384,128]{1,0:T(8,128)(2,1)S(1)} %get-tuple-element.38), channel_id=1, source_target_pairs={{0,8},{4,12},{8,0},{12,4},{16,24},{20,28},{24,16},{28,20},{1,9},{5... | collective-permute-start | bytes 294920 | tf_op jit(solution)/shard_map/ppermute | solution.py:117
  76.0 10.6 %collective-permute-start.24 = (bf16[384,512]{1,0:T(8,128)(2,1)S(1)}, bf16[384,512]{1,0:T(8,128)(2,1)S(1)}, u32[]{:S(2)}, u32[]{:S(2)}) collective-permute-start(bf16[384,512]{1,0:T(8,128)(2,1)S(1)} %pad_maximum_fusion.own), channel_id=1, source_target_pairs={{0,1},{1,0},{2,3},{3,2},{4,5},{5,4},{6,7},{7,6},{8,9},{9,8},{10,11... | collective-permute-start | bytes 1179656 | tf_op jit(solution)/shard_map/ppermute | solution.py:121
  78.4 9.0 %collective-permute-start.28 = (bf16[256,512]{1,0:T(8,128)(2,1)S(1)}, bf16[256,512]{1,0:T(8,128)(2,1)S(1)}, u32[]{:S(2)}, u32[]{:S(2)}) collective-permute-start(bf16[256,512]{1,0:T(8,128)(2,1)S(1)} %copy-done.1), channel_id=1, source_target_pairs={{0,8},{4,12},{8,0},{12,4},{16,24},{20,28},{24,16},{28,20},{1,9},{5... | collective-permute-start | bytes 786440 | tf_op jit(solution)/shard_map/ppermute | solution.py:117
  79.2 8.3 %collective-permute-start.29 = (bf16[256,512]{1,0:T(8,128)(2,1)S(1)}, bf16[256,512]{1,0:T(8,128)(2,1)S(1)}, u32[]{:S(2)}, u32[]{:S(2)}) collective-permute-start(bf16[256,512]{1,0:T(8,128)(2,1)S(1)} %copy-done.1), channel_id=1, source_target_pairs={{0,16},{4,20},{8,24},{12,28},{16,0},{20,4},{24,8},{28,12},{1,17},{... | collective-permute-start | bytes 786440 | tf_op jit(solution)/shard_map/ppermute | solution.py:117
  80.6 6.9 %collective-permute-start.27 = (bf16[384,512]{1,0:T(8,128)(2,1)S(1)}, bf16[384,512]{1,0:T(8,128)(2,1)S(1)}, u32[]{:S(2)}, u32[]{:S(2)}) collective-permute-start(bf16[384,512]{1,0:T(8,128)(2,1)S(1)} %pad_maximum_fusion.own), channel_id=1, source_target_pairs={{1,2},{2,1},{5,6},{6,5},{9,10},{10,9},{13,14},{14,13},{17,18},{18,... | collective-permute-start | bytes 1179656 | tf_op jit(solution)/shard_map/ppermute | solution.py:125
  81.3 8.8 %collective-permute-start.33 = (bf16[256,512]{1,0:T(8,128)(2,1)S(1)}, bf16[256,512]{1,0:T(8,128)(2,1)S(1)}, u32[]{:S(2)}, u32[]{:S(2)}) collective-permute-start(bf16[256,512]{1,0:T(8,128)(2,1)S(1)} %copy-done.1), channel_id=1, source_target_pairs={{0,4},{4,0},{8,12},{12,8},{16,20},{20,16},{24,28},{28,24},{1,5},{5... | collective-permute-start | bytes 786440 | tf_op jit(solution)/shard_map/ppermute | solution.py:117
  86.6 5.0 %collective-permute-start.25 = (bf16[384,512]{1,0:T(8,128)(2,1)S(1)}, bf16[384,512]{1,0:T(8,128)(2,1)S(1)}, u32[]{:S(2)}, u32[]{:S(2)}) collective-permute-start(bf16[384,512]{1,0:T(8,128)(2,1)S(1)} %collective-permute-done.24.near), channel_id=1, source_target_pairs={{1,2},{2,1},{5,6},{6,5},{9,10},{10,9},{13,14},{14,13},{17,18},{18,... | collective-permute-start | bytes 1179656 | tf_op jit(solution)/shard_map/ppermute | solution.py:125
  87.4 4.2 %collective-permute-start.34 = (bf16[256,512]{1,0:T(8,128)(2,1)S(1)}, bf16[256,512]{1,0:T(8,128)(2,1)S(1)}, u32[]{:S(2)}, u32[]{:S(2)}) collective-permute-start(bf16[256,512]{1,0:T(8,128)(2,1)S(1)} %collective-permute-done.28.x_ref.refs_1_), channel_id=1, source_target_pairs={{0,4},{4,0},{8,12},{12,8},{16,20},{20,16},{24,28},{28,24},{1,5},{5... | collective-permute-start | bytes 786440 | tf_op jit(solution)/shard_map/ppermute | solution.py:117
  87.5 15.1 %collective-permute-start.30 = (bf16[384,512]{1,0:T(8,128)(2,1)S(1)}, bf16[384,512]{1,0:T(8,128)(2,1)S(1)}, u32[]{:S(2)}, u32[]{:S(2)}) collective-permute-start(bf16[384,512]{1,0:T(8,128)(2,1)S(1)} %collective-permute-done.27.q1), channel_id=1, source_target_pairs={{1,0},{2,3},{5,4},{6,7},{9,8},{10,11},{13,12},{14,15},{17,16},{18,... | collective-permute-start | bytes 1179656 | tf_op jit(solution)/shard_map/ppermute | solution.py:129
  88.8 6.0 %collective-permute-start.31 = (bf16[128,512]{1,0:T(8,128)(2,1)S(1)}, bf16[128,512]{1,0:T(8,128)(2,1)S(1)}, u32[]{:S(2)}, u32[]{:S(2)}) collective-permute-start(bf16[128,512]{1,0:T(8,128)(2,1)S(1)} %get-tuple-element.45), channel_id=1, source_target_pairs={{0,8},{4,12},{8,0},{12,4},{16,24},{20,28},{24,16},{28,20},{1,9},{5... | collective-permute-start | bytes 393224 | tf_op jit(solution)/shard_map/ppermute | solution.py:117
  90.1 5.6 %collective-permute-start.32 = (bf16[128,512]{1,0:T(8,128)(2,1)S(1)}, bf16[128,512]{1,0:T(8,128)(2,1)S(1)}, u32[]{:S(2)}, u32[]{:S(2)}) collective-permute-start(bf16[128,512]{1,0:T(8,128)(2,1)S(1)} %get-tuple-element.46), channel_id=1, source_target_pairs={{0,16},{4,20},{8,24},{12,28},{16,0},{20,4},{24,8},{28,12},{1,17},{... | collective-permute-start | bytes 393224 | tf_op jit(solution)/shard_map/ppermute | solution.py:117
  91.6 6.4 %collective-permute-start.35 = (bf16[256,512]{1,0:T(8,128)(2,1)S(1)}, bf16[256,512]{1,0:T(8,128)(2,1)S(1)}, u32[]{:S(2)}, u32[]{:S(2)}) collective-permute-start(bf16[256,512]{1,0:T(8,128)(2,1)S(1)} %collective-permute-done.29.y_ref.refs_2_), channel_id=1, source_target_pairs={{0,4},{4,0},{8,12},{12,8},{16,20},{20,16},{24,28},{28,24},{1,5},{5... | collective-permute-start | bytes 786440 | tf_op jit(solution)/shard_map/ppermute | solution.py:117
  91.6 18.9 %collective-permute-start.26 = (bf16[384,512]{1,0:T(8,128)(2,1)S(1)}, bf16[384,512]{1,0:T(8,128)(2,1)S(1)}, u32[]{:S(2)}, u32[]{:S(2)}) collective-permute-start(bf16[384,512]{1,0:T(8,128)(2,1)S(1)} %collective-permute-done.25.q2), channel_id=1, source_target_pairs={{1,0},{2,3},{5,4},{6,7},{9,8},{10,11},{13,12},{14,15},{17,16},{18,... | collective-permute-start | bytes 1179656 | tf_op jit(solution)/shard_map/ppermute | solution.py:129
  94.8 3.1 %collective-permute-start.36 = (bf16[128,512]{1,0:T(8,128)(2,1)S(1)}, bf16[128,512]{1,0:T(8,128)(2,1)S(1)}, u32[]{:S(2)}, u32[]{:S(2)}) collective-permute-start(bf16[128,512]{1,0:T(8,128)(2,1)S(1)} %collective-permute-done.31.refs_3_), channel_id=1, source_target_pairs={{0,4},{4,0},{8,12},{12,8},{16,20},{20,16},{24,28},{28,24},{1,5},{5... | collective-permute-start | bytes 393224 | tf_op jit(solution)/shard_map/ppermute | solution.py:117
  95.7 2.2 %collective-permute-start.37 = (bf16[128,512]{1,0:T(8,128)(2,1)S(1)}, bf16[128,512]{1,0:T(8,128)(2,1)S(1)}, u32[]{:S(2)}, u32[]{:S(2)}) collective-permute-start(bf16[128,512]{1,0:T(8,128)(2,1)S(1)} %collective-permute-done.32.refs_4_), channel_id=1, source_target_pairs={{0,4},{4,0},{8,12},{12,8},{16,20},{20,16},{24,28},{28,24},{1,5},{5... | collective-permute-start | bytes 393224 | tf_op jit(solution)/shard_map/ppermute | solution.py:117

commit v8 on v7

--- a/solution.py
+++ b/solution.py
@@ -265,10 +265,11 @@
         query = pieces[m][0]
         qpos = block * rows + lax.broadcasted_iota(jnp.int32, (rows, 1), 0)
         begin = jnp.zeros((rows, 1), jnp.int32)
-        lowest = jnp.int32(0)
+        lowest = highest = jnp.int32(0)
         for d in range(start_ref.shape[0]):
             begin = jnp.where(start_ref[d] <= qpos, start_ref[d], begin)
             lowest = jnp.where(start_ref[d] <= block * rows, start_ref[d], lowest)
+            highest = jnp.where(start_ref[d] < after, start_ref[d], highest)
 
         def scores(number, after=after, query=query, begin=begin):
             first = after - KEYS * (number + 1)
@@ -279,10 +280,11 @@
             )
             return score, kpos, kpos >= begin, vals[place, :]
 
-        def tile(number, state, scores=scores):
+        def tile(number, state, scores=scores, masked=True):
             running, totals, accum = state
             score, _, keep, values = scores(number)
-            score = jnp.where(keep, score, -1e30)
+            if masked:
+                score = jnp.where(keep, score, -1e30)
             newmax = jnp.maximum(running, jnp.max(score, axis=1, keepdims=True))
             weight = jnp.exp2(score - newmax)
             factor = jnp.exp2(running - newmax)
@@ -299,7 +301,10 @@
         totals = jnp.sum(weight, axis=1, keepdims=True)
         accum = jnp.dot(weight.astype(jnp.bfloat16), values, preferred_element_type=jnp.float32)
         tiles = lax.div(after - lowest + KEYS - 1, KEYS)
-        running, totals, accum = lax.fori_loop(1, tiles, tile, (running, totals, accum))
+        whole = jnp.maximum(lax.div(after - highest, KEYS), 1)
+        state = (running, totals, accum)
+        state = lax.fori_loop(1, whole, functools.partial(tile, masked=False), state)
+        running, totals, accum = lax.fori_loop(whole, tiles, tile, state)
         outs[m][...] = (accum / totals).astype(jnp.bfloat16)
 
 

time: 113 us -> 112 us (level); the launches traced: 112 us -> 112 us
  waiting for transfers between devices: 55.9 us -> 57.7 us
where the time goes in v8:
time: 112 us
  waiting for transfers between devices  57.7 us (52%)
  starting transfers between devices  31.8 us (28%)
  Pallas kernels  16.5 us (15%)
  local copies, waits for them, and re-layouts  3.79 us (3%)
  other arithmetic  1.68 us (2%)
    ppermute x28, waiting for transfers between devices, swap(): return lax.ppermute(x, 'gx', [(i, i ^ mask) for i in range(2 * CHIPS)])  31 us
    ppermute x28, starting transfers between devices, swap(): return lax.ppermute(x, 'gx', [(i, i ^ mask) for i in range(2 * CHIPS)])  18.5 us
    ppermute x4, waiting for transfers between devices, outward(): return lax.ppermute(x, 'gy', [(1, 0), (2, 3)])  18.1 us
    ppermute x2, waiting for transfers between devices, outer(): return lax.ppermute(x, 'gy', [(0, 1), (1, 0), (2, 3), (3, 2)])  8.59 us
    pallas_call x1, Pallas kernels, attend(): pl.pallas_call(functools.partial(attend_kernel, scale=scale), in_specs=[s...  6.9 us
    ppermute x2, starting transfers between devices, outer(): return lax.ppermute(x, 'gy', [(0, 1), (1, 0), (2, 3), (3, 2)])  5.44 us
    ppermute x4, starting transfers between devices, outward(): return lax.ppermute(x, 'gy', [(1, 0), (2, 3)])  5.17 us
    pallas_call x2, Pallas kernels, project(): pl.pallas_call(functools.partial(project_kernel, pair=pair), in_specs=[sm...  5.15 us
  transfers between devices with their start and end apart: 38, of which 18 were waited for; matrix products, arithmetic and copies ran while one was open for 5% of the time, Pallas kernels for 5%

profile of v8, /device:TPU:0, one launch (start us, length us, event | category | flops | bytes accessed | tf_op | source)
XLA Modules:
  0.0 112.4 jit_solution(16160012021107752265)
XLA Ops:
  0.6 3.1 %collective-permute-start = (bf16[384,512]{1,0:T(8,128)(2,1)}, bf16[384,512]{1,0:T(8,128)(2,1)S(1)}, u32[]{:S(2)}, u32[]{:S(2)}) collective-permute-start(bf16[384,512]{1,0:T(8,128)(2,1)} %refs_0_.1), channel_id=1, source_target_pairs={{0,1},{1,0},{2,3},{3,2},{4,5},{5,4},{6,7},{7,6},{8,9},{9,8},{10,11... | collective-permute-start | bytes 1179656 | tf_op jit(solution)/shard_map/ppermute | solution.py:121
  3.7 0.7 collective-permute-start.1
  4.4 1.7 %reshape.193.refs_0_ = bf16[256,1536]{1,0:T(8,128)(2,1)S(1)} reshape(bf16[256,3,4,128]{3,2,1,0:T(4,128)(2,1)} %param.7) | data formatting | bytes 1572864 | tf_op jit(solution)/shard_map/reshape | solution.py:414
  6.1 1.6 %collective-permute-start.5 = (bf16[256,1536]{1,0:T(8,128)(2,1)S(1)}, bf16[256,1536]{1,0:T(8,128)(2,1)S(1)}, u32[]{:S(2)}, u32[]{:S(2)}) collective-permute-start(bf16[256,1536]{1,0:T(8,128)(2,1)S(1)} %reshape.193.refs_0_), channel_id=1, source_target_pairs={{0,8},{4,12},{8,0},{12,4},{16,24},{20,28},{24,16},{28,20},{1,9},{5... | collective-permute-start | bytes 2359304 | tf_op jit(solution)/shard_map/ppermute | solution.py:117
  7.6 1.5 %collective-permute-start.6 = (bf16[256,1536]{1,0:T(8,128)(2,1)S(1)}, bf16[256,1536]{1,0:T(8,128)(2,1)S(1)}, u32[]{:S(2)}, u32[]{:S(2)}) collective-permute-start(bf16[256,1536]{1,0:T(8,128)(2,1)S(1)} %reshape.193.refs_0_), channel_id=1, source_target_pairs={{0,16},{4,20},{8,24},{12,28},{16,0},{20,4},{24,8},{28,12},{1,17},{... | collective-permute-start | bytes 2359304 | tf_op jit(solution)/shard_map/ppermute | solution.py:117
  9.2 0.2 reduce-window.9
  9.4 0.1 select_reduce_fusion
  9.5 0.1 pad_add_fusion.where_ref
  9.6 0.8 fusion
  10.3 0.2 pad_maximum_fusion.3
  10.5 2.5 %collective-permute-done.refs_1_ = bf16[384,512]{1,0:T(8,128)(2,1)S(1)} collective-permute-done((bf16[384,512]{1,0:T(8,128)(2,1)}, bf16[384,512]{1,0:T(8,128)(2,1)S(1)}, u32[]{:S(2)}, u32[]{:S(2)}) %collective-permute-start) | collective-permute-done | bytes 393248 | tf_op jit(solution)/shard_map/ppermute | solution.py:121
  13.1 0.7 collective-permute-start.3
  13.7 1.3 %collective-permute-start.2 = (bf16[384,512]{1,0:T(8,128)(2,1)S(1)}, bf16[384,512]{1,0:T(8,128)(2,1)S(1)}, u32[]{:S(2)}, u32[]{:S(2)}) collective-permute-start(bf16[384,512]{1,0:T(8,128)(2,1)S(1)} %collective-permute-done.1.refs_2_), channel_id=1, source_target_pairs={{1,0},{2,3},{5,4},{6,7},{9,8},{10,11},{13,12},{14,15},{17,16},{18,... | collective-permute-start | bytes 1179656 | tf_op jit(solution)/shard_map/ppermute | solution.py:129
  15.1 1.3 %collective-permute-start.4 = (bf16[384,512]{1,0:T(8,128)(2,1)S(1)}, bf16[384,512]{1,0:T(8,128)(2,1)S(1)}, u32[]{:S(2)}, u32[]{:S(2)}) collective-permute-start(bf16[384,512]{1,0:T(8,128)(2,1)S(1)} %collective-permute-done.3.refs_4_), channel_id=1, source_target_pairs={{1,0},{2,3},{5,4},{6,7},{9,8},{10,11},{13,12},{14,15},{17,16},{18,... | collective-permute-start | bytes 1179656 | tf_op jit(solution)/shard_map/ppermute | solution.py:129
  16.4 8.8 %collective-permute-done.5.x_ref.refs_1_ = bf16[256,1536]{1,0:T(8,128)(2,1)S(1)} collective-permute-done((bf16[256,1536]{1,0:T(8,128)(2,1)S(1)}, bf16[256,1536]{1,0:T(8,128)(2,1)S(1)}, u32[]{:S(2)}, u32[]{:S(2)}) %collective-permute-start.5) | collective-permute-done | bytes 786464 | tf_op jit(solution)/shard_map/ppermute | solution.py:117
  25.1 1.2 %collective-permute-done.6.y_ref.refs_2_ = bf16[256,1536]{1,0:T(8,128)(2,1)S(1)} collective-permute-done((bf16[256,1536]{1,0:T(8,128)(2,1)S(1)}, bf16[256,1536]{1,0:T(8,128)(2,1)S(1)}, u32[]{:S(2)}, u32[]{:S(2)}) %collective-permute-start.6) | collective-permute-done | bytes 786464 | tf_op jit(solution)/shard_map/ppermute | solution.py:117
  26.4 0.6 collective-permute-start.7
  27.0 1.5 %collective-permute-start.8 = (bf16[128,1536]{1,0:T(8,128)(2,1)S(1)}, bf16[128,1536]{1,0:T(8,128)(2,1)S(1)}, u32[]{:S(2)}, u32[]{:S(2)}) collective-permute-start(bf16[128,1536]{1,0:T(8,128)(2,1)S(1)} %get-tuple-element.31), channel_id=1, source_target_pairs={{0,16},{4,20},{8,24},{12,28},{16,0},{20,4},{24,8},{28,12},{1,17},{... | collective-permute-start | bytes 1179656 | tf_op jit(solution)/shard_map/ppermute | solution.py:117
  28.5 0.5 collective-permute-start.10
  29.1 6.9 %collective-permute-done.4.refs_5_ = bf16[384,512]{1,0:T(8,128)(2,1)S(1)} collective-permute-done((bf16[384,512]{1,0:T(8,128)(2,1)S(1)}, bf16[384,512]{1,0:T(8,128)(2,1)S(1)}, u32[]{:S(2)}, u32[]{:S(2)}) %collective-permute-start.4) | collective-permute-done | bytes 393248 | tf_op jit(solution)/shard_map/ppermute | solution.py:129
  36.0 0.5 collective-permute-start.12
  36.5 0.1 collective-permute-start.13
  36.5 1.3 %normalize.1.x_ref = bf16[384,2048]{1,0:T(8,128)(2,1)S(1)} custom-call(s32[3]{0:T(128)S(1)} %pad_add_fusion.where_ref, bf16[384,512]{1,0:T(8,128)(2,1)S(1)} %copy-done, bf16[384,512]{1,0:T(8,128)(2,1)S(1)} %collective-permute-done.refs_1_, bf16[384,512]{1,0:T(8,128)(2,1)S(1)} %collective-permute-done.1.refs_2_, ...), custom_call_target="tpu_custom_call" | custom-call | flops 8589934592 | bytes 8388608 | tf_op jit(solution)/shard_map/normalize/pallas_call | solution.py:197
  37.8 1.0 collective-permute-done.12.refs_8_
  38.8 0.6 collective-permute-done.13.refs_9_
  39.4 2.6 %project.3 = (bf16[3,384,128]{2,1,0:T(8,128)(2,1)S(1)}, bf16[3,384,128]{2,1,0:T(8,128)(2,1)S(1)}) custom-call(s32[3]{0:T(128)S(1)} %pad_add_fusion.where_ref, bf16[384,2048]{1,0:T(8,128)(2,1)S(1)} %normalize.1.x_ref, f32[384,128]{1,0:T(8,128)S(1)} %get-tuple-element.28.cos_ref, f32[384,128]{1,0:T(8,128)S(1)} %get-tuple-element.29.sin_ref, ...), custom_call_target="tpu_custom_call" | custom-call | flops 1207959552 | bytes 8388608 | tf_op jit(solution)/shard_map/project/pallas_call | solution.py:238
  42.0 1.6 %collective-permute-start.14 = (bf16[3,384,128]{2,1,0:T(8,128)(2,1)S(1)}, bf16[3,384,128]{2,1,0:T(8,128)(2,1)S(1)}, u32[]{:S(2)}, u32[]{:S(2)}) collective-permute-start(bf16[3,384,128]{2,1,0:T(8,128)(2,1)S(1)} %get-tuple-element.33), channel_id=1, source_target_pairs={{0,8},{4,12},{8,0},{12,4},{16,24},{20,28},{24,16},{28,20},{1,9},{5... | collective-permute-start | bytes 884744 | tf_op jit(solution)/shard_map/ppermute | solution.py:117
  43.5 1.5 %collective-permute-start.15 = (bf16[3,384,128]{2,1,0:T(8,128)(2,1)S(1)}, bf16[3,384,128]{2,1,0:T(8,128)(2,1)S(1)}, u32[]{:S(2)}, u32[]{:S(2)}) collective-permute-start(bf16[3,384,128]{2,1,0:T(8,128)(2,1)S(1)} %get-tuple-element.34), channel_id=1, source_target_pairs={{0,16},{4,20},{8,24},{12,28},{16,0},{20,4},{24,8},{28,12},{1,17},{... | collective-permute-start | bytes 884744 | tf_op jit(solution)/shard_map/ppermute | solution.py:117
  45.0 2.6 %project.2 = (bf16[3,384,128]{2,1,0:T(8,128)(2,1)S(1)}, bf16[3,384,128]{2,1,0:T(8,128)(2,1)S(1)}) custom-call(s32[3]{0:T(128)S(1)} %pad_add_fusion.where_ref, bf16[384,2048]{1,0:T(8,128)(2,1)S(1)} %normalize.1.x_ref, f32[384,128]{1,0:T(8,128)S(1)} %get-tuple-element.28.cos_ref, f32[384,128]{1,0:T(8,128)S(1)} %get-tuple-element.29.sin_ref, ...), custom_call_target="tpu_custom_call" | custom-call | flops 1207959552 | bytes 8388608 | tf_op jit(solution)/shard_map/project/pallas_call | solution.py:238
  47.6 0.5 collective-permute-start.16
  48.2 3.7 %collective-permute-done.14.refs_1_ = bf16[3,384,128]{2,1,0:T(8,128)(2,1)S(1)} collective-permute-done((bf16[3,384,128]{2,1,0:T(8,128)(2,1)S(1)}, bf16[3,384,128]{2,1,0:T(8,128)(2,1)S(1)}, u32[]{:S(2)}, u32[]{:S(2)}) %collective-permute-start.14) | collective-permute-done | bytes 294944 | tf_op jit(solution)/shard_map/ppermute | solution.py:117
  51.9 6.7 %collective-permute-done.15.refs_2_ = bf16[3,384,128]{2,1,0:T(8,128)(2,1)S(1)} collective-permute-done((bf16[3,384,128]{2,1,0:T(8,128)(2,1)S(1)}, bf16[3,384,128]{2,1,0:T(8,128)(2,1)S(1)}, u32[]{:S(2)}, u32[]{:S(2)}) %collective-permute-start.15) | collective-permute-done | bytes 294944 | tf_op jit(solution)/shard_map/ppermute | solution.py:117
  58.6 0.5 collective-permute-start.20
  59.1 1.1 collective-permute-done.19.refs_6_
  60.2 0.4 collective-permute-done.20.refs_7_
  60.6 6.9 %attend.1 = (bf16[384,128]{1,0:T(8,128)(2,1)S(1)}, bf16[384,128]{1,0:T(8,128)(2,1)S(1)}, bf16[384,128]{1,0:T(8,128)(2,1)S(1)}, bf16[384,128]{1,0:T(8,128)(2,1)S(1)}) custom-call(s32[3]{0:T(128)S(1)} %pad_add_fusion.where_ref, s32[6]{0:T(128)S(1)} %bitcast_subtract_fusion.start_ref, bf16[3,384,128]{2,1,0:T(8,128)(2,1)S(1)} %get-tuple-element.32.refs_0_, ...), custom_call_target="tpu_custom_call" | custom-call | flops 2415919104 | bytes 8388608 | tf_op jit(solution)/shard_map/attend/pallas_call | solution.py:314
  67.5 1.6 %collective-permute-start.21 = (bf16[384,128]{1,0:T(8,128)(2,1)S(1)}, bf16[384,128]{1,0:T(8,128)(2,1)S(1)}, u32[]{:S(2)}, u32[]{:S(2)}) collective-permute-start(bf16[384,128]{1,0:T(8,128)(2,1)S(1)} %get-tuple-element.36), channel_id=1, source_target_pairs={{0,24},{4,28},{8,16},{12,20},{16,8},{20,12},{24,0},{28,4},{1,25},{... | collective-permute-start | bytes 294920 | tf_op jit(solution)/shard_map/ppermute | solution.py:117
  69.1 0.8 collective-permute-start.22
  69.9 1.2 %collective-permute-start.23 = (bf16[384,128]{1,0:T(8,128)(2,1)S(1)}, bf16[384,128]{1,0:T(8,128)(2,1)S(1)}, u32[]{:S(2)}, u32[]{:S(2)}) collective-permute-start(bf16[384,128]{1,0:T(8,128)(2,1)S(1)} %get-tuple-element.38), channel_id=1, source_target_pairs={{0,8},{4,12},{8,0},{12,4},{16,24},{20,28},{24,16},{28,20},{1,9},{5... | collective-permute-start | bytes 294920 | tf_op jit(solution)/shard_map/ppermute | solution.py:117
  71.1 2.8 %collective-permute-done.21 = bf16[384,128]{1,0:T(8,128)(2,1)S(1)} collective-permute-done((bf16[384,128]{1,0:T(8,128)(2,1)S(1)}, bf16[384,128]{1,0:T(8,128)(2,1)S(1)}, u32[]{:S(2)}, u32[]{:S(2)}) %collective-permute-start.21) | collective-permute-done | bytes 98336 | tf_op jit(solution)/shard_map/ppermute | solution.py:117
  73.9 1.5 %collective-permute-done.22 = bf16[384,128]{1,0:T(8,128)(2,1)S(1)} collective-permute-done((bf16[384,128]{1,0:T(8,128)(2,1)S(1)}, bf16[384,128]{1,0:T(8,128)(2,1)S(1)}, u32[]{:S(2)}, u32[]{:S(2)}) %collective-permute-start.22) | collective-permute-done | bytes 98336 | tf_op jit(solution)/shard_map/ppermute | solution.py:117
  75.4 0.1 collective-permute-done.23
  75.5 0.1 broadcast_select_fusion.5
  75.7 2.4 %collective-permute-start.24 = (bf16[384,512]{1,0:T(8,128)(2,1)S(1)}, bf16[384,512]{1,0:T(8,128)(2,1)S(1)}, u32[]{:S(2)}, u32[]{:S(2)}) collective-permute-start(bf16[384,512]{1,0:T(8,128)(2,1)S(1)} %pad_maximum_fusion.own), channel_id=1, source_target_pairs={{0,1},{1,0},{2,3},{3,2},{4,5},{5,4},{6,7},{7,6},{8,9},{9,8},{10,11... | collective-permute-start | bytes 1179656 | tf_op jit(solution)/shard_map/ppermute | solution.py:121
  78.0 0.8 collective-permute-start.28
  78.9 1.2 %collective-permute-start.29 = (bf16[256,512]{1,0:T(8,128)(2,1)S(1)}, bf16[256,512]{1,0:T(8,128)(2,1)S(1)}, u32[]{:S(2)}, u32[]{:S(2)}) collective-permute-start(bf16[256,512]{1,0:T(8,128)(2,1)S(1)} %copy-done.1), channel_id=1, source_target_pairs={{0,16},{4,20},{8,24},{12,28},{16,0},{20,4},{24,8},{28,12},{1,17},{... | collective-permute-start | bytes 786440 | tf_op jit(solution)/shard_map/ppermute | solution.py:117
  80.0 0.7 collective-permute-start.27
  80.7 0.1 collective-permute-start.33
  80.8 6.1 %collective-permute-done.24.near = bf16[384,512]{1,0:T(8,128)(2,1)S(1)} collective-permute-done((bf16[384,512]{1,0:T(8,128)(2,1)S(1)}, bf16[384,512]{1,0:T(8,128)(2,1)S(1)}, u32[]{:S(2)}, u32[]{:S(2)}) %collective-permute-start.24) | collective-permute-done | bytes 393248 | tf_op jit(solution)/shard_map/ppermute | solution.py:121
  86.9 0.7 collective-permute-start.25
  87.6 0.1 collective-permute-start.34
  87.8 1.3 %collective-permute-start.30 = (bf16[384,512]{1,0:T(8,128)(2,1)S(1)}, bf16[384,512]{1,0:T(8,128)(2,1)S(1)}, u32[]{:S(2)}, u32[]{:S(2)}) collective-permute-start(bf16[384,512]{1,0:T(8,128)(2,1)S(1)} %collective-permute-done.27.q1), channel_id=1, source_target_pairs={{1,0},{2,3},{5,4},{6,7},{9,8},{10,11},{13,12},{14,15},{17,16},{18,... | collective-permute-start | bytes 1179656 | tf_op jit(solution)/shard_map/ppermute | solution.py:129
  89.1 1.3 %collective-permute-start.31 = (bf16[128,512]{1,0:T(8,128)(2,1)S(1)}, bf16[128,512]{1,0:T(8,128)(2,1)S(1)}, u32[]{:S(2)}, u32[]{:S(2)}) collective-permute-start(bf16[128,512]{1,0:T(8,128)(2,1)S(1)} %get-tuple-element.45), channel_id=1, source_target_pairs={{0,8},{4,12},{8,0},{12,4},{16,24},{20,28},{24,16},{28,20},{1,9},{5... | collective-permute-start | bytes 393224 | tf_op jit(solution)/shard_map/ppermute | solution.py:117
  90.3 1.0 collective-permute-start.32
  91.4 0.1 collective-permute-start.35
  91.5 1.3 %collective-permute-start.26 = (bf16[384,512]{1,0:T(8,128)(2,1)S(1)}, bf16[384,512]{1,0:T(8,128)(2,1)S(1)}, u32[]{:S(2)}, u32[]{:S(2)}) collective-permute-start(bf16[384,512]{1,0:T(8,128)(2,1)S(1)} %collective-permute-done.25.q2), channel_id=1, source_target_pairs={{1,0},{2,3},{5,4},{6,7},{9,8},{10,11},{13,12},{14,15},{17,16},{18,... | collective-permute-start | bytes 1179656 | tf_op jit(solution)/shard_map/ppermute | solution.py:129
  92.8 2.2 %collective-permute-done.31.refs_3_ = bf16[128,512]{1,0:T(8,128)(2,1)S(1)} collective-permute-done((bf16[128,512]{1,0:T(8,128)(2,1)S(1)}, bf16[128,512]{1,0:T(8,128)(2,1)S(1)}, u32[]{:S(2)}, u32[]{:S(2)}) %collective-permute-start.31) | collective-permute-done | bytes 131104 | tf_op jit(solution)/shard_map/ppermute | solution.py:117
  95.0 0.9 collective-permute-done.32.refs_4_
  96.0 1.1 copy.11
  97.1 1.1 copy.10
  98.1 5.5 %collective-permute-done.30.p2 = bf16[384,512]{1,0:T(8,128)(2,1)S(1)} collective-permute-done((bf16[384,512]{1,0:T(8,128)(2,1)S(1)}, bf16[384,512]{1,0:T(8,128)(2,1)S(1)}, u32[]{:S(2)}, u32[]{:S(2)}) %collective-permute-start.30) | collective-permute-done | bytes 393248 | tf_op jit(solution)/shard_map/ppermute | solution.py:129
  103.6 1.5 %early.1 = (f32[384,512]{1,0:T(8,128)S(1)}, bf16[512,512]{1,0:T(8,128)(2,1)S(1)}) custom-call(s32[3]{0:T(128)S(1)} %pad_add_fusion.where_ref, bf16[384,512]{1,0:T(8,128)(2,1)S(1)} %pad_maximum_fusion.own, bf16[384,512]{1,0:T(8,128)(2,1)S(1)} %collective-permute-done.24.near, bf16[384,512]{1,0:T(8,128)(2,1)S(1)} %collective-permute-done.27.q1, ...), custom_call_target="tpu_custom_call" | custom-call | flops 1073741824 | bytes 8388608 | tf_op jit(solution)/shard_map/early/pallas_call | solution.py:354
  105.1 5.7 %collective-permute-done.26.p3 = bf16[384,512]{1,0:T(8,128)(2,1)S(1)} collective-permute-done((bf16[384,512]{1,0:T(8,128)(2,1)S(1)}, bf16[384,512]{1,0:T(8,128)(2,1)S(1)}, u32[]{:S(2)}, u32[]{:S(2)}) %collective-permute-start.26) | collective-permute-done | bytes 393248 | tf_op jit(solution)/shard_map/ppermute | solution.py:129
  110.8 1.7 %last.1 = bf16[384,512]{1,0:T(8,128)(2,1)} custom-call(s32[3]{0:T(128)S(1)} %pad_add_fusion.where_ref, bf16[384,512]{1,0:T(8,128)(2,1)S(1)} %collective-permute-done.25.q2, bf16[384,512]{1,0:T(8,128)(2,1)S(1)} %collective-permute-done.26.p3, f32[384,512]{1,0:T(8,128)S(1)} %get-tuple-element.47.total_ref, bf16[512,512]{1,0:T(8,128)(2,1)S(1)} %get-tuple-element.48.w_ref), custom_call_target="tpu_custom_call" | custom-call | flops 201326592 | bytes 8388608 | tf_op jit(solution)/shard_map/last/pallas_call | solution.py:377
  (50 shorter events, 0.5 us)
Async XLA Ops:
  0.6 8.5 %copy-start.3 = (s32[6]{0:T(128)S(1)}, s32[6]{0:T(128)}, u32[]{:S(2)}) copy-start(s32[6]{0:T(128)} %param.9) | copy-start | bytes 76
  0.6 12.4 %collective-permute-start = (bf16[384,512]{1,0:T(8,128)(2,1)}, bf16[384,512]{1,0:T(8,128)(2,1)S(1)}, u32[]{:S(2)}, u32[]{:S(2)}) collective-permute-start(bf16[384,512]{1,0:T(8,128)(2,1)} %refs_0_.1), channel_id=1, source_target_pairs={{0,1},{1,0},{2,3},{3,2},{4,5},{5,4},{6,7},{7,6},{8,9},{9,8},{10,11... | collective-permute-start | bytes 1179656 | tf_op jit(solution)/shard_map/ppermute | solution.py:121
  3.7 10.0 %collective-permute-start.1 = (bf16[384,512]{1,0:T(8,128)(2,1)}, bf16[384,512]{1,0:T(8,128)(2,1)S(1)}, u32[]{:S(2)}, u32[]{:S(2)}) collective-permute-start(bf16[384,512]{1,0:T(8,128)(2,1)} %refs_0_.1), channel_id=1, source_target_pairs={{1,2},{2,1},{5,6},{6,5},{9,10},{10,9},{13,14},{14,13},{17,18},{18,... | collective-permute-start | bytes 1179656 | tf_op jit(solution)/shard_map/ppermute | solution.py:125
  6.1 19.1 %collective-permute-start.5 = (bf16[256,1536]{1,0:T(8,128)(2,1)S(1)}, bf16[256,1536]{1,0:T(8,128)(2,1)S(1)}, u32[]{:S(2)}, u32[]{:S(2)}) collective-permute-start(bf16[256,1536]{1,0:T(8,128)(2,1)S(1)} %reshape.193.refs_0_), channel_id=1, source_target_pairs={{0,8},{4,12},{8,0},{12,4},{16,24},{20,28},{24,16},{28,20},{1,9},{5... | collective-permute-start | bytes 2359304 | tf_op jit(solution)/shard_map/ppermute | solution.py:117
  7.6 18.7 %collective-permute-start.6 = (bf16[256,1536]{1,0:T(8,128)(2,1)S(1)}, bf16[256,1536]{1,0:T(8,128)(2,1)S(1)}, u32[]{:S(2)}, u32[]{:S(2)}) collective-permute-start(bf16[256,1536]{1,0:T(8,128)(2,1)S(1)} %reshape.193.refs_0_), channel_id=1, source_target_pairs={{0,16},{4,20},{8,24},{12,28},{16,0},{20,4},{24,8},{28,12},{1,17},{... | collective-permute-start | bytes 2359304 | tf_op jit(solution)/shard_map/ppermute | solution.py:117
  9.6 27.0 %copy-start = (bf16[384,512]{1,0:T(8,128)(2,1)S(1)}, bf16[384,512]{1,0:T(8,128)(2,1)}, u32[]{:S(2)}) copy-start(bf16[384,512]{1,0:T(8,128)(2,1)} %refs_0_.1) | copy-start | bytes 1179652
  9.6 27.0 %copy-start.2 = (f32[2048]{0:T(1024)S(1)}, f32[2048]{0:T(1024)}, u32[]{:S(2)}) copy-start(f32[2048]{0:T(1024)} %param.6) | copy-start | bytes 24580
  13.1 2.0 %collective-permute-start.3 = (bf16[384,512]{1,0:T(8,128)(2,1)S(1)}, bf16[384,512]{1,0:T(8,128)(2,1)S(1)}, u32[]{:S(2)}, u32[]{:S(2)}) collective-permute-start(bf16[384,512]{1,0:T(8,128)(2,1)S(1)} %collective-permute-done.refs_1_), channel_id=1, source_target_pairs={{1,2},{2,1},{5,6},{6,5},{9,10},{10,9},{13,14},{14,13},{17,18},{18,... | collective-permute-start | bytes 1179656 | tf_op jit(solution)/shard_map/ppermute | solution.py:125
  13.7 14.8 %collective-permute-start.2 = (bf16[384,512]{1,0:T(8,128)(2,1)S(1)}, bf16[384,512]{1,0:T(8,128)(2,1)S(1)}, u32[]{:S(2)}, u32[]{:S(2)}) collective-permute-start(bf16[384,512]{1,0:T(8,128)(2,1)S(1)} %collective-permute-done.1.refs_2_), channel_id=1, source_target_pairs={{1,0},{2,3},{5,4},{6,7},{9,8},{10,11},{13,12},{14,15},{17,16},{18,... | collective-permute-start | bytes 1179656 | tf_op jit(solution)/shard_map/ppermute | solution.py:129
  15.1 20.9 %collective-permute-start.4 = (bf16[384,512]{1,0:T(8,128)(2,1)S(1)}, bf16[384,512]{1,0:T(8,128)(2,1)S(1)}, u32[]{:S(2)}, u32[]{:S(2)}) collective-permute-start(bf16[384,512]{1,0:T(8,128)(2,1)S(1)} %collective-permute-done.3.refs_4_), channel_id=1, source_target_pairs={{1,0},{2,3},{5,4},{6,7},{9,8},{10,11},{13,12},{14,15},{17,16},{18,... | collective-permute-start | bytes 1179656 | tf_op jit(solution)/shard_map/ppermute | solution.py:129
  26.4 9.5 %collective-permute-start.7 = (bf16[128,1536]{1,0:T(8,128)(2,1)S(1)}, bf16[128,1536]{1,0:T(8,128)(2,1)S(1)}, u32[]{:S(2)}, u32[]{:S(2)}) collective-permute-start(bf16[128,1536]{1,0:T(8,128)(2,1)S(1)} %get-tuple-element.30), channel_id=1, source_target_pairs={{0,8},{4,12},{8,0},{12,4},{16,24},{20,28},{24,16},{28,20},{1,9},{5... | collective-permute-start | bytes 1179656 | tf_op jit(solution)/shard_map/ppermute | solution.py:117
  27.0 9.4 %collective-permute-start.8 = (bf16[128,1536]{1,0:T(8,128)(2,1)S(1)}, bf16[128,1536]{1,0:T(8,128)(2,1)S(1)}, u32[]{:S(2)}, u32[]{:S(2)}) collective-permute-start(bf16[128,1536]{1,0:T(8,128)(2,1)S(1)} %get-tuple-element.31), channel_id=1, source_target_pairs={{0,16},{4,20},{8,24},{12,28},{16,0},{20,4},{24,8},{28,12},{1,17},{... | collective-permute-start | bytes 1179656 | tf_op jit(solution)/shard_map/ppermute | solution.py:117
  28.5 9.3 %collective-permute-start.9 = (bf16[256,1536]{1,0:T(8,128)(2,1)S(1)}, bf16[256,1536]{1,0:T(8,128)(2,1)S(1)}, u32[]{:S(2)}, u32[]{:S(2)}) collective-permute-start(bf16[256,1536]{1,0:T(8,128)(2,1)S(1)} %reshape.193.refs_0_), channel_id=1, source_target_pairs={{0,4},{4,0},{8,12},{12,8},{16,20},{20,16},{24,28},{28,24},{1,5},{5... | collective-permute-start | bytes 2359304 | tf_op jit(solution)/shard_map/ppermute | solution.py:117
  28.5 10.8 %collective-permute-start.10 = (bf16[256,1536]{1,0:T(8,128)(2,1)S(1)}, bf16[256,1536]{1,0:T(8,128)(2,1)S(1)}, u32[]{:S(2)}, u32[]{:S(2)}) collective-permute-start(bf16[256,1536]{1,0:T(8,128)(2,1)S(1)} %collective-permute-done.5.x_ref.refs_1_), channel_id=1, source_target_pairs={{0,4},{4,0},{8,12},{12,8},{16,20},{20,16},{24,28},{28,24},{1,5},{5... | collective-permute-start | bytes 2359304 | tf_op jit(solution)/shard_map/ppermute | solution.py:117
  36.0 3.4 %collective-permute-start.11 = (bf16[256,1536]{1,0:T(8,128)(2,1)S(1)}, bf16[256,1536]{1,0:T(8,128)(2,1)S(1)}, u32[]{:S(2)}, u32[]{:S(2)}) collective-permute-start(bf16[256,1536]{1,0:T(8,128)(2,1)S(1)} %collective-permute-done.6.y_ref.refs_2_), channel_id=1, source_target_pairs={{0,4},{4,0},{8,12},{12,8},{16,20},{20,16},{24,28},{28,24},{1,5},{5... | collective-permute-start | bytes 2359304 | tf_op jit(solution)/shard_map/ppermute | solution.py:117
  36.0 2.8 %collective-permute-start.12 = (bf16[128,1536]{1,0:T(8,128)(2,1)S(1)}, bf16[128,1536]{1,0:T(8,128)(2,1)S(1)}, u32[]{:S(2)}, u32[]{:S(2)}) collective-permute-start(bf16[128,1536]{1,0:T(8,128)(2,1)S(1)} %collective-permute-done.7.refs_3_), channel_id=1, source_target_pairs={{0,4},{4,0},{8,12},{12,8},{16,20},{20,16},{24,28},{28,24},{1,5},{5... | collective-permute-start | bytes 1179656 | tf_op jit(solution)/shard_map/ppermute | solution.py:117
  36.5 2.9 %collective-permute-start.13 = (bf16[128,1536]{1,0:T(8,128)(2,1)S(1)}, bf16[128,1536]{1,0:T(8,128)(2,1)S(1)}, u32[]{:S(2)}, u32[]{:S(2)}) collective-permute-start(bf16[128,1536]{1,0:T(8,128)(2,1)S(1)} %collective-permute-done.8.refs_4_), channel_id=1, source_target_pairs={{0,4},{4,0},{8,12},{12,8},{16,20},{20,16},{24,28},{28,24},{1,5},{5... | collective-permute-start | bytes 1179656 | tf_op jit(solution)/shard_map/ppermute | solution.py:117
  42.0 9.9 %collective-permute-start.14 = (bf16[3,384,128]{2,1,0:T(8,128)(2,1)S(1)}, bf16[3,384,128]{2,1,0:T(8,128)(2,1)S(1)}, u32[]{:S(2)}, u32[]{:S(2)}) collective-permute-start(bf16[3,384,128]{2,1,0:T(8,128)(2,1)S(1)} %get-tuple-element.33), channel_id=1, source_target_pairs={{0,8},{4,12},{8,0},{12,4},{16,24},{20,28},{24,16},{28,20},{1,9},{5... | collective-permute-start | bytes 884744 | tf_op jit(solution)/shard_map/ppermute | solution.py:117
  43.5 15.1 %collective-permute-start.15 = (bf16[3,384,128]{2,1,0:T(8,128)(2,1)S(1)}, bf16[3,384,128]{2,1,0:T(8,128)(2,1)S(1)}, u32[]{:S(2)}, u32[]{:S(2)}) collective-permute-start(bf16[3,384,128]{2,1,0:T(8,128)(2,1)S(1)} %get-tuple-element.34), channel_id=1, source_target_pairs={{0,16},{4,20},{8,24},{12,28},{16,0},{20,4},{24,8},{28,12},{1,17},{... | collective-permute-start | bytes 884744 | tf_op jit(solution)/shard_map/ppermute | solution.py:117
  47.6 11.0 %collective-permute-start.16 = (bf16[3,384,128]{2,1,0:T(8,128)(2,1)S(1)}, bf16[3,384,128]{2,1,0:T(8,128)(2,1)S(1)}, u32[]{:S(2)}, u32[]{:S(2)}) collective-permute-start(bf16[3,384,128]{2,1,0:T(8,128)(2,1)S(1)} %get-tuple-element.35), channel_id=1, source_target_pairs={{0,24},{4,28},{8,16},{12,20},{16,8},{20,12},{24,0},{28,4},{1,25},{... | collective-permute-start | bytes 884744 | tf_op jit(solution)/shard_map/ppermute | solution.py:117
  48.2 11.0 %collective-permute-start.17 = (bf16[3,384,128]{2,1,0:T(8,128)(2,1)S(1)}, bf16[3,384,128]{2,1,0:T(8,128)(2,1)S(1)}, u32[]{:S(2)}, u32[]{:S(2)}) collective-permute-start(bf16[3,384,128]{2,1,0:T(8,128)(2,1)S(1)} %get-tuple-element.32.refs_0_), channel_id=1, source_target_pairs={{0,4},{4,0},{8,12},{12,8},{16,20},{20,16},{24,28},{28,24},{1,5},{5... | collective-permute-start | bytes 884744 | tf_op jit(solution)/shard_map/ppermute | solution.py:117
  51.9 7.2 %collective-permute-start.18 = (bf16[3,384,128]{2,1,0:T(8,128)(2,1)S(1)}, bf16[3,384,128]{2,1,0:T(8,128)(2,1)S(1)}, u32[]{:S(2)}, u32[]{:S(2)}) collective-permute-start(bf16[3,384,128]{2,1,0:T(8,128)(2,1)S(1)} %collective-permute-done.14.refs_1_), channel_id=1, source_target_pairs={{0,4},{4,0},{8,12},{12,8},{16,20},{20,16},{24,28},{28,24},{1,5},{5... | collective-permute-start | bytes 884744 | tf_op jit(solution)/shard_map/ppermute | solution.py:117
  58.6 1.6 %collective-permute-start.19 = (bf16[3,384,128]{2,1,0:T(8,128)(2,1)S(1)}, bf16[3,384,128]{2,1,0:T(8,128)(2,1)S(1)}, u32[]{:S(2)}, u32[]{:S(2)}) collective-permute-start(bf16[3,384,128]{2,1,0:T(8,128)(2,1)S(1)} %collective-permute-done.15.refs_2_), channel_id=1, source_target_pairs={{0,4},{4,0},{8,12},{12,8},{16,20},{20,16},{24,28},{28,24},{1,5},{5... | collective-permute-start | bytes 884744 | tf_op jit(solution)/shard_map/ppermute | solution.py:117
  58.6 2.0 %collective-permute-start.20 = (bf16[3,384,128]{2,1,0:T(8,128)(2,1)S(1)}, bf16[3,384,128]{2,1,0:T(8,128)(2,1)S(1)}, u32[]{:S(2)}, u32[]{:S(2)}) collective-permute-start(bf16[3,384,128]{2,1,0:T(8,128)(2,1)S(1)} %collective-permute-done.16.refs_3_), channel_id=1, source_target_pairs={{0,4},{4,0},{8,12},{12,8},{16,20},{20,16},{24,28},{28,24},{1,5},{5... | collective-permute-start | bytes 884744 | tf_op jit(solution)/shard_map/ppermute | solution.py:117
  67.5 10.5 %copy-start.1 = (bf16[256,512]{1,0:T(8,128)(2,1)S(1)}, bf16[256,512]{1,0:T(8,128)(2,1)}, u32[]{:S(2)}) copy-start(bf16[256,512]{1,0:T(8,128)(2,1)} %refs_0_.2) | copy-start | bytes 786436
  67.5 6.4 %collective-permute-start.21 = (bf16[384,128]{1,0:T(8,128)(2,1)S(1)}, bf16[384,128]{1,0:T(8,128)(2,1)S(1)}, u32[]{:S(2)}, u32[]{:S(2)}) collective-permute-start(bf16[384,128]{1,0:T(8,128)(2,1)S(1)} %get-tuple-element.36), channel_id=1, source_target_pairs={{0,24},{4,28},{8,16},{12,20},{16,8},{20,12},{24,0},{28,4},{1,25},{... | collective-permute-start | bytes 294920 | tf_op jit(solution)/shard_map/ppermute | solution.py:117
  69.1 6.3 %collective-permute-start.22 = (bf16[384,128]{1,0:T(8,128)(2,1)S(1)}, bf16[384,128]{1,0:T(8,128)(2,1)S(1)}, u32[]{:S(2)}, u32[]{:S(2)}) collective-permute-start(bf16[384,128]{1,0:T(8,128)(2,1)S(1)} %get-tuple-element.37), channel_id=1, source_target_pairs={{0,16},{4,20},{8,24},{12,28},{16,0},{20,4},{24,8},{28,12},{1,17},{... | collective-permute-start | bytes 294920 | tf_op jit(solution)/shard_map/ppermute | solution.py:117
  69.9 5.6 %collective-permute-start.23 = (bf16[384,128]{1,0:T(8,128)(2,1)S(1)}, bf16[384,128]{1,0:T(8,128)(2,1)S(1)}, u32[]{:S(2)}, u32[]{:S(2)}) collective-permute-start(bf16[384,128]{1,0:T(8,128)(2,1)S(1)} %get-tuple-element.38), channel_id=1, source_target_pairs={{0,8},{4,12},{8,0},{12,4},{16,24},{20,28},{24,16},{28,20},{1,9},{5... | collective-permute-start | bytes 294920 | tf_op jit(solution)/shard_map/ppermute | solution.py:117
  75.7 11.2 %collective-permute-start.24 = (bf16[384,512]{1,0:T(8,128)(2,1)S(1)}, bf16[384,512]{1,0:T(8,128)(2,1)S(1)}, u32[]{:S(2)}, u32[]{:S(2)}) collective-permute-start(bf16[384,512]{1,0:T(8,128)(2,1)S(1)} %pad_maximum_fusion.own), channel_id=1, source_target_pairs={{0,1},{1,0},{2,3},{3,2},{4,5},{5,4},{6,7},{7,6},{8,9},{9,8},{10,11... | collective-permute-start | bytes 1179656 | tf_op jit(solution)/shard_map/ppermute | solution.py:121
  78.0 9.6 %collective-permute-start.28 = (bf16[256,512]{1,0:T(8,128)(2,1)S(1)}, bf16[256,512]{1,0:T(8,128)(2,1)S(1)}, u32[]{:S(2)}, u32[]{:S(2)}) collective-permute-start(bf16[256,512]{1,0:T(8,128)(2,1)S(1)} %copy-done.1), channel_id=1, source_target_pairs={{0,8},{4,12},{8,0},{12,4},{16,24},{20,28},{24,16},{28,20},{1,9},{5... | collective-permute-start | bytes 786440 | tf_op jit(solution)/shard_map/ppermute | solution.py:117
  78.9 8.8 %collective-permute-start.29 = (bf16[256,512]{1,0:T(8,128)(2,1)S(1)}, bf16[256,512]{1,0:T(8,128)(2,1)S(1)}, u32[]{:S(2)}, u32[]{:S(2)}) collective-permute-start(bf16[256,512]{1,0:T(8,128)(2,1)S(1)} %copy-done.1), channel_id=1, source_target_pairs={{0,16},{4,20},{8,24},{12,28},{16,0},{20,4},{24,8},{28,12},{1,17},{... | collective-permute-start | bytes 786440 | tf_op jit(solution)/shard_map/ppermute | solution.py:117
  80.0 7.7 %collective-permute-start.27 = (bf16[384,512]{1,0:T(8,128)(2,1)S(1)}, bf16[384,512]{1,0:T(8,128)(2,1)S(1)}, u32[]{:S(2)}, u32[]{:S(2)}) collective-permute-start(bf16[384,512]{1,0:T(8,128)(2,1)S(1)} %pad_maximum_fusion.own), channel_id=1, source_target_pairs={{1,2},{2,1},{5,6},{6,5},{9,10},{10,9},{13,14},{14,13},{17,18},{18,... | collective-permute-start | bytes 1179656 | tf_op jit(solution)/shard_map/ppermute | solution.py:125
  80.7 9.6 %collective-permute-start.33 = (bf16[256,512]{1,0:T(8,128)(2,1)S(1)}, bf16[256,512]{1,0:T(8,128)(2,1)S(1)}, u32[]{:S(2)}, u32[]{:S(2)}) collective-permute-start(bf16[256,512]{1,0:T(8,128)(2,1)S(1)} %copy-done.1), channel_id=1, source_target_pairs={{0,4},{4,0},{8,12},{12,8},{16,20},{20,16},{24,28},{28,24},{1,5},{5... | collective-permute-start | bytes 786440 | tf_op jit(solution)/shard_map/ppermute | solution.py:117
  86.9 4.6 %collective-permute-start.25 = (bf16[384,512]{1,0:T(8,128)(2,1)S(1)}, bf16[384,512]{1,0:T(8,128)(2,1)S(1)}, u32[]{:S(2)}, u32[]{:S(2)}) collective-permute-start(bf16[384,512]{1,0:T(8,128)(2,1)S(1)} %collective-permute-done.24.near), channel_id=1, source_target_pairs={{1,2},{2,1},{5,6},{6,5},{9,10},{10,9},{13,14},{14,13},{17,18},{18,... | collective-permute-start | bytes 1179656 | tf_op jit(solution)/shard_map/ppermute | solution.py:125
  87.6 3.8 %collective-permute-start.34 = (bf16[256,512]{1,0:T(8,128)(2,1)S(1)}, bf16[256,512]{1,0:T(8,128)(2,1)S(1)}, u32[]{:S(2)}, u32[]{:S(2)}) collective-permute-start(bf16[256,512]{1,0:T(8,128)(2,1)S(1)} %collective-permute-done.28.x_ref.refs_1_), channel_id=1, source_target_pairs={{0,4},{4,0},{8,12},{12,8},{16,20},{20,16},{24,28},{28,24},{1,5},{5... | collective-permute-start | bytes 786440 | tf_op jit(solution)/shard_map/ppermute | solution.py:117
  87.8 15.9 %collective-permute-start.30 = (bf16[384,512]{1,0:T(8,128)(2,1)S(1)}, bf16[384,512]{1,0:T(8,128)(2,1)S(1)}, u32[]{:S(2)}, u32[]{:S(2)}) collective-permute-start(bf16[384,512]{1,0:T(8,128)(2,1)S(1)} %collective-permute-done.27.q1), channel_id=1, source_target_pairs={{1,0},{2,3},{5,4},{6,7},{9,8},{10,11},{13,12},{14,15},{17,16},{18,... | collective-permute-start | bytes 1179656 | tf_op jit(solution)/shard_map/ppermute | solution.py:129
  89.1 6.0 %collective-permute-start.31 = (bf16[128,512]{1,0:T(8,128)(2,1)S(1)}, bf16[128,512]{1,0:T(8,128)(2,1)S(1)}, u32[]{:S(2)}, u32[]{:S(2)}) collective-permute-start(bf16[128,512]{1,0:T(8,128)(2,1)S(1)} %get-tuple-element.45), channel_id=1, source_target_pairs={{0,8},{4,12},{8,0},{12,4},{16,24},{20,28},{24,16},{28,20},{1,9},{5... | collective-permute-start | bytes 393224 | tf_op jit(solution)/shard_map/ppermute | solution.py:117
  90.3 5.6 %collective-permute-start.32 = (bf16[128,512]{1,0:T(8,128)(2,1)S(1)}, bf16[128,512]{1,0:T(8,128)(2,1)S(1)}, u32[]{:S(2)}, u32[]{:S(2)}) collective-permute-start(bf16[128,512]{1,0:T(8,128)(2,1)S(1)} %get-tuple-element.46), channel_id=1, source_target_pairs={{0,16},{4,20},{8,24},{12,28},{16,0},{20,4},{24,8},{28,12},{1,17},{... | collective-permute-start | bytes 393224 | tf_op jit(solution)/shard_map/ppermute | solution.py:117
  91.4 6.7 %collective-permute-start.35 = (bf16[256,512]{1,0:T(8,128)(2,1)S(1)}, bf16[256,512]{1,0:T(8,128)(2,1)S(1)}, u32[]{:S(2)}, u32[]{:S(2)}) collective-permute-start(bf16[256,512]{1,0:T(8,128)(2,1)S(1)} %collective-permute-done.29.y_ref.refs_2_), channel_id=1, source_target_pairs={{0,4},{4,0},{8,12},{12,8},{16,20},{20,16},{24,28},{28,24},{1,5},{5... | collective-permute-start | bytes 786440 | tf_op jit(solution)/shard_map/ppermute | solution.py:117
  91.5 19.3 %collective-permute-start.26 = (bf16[384,512]{1,0:T(8,128)(2,1)S(1)}, bf16[384,512]{1,0:T(8,128)(2,1)S(1)}, u32[]{:S(2)}, u32[]{:S(2)}) collective-permute-start(bf16[384,512]{1,0:T(8,128)(2,1)S(1)} %collective-permute-done.25.q2), channel_id=1, source_target_pairs={{1,0},{2,3},{5,4},{6,7},{9,8},{10,11},{13,12},{14,15},{17,16},{18,... | collective-permute-start | bytes 1179656 | tf_op jit(solution)/shard_map/ppermute | solution.py:129
  95.0 3.1 %collective-permute-start.36 = (bf16[128,512]{1,0:T(8,128)(2,1)S(1)}, bf16[128,512]{1,0:T(8,128)(2,1)S(1)}, u32[]{:S(2)}, u32[]{:S(2)}) collective-permute-start(bf16[128,512]{1,0:T(8,128)(2,1)S(1)} %collective-permute-done.31.refs_3_), channel_id=1, source_target_pairs={{0,4},{4,0},{8,12},{12,8},{16,20},{20,16},{24,28},{28,24},{1,5},{5... | collective-permute-start | bytes 393224 | tf_op jit(solution)/shard_map/ppermute | solution.py:117
  95.9 2.2 %collective-permute-start.37 = (bf16[128,512]{1,0:T(8,128)(2,1)S(1)}, bf16[128,512]{1,0:T(8,128)(2,1)S(1)}, u32[]{:S(2)}, u32[]{:S(2)}) collective-permute-start(bf16[128,512]{1,0:T(8,128)(2,1)S(1)} %collective-permute-done.32.refs_4_), channel_id=1, source_target_pairs={{0,4},{4,0},{8,12},{12,8},{16,20},{20,16},{24,28},{28,24},{1,5},{5... | collective-permute-start | bytes 393224 | tf_op jit(solution)/shard_map/ppermute | solution.py:117
